TPU v7x, 32 devices: a whole 2x2x4 slice. The times are simulated.
32 devices in a mesh: dp: 8 (over z, y), fsdp: 4 (over x, core).
Axes of the slice: x: 2, y: 2, z: 4, core: 2. Of those that a mesh axis runs over, the one named last changes fastest.
Arguments:
- tokens: bfloat16 [16384, 1024], P(('dp', 'fsdp')), may hold values from -6 to 6
- seq_lengths: int32 [32, 4], P(('dp', 'fsdp')), may hold values from 0 to 512, as said below
- w_query: bfloat16 [1024, 256], P(('dp', 'fsdp')), may hold values from -0.1875 to 0.1875
- w_key: bfloat16 [1024, 256], P(('dp', 'fsdp')), may hold values from -0.1875 to 0.1875
- w_value: bfloat16 [1024, 1024], P(('dp', 'fsdp')), may hold values from -0.1875 to 0.1875
- w_output: bfloat16 [1024, 1024], P(None, ('dp', 'fsdp')), may hold values from -2 to 2
- w_gate: bfloat16 [1024, 2752], P(('dp', 'fsdp')), may hold values from -0.1875 to 0.1875
- w_up: bfloat16 [1024, 2752], P(('dp', 'fsdp')), may hold values from -0.1875 to 0.1875
- w_down: bfloat16 [2752, 1024], P(None, ('dp', 'fsdp')), may hold values from -0.15625 to 0.15625
- gain_attn: float32 [1024], P(('dp', 'fsdp')), may hold values from 0.1 to 1.9
- gain_mlp: float32 [1024], P(('dp', 'fsdp')), may hold values from 0.1 to 1.9
- cotangent: bfloat16 [16384, 1024], P(('dp', 'fsdp')), may hold values from -6 to 6
Outputs:
- layer_out: bfloat16 [16384, 1024], P(('dp', 'fsdp'))
- grad_tokens: bfloat16 [16384, 1024], P(('dp', 'fsdp'))
- grad_query: float32 [1024, 256], P(('dp', 'fsdp'))
- grad_key: float32 [1024, 256], P(('dp', 'fsdp'))
- grad_value: float32 [1024, 1024], P(('dp', 'fsdp'))
- grad_output: float32 [1024, 1024], P(None, ('dp', 'fsdp'))
- grad_gate: float32 [1024, 2752], P(('dp', 'fsdp'))
- grad_up: float32 [1024, 2752], P(('dp', 'fsdp'))
- grad_down: float32 [2752, 1024], P(None, ('dp', 'fsdp'))
- grad_gain_attn: float32 [1024], P(('dp', 'fsdp'))
- grad_gain_mlp: float32 [1024], P(('dp', 'fsdp'))
Inputs may be any that keep to these rules, and one draw needn't show every extreme that they name: `seq_lengths`: row r lists the lengths of the sequences packed back to back from position 0 of buffer r; a length is 0 (an unused slot) or 128 or more, a row sums to at most 512, and positions past the sum are padding.
All inputs are finite; a program needn't handle non-finite values.
Results may differ from a plain program's by a relative error of at most 0.034.
Values may be sent and summed in bfloat16 or wider, within the bound.
No kernel may reach another device: no remote copies, remote signals or barrier semaphores. Data moves between devices by JAX's collectives and lax.ppermute only.
A program may use at most 192 MiB of HBM per device.

v0:
```python
import math

import jax
import jax.numpy as jnp
from jax import lax
from jax.sharding import PartitionSpec as P

H = 16
F = 16


EPS = 1e-05
GROUP_HEADS = 4


def head_major(values, group_count):
    rows = values.shape[0]
    return values.reshape(rows, group_count, GROUP_HEADS, -1).transpose(1, 0, 2, 3)


def row_major(values):
    return values.transpose(1, 0, 2, 3).reshape(values.shape[1], -1)


def norm_back(grad_normed, inputs, inverse, gain):
    scaled = grad_normed * gain
    grad_inputs = inverse * scaled - inputs * inverse**3 * jnp.mean(
        scaled * inputs, axis=-1, keepdims=True
    )
    grad_gain = jnp.sum(grad_normed * inputs * inverse, axis=0)
    return (grad_inputs, grad_gain)


def attend_group(query_g, key_g, mask_block, pad_block, scale):
    scores = jnp.einsum("thf,shf->hts", query_g, key_g, preferred_element_type=jnp.float32) * scale
    raw_weights = (1.0 + scores + 0.5 * scores * scores) * mask_block[None]
    totals = jnp.sum(raw_weights, axis=-1, keepdims=True) + pad_block[None, :, None]
    return (scores, raw_weights, totals)


def local(
    tokens,
    seq_lengths,
    w_query,
    w_key,
    w_value,
    w_output,
    w_gate,
    w_up,
    w_down,
    gain_attn,
    gain_mlp,
    cotangent,
):
    output_shard = w_output.T
    down_shard = w_down.T
    gathered = (
        lax.all_gather(w_query, ("dp", "fsdp"), axis=0, tiled=True),
        lax.all_gather(w_key, ("dp", "fsdp"), axis=0, tiled=True),
        lax.all_gather(w_value, ("dp", "fsdp"), axis=0, tiled=True),
        lax.all_gather(output_shard, ("dp", "fsdp"), axis=0, tiled=True),
        lax.all_gather(w_gate, ("dp", "fsdp"), axis=0, tiled=True),
        lax.all_gather(w_up, ("dp", "fsdp"), axis=0, tiled=True),
        lax.all_gather(down_shard, ("dp", "fsdp"), axis=0, tiled=True),
        lax.all_gather(gain_attn.astype(jnp.bfloat16), ("dp", "fsdp"), axis=0, tiled=True).astype(
            gain_attn.dtype
        ),
        lax.all_gather(gain_mlp.astype(jnp.bfloat16), ("dp", "fsdp"), axis=0, tiled=True).astype(
            gain_mlp.dtype
        ),
    )
    query_w, key_w, value_w, output_t, gate_w, up_w, down_t, gain_one, gain_two = gathered
    output_w = output_t.T
    down_w = down_t.T
    rows = tokens.shape[0]
    block_rows = min(512, rows)
    group_count = H // GROUP_HEADS
    scale = 1.0 / math.sqrt(F)
    positions = jnp.arange(rows, dtype=jnp.int32)
    ends = jnp.cumsum(seq_lengths[0], dtype=jnp.int32)
    segment = jnp.sum((positions[:, None] >= ends[None, :]).astype(jnp.int32), axis=1)
    valid_rows = (positions < ends[-1]).astype(jnp.float32)

    def block_mask(block_index):
        start = block_index * block_rows
        stop = start + block_rows
        allowed = (positions[None, :stop] <= positions[start:stop, None]) & (
            segment[None, :stop] == segment[start:stop, None]
        )
        return (allowed.astype(jnp.float32) * valid_rows[start:stop, None], 1.0 - valid_rows)

    tokens_f = tokens.astype(jnp.float32)
    inverse_one = lax.rsqrt(jnp.mean(tokens_f * tokens_f, axis=-1, keepdims=True) + EPS)
    normed_one = (tokens_f * inverse_one * gain_one).astype(jnp.bfloat16)
    queries = jnp.dot(normed_one, query_w, preferred_element_type=jnp.float32).astype(jnp.bfloat16)
    key_rows = jnp.dot(normed_one, key_w, preferred_element_type=jnp.float32).astype(jnp.bfloat16)
    value_rows = jnp.dot(normed_one, value_w, preferred_element_type=jnp.float32).astype(
        jnp.bfloat16
    )
    query_groups = head_major(queries, group_count)
    key_groups = head_major(key_rows, group_count)
    value_groups = head_major(value_rows, group_count)
    block_index = 0
    start = block_index * block_rows
    stop = start + block_rows
    mask_block, pad_block = block_mask(block_index)

    def forward_group(items):
        query_g, key_g, value_g = items
        scores, raw_weights, totals = attend_group(query_g, key_g, mask_block, pad_block, scale)
        probs = (raw_weights / totals).astype(jnp.bfloat16)
        return jnp.einsum("hts,shd->thd", probs, value_g, preferred_element_type=jnp.float32)

    mixed_block = lax.map(forward_group, (query_groups, key_groups, value_groups))
    mixed_parts = row_major(mixed_block)
    mixed = mixed_parts.astype(jnp.bfloat16)
    resid = tokens_f + jnp.dot(mixed, output_w, preferred_element_type=jnp.float32)
    inverse_two = lax.rsqrt(jnp.mean(resid * resid, axis=-1, keepdims=True) + EPS)
    normed_two = (resid * inverse_two * gain_two).astype(jnp.bfloat16)
    gate = jnp.dot(normed_two, gate_w, preferred_element_type=jnp.float32)
    upper = jnp.dot(normed_two, up_w, preferred_element_type=jnp.float32)
    silu_gate = jax.nn.silu(gate)
    hidden = (silu_gate * upper).astype(jnp.bfloat16)
    layer_out = (resid + jnp.dot(hidden, down_w, preferred_element_type=jnp.float32)).astype(
        jnp.bfloat16
    )
    regathered = (
        lax.all_gather(w_query, ("dp", "fsdp"), axis=0, tiled=True),
        lax.all_gather(w_key, ("dp", "fsdp"), axis=0, tiled=True),
        lax.all_gather(w_value, ("dp", "fsdp"), axis=0, tiled=True),
        lax.all_gather(output_shard, ("dp", "fsdp"), axis=0, tiled=True),
        lax.all_gather(w_gate, ("dp", "fsdp"), axis=0, tiled=True),
        lax.all_gather(w_up, ("dp", "fsdp"), axis=0, tiled=True),
        lax.all_gather(down_shard, ("dp", "fsdp"), axis=0, tiled=True),
        lax.all_gather(gain_attn.astype(jnp.bfloat16), ("dp", "fsdp"), axis=0, tiled=True).astype(
            gain_attn.dtype
        ),
        lax.all_gather(gain_mlp.astype(jnp.bfloat16), ("dp", "fsdp"), axis=0, tiled=True).astype(
            gain_mlp.dtype
        ),
    )
    query_w, key_w, value_w, output_t, gate_w, up_w, down_t, gain_one, gain_two = regathered
    output_w = output_t.T
    down_w = down_t.T
    grad_out_f = cotangent.astype(jnp.float32)
    grad_down_t = jnp.einsum("td,tf->df", cotangent, hidden, preferred_element_type=jnp.float32)
    grad_hidden = (
        jnp.einsum("td,fd->tf", cotangent, down_w, preferred_element_type=jnp.float32)
        .astype(jnp.bfloat16)
        .astype(jnp.float32)
    )
    sigmoid_gate = jax.nn.sigmoid(gate)
    grad_gate_rows = (
        grad_hidden * upper * sigmoid_gate * (1.0 + gate * (1.0 - sigmoid_gate))
    ).astype(jnp.bfloat16)
    grad_up_rows = (grad_hidden * silu_gate).astype(jnp.bfloat16)
    grad_gate_w = jnp.einsum(
        "td,tf->df", normed_two, grad_gate_rows, preferred_element_type=jnp.float32
    )
    grad_up_w = jnp.einsum(
        "td,tf->df", normed_two, grad_up_rows, preferred_element_type=jnp.float32
    )
    grad_normed_two = jnp.einsum(
        "tf,df->td", grad_gate_rows, gate_w, preferred_element_type=jnp.float32
    )
    grad_normed_two = grad_normed_two + jnp.einsum(
        "tf,df->td", grad_up_rows, up_w, preferred_element_type=jnp.float32
    )
    grad_resid_norm, grad_gain_two = norm_back(grad_normed_two, resid, inverse_two, gain_two)
    grad_resid = grad_out_f + grad_resid_norm
    grad_proj_out = grad_resid.astype(jnp.bfloat16)
    grad_output_t = jnp.einsum(
        "td,tv->dv", grad_proj_out, mixed, preferred_element_type=jnp.float32
    )
    grad_mixed = jnp.einsum(
        "td,vd->tv", grad_proj_out, output_w, preferred_element_type=jnp.float32
    ).astype(jnp.bfloat16)
    grad_groups = head_major(grad_mixed, group_count)
    grad_key_total = jnp.zeros(key_groups.shape, jnp.float32)
    grad_value_total = jnp.zeros(value_groups.shape, jnp.float32)
    block_index = 0
    start = block_index * block_rows
    stop = start + block_rows
    mask_block, pad_block = block_mask(block_index)

    def backward_group(items):
        query_g, key_g, value_g, grad_g = items
        scores, raw_weights, totals = attend_group(query_g, key_g, mask_block, pad_block, scale)
        probs_f = raw_weights / totals
        probs_b = probs_f.astype(jnp.bfloat16)
        grad_probs = jnp.einsum("thd,shd->hts", grad_g, value_g, preferred_element_type=jnp.float32)
        grad_raw = (grad_probs - jnp.sum(grad_probs * probs_f, axis=-1, keepdims=True)) / totals
        grad_scores = (grad_raw * mask_block[None] * (1.0 + scores)).astype(jnp.bfloat16)
        grad_query_g = (
            jnp.einsum("hts,shf->thf", grad_scores, key_g, preferred_element_type=jnp.float32)
            * scale
        )
        grad_key_g = (
            jnp.einsum("hts,thf->shf", grad_scores, query_g, preferred_element_type=jnp.float32)
            * scale
        )
        grad_value_g = jnp.einsum(
            "hts,thd->shd", probs_b, grad_g, preferred_element_type=jnp.float32
        )
        return (grad_query_g, grad_key_g, grad_value_g)

    block_query, block_key, block_value = lax.map(
        backward_group, (query_groups, key_groups, value_groups, grad_groups)
    )
    grad_key_total = grad_key_total.at[:, :stop].add(block_key)
    grad_value_total = grad_value_total.at[:, :stop].add(block_value)
    grad_queries = row_major(block_query).astype(jnp.bfloat16)
    grad_keys = row_major(grad_key_total).astype(jnp.bfloat16)
    grad_values = row_major(grad_value_total).astype(jnp.bfloat16)
    grad_query_w = jnp.einsum(
        "td,tf->df", normed_one, grad_queries, preferred_element_type=jnp.float32
    )
    grad_key_w = jnp.einsum("td,tf->df", normed_one, grad_keys, preferred_element_type=jnp.float32)
    grad_value_w = jnp.einsum(
        "td,tf->df", normed_one, grad_values, preferred_element_type=jnp.float32
    )
    grad_normed_one = jnp.einsum(
        "tf,df->td", grad_queries, query_w, preferred_element_type=jnp.float32
    )
    grad_normed_one = grad_normed_one + jnp.einsum(
        "tf,df->td", grad_keys, key_w, preferred_element_type=jnp.float32
    )
    grad_normed_one = grad_normed_one + jnp.einsum(
        "tf,df->td", grad_values, value_w, preferred_element_type=jnp.float32
    )
    grad_tokens_norm, grad_gain_one = norm_back(grad_normed_one, tokens_f, inverse_one, gain_one)
    grad_input = (grad_resid + grad_tokens_norm).astype(jnp.bfloat16)
    summed_all = (
        lax.psum_scatter(grad_query_w, ("dp", "fsdp"), scatter_dimension=0, tiled=True),
        lax.psum_scatter(grad_key_w, ("dp", "fsdp"), scatter_dimension=0, tiled=True),
        lax.psum_scatter(grad_value_w, ("dp", "fsdp"), scatter_dimension=0, tiled=True),
        lax.psum_scatter(grad_output_t, ("dp", "fsdp"), scatter_dimension=0, tiled=True),
        lax.psum_scatter(grad_gate_w, ("dp", "fsdp"), scatter_dimension=0, tiled=True),
        lax.psum_scatter(grad_up_w, ("dp", "fsdp"), scatter_dimension=0, tiled=True),
        lax.psum_scatter(grad_down_t, ("dp", "fsdp"), scatter_dimension=0, tiled=True),
        lax.psum_scatter(grad_gain_one, ("dp", "fsdp"), scatter_dimension=0, tiled=True),
        lax.psum_scatter(grad_gain_two, ("dp", "fsdp"), scatter_dimension=0, tiled=True),
    )
    return (
        layer_out,
        grad_input,
        summed_all[0],
        summed_all[1],
        summed_all[2],
        summed_all[3].T,
        summed_all[4],
        summed_all[5],
        summed_all[6].T,
        summed_all[7],
        summed_all[8],
    )


def solution(mesh):
    return jax.shard_map(
        local,
        mesh=mesh,
        in_specs=(
            P(("dp", "fsdp"), None),
            P(("dp", "fsdp"), None),
            P(("dp", "fsdp"), None),
            P(("dp", "fsdp"), None),
            P(("dp", "fsdp"), None),
            P(None, ("dp", "fsdp")),
            P(("dp", "fsdp"), None),
            P(("dp", "fsdp"), None),
            P(None, ("dp", "fsdp")),
            P(("dp", "fsdp")),
            P(("dp", "fsdp")),
            P(("dp", "fsdp"), None),
        ),
        out_specs=(
            P(("dp", "fsdp"), None),
            P(("dp", "fsdp"), None),
            P(("dp", "fsdp"), None),
            P(("dp", "fsdp"), None),
            P(("dp", "fsdp"), None),
            P(None, ("dp", "fsdp")),
            P(("dp", "fsdp"), None),
            P(("dp", "fsdp"), None),
            P(None, ("dp", "fsdp")),
            P(("dp", "fsdp")),
            P(("dp", "fsdp")),
        ),
        check_vma=False,
    )
```

profile of v0, /device:TPU:0, one launch (start us, length us, event | category | flops | bytes accessed | tf_op | source)
XLA Modules:
  0.0 1475.6 jit_solution(11849581055380983294)
XLA Ops:
  12.3 42.0 %all-reduce.5 = (bf16[1024]{0:T(1024)(128)(2,1)S(1)}, bf16[1024]{0:T(1024)(128)(2,1)S(1)}) all-reduce(bf16[1024]{0:T(1024)(128)(2,1)S(1)} %dynamic-update-slice.4, bf16[1024]{0:T(1024)(128)(2,1)S(1)} %dynamic-update-slice.5), channel_id=1, replica_groups=mesh['dp'=8,'fsdp'=4] {'dp','fsdp'}, use_global_device_ids=true, to_apply=%add | all-reduce | flops 2048 | bytes 8192
  58.8 42.3 %all_gather.38 = bf16[1024,256]{1,0:T(8,128)(2,1)S(1)} all-gather(bf16[32,256]{1,0:T(8,128)(2,1)} %param.26), channel_id=1, replica_groups=mesh['dp'=8,'fsdp'=4] {'dp','fsdp'}, dimensions={0}, use_global_device_ids=true | all-gather | bytes 540672 | tf_op jit(solution)/shard_map/all_gather | solution.py:58
  101.1 38.6 %all_gather.39 = bf16[1024,256]{1,0:T(8,128)(2,1)S(1)} all-gather(bf16[32,256]{1,0:T(8,128)(2,1)} %param.27), channel_id=1, replica_groups=mesh['dp'=8,'fsdp'=4] {'dp','fsdp'}, dimensions={0}, use_global_device_ids=true | all-gather | bytes 540672 | tf_op jit(solution)/shard_map/all_gather | solution.py:59
  147.9 17.4 %while.34 = (s32[]{:T(128)}, bf16[4,512,4,64]{1,3,2,0:T(8,128)(2,1)S(1)}, bf16[4,512,4,64]{1,3,2,0:T(8,128)(2,1)S(1)}, bf16[4,512,4,16]{1,3,2,0:T(8,128)(2,1)}, ...) while((s32[]{:T(128)}, ...), condition=%wide.region_5.6_spmd.clone, body=%wide.region_3.5_spmd.clone.sunk | while | flops 184550912 | bytes 12494953 | solution.py:114
  170.3 28.3 %all-gather.14.cloned.1.call-done = bf16[1024,2752]{1,0:T(8,128)(2,1)} async-done(((bf16[32,2752]{1,0:T(8,128)(2,1)}), bf16[1024,2752]{1,0:T(8,128)(2,1)}) %all-gather.14.cloned.1.call-update) | async-done | bytes 5636112 | tf_op jit(solution)/shard_map/all_gather | solution.py:64
  198.6 7.7 convolution_convert_fusion
  206.2 61.3 %all-gather.10.cloned.1.call-done = bf16[1024,2752]{1,0:T(8,128)(2,1)} async-done(((bf16[32,2752]{1,0:T(8,128)(2,1)}), bf16[1024,2752]{1,0:T(8,128)(2,1)}) %all-gather.10.cloned.1.call-update) | async-done | bytes 5636112 | tf_op jit(solution)/shard_map/all_gather | solution.py:62
  267.6 9.0 fusion.143
  276.6 59.9 %all-gather.12.cloned.1.call-done = bf16[1024,2752]{1,0:T(8,128)(2,1)} async-done(((bf16[32,2752]{1,0:T(8,128)(2,1)}), bf16[1024,2752]{1,0:T(8,128)(2,1)}) %all-gather.12.cloned.1.call-update) | async-done | bytes 5636112 | tf_op jit(solution)/shard_map/all_gather | solution.py:63
  336.5 12.1 fusion.114
  353.8 7.2 multiply_reduce_fusion.1
  367.1 90.5 %while.35 = (s32[]{:T(128)}, bf16[4,512,4,16]{1,3,2,0:T(8,128)(2,1)}, bf16[4,512,4,16]{1,3,2,0:T(8,128)(2,1)S(1)}, bf16[4,512,4,64]{1,3,2,0:T(8,128)(2,1)}, bf16...) while((s32[]{:T(128)}, ...), condition=%wide.region_11.12_spmd.clone, body=%wide.region_8.11_spmd.clone.sunk | while | flops 820058624 | bytes 35995776 | solution.py:207
  372.1 7.0 fusion.227
  379.1 6.5 fusion.228
  394.7 6.9 fusion.227
  417.2 7.0 fusion.227
  424.2 6.5 fusion.228
  439.8 7.0 fusion.227
  446.8 6.5 fusion.228
  473.3 9.7 fusion.147
  483.0 11.3 fusion.140
  494.6 9.3 convolution_bitcast_fusion
  503.9 11.9 copy.55
  523.0 39.9 %all-reduce.4 = (f32[1024]{0:T(1024)S(1)}, f32[1024]{0:T(1024)S(1)}) all-reduce(f32[1024]{0:T(1024)S(1)} %get-tuple-element.367, f32[1024]{0:T(1024)S(1)} %copy-done.16), channel_id=9, replica_groups=mesh['dp'=8,'fsdp'=4] {'dp','fsdp'}, use_global_device_ids=true, to_apply=%region_21.22.clone | all-reduce | flops 2048 | bytes 16384
  567.6 6.8 add_convert_fusion
  574.4 20.2 %reduce-scatter.10.cloned.1.call-done = f32[32,256]{1,0:T(8,128)} async-done(((f32[1024,256]{1,0:T(8,128)}), f32[32,256]{1,0:T(8,128)}) %reduce-scatter.10.cloned.1.call-update) | async-done | bytes 32784 | tf_op jit(solution)/shard_map/reduce_scatter | solution.py:234
  594.7 133.7 %reduce-scatter.12.cloned.1.call-done = f32[32,256]{1,0:T(8,128)} async-done(((f32[1024,256]{1,0:T(8,128)}), f32[32,256]{1,0:T(8,128)}) %reduce-scatter.12.cloned.1.call-update) | async-done | bytes 32784 | tf_op jit(solution)/shard_map/reduce_scatter | solution.py:235
  728.3 139.6 %reduce-scatter.14.cloned.1.call-done = f32[32,1024]{1,0:T(8,128)} async-done(((f32[1024,1024]{1,0:T(8,128)}), f32[32,1024]{1,0:T(8,128)}) %reduce-scatter.14.cloned.1.call-update) | async-done | bytes 131088 | tf_op jit(solution)/shard_map/reduce_scatter | solution.py:236
  868.0 139.6 %reduce-scatter.16.cloned.1.call-done = f32[32,1024]{1,0:T(8,128)} async-done(((f32[1024,1024]{1,0:T(8,128)}), f32[32,1024]{1,0:T(8,128)}) %reduce-scatter.16.cloned.1.call-update) | async-done | bytes 131088 | tf_op jit(solution)/shard_map/reduce_scatter | solution.py:237
  1007.6 153.8 %reduce-scatter.18.cloned.1.call-done = f32[32,2752]{1,0:T(8,128)} async-done(((f32[1024,2752]{1,0:T(8,128)}), f32[32,2752]{1,0:T(8,128)}) %reduce-scatter.18.cloned.1.call-update) | async-done | bytes 352272 | tf_op jit(solution)/shard_map/reduce_scatter | solution.py:238
  1161.4 153.7 %reduce-scatter.20.cloned.1.call-done = f32[32,2752]{1,0:T(8,128)} async-done(((f32[1024,2752]{1,0:T(8,128)}), f32[32,2752]{1,0:T(8,128)}) %reduce-scatter.20.cloned.1.call-update) | async-done | bytes 352272 | tf_op jit(solution)/shard_map/reduce_scatter | solution.py:239
  1315.1 153.4 %reduce-scatter.22.cloned.1.call-done = f32[32,2752]{1,0:T(8,128)} async-done(((f32[1024,2752]{1,0:T(8,128)}), f32[32,2752]{1,0:T(8,128)}) %reduce-scatter.22.cloned.1.call-update) | async-done | bytes 352272
  (150 shorter events, 121.5 us)
Async XLA Ops:
  7.2 135.3 %copy-start = (bf16[512,1024]{1,0:T(8,128)(2,1)S(1)}, bf16[512,1024]{1,0:T(8,128)(2,1)}, u32[]{:S(2)}) copy-start(bf16[512,1024]{1,0:T(8,128)(2,1)} %param.24) | copy-start | bytes 3145732
  7.2 136.6 %all-gather.6.cloned.1.call-start = ((), (), s32[]{:S(2)}) async-start(), calls=%async_computation.7 | async-start | bytes 2162688 | tf_op jit(solution)/shard_map/all_gather | solution.py:60
  7.9 157.4 %all-gather.8.cloned.1.call-start = ((), (), s32[]{:S(2)}) async-start(), calls=%async_computation.8 | async-start | bytes 2162688 | tf_op jit(solution)/shard_map/all_gather | solution.py:61
  8.7 189.9 %all-gather.14.cloned.1.call-start = ((), (), s32[]{:S(2)}) async-start(), calls=%async_computation.11 | async-start | bytes 5947392 | tf_op jit(solution)/shard_map/all_gather | solution.py:64
  9.4 258.2 %all-gather.10.cloned.1.call-start = ((), (), s32[]{:S(2)}) async-start(), calls=%async_computation.9 | async-start | bytes 5947392 | tf_op jit(solution)/shard_map/all_gather | solution.py:62
  10.0 326.5 %all-gather.12.cloned.1.call-start = ((), (), s32[]{:S(2)}) async-start(), calls=%async_computation.10 | async-start | bytes 5947392 | tf_op jit(solution)/shard_map/all_gather | solution.py:63
  10.6 584.1 %reduce-scatter.10.cloned.1.call-start = ((), (), s32[]{:S(2)}) async-start(), calls=%async_computation.12 | async-start | bytes 1081344 | tf_op jit(solution)/shard_map/reduce_scatter | solution.py:234
  54.4 89.4 %copy-start.11 = (f32[1024]{0:T(1024)}, f32[1024]{0:T(1024)S(1)}, u32[]{:S(2)}) copy-start(f32[1024]{0:T(1024)S(1)} %convert_element_type.132) | copy-start | bytes 12292
  58.8 85.0 %copy-start.13 = (f32[512]{0:T(512)}, f32[512]{0:T(512)S(1)}, u32[]{:S(2)}) copy-start(f32[512]{0:T(512)S(1)} %get-tuple-element.418) | copy-start | bytes 6148
  101.1 38.6 %copy-start.7 = (bf16[1024,256]{1,0:T(8,128)(2,1)}, bf16[1024,256]{1,0:T(8,128)(2,1)S(1)}, u32[]{:S(2)}) copy-start(bf16[1024,256]{1,0:T(8,128)(2,1)S(1)} %all_gather.38) | copy-start | bytes 1572868
  139.7 2.8 copy-start.5
  165.3 1.3 copy-start.10
  170.0 183.8 %copy-start.2 = (f32[512,1024]{1,0:T(8,128)}, f32[512,1024]{1,0:T(8,128)S(1)}, u32[]{:S(2)}) copy-start(f32[512,1024]{1,0:T(8,128)S(1)} %get-tuple-element.422) | copy-start | bytes 6291460
  170.3 166.2 %copy-start.9 = (bf16[512,1024]{1,0:T(8,128)(2,1)}, bf16[512,1024]{1,0:T(8,128)(2,1)S(1)}, u32[]{:S(2)}) copy-start(bf16[512,1024]{1,0:T(8,128)(2,1)S(1)} %multiply_convert_fusion.2) | copy-start | bytes 3145732
  336.5 12.1 copy-start.17
  348.7 5.2 copy-start.18
  353.8 7.2 copy-start.8
  361.0 2.3 copy-start.19
  367.0 90.5 %copy-start.12 = (f32[1024]{0:T(1024)S(1)}, f32[1024]{0:T(1024)}, u32[]{:S(2)}) copy-start(f32[1024]{0:T(1024)} %copy-done.11) | copy-start | bytes 12292
  367.1 90.5 %copy-start.14 = (f32[512]{0:T(512)S(1)}, f32[512]{0:T(512)}, u32[]{:S(2)}) copy-start(f32[512]{0:T(512)} %copy-done.13) | copy-start | bytes 6148
  457.5 6.0 copy-start.1
  460.5 267.8 %reduce-scatter.12.cloned.1.call-start = ((), (), s32[]{:S(2)}) async-start(), calls=%async_computation.13 | async-start | bytes 1081344 | tf_op jit(solution)/shard_map/reduce_scatter | solution.py:235
  463.5 404.5 %reduce-scatter.14.cloned.1.call-start = ((), (), s32[]{:S(2)}) async-start(), calls=%async_computation.14 | async-start | bytes 4325376 | tf_op jit(solution)/shard_map/reduce_scatter | solution.py:236
  468.2 539.4 %reduce-scatter.16.cloned.1.call-start = ((), (), s32[]{:S(2)}) async-start(), calls=%async_computation.15 | async-start | bytes 4325376 | tf_op jit(solution)/shard_map/reduce_scatter | solution.py:237
  472.8 688.6 %reduce-scatter.18.cloned.1.call-start = ((), (), s32[]{:S(2)}) async-start(), calls=%async_computation.16 | async-start | bytes 11894784 | tf_op jit(solution)/shard_map/reduce_scatter | solution.py:238
  483.0 832.1 %reduce-scatter.20.cloned.1.call-start = ((), (), s32[]{:S(2)}) async-start(), calls=%async_computation.17 | async-start | bytes 11894784 | tf_op jit(solution)/shard_map/reduce_scatter | solution.py:239
  494.4 974.1 %reduce-scatter.22.cloned.1.call-start = ((), (), s32[]{:S(2)}) async-start(), calls=%async_computation.18 | async-start | bytes 11894784
  517.4 3.3 copy-start.6
  520.7 2.4 copy-start.16
  520.7 43.5 %copy-start.15 = (f32[512]{0:T(512)S(1)}, f32[512]{0:T(512)}, u32[]{:S(2)}) copy-start(f32[512]{0:T(512)} %get-tuple-element.417) | copy-start | bytes 6148
  563.0 4.6 copy-start.3
  563.0 4.6 copy-start.20
  (1 other events, 1.0 us)
Sparse Core Ops, SparseCore 0:
  10.9 59.1 all-gather.5
  73.0 56.1 all-gather.7
  132.0 66.5 all-gather.13
  201.3 66.2 all-gather.9
  270.2 66.2 all-gather.11
  460.6 133.9 reduce-scatter.9
  597.6 130.7 reduce-scatter.11
  731.2 136.7 reduce-scatter.13
  870.8 136.7 reduce-scatter.15
  1010.3 150.9 reduce-scatter.17
  1164.3 150.8 reduce-scatter.19
  1317.9 150.6 reduce-scatter.21
where the time goes:
time: 1480 us
  waiting for transfers between devices  1050 us (71%)
  matrix products  213 us (14%)
  blocking collectives  163 us (11%)
  local copies, waits for them, and re-layouts  19 us (1%)
  other arithmetic  18 us (1%)
    unnamed x13, waiting for transfers between devices  157 us
    reduce_scatter x1, waiting for transfers between devices, local(): lax.psum_scatter(grad_gate_w, ('dp', 'fsdp'), scatter_dimension=0, tiled=...  154 us
    reduce_scatter x1, waiting for transfers between devices, local(): lax.psum_scatter(grad_up_w, ('dp', 'fsdp'), scatter_dimension=0, tiled=True)  154 us
    reduce_scatter x1, waiting for transfers between devices, local(): lax.psum_scatter(grad_output_t, ('dp', 'fsdp'), scatter_dimension=0, tile...  140 us
    reduce_scatter x1, waiting for transfers between devices, local(): lax.psum_scatter(grad_value_w, ('dp', 'fsdp'), scatter_dimension=0, tiled...  140 us
    reduce_scatter x1, waiting for transfers between devices, local(): lax.psum_scatter(grad_key_w, ('dp', 'fsdp'), scatter_dimension=0, tiled=T...  134 us
    unnamed x2, blocking collectives  82 us
    all_gather x1, waiting for transfers between devices, local(): lax.all_gather(w_gate, ('dp', 'fsdp'), axis=0, tiled=True)  61.3 us
  transfers between devices with their start and end apart: 12, of which 10 were waited for; matrix products, arithmetic and copies ran while one was open for 8% of the time, Pallas kernels for 0%

commit v1 on v0

v1 whole, which is shorter than its diff:
```python
import functools
import math

import jax
import jax.numpy as jnp
from jax import lax
from jax.experimental import pallas as pl
from jax.experimental.pallas import tpu as pltpu
from jax.sharding import PartitionSpec as P

H = 16
F = 16
EPS = 1e-05
AXES = ("dp", "fsdp")
LANES = 128
VMEM_BYTES = 64000000
F32 = jnp.float32
BF16 = jnp.bfloat16

VMEM_SPEC = pl.BlockSpec(memory_space=pltpu.VMEM)
SMEM_SPEC = pl.BlockSpec(memory_space=pltpu.SMEM)
ANY_SPEC = pl.BlockSpec(memory_space=pl.ANY)


def dot_nn(a, b):
    return lax.dot_general(a, b, (((1,), (0,)), ((), ())), preferred_element_type=F32)


def dot_nt(a, b):
    return lax.dot_general(a, b, (((1,), (1,)), ((), ())), preferred_element_type=F32)


def dot_tn(a, b):
    return lax.dot_general(a, b, (((0,), (0,)), ((), ())), preferred_element_type=F32)


class Layout:
    def __init__(self, mesh):
        dp, fsdp = mesh.shape["dp"], mesh.shape["fsdp"]
        self.count = dp * fsdp
        x_bits = int(math.log2(fsdp)) - 1
        y_bits = int(math.log2(dp)) // 3
        all_bits = int(math.log2(self.count))
        self.x = [1 << (1 + i) for i in range(x_bits)]
        self.y = [1 << (1 + x_bits + i) for i in range(y_bits)]
        self.z = [1 << i for i in range(1 + x_bits + y_bits, all_bits)]

    def swap(self, value, bit):
        return lax.ppermute(value, AXES, [(i, i ^ bit) for i in range(self.count)])


def masks_of(bits):
    masks = [0]
    for bit in bits:
        masks = masks + [m | bit for m in masks]
    return masks


def gather(lay, block_own, block_other):
    found = {0: jnp.stack([block_own, block_other])}
    for bit in reversed(lay.z):
        found.update({m | bit: lay.swap(v, bit) for m, v in list(found.items())})
    z_masks = masks_of(lay.z)
    pieces = []
    for half, order in ((0, lay.x + lay.y), (1, lay.y + lay.x)):
        held = jnp.stack([found[m][half] for m in z_masks])
        masks = [m | half for m in z_masks]
        for bit in order[:-1]:
            came = lay.swap(held, bit)
            held = jnp.concatenate([held, came], axis=0)
            masks = masks + [m | bit for m in masks]
        pieces.append((held, masks))
        pieces.append((lay.swap(held, order[-1]), [m | order[-1] for m in masks]))
    return pieces


def scatter_masks(lay):
    z_masks = masks_of(lay.z)
    arrays = []
    for half, order in ((0, lay.x + lay.y), (1, lay.y + lay.x)):
        masks = [m | half for m in z_masks]
        for bit in order[:-1]:
            masks = masks + [m | bit for m in masks]
        arrays.append(masks)
        arrays.append([m | order[-1] for m in masks])
    return arrays


def add_low(a, b):
    return (a.astype(F32) + b.astype(F32)).astype(BF16)


def reduce_blocks(lay, arrays):
    ends = []
    for half, order in ((0, lay.x + lay.y), (1, lay.y + lay.x)):
        kept, sent = arrays[2 * half], arrays[2 * half + 1]
        came = lay.swap(sent, order[-1])
        for bit in reversed(order[:-1]):
            n = kept.shape[0] // 2
            sent = add_low(kept[n:], came[n:])
            kept = add_low(kept[:n], came[:n])
            came = lay.swap(sent, bit)
        ends.append((kept, came))
    z_masks = masks_of(lay.z)

    def block(i):
        return jnp.stack([kept[i].astype(F32) + came[i].astype(F32) for kept, came in ends])

    held = {m: block(i) for i, m in enumerate(z_masks)}
    for bit in lay.z:
        for m in [m for m in held if m & bit]:
            came = lay.swap(held.pop(m).astype(BF16), bit)
            held[m ^ bit] = held[m ^ bit] + came.astype(F32)
    return held[0]


class Blocks:
    def __init__(self, lay, rows):
        self.lay = lay
        self.rows = rows
        self.direct = rows % 16 == 0
        self.shape = (lay.count, rows) if self.direct else (1, lay.count * rows)

    def order(self, index):
        return jnp.bitwise_xor(index, jnp.arange(self.lay.count))

    def arrays(self, pieces, index):
        if self.direct:
            return [a for a, _ in pieces]
        masks = [m for _, ms in pieces for m in ms]
        whole = jnp.concatenate([a for a, _ in pieces], axis=0)
        place = [0] * len(masks)
        for i, m in enumerate(masks):
            place[m] = i
        whole = jnp.take(whole, jnp.asarray(place)[self.order(index)], axis=0)
        return [whole.reshape(1, -1, whole.shape[-1])]

    def copies_in(self, index, refs, masks, out_ref, sem):
        if not self.direct:
            return [pltpu.make_async_copy(refs[0], out_ref, sem)]
        return [
            pltpu.make_async_copy(
                ref.at[i], out_ref.at[jnp.bitwise_xor(index, m)], sem
            )
            for ref, ms in zip(refs, masks)
            for i, m in enumerate(ms)
        ]

    def out_shapes(self, masks, columns):
        if self.direct:
            return [jax.ShapeDtypeStruct((len(m), self.rows, columns), BF16) for m in masks]
        return [jax.ShapeDtypeStruct((1, self.lay.count * self.rows, columns), BF16)]

    def copies_out(self, index, in_ref, refs, masks, sem):
        if not self.direct:
            return [pltpu.make_async_copy(in_ref, refs[0], sem)]
        return [
            pltpu.make_async_copy(
                in_ref.at[jnp.bitwise_xor(index, m)], ref.at[i], sem
            )
            for ref, ms in zip(refs, masks)
            for i, m in enumerate(ms)
        ]

    def split(self, outs, masks, index):
        if self.direct:
            return outs
        whole = outs[0].reshape(self.lay.count, self.rows, -1)
        whole = jnp.take(whole, self.order(index), axis=0)
        return [jnp.take(whole, jnp.asarray(m), axis=0) for m in masks]


def start_all(copies):
    for copy in copies:
        copy.start()


def whole(ref):
    value = ref[...]
    return value.reshape(-1, value.shape[-1])


def cost(flops, moved):
    return pl.CostEstimate(flops=int(flops), bytes_accessed=int(moved), transcendentals=0)


def params():
    return pltpu.CompilerParams(vmem_limit_bytes=VMEM_BYTES)


def row_chunks(total, size, body):
    def step(i, carry):
        body(pl.ds(pl.multiple_of(i * size, size), size))
        return carry

    lax.fori_loop(0, total // size, step, 0)


def make_mask(seq_ref, b, mask_ref):
    rows, cols = mask_ref.shape
    slots = seq_ref.shape[1]
    ends = []
    total = jnp.int32(0)
    for j in range(slots):
        total = total + seq_ref[b, j]
        ends.append(total)

    def body(at):
        t = lax.broadcasted_iota(jnp.int32, (at.size, cols), 0) + at.start
        s = lax.broadcasted_iota(jnp.int32, (at.size, cols), 1)
        seg_t = jnp.zeros_like(t)
        seg_s = jnp.zeros_like(s)
        for e in ends:
            seg_t = seg_t + (t >= e).astype(jnp.int32)
            seg_s = seg_s + (s >= e).astype(jnp.int32)
        seen = (s <= t) & (seg_t == seg_s) & (t < total)
        mask_ref[at, :] = jnp.where(seen, 0.5, 0.0).astype(F32)

    row_chunks(rows, 64, body)
    return total


def attn_fwd(blk, masks, index, seq, tok, arrays, dims):
    n_tok, width, buffers = tok.shape[0], tok.shape[1], seq.shape[0]
    length = n_tok // buffers
    nq, nv, cols = dims
    n_qkv = 2 * nq + nv
    n_in = len(arrays)

    def body(index_ref, seq_ref, tok_ref, *refs):
        w_in = refs[:n_in]
        normed_ref, qkv_ref, y_ref, dinv_ref, part_ref, gain_ref, w_ref = refs[n_in : n_in + 7]
        mask_ref, sem = refs[n_in + 7 :]
        copies = blk.copies_in(index_ref[0], w_in, masks, w_ref, sem)
        start_all(copies)
        pltpu.make_async_copy(w_ref, w_ref, sem).wait()
        w_gain = w_ref[:, :, n_qkv + nv :].reshape(width, LANES).astype(F32).T
        gain_ref[0:1, :] = w_gain[0:1] + w_gain[1:2]
        gain_ref[1:2, :] = w_gain[2:3] + w_gain[3:4]
        gain_ref[2:8, :] = jnp.zeros((6, width), F32)
        gain = gain_ref[0:1, :]

        def project(at):
            x = tok_ref[at, :].astype(F32)
            inverse = lax.rsqrt(jnp.mean(x * x, axis=-1, keepdims=True) + EPS)
            normed = (x * inverse * gain).astype(BF16)
            normed_ref[at, :] = normed
            w = w_ref[:, :, :n_qkv].reshape(width, n_qkv)
            qkv_ref[at, :] = dot_nn(normed, w).astype(BF16)

        row_chunks(n_tok, 256, project)

        for b in range(buffers):
            total = make_mask(seq_ref, b, mask_ref)
            base = b * length

            def pair(hp, carry):
                lane = lax.broadcasted_iota(jnp.int32, (1, LANES), 1)
                k = qkv_ref[base : base + length, nq : 2 * nq]
                v_at = pl.ds(pl.multiple_of(2 * nq + hp * LANES, LANES), LANES)
                v = qkv_ref[base : base + length, v_at]
                step = length // 2
                for tb in range(2):
                    rows = slice(base + tb * step, base + (tb + 1) * step)
                    seen = (tb + 1) * step
                    q = qkv_ref[rows, :nq] * jnp.asarray(0.25, BF16)
                    mask = mask_ref[tb * step : (tb + 1) * step, :seen]
                    row = lax.broadcasted_iota(jnp.int32, (step, 1), 0) + tb * step
                    pad = (row >= total).astype(F32)
                    found = []
                    for j in range(2):
                        k_h = jnp.where(lane // F == 2 * hp + j, k[:seen], jnp.zeros((), BF16))
                        v_h = jnp.where(lane // 64 == j, v[:seen], jnp.ones((), BF16))
                        one = dot_nt(q, k_h) + 1.0
                        weights = ((one * one + 1.0) * mask).astype(BF16)
                        mixed = dot_nn(weights, v_h)
                        inverse = 1.0 / (pltpu.roll(mixed, 64, 1) + pad)
                        found.append((mixed * inverse, inverse))
                    low = lane < 64
                    y_at = pl.ds(pl.multiple_of(hp * LANES, LANES), LANES)
                    y_ref[rows, y_at] = jnp.where(low, found[0][0], found[1][0]).astype(BF16)
                    dinv_ref[rows, y_at] = jnp.where(low, found[0][1], found[1][1])
                return carry

            lax.fori_loop(0, nv // LANES, pair, 0)

        def output(at):
            w = w_ref[:, :, n_qkv : n_qkv + nv].reshape(width, nv)
            part_ref[at, :] = dot_nt(y_ref[at, :], w).astype(BF16)

        row_chunks(n_tok, 256, output)

    out = lambda *s, t=BF16: jax.ShapeDtypeStruct(s, t)
    return pl.pallas_call(
        body,
        name="attn_fwd",
        out_shape=(
            out(n_tok, width),
            out(n_tok, n_qkv),
            out(n_tok, nv),
            out(n_tok, nv, t=F32),
            out(n_tok, width),
            out(8, width, t=F32),
            out(*blk.shape, cols),
        ),
        in_specs=[SMEM_SPEC, SMEM_SPEC, VMEM_SPEC] + [ANY_SPEC] * n_in,
        out_specs=(VMEM_SPEC,) * 7,
        scratch_shapes=[pltpu.VMEM((length, length), F32), pltpu.SemaphoreType.DMA],
        compiler_params=params(),
        cost_estimate=cost(1.5e10, 1e7),
    )(index, seq, tok, *arrays)


def residual(tok, part, came, gains):
    n_tok, width = tok.shape
    half = n_tok // 2

    def body(tok_ref, part_ref, came_ref, gain_ref, hres_ref, normed_ref):
        gain = gain_ref[1:2, :]

        def rows(at, other):
            x = tok_ref[at, :].astype(F32)
            x = x + (part_ref[at, :].astype(F32) + came_ref[other, :].astype(F32))
            hres_ref[at, :] = x
            inverse = lax.rsqrt(jnp.mean(x * x, axis=-1, keepdims=True) + EPS)
            normed_ref[at, :] = (x * inverse * gain).astype(BF16)

        def step(i, carry):
            lo = pl.ds(pl.multiple_of(i * 128, 128), 128)
            hi = pl.ds(pl.multiple_of(half + i * 128, 128), 128)
            rows(lo, hi)
            rows(hi, lo)
            return carry

        lax.fori_loop(0, half // 128, step, 0)

    return pl.pallas_call(
        body,
        name="residual",
        out_shape=(
            jax.ShapeDtypeStruct((n_tok, width), F32),
            jax.ShapeDtypeStruct((n_tok, width), BF16),
        ),
        in_specs=[VMEM_SPEC] * 4,
        out_specs=(VMEM_SPEC,) * 2,
        compiler_params=params(),
        cost_estimate=cost(1e7, 1.2e7),
    )(tok, part, came, gains)


def down_back(blk, masks, index, grad_out, arrays, cols):
    n_tok, width = grad_out.shape
    n_in = len(arrays)

    def body(index_ref, grad_ref, *refs):
        d_act_ref, w_ref, sem = refs[n_in:]
        start_all(blk.copies_in(index_ref[0], refs[:n_in], masks, w_ref, sem))
        pltpu.make_async_copy(w_ref, w_ref, sem).wait()

        def rows(at):
            d_act_ref[at, :] = dot_nn(grad_ref[at, :], whole(w_ref)).astype(BF16)

        row_chunks(n_tok, 256, rows)

    return pl.pallas_call(
        body,
        name="down_back",
        out_shape=(
            jax.ShapeDtypeStruct((n_tok, cols), BF16),
            jax.ShapeDtypeStruct((*blk.shape, cols), BF16),
        ),
        in_specs=[SMEM_SPEC, VMEM_SPEC] + [ANY_SPEC] * n_in,
        out_specs=(VMEM_SPEC,) * 2,
        scratch_shapes=[pltpu.SemaphoreType.DMA],
        compiler_params=params(),
        cost_estimate=cost(2 * n_tok * width * cols, 1e7),
    )(index, grad_out, *arrays)


def gated(blk, masks, index, normed, d_act, gate_arrays, up_arrays, cols):
    n_tok, width = normed.shape
    n_in = len(gate_arrays)

    def body(index_ref, normed_ref, d_act_ref, *refs):
        gate_in, up_in = refs[:n_in], refs[n_in : 2 * n_in]
        act_ref, d_gate_ref, d_up_ref, wg_ref, wu_ref, sems = refs[2 * n_in :]
        start_all(blk.copies_in(index_ref[0], gate_in, masks, wg_ref, sems.at[0]))
        start_all(blk.copies_in(index_ref[0], up_in, masks, wu_ref, sems.at[1]))
        pltpu.make_async_copy(wg_ref, wg_ref, sems.at[0]).wait()
        pltpu.make_async_copy(wu_ref, wu_ref, sems.at[1]).wait()

        def rows(at):
            x = normed_ref[at, :]
            gate = dot_nn(x, whole(wg_ref))
            up = dot_nn(x, whole(wu_ref))
            sig = 1.0 / (1.0 + jnp.exp(-gate))
            silu = gate * sig
            act_ref[at, :] = (silu * up).astype(BF16)
            d = d_act_ref[at, :].astype(F32)
            d_gate_ref[at, :] = (d * up * sig * (1.0 + gate * (1.0 - sig))).astype(BF16)
            d_up_ref[at, :] = (d * silu).astype(BF16)

        row_chunks(n_tok, 256, rows)

    out = jax.ShapeDtypeStruct((n_tok, cols), BF16)
    w_out = jax.ShapeDtypeStruct((*blk.shape, cols), BF16)
    return pl.pallas_call(
        body,
        name="gated",
        out_shape=(out, out, out, w_out, w_out),
        in_specs=[SMEM_SPEC, VMEM_SPEC, VMEM_SPEC] + [ANY_SPEC] * (2 * n_in),
        out_specs=(VMEM_SPEC,) * 5,
        scratch_shapes=[pltpu.SemaphoreType.DMA((2,))],
        compiler_params=params(),
        cost_estimate=cost(4 * n_tok * width * cols, 2e7),
    )(index, normed, d_act, *gate_arrays, *up_arrays)


def weight_grad(blk, masks, index, lefts, rights, extra=None, name="weight_grad"):
    n_tok, width = lefts[0].shape
    sizes = [r.shape[1] for r in rights]
    cols = sum(sizes) + (LANES if extra is not None else 0)
    out_shapes = blk.out_shapes(masks, cols)
    n_out = len(out_shapes)
    n = len(lefts)
    chunk = 256

    def body(index_ref, *refs):
        left_refs, right_refs = refs[:n], refs[n : 2 * n]
        rest = refs[2 * n :]
        if extra is not None:
            extra_ref, rest = rest[0], rest[1:]
        outs, total_ref, sem = rest[:n_out], rest[n_out], rest[n_out + 1]
        per = chunk // blk.rows if blk.direct else 1

        def step(i, carry):
            at = pl.ds(pl.multiple_of(i * chunk, chunk), chunk)
            start = 0
            for left, right, size in zip(left_refs, right_refs, sizes):
                value = dot_tn(left[:, at], right[...]).astype(BF16)
                if blk.direct:
                    total_ref[pl.ds(i * per, per), :, start : start + size] = value.reshape(
                        per, blk.rows, size
                    )
                else:
                    total_ref[0, at, start : start + size] = value
                start += size
            return carry

        lax.fori_loop(0, width // chunk, step, 0)
        if extra is not None:
            value = jnp.concatenate(
                [extra_ref[...], jnp.zeros((LANES - extra_ref.shape[0], width), F32)], axis=0
            )
            value = value.T.astype(BF16)
            total_ref[:, :, cols - LANES :] = value.reshape(*blk.shape, LANES)
        copies = blk.copies_out(index_ref[0], total_ref, outs, masks, sem)
        start_all(copies)
        pltpu.make_async_copy(total_ref, total_ref, sem).wait()

    extras = [] if extra is None else [extra]
    return pl.pallas_call(
        body,
        name=name,
        out_shape=tuple(out_shapes),
        in_specs=[SMEM_SPEC] + [VMEM_SPEC] * (2 * n + len(extras)),
        out_specs=(ANY_SPEC,) * n_out,
        scratch_shapes=[pltpu.VMEM((*blk.shape, cols), BF16), pltpu.SemaphoreType.DMA],
        compiler_params=params(),
        cost_estimate=cost(2 * n_tok * width * cols, 1e7),
    )(index, *lefts, *rights, *extras)


def sum_nt(lefts, rights, name):
    n_tok = lefts[0].shape[0]
    width = rights[0].shape[0] * rights[0].shape[1]
    n = len(lefts)

    def body(*refs):
        left_refs, right_refs, out_ref = refs[:n], refs[n : 2 * n], refs[2 * n]

        def rows(at):
            total = dot_nt(left_refs[0][at, :], whole(right_refs[0]))
            for left, right in zip(left_refs[1:], right_refs[1:]):
                total = total + dot_nt(left[at, :], whole(right))
            out_ref[at, :] = total.astype(BF16)

        row_chunks(n_tok, 256, rows)

    return pl.pallas_call(
        body,
        name=name,
        out_shape=jax.ShapeDtypeStruct((n_tok, width), BF16),
        in_specs=[VMEM_SPEC] * (2 * n),
        out_specs=VMEM_SPEC,
        compiler_params=params(),
        cost_estimate=cost(2 * n_tok * width * sum(x.shape[1] for x in lefts), 1e7),
    )(*lefts, *rights)


def norm_back(part, came, hres, grad_out, gains, w0, dims):
    n_tok, width = hres.shape
    half = n_tok // 2
    nq, nv, _ = dims
    n_qkv = 2 * nq + nv

    def body(part_ref, came_ref, hres_ref, c_ref, gain_ref, w_ref, dh_ref, do_ref, dy_ref, gg_ref):
        gain = gain_ref[1:2, :]
        gg_ref[...] = jnp.zeros_like(gg_ref)
        size = 256

        def rows(at, other, own):
            d = part_ref[at, :].astype(F32) + came_ref[other, :].astype(F32)
            h = hres_ref[at, :]
            inverse = lax.rsqrt(jnp.mean(h * h, axis=-1, keepdims=True) + EPS)
            hr = h * inverse
            gg_ref[...] += jnp.sum((d * hr).reshape(-1, 8, width), axis=0)
            dg = d * gain
            back = inverse * (dg - hr * jnp.mean(dg * hr, axis=-1, keepdims=True))
            dh = c_ref[at, :].astype(F32) + back
            if own:
                dh_ref[at, :] = dh
            low = dh.astype(BF16)
            do_ref[at, :] = low
            w = w_ref[:, :, n_qkv : n_qkv + nv].reshape(width, nv)
            dy_ref[at, :] = dot_nn(low, w).astype(BF16)

        def step(i, carry):
            lo = pl.ds(pl.multiple_of(i * size, size), size)
            hi = pl.ds(pl.multiple_of(half + i * size, size), size)
            rows(lo, hi, True)
            rows(hi, lo, False)
            return carry

        lax.fori_loop(0, half // size, step, 0)

    out = lambda *s, t=BF16: jax.ShapeDtypeStruct(s, t)
    return pl.pallas_call(
        body,
        name="norm_back",
        out_shape=(out(half, width, t=F32), out(n_tok, width), out(n_tok, nv), out(8, width, t=F32)),
        in_specs=[VMEM_SPEC] * 6,
        out_specs=(VMEM_SPEC,) * 4,
        compiler_params=params(),
        cost_estimate=cost(2 * n_tok * width * nv, 1.4e7),
    )(part, came, hres, grad_out, gains, w0)


def attn_bwd(seq, qkv, y, dy, dinv, dims):
    n_tok, buffers = qkv.shape[0], seq.shape[0]
    length = n_tok // buffers
    nq, nv, _ = dims

    def body(seq_ref, qkv_ref, y_ref, dy_ref, dinv_ref, out_ref, mask_ref, dq_acc, dk_acc, dv_acc):
        for b in range(buffers):
            make_mask(seq_ref, b, mask_ref)
            base = b * length
            dq_acc[...] = jnp.zeros_like(dq_acc)
            dk_acc[...] = jnp.zeros_like(dk_acc)

            def pair(hp, carry):
                lane = lax.broadcasted_iota(jnp.int32, (1, LANES), 1)
                zero = jnp.zeros((), BF16)
                k = qkv_ref[base : base + length, nq : 2 * nq]
                v_at = pl.ds(pl.multiple_of(2 * nq + hp * LANES, LANES), LANES)
                y_at = pl.ds(pl.multiple_of(hp * LANES, LANES), LANES)
                v = qkv_ref[base : base + length, v_at]
                dv_acc[...] = jnp.zeros_like(dv_acc)
                step = length // 2
                for tb in range(2):
                    rows = slice(base + tb * step, base + (tb + 1) * step)
                    here = slice(tb * step, (tb + 1) * step)
                    seen = (tb + 1) * step
                    q = qkv_ref[rows, :nq] * jnp.asarray(0.25, BF16)
                    mask = mask_ref[here, :seen]
                    dyn = dy_ref[rows, y_at].astype(F32) * dinv_ref[rows, y_at]
                    dot_y = dyn * y_ref[rows, y_at].astype(F32)
                    dyn = dyn.astype(BF16)
                    for j in range(2):
                        mine = lane // F == 2 * hp + j
                        side = lane // 64 == j
                        k_h = jnp.where(mine, k[:seen], zero)
                        v_h = jnp.where(side, v[:seen], zero)
                        one = dot_nt(q, k_h) + 1.0
                        half_one = one * mask
                        weights = (half_one * one + mask).astype(BF16)
                        d_p = dot_nt(dyn, v_h)
                        shift = jnp.sum(jnp.where(side, dot_y, 0.0), axis=-1, keepdims=True)
                        d_a = ((d_p - shift) * half_one).astype(BF16)
                        dv_acc[:seen, :] += dot_tn(weights, jnp.where(side, dyn, zero))
                        dq_acc[here, :] += dot_nn(d_a, k_h)
                        dk_acc[:seen, :] += dot_tn(d_a, jnp.where(mine, q, zero))
                out_ref[base : base + length, v_at] = dv_acc[...].astype(BF16)
                return carry

            lax.fori_loop(0, nv // LANES, pair, 0)
            out_ref[base : base + length, :nq] = (dq_acc[...] * 0.5).astype(BF16)
            out_ref[base : base + length, nq : 2 * nq] = (dk_acc[...] * 2.0).astype(BF16)

    return pl.pallas_call(
        body,
        name="attn_bwd",
        out_shape=jax.ShapeDtypeStruct(qkv.shape, BF16),
        in_specs=[SMEM_SPEC] + [VMEM_SPEC] * 4,
        out_specs=VMEM_SPEC,
        scratch_shapes=[
            pltpu.VMEM((length, length), F32),
            pltpu.VMEM((length, nq), F32),
            pltpu.VMEM((length, nq), F32),
            pltpu.VMEM((length, LANES), F32),
        ],
        compiler_params=params(),
        cost_estimate=cost(2e10, 6e6),
    )(seq, qkv, y, dy, dinv)


def norm_one_part(d_qkv, w0, tok, dims):
    n_tok, width = tok.shape
    nq, nv, _ = dims
    n_qkv = 2 * nq + nv

    def body(d_ref, w_ref, tok_ref, out_ref, gg_ref):
        gg_ref[...] = jnp.zeros_like(gg_ref)

        def rows(at):
            d = dot_nt(d_ref[at, :], w_ref[:, :, :n_qkv].reshape(width, n_qkv))
            out_ref[at, :] = d.astype(BF16)
            x = tok_ref[at, :].astype(F32)
            inverse = lax.rsqrt(jnp.mean(x * x, axis=-1, keepdims=True) + EPS)
            gg_ref[...] += jnp.sum((d * (x * inverse)).reshape(-1, 8, width), axis=0)

        row_chunks(n_tok, 256, rows)

    return pl.pallas_call(
        body,
        name="norm_one_part",
        out_shape=(
            jax.ShapeDtypeStruct((n_tok, width), BF16),
            jax.ShapeDtypeStruct((8, width), F32),
        ),
        in_specs=[VMEM_SPEC] * 3,
        out_specs=(VMEM_SPEC,) * 2,
        compiler_params=params(),
        cost_estimate=cost(2 * n_tok * width * n_qkv, 8e6),
    )(d_qkv, w0, tok)


def finish(part, came, tok, dh, gains, hres, out_part, out_came):
    rows_all, width = tok.shape

    def body(part_ref, came_ref, tok_ref, dh_ref, gain_ref, h_ref, op_ref, oc_ref, grad_ref, out_ref):
        gain = gain_ref[0:1, :]

        def rows(at):
            d = (part_ref[at, :].astype(F32) + came_ref[at, :].astype(F32)) * gain
            x = tok_ref[at, :].astype(F32)
            inverse = lax.rsqrt(jnp.mean(x * x, axis=-1, keepdims=True) + EPS)
            xr = x * inverse
            back = inverse * (d - xr * jnp.mean(d * xr, axis=-1, keepdims=True))
            grad_ref[at, :] = (dh_ref[at, :] + back).astype(BF16)
            both = op_ref[at, :].astype(F32) + oc_ref[at, :].astype(F32)
            out_ref[at, :] = (h_ref[at, :] + both).astype(BF16)

        row_chunks(rows_all, 128, rows)

    top = pl.BlockSpec((rows_all, width), lambda i: (0, 0))
    out = jax.ShapeDtypeStruct((rows_all, width), BF16)
    return pl.pallas_call(
        body,
        name="finish",
        grid=(1,),
        out_shape=(out, out),
        in_specs=[top, top, top, top, pl.BlockSpec((8, width), lambda i: (0, 0)), top, top, top],
        out_specs=(top, top),
        compiler_params=params(),
        cost_estimate=cost(1e7, 1e7),
    )(part, came, tok, dh, gains, hres, out_part, out_came)


def local(
    lay,
    tokens,
    seq_lengths,
    w_query,
    w_key,
    w_value,
    w_output,
    w_gate,
    w_up,
    w_down,
    gain_attn,
    gain_mlp,
    cotangent,
):
    me = lax.axis_index(AXES).astype(jnp.int32)
    core = me % 2
    index = me.reshape(1)
    rows, length = w_query.shape[0], tokens.shape[0]
    nq, nv, nf = w_query.shape[1] // 2, w_value.shape[1] // 2, w_gate.shape[1] // 2

    def halves(w):
        n = w.shape[1] // 2
        low, high = w[:, :n], w[:, n:]
        return jnp.where(core == 0, low, high), jnp.where(core == 0, high, low)

    def split_gain(g):
        high = lax.reduce_precision(g, 8, 7)
        return [high.astype(BF16)[:, None], (g - high).astype(BF16)[:, None]]

    gain_cols = split_gain(gain_attn) + split_gain(gain_mlp)
    gain_block = jnp.concatenate(gain_cols + [jnp.zeros((rows, LANES - 4), BF16)], axis=1)
    parts = [halves(w) for w in (w_query, w_key, w_value, w_output.T)]
    mine0 = jnp.concatenate([p[0] for p in parts] + [gain_block], axis=1)
    give0 = jnp.concatenate([p[1] for p in parts] + [gain_block], axis=1)
    other0 = lay.swap(give0, 1)
    ffn = [halves(w) for w in (w_down.T, w_gate, w_up)]
    others = lay.swap(jnp.stack([p[1] for p in ffn]), 1)

    seq = jnp.concatenate([seq_lengths, lay.swap(seq_lengths, 1)], axis=0)
    tok = jnp.concatenate([tokens, lay.swap(tokens, 1)], axis=0)
    grad_out = jnp.concatenate([cotangent, lay.swap(cotangent, 1)], axis=0)

    blk = Blocks(lay, rows)
    pieces0 = gather(lay, mine0, other0)
    pieces_d = gather(lay, ffn[0][0], others[0])
    pieces_g = gather(lay, ffn[1][0], others[1])
    pieces_u = gather(lay, ffn[2][0], others[2])
    in_masks = [m for _, m in pieces0]
    dims = (nq, nv, mine0.shape[1])

    normed_one, qkv, y, dinv, part_o, gains, w0 = attn_fwd(
        blk, in_masks, index, seq, tok, blk.arrays(pieces0, me), dims
    )
    came_o = lay.swap(part_o, 1)
    d_act, w_d = down_back(blk, in_masks, index, grad_out, blk.arrays(pieces_d, me), nf)
    hres, normed_two = residual(tok, part_o, came_o, gains)
    act, d_gate, d_up, w_g, w_u = gated(
        blk, in_masks, index, normed_two, d_act, blk.arrays(pieces_g, me), blk.arrays(pieces_u, me), nf
    )

    out_masks = scatter_masks(lay)

    def reduced(lefts, rights, extra=None, name="weight_grad"):
        outs = weight_grad(blk, out_masks, index, lefts, rights, extra, name)
        return reduce_blocks(lay, blk.split(outs, out_masks, me))

    sum_g = reduced([normed_two], [d_gate], name="grad_gate")
    part_n2 = sum_nt([d_gate, d_up], [w_g, w_u], "d_norm2")
    came_n2 = lay.swap(part_n2, 1)
    sum_u = reduced([normed_two], [d_up], name="grad_up")
    sum_d = reduced([grad_out], [act], name="grad_down")
    d_h, d_o, d_y, gg_mlp = norm_back(part_n2, came_n2, hres, grad_out, gains, w0, dims)
    part_out = sum_nt([act], [w_d], "down")
    came_out = lay.swap(part_out[length:], 1)
    d_qkv = attn_bwd(seq, qkv, y, d_y, dinv, dims)
    part_n1, gg_attn = norm_one_part(d_qkv, w0, tok, dims)
    came_n1 = lay.swap(part_n1[length:], 1)
    gg = jnp.stack([jnp.sum(gg_attn, axis=0), jnp.sum(gg_mlp, axis=0)] + [jnp.zeros_like(gg_mlp[0])] * 6)
    sum_0 = reduced([normed_one, d_o], [d_qkv, y], gg, name="grad_attn")
    grad_tokens, layer_out = finish(part_n1, came_n1, tokens, d_h, gains, hres, part_out, came_out)

    sums = [sum_0, sum_d, sum_g, sum_u]
    came = lay.swap(jnp.concatenate([s[1] for s in sums], axis=1), 1)
    mine = jnp.concatenate([s[0] for s in sums], axis=1)

    def joined(start, size):
        own, other = mine[:, start : start + size], came[:, start : start + size]
        return jnp.where(
            core == 0,
            jnp.concatenate([own, other], axis=1),
            jnp.concatenate([other, own], axis=1),
        )

    at = 2 * nq + 2 * nv
    base = at + LANES
    return (
        layer_out,
        grad_tokens,
        joined(0, nq),
        joined(nq, nq),
        joined(2 * nq, nv),
        joined(2 * nq + nv, nv).T,
        joined(base + nf, nf),
        joined(base + 2 * nf, nf),
        joined(base, nf).T,
        mine[:, at] + came[:, at],
        mine[:, at + 1],
    )


def solution(mesh):
    rows, cols, flat = P(AXES, None), P(None, AXES), P(AXES)
    return jax.shard_map(
        functools.partial(local, Layout(mesh)),
        mesh=mesh,
        in_specs=(rows, rows, rows, rows, rows, cols, rows, rows, cols, flat, flat, rows),
        out_specs=(rows, rows, rows, rows, rows, cols, rows, rows, cols, flat, flat),
        check_vma=False,
    )
```

time: 1480 us -> 431 us (0.29)
  waiting for transfers between devices: 1050 us -> 151 us
  matrix products: 213 us -> 0 us
  blocking collectives: 163 us -> 0 us
  Pallas kernels: 0 us -> 149 us
  starting transfers between devices: 1.05 us -> 73 us
    reduce_scatter x6 -> x0, waiting for transfers between devices: 741 us -> none  [the longest x1 154 us: local(): lax.psum_scatter(grad_gate_w, ('dp', 'fsdp'), scatter_dimension=0, tiled=...]
    dot_general x45 -> x0, matrix products: 213 us -> none  [the longest x4 27.8 us: backward_group(): jnp.einsum('hts,shf->thf', grad_scores, key_g, preferred_element_type=jnp...]
    unnamed x13 -> x0, waiting for transfers between devices: 157 us -> none
    ppermute x0 -> x66, waiting for transfers between devices: none -> 151 us  [swap(): return lax.ppermute(value, AXES, [(i, i ^ bit) for i in range(self.count)])]
    all_gather x5 -> x0, waiting for transfers between devices: 150 us -> none  [the longest x1 61.3 us: local(): lax.all_gather(w_gate, ('dp', 'fsdp'), axis=0, tiled=True)]
    pallas_call x0 -> x14, Pallas kernels: none -> 149 us  [the longest x4 32.8 us: weight_grad(): pl.pallas_call(body, name=name, out_shape=tuple(out_shapes), in_specs=[SM...]
    unnamed x2 -> x0, blocking collectives: 82 us -> none
    all_gather x2 -> x0, blocking collectives: 80.9 us -> none  [the longest x1 42.3 us: local(): lax.all_gather(w_query, ('dp', 'fsdp'), axis=0, tiled=True)]
  transfers between devices with their start and end apart: 12 -> 66, of which waited for: 10 -> 34; matrix products, arithmetic and copies ran while one was open for 8% -> 10% of each run, Pallas kernels for 0% -> 29%
where the time goes in v1:
time: 431 us; the launch traced here: 430 us
  waiting for transfers between devices  151 us (35%)
  Pallas kernels  149 us (35%)
  starting transfers between devices  73 us (17%)
  local copies, waits for them, and re-layouts  28.5 us (7%)
  other arithmetic  26.8 us (6%)
    ppermute x66, waiting for transfers between devices, swap(): return lax.ppermute(value, AXES, [(i, i ^ bit) for i in range(self.count)])  151 us
    ppermute x66, starting transfers between devices, swap(): return lax.ppermute(value, AXES, [(i, i ^ bit) for i in range(self.count)])  73 us
    pallas_call x4, Pallas kernels, weight_grad(): pl.pallas_call(body, name=name, out_shape=tuple(out_shapes), in_specs=[SM...  32.8 us
    pallas_call x1, Pallas kernels, attn_fwd(): pl.pallas_call(body, name='attn_fwd', out_shape=(out(n_tok, width), out(n...  21.3 us
    pallas_call x2, Pallas kernels, sum_nt(): pl.pallas_call(body, name=name, out_shape=jax.ShapeDtypeStruct((n_tok, wi...  21.2 us
    pallas_call x1, Pallas kernels, attn_bwd(): pl.pallas_call(body, name='attn_bwd', out_shape=jax.ShapeDtypeStruct(qkv....  18.5 us
    pallas_call x1, Pallas kernels, gated(): pl.pallas_call(body, name='gated', out_shape=(out, out, out, w_out, w_out...  16.3 us
    pallas_call x1, Pallas kernels, norm_back(): pl.pallas_call(body, name='norm_back', out_shape=(out(half, width, t=F32)...  9.99 us
  transfers between devices with their start and end apart: 66, of which 34 were waited for; matrix products, arithmetic and copies ran while one was open for 10% of the time, Pallas kernels for 29%

profile of v1, /device:TPU:0, one launch (start us, length us, event | category | flops | bytes accessed | tf_op | source)
XLA Modules:
  0.0 430.1 jit_solution(8102300983214624391)
XLA Ops:
  21.3 5.2 %collective-permute-done.3 = bf16[2,32,1408]{2,1,0:T(8,128)(2,1)S(1)} collective-permute-done((bf16[2,32,1408]{2,1,0:T(8,128)(2,1)S(1)}, bf16[2,32,1408]{2,1,0:T(8,128)(2,1)S(1)}, u32[]{:S(2)}, u32[]{:S(2)}) %collective-permute-start.3) | collective-permute-done | bytes 180256 | tf_op jit(solution)/shard_map/ppermute | solution.py:49
  30.1 3.4 collective-permute-done.27
  80.3 7.2 %collective-permute-done.9.refs_3_ = bf16[8,32,1408]{2,1,0:T(8,128)(2,1)S(1)} collective-permute-done((bf16[8,32,1408]{2,1,0:T(8,128)(2,1)S(1)}, bf16[8,32,1408]{2,1,0:T(8,128)(2,1)S(1)}, u32[]{:S(2)}, u32[]{:S(2)}) %collective-permute-start.9) | collective-permute-done | bytes 720928 | tf_op jit(solution)/shard_map/ppermute | solution.py:49
  93.7 21.3 %attn_fwd.1 = (bf16[1024,1024]{1,0:T(8,128)(2,1)}, bf16[1024,768]{1,0:T(8,128)(2,1)}, bf16[1024,512]{1,0:T(8,128)(2,1)}, f32[1024,512]{1,0:T(8,128)}, bf16[1024,...) custom-call(s32[1]{0:T(128)} %bitcast.index_ref, s32[2,4]{1,0:T(2,128)} %pad_add_fusion.seq_ref, ...), custom_call_target="tpu_custom_call" | custom-call | flops 15000000512 | bytes 10000000 | tf_op jit(solution)/shard_map/attn_fwd/pallas_call | solution.py:294
  124.5 3.5 collective-permute-done.25
  134.2 13.4 %collective-permute-done.19.refs_3_ = bf16[8,32,1376]{2,1,0:T(8,128)(2,1)S(1)} collective-permute-done((bf16[8,32,1376]{2,1,0:T(8,128)(2,1)}, bf16[8,32,1376]{2,1,0:T(8,128)(2,1)S(1)}, u32[]{:S(2)}, u32[]{:S(2)}) %collective-permute-start.19) | collective-permute-done | bytes 704544 | tf_op jit(solution)/shard_map/ppermute | solution.py:49
  152.2 8.9 %down_back.1 = (bf16[1024,1376]{1,0:T(8,128)(2,1)}, bf16[32,32,1376]{2,1,0:T(8,128)(2,1)}) custom-call(s32[1]{0:T(128)} %bitcast.index_ref, bf16[1024,1024]{1,0:T(8,128)(2,1)} %copy-done.1, bf16[8,32,1376]{2,1,0:T(8,128)(2,1)} %constant_dynamic-update-slice_fusion.14.refs_0_, bf16[8,32,1376]{2,1,0:T(8,128)(2,1)} %copy-done.25, ...), custom_call_target="tpu_custom_call" | custom-call | flops 2885681152 | bytes 10000000 | tf_op jit(solution)/shard_map/down_back/pallas_call | solution.py:365
  161.1 6.8 %residual.1 = (f32[1024,1024]{1,0:T(8,128)}, bf16[1024,1024]{1,0:T(8,128)(2,1)}) custom-call(bf16[1024,1024]{1,0:T(8,128)(2,1)} %copy-done, bf16[1024,1024]{1,0:T(8,128)(2,1)} %get-tuple-element.53.part_ref, bf16[1024,1024]{1,0:T(8,128)(2,1)} %collective-permute-done.10.came_ref, f32[8,1024]{1,0:T(8,128)} %get-tuple-element.54.gain_ref), custom_call_target="tpu_custom_call" | custom-call | flops 10000000 | bytes 12000000 | tf_op jit(solution)/shard_map/residual/pallas_call | solution.py:337
  167.9 10.0 %collective-permute-done.26.refs_3_ = bf16[8,32,1376]{2,1,0:T(8,128)(2,1)} collective-permute-done((bf16[8,32,1376]{2,1,0:T(8,128)(2,1)}, bf16[8,32,1376]{2,1,0:T(8,128)(2,1)}, u32[]{:S(2)}, u32[]{:S(2)}) %collective-permute-start.26) | collective-permute-done | bytes 704544 | tf_op jit(solution)/shard_map/ppermute | solution.py:49
  177.9 16.3 %gated.1 = (bf16[1024,1376]{1,0:T(8,128)(2,1)}, bf16[1024,1376]{1,0:T(8,128)(2,1)}, bf16[1024,1376]{1,0:T(8,128)(2,1)}, bf16[32,32,1376]{2,1,0:T(8,128)(2,1)}, bf16[32,32,1376]{2,1,0:T(8,128)(2,1)}) custom-call(s32[1]{0:T(128)} %bitcast.index_ref, bf16[1024,1024]{1,0:T(8,128)(2,1)} %get-tuple-element.55.normed_ref.refs_0_, ...), custom_call_target="tpu_custom_call" | custom-call | flops 5771362304 | bytes 20000000 | tf_op jit(solution)/shard_map/gated/pallas_call | solution.py:407
  194.2 8.1 %grad_up.1 = (bf16[8,32,1376]{2,1,0:T(8,128)(2,1)}, bf16[8,32,1376]{2,1,0:T(8,128)(2,1)}, bf16[8,32,1376]{2,1,0:T(8,128)(2,1)}, bf16[8,32,1376]{2,1,0:T(8,128)(2,1)}) custom-call(s32[1]{0:T(128)} %bitcast.index_ref, bf16[1024,1024]{1,0:T(8,128)(2,1)} %get-tuple-element.55.normed_ref.refs_0_, bf16[1024,1376]{1,0:T(8,128)(2,1)} %get-tuple-element.58.refs_1_), custom_call_target="tpu_custom_call" | custom-call | flops 2885681152 | bytes 10000000 | tf_op jit(solution)/shard_map/grad_up/pallas_call | solution.py:462
  204.1 8.2 %grad_gate.1 = (bf16[8,32,1376]{2,1,0:T(8,128)(2,1)}, bf16[8,32,1376]{2,1,0:T(8,128)(2,1)}, bf16[8,32,1376]{2,1,0:T(8,128)(2,1)}, bf16[8,32,1376]{2,1,0:T(8,128)(2,1)}) custom-call(s32[1]{0:T(128)} %bitcast.index_ref, bf16[1024,1024]{1,0:T(8,128)(2,1)} %get-tuple-element.55.normed_ref.refs_0_, bf16[1024,1376]{1,0:T(8,128)(2,1)} %get-tuple-element.57.refs_0_.refs_1_), custom_call_target="tpu_custom_call" | custom-call | flops 2885681152 | bytes 10000000 | tf_op jit(solution)/shard_map/grad_gate/pallas_call | solution.py:462
  214.7 8.1 %grad_down.1 = (bf16[8,32,1376]{2,1,0:T(8,128)(2,1)}, bf16[8,32,1376]{2,1,0:T(8,128)(2,1)}, bf16[8,32,1376]{2,1,0:T(8,128)(2,1)}, bf16[8,32,1376]{2,1,0:T(8,128)(2,1)}) custom-call(s32[1]{0:T(128)} %bitcast.index_ref, bf16[1024,1024]{1,0:T(8,128)(2,1)} %copy-done.1, bf16[1024,1376]{1,0:T(8,128)(2,1)} %get-tuple-element.67.refs_0_.refs_1_), custom_call_target="tpu_custom_call" | custom-call | flops 2885681152 | bytes 10000000 | tf_op jit(solution)/shard_map/grad_down/pallas_call | solution.py:462
  223.7 12.9 %d_norm2.1.part_ref = bf16[1024,1024]{1,0:T(8,128)(2,1)} custom-call(bf16[1024,1376]{1,0:T(8,128)(2,1)} %get-tuple-element.57.refs_0_.refs_1_, bf16[1024,1376]{1,0:T(8,128)(2,1)} %get-tuple-element.58.refs_1_, bf16[32,32,1376]{2,1,0:T(8,128)(2,1)} %get-tuple-element.59.refs_2_, bf16[32,32,1376]{2,1,0:T(8,128)(2,1)} %get-tuple-element.60.refs_3_), custom_call_target="tpu_custom_call" | custom-call | flops 5771362304 | bytes 10000000 | tf_op jit(solution)/shard_map/d_norm2/pallas_call | solution.py:490
  236.7 8.3 %down.1.op_ref = bf16[1024,1024]{1,0:T(8,128)(2,1)} custom-call(bf16[1024,1376]{1,0:T(8,128)(2,1)} %get-tuple-element.67.refs_0_.refs_1_, bf16[32,32,1376]{2,1,0:T(8,128)(2,1)} %get-tuple-element.68.refs_1_), custom_call_target="tpu_custom_call" | custom-call | flops 2885681152 | bytes 10000000 | tf_op jit(solution)/shard_map/down/pallas_call | solution.py:490
  255.2 10.6 %collective-permute-done.46 = bf16[8,32,1376]{2,1,0:T(8,128)(2,1)S(1)} collective-permute-done((bf16[8,32,1376]{2,1,0:T(8,128)(2,1)}, bf16[8,32,1376]{2,1,0:T(8,128)(2,1)S(1)}, u32[]{:S(2)}, u32[]{:S(2)}) %collective-permute-start.46) | collective-permute-done | bytes 704544 | tf_op jit(solution)/shard_map/ppermute | solution.py:49
  266.8 6.7 %collective-permute-done.59 = bf16[4,32,1376]{2,1,0:T(8,128)(2,1)S(1)} collective-permute-done((bf16[4,32,1376]{2,1,0:T(8,128)(2,1)S(1)}, bf16[4,32,1376]{2,1,0:T(8,128)(2,1)S(1)}, u32[]{:S(2)}, u32[]{:S(2)}) %collective-permute-start.59) | collective-permute-done | bytes 352288 | tf_op jit(solution)/shard_map/ppermute | solution.py:49
  275.8 5.4 %collective-permute-done.52 = bf16[4,32,1376]{2,1,0:T(8,128)(2,1)S(1)} collective-permute-done((bf16[4,32,1376]{2,1,0:T(8,128)(2,1)S(1)}, bf16[4,32,1376]{2,1,0:T(8,128)(2,1)S(1)}, u32[]{:S(2)}, u32[]{:S(2)}) %collective-permute-start.52) | collective-permute-done | bytes 352288 | tf_op jit(solution)/shard_map/ppermute | solution.py:49
  290.2 5.0 %collective-permute-done.63 = bf16[2,32,1376]{2,1,0:T(8,128)(2,1)S(1)} collective-permute-done((bf16[2,32,1376]{2,1,0:T(8,128)(2,1)S(1)}, bf16[2,32,1376]{2,1,0:T(8,128)(2,1)S(1)}, u32[]{:S(2)}, u32[]{:S(2)}) %collective-permute-start.63) | collective-permute-done | bytes 176160 | tf_op jit(solution)/shard_map/ppermute | solution.py:49
  296.7 4.5 %collective-permute-done.56 = bf16[2,32,1376]{2,1,0:T(8,128)(2,1)S(1)} collective-permute-done((bf16[2,32,1376]{2,1,0:T(8,128)(2,1)S(1)}, bf16[2,32,1376]{2,1,0:T(8,128)(2,1)S(1)}, u32[]{:S(2)}, u32[]{:S(2)}) %collective-permute-start.56) | collective-permute-done | bytes 176160 | tf_op jit(solution)/shard_map/ppermute | solution.py:49
  302.5 6.5 %collective-permute-done.49 = bf16[2,32,1376]{2,1,0:T(8,128)(2,1)S(1)} collective-permute-done((bf16[2,32,1376]{2,1,0:T(8,128)(2,1)S(1)}, bf16[2,32,1376]{2,1,0:T(8,128)(2,1)S(1)}, u32[]{:S(2)}, u32[]{:S(2)}) %collective-permute-start.49) | collective-permute-done | bytes 176160 | tf_op jit(solution)/shard_map/ppermute | solution.py:49
  312.9 8.5 %collective-permute-done.64 = bf16[2,32,1376]{2,1,0:T(8,128)(2,1)S(1)} collective-permute-done((bf16[2,32,1376]{2,1,0:T(8,128)(2,1)S(1)}, bf16[2,32,1376]{2,1,0:T(8,128)(2,1)S(1)}, u32[]{:S(2)}, u32[]{:S(2)}) %collective-permute-start.64) | collective-permute-done | bytes 176160 | tf_op jit(solution)/shard_map/ppermute | solution.py:49
  324.4 5.8 %collective-permute-done.57 = bf16[2,32,1376]{2,1,0:T(8,128)(2,1)S(1)} collective-permute-done((bf16[2,32,1376]{2,1,0:T(8,128)(2,1)S(1)}, bf16[2,32,1376]{2,1,0:T(8,128)(2,1)S(1)}, u32[]{:S(2)}, u32[]{:S(2)}) %collective-permute-start.57) | collective-permute-done | bytes 176160 | tf_op jit(solution)/shard_map/ppermute | solution.py:49
  333.6 10.0 %norm_back.1 = (f32[512,1024]{1,0:T(8,128)}, bf16[1024,1024]{1,0:T(8,128)(2,1)}, bf16[1024,512]{1,0:T(8,128)(2,1)}, f32[8,1024]{1,0:T(8,128)}) custom-call(bf16[1024,1024]{1,0:T(8,128)(2,1)} %d_norm2.1.part_ref, bf16[1024,1024]{1,0:T(8,128)(2,1)} %copy-done.4, f32[1024,1024]{1,0:T(8,128)} %get-tuple-element.61.hres_ref.h_ref, bf16[1024,1024]{1,0:T(8,128)(2,1)} %copy-done.1, ...), custom_call_target="tpu_custom_call" | custom-call | flops 1073741824 | bytes 14000000 | tf_op jit(solution)/shard_map/norm_back/pallas_call | solution.py:538
  343.6 18.5 %attn_bwd.1.d_ref.refs_2_ = bf16[1024,768]{1,0:T(8,128)(2,1)} custom-call(s32[2,4]{1,0:T(2,128)} %pad_add_fusion.seq_ref, bf16[1024,768]{1,0:T(8,128)(2,1)} %get-tuple-element.51.qkv_ref, bf16[1024,512]{1,0:T(8,128)(2,1)} %get-tuple-element.52.y_ref.refs_3_, bf16[1024,512]{1,0:T(8,128)(2,1)} %get-tuple-element.63.dy_ref, f32[1024,512]{1,0:T(8,128)} %get-tuple-element.64.dinv_ref), custom_call_target="tpu_custom_call" | custom-call | flops 20000000000 | bytes 6000000 | tf_op jit(solution)/shard_map/attn_bwd/pallas_call | solution.py:600
  362.1 6.8 %norm_one_part.1 = (bf16[1024,1024]{1,0:T(8,128)(2,1)}, f32[8,1024]{1,0:T(8,128)}) custom-call(bf16[1024,768]{1,0:T(8,128)(2,1)} %attn_bwd.1.d_ref.refs_2_, bf16[32,32,1408]{2,1,0:T(8,128)(2,1)} %get-tuple-element.62.w_ref, bf16[1024,1024]{1,0:T(8,128)(2,1)} %copy-done), custom_call_target="tpu_custom_call" | custom-call | flops 1610612736 | bytes 8000000 | tf_op jit(solution)/shard_map/norm_one_part/pallas_call | solution.py:634
  370.4 8.4 %grad_attn.1 = (bf16[8,32,1408]{2,1,0:T(8,128)(2,1)}, bf16[8,32,1408]{2,1,0:T(8,128)(2,1)}, bf16[8,32,1408]{2,1,0:T(8,128)(2,1)}, bf16[8,32,1408]{2,1,0:T(8,128)(2,1)}) custom-call(s32[1]{0:T(128)} %bitcast.index_ref, bf16[1024,1024]{1,0:T(8,128)(2,1)} %get-tuple-element.71.refs_0_, bf16[1024,1024]{1,0:T(8,128)(2,1)} %get-tuple-element.72.refs_1_, ...), custom_call_target="tpu_custom_call" | custom-call | flops 2952790016 | bytes 10000000 | tf_op jit(solution)/shard_map/grad_attn/pallas_call | solution.py:462
  383.6 10.7 %collective-permute-done.37 = bf16[8,32,1408]{2,1,0:T(8,128)(2,1)S(1)} collective-permute-done((bf16[8,32,1408]{2,1,0:T(8,128)(2,1)}, bf16[8,32,1408]{2,1,0:T(8,128)(2,1)S(1)}, u32[]{:S(2)}, u32[]{:S(2)}) %collective-permute-start.37) | collective-permute-done | bytes 720928 | tf_op jit(solution)/shard_map/ppermute | solution.py:49
  399.1 3.9 collective-permute-done.38
  406.8 3.4 collective-permute-done.42
  412.2 5.9 %collective-permute-done.43 = bf16[2,32,1408]{2,1,0:T(8,128)(2,1)S(1)} collective-permute-done((bf16[2,32,1408]{2,1,0:T(8,128)(2,1)S(1)}, bf16[2,32,1408]{2,1,0:T(8,128)(2,1)S(1)}, u32[]{:S(2)}, u32[]{:S(2)}) %collective-permute-start.43) | collective-permute-done | bytes 180256 | tf_op jit(solution)/shard_map/ppermute | solution.py:49
  419.3 6.5 %finish.1 = (bf16[512,1024]{1,0:T(8,128)(2,1)}, bf16[512,1024]{1,0:T(8,128)(2,1)}) custom-call(bf16[1024,1024]{1,0:T(8,128)(2,1)} %get-tuple-element.65.part_ref, bf16[512,1024]{1,0:T(8,128)(2,1)} %collective-permute-done.35.came_ref, bf16[512,1024]{1,0:T(8,128)(2,1)} %tok_ref.1, f32[512,1024]{1,0:T(8,128)} %get-tuple-element.66.dh_ref, ...), custom_call_target="tpu_custom_call" | custom-call | flops 10000000 | bytes 10000000 | tf_op jit(solution)/shard_map/finish/pallas_call | solution.py:668
  (284 shorter events, 160.0 us)
Async XLA Ops:
  4.0 16.0 %collective-permute-start.12 = (bf16[3,32,1376]{2,1,0:T(8,128)(2,1)S(1)}, bf16[3,32,1376]{2,1,0:T(8,128)(2,1)S(1)}, u32[]{:S(2)}, u32[]{:S(2)}) collective-permute-start(bf16[3,32,1376]{2,1,0:T(8,128)(2,1)S(1)} %pad_maximum_fusion.8), channel_id=1, source_target_pairs={{0,1},{1,0},{2,3},{3,2},{4,5},{5,4},{6,7},{7,6},{8,9},{9,8},{10,11... | collective-permute-start | bytes 792584 | tf_op jit(solution)/shard_map/ppermute | solution.py:49
  4.5 129.4 %collective-permute-start.11 = (bf16[512,1024]{1,0:T(8,128)(2,1)}, bf16[512,1024]{1,0:T(8,128)(2,1)}, u32[]{:S(2)}, u32[]{:S(2)}) collective-permute-start(bf16[512,1024]{1,0:T(8,128)(2,1)} %param.23), channel_id=1, source_target_pairs={{0,1},{1,0},{2,3},{3,2},{4,5},{5,4},{6,7},{7,6},{8,9},{9,8},{10,11... | collective-permute-start | bytes 3145736 | tf_op jit(solution)/shard_map/ppermute | solution.py:49
  9.9 67.6 %collective-permute-start.1 = (bf16[512,1024]{1,0:T(8,128)(2,1)}, bf16[512,1024]{1,0:T(8,128)(2,1)}, u32[]{:S(2)}, u32[]{:S(2)}) collective-permute-start(bf16[512,1024]{1,0:T(8,128)(2,1)} %tok_ref.1), channel_id=1, source_target_pairs={{0,1},{1,0},{2,3},{3,2},{4,5},{5,4},{6,7},{7,6},{8,9},{9,8},{10,11... | collective-permute-start | bytes 3145736 | tf_op jit(solution)/shard_map/ppermute | solution.py:49
  65.1 49.9 %collective-permute-start.32 = (bf16[4,32,1376]{2,1,0:T(8,128)(2,1)}, bf16[4,32,1376]{2,1,0:T(8,128)(2,1)}, u32[]{:S(2)}, u32[]{:S(2)}) collective-permute-start(bf16[4,32,1376]{2,1,0:T(8,128)(2,1)} %pad_maximum_fusion.7), channel_id=1, source_target_pairs={{0,4},{1,5},{2,6},{3,7},{4,0},{5,1},{6,2},{7,3},{8,12},{9,13},{10,... | collective-permute-start | bytes 1056776 | tf_op jit(solution)/shard_map/ppermute | solution.py:49
  67.6 19.9 %collective-permute-start.9 = (bf16[8,32,1408]{2,1,0:T(8,128)(2,1)S(1)}, bf16[8,32,1408]{2,1,0:T(8,128)(2,1)S(1)}, u32[]{:S(2)}, u32[]{:S(2)}) collective-permute-start(bf16[8,32,1408]{2,1,0:T(8,128)(2,1)S(1)} %constant_dynamic-update-slice_fusion.7.refs_2_), channel_id=1, source_target_pairs={{0,2},{1,3},{2,0},{3,1},{4,6},{5,7},{6,4},{7,5},{8,10},{9,11},{10,... | collective-permute-start | bytes 2162696 | tf_op jit(solution)/shard_map/ppermute | solution.py:49
  72.1 20.0 %collective-permute-start.7 = (bf16[8,32,1408]{2,1,0:T(8,128)(2,1)S(1)}, bf16[8,32,1408]{2,1,0:T(8,128)(2,1)S(1)}, u32[]{:S(2)}, u32[]{:S(2)}) collective-permute-start(bf16[8,32,1408]{2,1,0:T(8,128)(2,1)S(1)} %constant_dynamic-update-slice_fusion.2.refs_0_), channel_id=1, source_target_pairs={{0,4},{1,5},{2,6},{3,7},{4,0},{5,1},{6,2},{7,3},{8,12},{9,13},{10,... | collective-permute-start | bytes 2162696 | tf_op jit(solution)/shard_map/ppermute | solution.py:49
  77.5 45.8 %collective-permute-start.30 = (bf16[4,32,1376]{2,1,0:T(8,128)(2,1)S(1)}, bf16[4,32,1376]{2,1,0:T(8,128)(2,1)}, u32[]{:S(2)}, u32[]{:S(2)}) collective-permute-start(bf16[4,32,1376]{2,1,0:T(8,128)(2,1)S(1)} %pad_maximum_fusion.6), channel_id=1, source_target_pairs={{0,2},{1,3},{2,0},{3,1},{4,6},{5,7},{6,4},{7,5},{8,10},{9,11},{10,... | collective-permute-start | bytes 1056776 | tf_op jit(solution)/shard_map/ppermute | solution.py:49
  87.5 29.4 %collective-permute-start.18 = (bf16[4,32,1376]{2,1,0:T(8,128)(2,1)}, bf16[4,32,1376]{2,1,0:T(8,128)(2,1)}, u32[]{:S(2)}, u32[]{:S(2)}) collective-permute-start(bf16[4,32,1376]{2,1,0:T(8,128)(2,1)} %pad_maximum_fusion.3), channel_id=1, source_target_pairs={{0,4},{1,5},{2,6},{3,7},{4,0},{5,1},{6,2},{7,3},{8,12},{9,13},{10,... | collective-permute-start | bytes 1056776 | tf_op jit(solution)/shard_map/ppermute | solution.py:49
  92.1 28.5 %collective-permute-start.16 = (bf16[4,32,1376]{2,1,0:T(8,128)(2,1)}, bf16[4,32,1376]{2,1,0:T(8,128)(2,1)}, u32[]{:S(2)}, u32[]{:S(2)}) collective-permute-start(bf16[4,32,1376]{2,1,0:T(8,128)(2,1)} %pad_maximum_fusion.2), channel_id=1, source_target_pairs={{0,2},{1,3},{2,0},{3,1},{4,6},{5,7},{6,4},{7,5},{8,10},{9,11},{10,... | collective-permute-start | bytes 1056776 | tf_op jit(solution)/shard_map/ppermute | solution.py:49
  115.0 46.1 %collective-permute-start.10 = (bf16[1024,1024]{1,0:T(8,128)(2,1)}, bf16[1024,1024]{1,0:T(8,128)(2,1)}, u32[]{:S(2)}, u32[]{:S(2)}) collective-permute-start(bf16[1024,1024]{1,0:T(8,128)(2,1)} %get-tuple-element.53.part_ref), channel_id=1, source_target_pairs={{0,1},{1,0},{2,3},{3,2},{4,5},{5,4},{6,7},{7,6},{8,9},{9,8},{10,11... | collective-permute-start | bytes 6291464 | tf_op jit(solution)/shard_map/ppermute | solution.py:49
  123.3 24.3 %collective-permute-start.19 = (bf16[8,32,1376]{2,1,0:T(8,128)(2,1)}, bf16[8,32,1376]{2,1,0:T(8,128)(2,1)S(1)}, u32[]{:S(2)}, u32[]{:S(2)}) collective-permute-start(bf16[8,32,1376]{2,1,0:T(8,128)(2,1)} %constant_dynamic-update-slice_fusion.19.refs_2_), channel_id=1, source_target_pairs={{0,2},{1,3},{2,0},{3,1},{4,6},{5,7},{6,4},{7,5},{8,10},{9,11},{10,... | collective-permute-start | bytes 2113544 | tf_op jit(solution)/shard_map/ppermute | solution.py:49
  128.0 20.5 %collective-permute-start.17 = (bf16[8,32,1376]{2,1,0:T(8,128)(2,1)}, bf16[8,32,1376]{2,1,0:T(8,128)(2,1)S(1)}, u32[]{:S(2)}, u32[]{:S(2)}) collective-permute-start(bf16[8,32,1376]{2,1,0:T(8,128)(2,1)} %constant_dynamic-update-slice_fusion.14.refs_0_), channel_id=1, source_target_pairs={{0,4},{1,5},{2,6},{3,7},{4,0},{5,1},{6,2},{7,3},{8,12},{9,13},{10,... | collective-permute-start | bytes 2113544 | tf_op jit(solution)/shard_map/ppermute | solution.py:49
  132.2 35.6 %collective-permute-start.33 = (bf16[8,32,1376]{2,1,0:T(8,128)(2,1)}, bf16[8,32,1376]{2,1,0:T(8,128)(2,1)}, u32[]{:S(2)}, u32[]{:S(2)}) collective-permute-start(bf16[8,32,1376]{2,1,0:T(8,128)(2,1)} %constant_dynamic-update-slice_fusion.39.refs_6_), channel_id=1, source_target_pairs={{0,2},{1,3},{2,0},{3,1},{4,6},{5,7},{6,4},{7,5},{8,10},{9,11},{10,... | collective-permute-start | bytes 2113544 | tf_op jit(solution)/shard_map/ppermute | solution.py:49
  133.9 34.0 %collective-permute-start.31 = (bf16[8,32,1376]{2,1,0:T(8,128)(2,1)}, bf16[8,32,1376]{2,1,0:T(8,128)(2,1)}, u32[]{:S(2)}, u32[]{:S(2)}) collective-permute-start(bf16[8,32,1376]{2,1,0:T(8,128)(2,1)} %constant_dynamic-update-slice_fusion.34.refs_4_), channel_id=1, source_target_pairs={{0,4},{1,5},{2,6},{3,7},{4,0},{5,1},{6,2},{7,3},{8,12},{9,13},{10,... | collective-permute-start | bytes 2113544 | tf_op jit(solution)/shard_map/ppermute | solution.py:49
  147.6 30.3 %collective-permute-start.26 = (bf16[8,32,1376]{2,1,0:T(8,128)(2,1)}, bf16[8,32,1376]{2,1,0:T(8,128)(2,1)}, u32[]{:S(2)}, u32[]{:S(2)}) collective-permute-start(bf16[8,32,1376]{2,1,0:T(8,128)(2,1)} %constant_dynamic-update-slice_fusion.29.refs_2_), channel_id=1, source_target_pairs={{0,2},{1,3},{2,0},{3,1},{4,6},{5,7},{6,4},{7,5},{8,10},{9,11},{10,... | collective-permute-start | bytes 2113544 | tf_op jit(solution)/shard_map/ppermute | solution.py:49
  148.5 29.4 %collective-permute-start.24 = (bf16[8,32,1376]{2,1,0:T(8,128)(2,1)}, bf16[8,32,1376]{2,1,0:T(8,128)(2,1)}, u32[]{:S(2)}, u32[]{:S(2)}) collective-permute-start(bf16[8,32,1376]{2,1,0:T(8,128)(2,1)} %constant_dynamic-update-slice_fusion.24.refs_0_), channel_id=1, source_target_pairs={{0,4},{1,5},{2,6},{3,7},{4,0},{5,1},{6,2},{7,3},{8,12},{9,13},{10,... | collective-permute-start | bytes 2113544 | tf_op jit(solution)/shard_map/ppermute | solution.py:49
  202.4 44.0 %collective-permute-start.58 = (bf16[8,32,1376]{2,1,0:T(8,128)(2,1)}, bf16[8,32,1376]{2,1,0:T(8,128)(2,1)}, u32[]{:S(2)}, u32[]{:S(2)}) collective-permute-start(bf16[8,32,1376]{2,1,0:T(8,128)(2,1)} %get-tuple-element.88), channel_id=1, source_target_pairs={{0,4},{1,5},{2,6},{3,7},{4,0},{5,1},{6,2},{7,3},{8,12},{9,13},{10,... | collective-permute-start | bytes 2113544 | tf_op jit(solution)/shard_map/ppermute | solution.py:49
  203.2 45.7 %collective-permute-start.60 = (bf16[8,32,1376]{2,1,0:T(8,128)(2,1)}, bf16[8,32,1376]{2,1,0:T(8,128)(2,1)}, u32[]{:S(2)}, u32[]{:S(2)}) collective-permute-start(bf16[8,32,1376]{2,1,0:T(8,128)(2,1)} %get-tuple-element.90), channel_id=1, source_target_pairs={{0,2},{1,3},{2,0},{3,1},{4,6},{5,7},{6,4},{7,5},{8,10},{9,11},{10,... | collective-permute-start | bytes 2113544 | tf_op jit(solution)/shard_map/ppermute | solution.py:49
  212.3 38.1 %collective-permute-start.51 = (bf16[8,32,1376]{2,1,0:T(8,128)(2,1)}, bf16[8,32,1376]{2,1,0:T(8,128)(2,1)}, u32[]{:S(2)}, u32[]{:S(2)}) collective-permute-start(bf16[8,32,1376]{2,1,0:T(8,128)(2,1)} %get-tuple-element.84), channel_id=1, source_target_pairs={{0,4},{1,5},{2,6},{3,7},{4,0},{5,1},{6,2},{7,3},{8,12},{9,13},{10,... | collective-permute-start | bytes 2113544 | tf_op jit(solution)/shard_map/ppermute | solution.py:49
  213.6 38.7 %collective-permute-start.53 = (bf16[8,32,1376]{2,1,0:T(8,128)(2,1)}, bf16[8,32,1376]{2,1,0:T(8,128)(2,1)S(1)}, u32[]{:S(2)}, u32[]{:S(2)}) collective-permute-start(bf16[8,32,1376]{2,1,0:T(8,128)(2,1)} %get-tuple-element.86), channel_id=1, source_target_pairs={{0,2},{1,3},{2,0},{3,1},{4,6},{5,7},{6,4},{7,5},{8,10},{9,11},{10,... | collective-permute-start | bytes 2113544 | tf_op jit(solution)/shard_map/ppermute | solution.py:49
  222.9 30.8 %collective-permute-start.44 = (bf16[8,32,1376]{2,1,0:T(8,128)(2,1)}, bf16[8,32,1376]{2,1,0:T(8,128)(2,1)S(1)}, u32[]{:S(2)}, u32[]{:S(2)}) collective-permute-start(bf16[8,32,1376]{2,1,0:T(8,128)(2,1)} %get-tuple-element.80), channel_id=1, source_target_pairs={{0,4},{1,5},{2,6},{3,7},{4,0},{5,1},{6,2},{7,3},{8,12},{9,13},{10,... | collective-permute-start | bytes 2113544 | tf_op jit(solution)/shard_map/ppermute | solution.py:49
  246.4 19.3 %collective-permute-start.46 = (bf16[8,32,1376]{2,1,0:T(8,128)(2,1)}, bf16[8,32,1376]{2,1,0:T(8,128)(2,1)S(1)}, u32[]{:S(2)}, u32[]{:S(2)}) collective-permute-start(bf16[8,32,1376]{2,1,0:T(8,128)(2,1)} %get-tuple-element.82), channel_id=1, source_target_pairs={{0,2},{1,3},{2,0},{3,1},{4,6},{5,7},{6,4},{7,5},{8,10},{9,11},{10,... | collective-permute-start | bytes 2113544 | tf_op jit(solution)/shard_map/ppermute | solution.py:49
  248.9 83.3 %collective-permute-start.34 = (bf16[1024,1024]{1,0:T(8,128)(2,1)S(1)}, bf16[1024,1024]{1,0:T(8,128)(2,1)S(1)}, u32[]{:S(2)}, u32[]{:S(2)}) collective-permute-start(bf16[1024,1024]{1,0:T(8,128)(2,1)S(1)} %copy-done.3), channel_id=1, source_target_pairs={{0,1},{1,0},{2,3},{3,2},{4,5},{5,4},{6,7},{7,6},{8,9},{9,8},{10,11... | collective-permute-start | bytes 6291464 | tf_op jit(solution)/shard_map/ppermute | solution.py:49
  250.4 168.9 %collective-permute-start.36 = (bf16[512,1024]{1,0:T(8,128)(2,1)S(1)}, bf16[512,1024]{1,0:T(8,128)(2,1)}, u32[]{:S(2)}, u32[]{:S(2)}) collective-permute-start(bf16[512,1024]{1,0:T(8,128)(2,1)S(1)} %slice.675), channel_id=1, source_target_pairs={{0,1},{1,0},{2,3},{3,2},{4,5},{5,4},{6,7},{7,6},{8,9},{9,8},{10,11... | collective-permute-start | bytes 3145736 | tf_op jit(solution)/shard_map/ppermute | solution.py:49
  252.3 21.2 %collective-permute-start.59 = (bf16[4,32,1376]{2,1,0:T(8,128)(2,1)S(1)}, bf16[4,32,1376]{2,1,0:T(8,128)(2,1)S(1)}, u32[]{:S(2)}, u32[]{:S(2)}) collective-permute-start(bf16[4,32,1376]{2,1,0:T(8,128)(2,1)S(1)} %get-tuple-element.100), channel_id=1, source_target_pairs={{0,2},{1,3},{2,0},{3,1},{4,6},{5,7},{6,4},{7,5},{8,10},{9,11},{10,... | collective-permute-start | bytes 1056776 | tf_op jit(solution)/shard_map/ppermute | solution.py:49
  253.7 21.1 %collective-permute-start.61 = (bf16[4,32,1376]{2,1,0:T(8,128)(2,1)S(1)}, bf16[4,32,1376]{2,1,0:T(8,128)(2,1)S(1)}, u32[]{:S(2)}, u32[]{:S(2)}) collective-permute-start(bf16[4,32,1376]{2,1,0:T(8,128)(2,1)S(1)} %get-tuple-element.102), channel_id=1, source_target_pairs={{0,4},{1,5},{2,6},{3,7},{4,0},{5,1},{6,2},{7,3},{8,12},{9,13},{10,... | collective-permute-start | bytes 1056776 | tf_op jit(solution)/shard_map/ppermute | solution.py:49
  265.7 15.4 %collective-permute-start.52 = (bf16[4,32,1376]{2,1,0:T(8,128)(2,1)S(1)}, bf16[4,32,1376]{2,1,0:T(8,128)(2,1)S(1)}, u32[]{:S(2)}, u32[]{:S(2)}) collective-permute-start(bf16[4,32,1376]{2,1,0:T(8,128)(2,1)S(1)} %get-tuple-element.104), channel_id=1, source_target_pairs={{0,2},{1,3},{2,0},{3,1},{4,6},{5,7},{6,4},{7,5},{8,10},{9,11},{10,... | collective-permute-start | bytes 1056776 | tf_op jit(solution)/shard_map/ppermute | solution.py:49
  284.5 26.5 %collective-permute-start.62 = (bf16[2,32,1376]{2,1,0:T(8,128)(2,1)S(1)}, bf16[2,32,1376]{2,1,0:T(8,128)(2,1)S(1)}, u32[]{:S(2)}, u32[]{:S(2)}) collective-permute-start(bf16[2,32,1376]{2,1,0:T(8,128)(2,1)S(1)} %pad_maximum_fusion.19), channel_id=1, source_target_pairs={{0,8},{1,9},{2,10},{3,11},{4,12},{5,13},{6,14},{7,15},{8,0},{9,1},... | collective-permute-start | bytes 528392 | tf_op jit(solution)/shard_map/ppermute | solution.py:49
  288.6 32.8 %collective-permute-start.55 = (bf16[2,32,1376]{2,1,0:T(8,128)(2,1)S(1)}, bf16[2,32,1376]{2,1,0:T(8,128)(2,1)S(1)}, u32[]{:S(2)}, u32[]{:S(2)}) collective-permute-start(bf16[2,32,1376]{2,1,0:T(8,128)(2,1)S(1)} %pad_maximum_fusion.17), channel_id=1, source_target_pairs={{0,8},{1,9},{2,10},{3,11},{4,12},{5,13},{6,14},{7,15},{8,0},{9,1},... | collective-permute-start | bytes 528392 | tf_op jit(solution)/shard_map/ppermute | solution.py:49
  311.0 19.3 %collective-permute-start.48 = (bf16[2,32,1376]{2,1,0:T(8,128)(2,1)S(1)}, bf16[2,32,1376]{2,1,0:T(8,128)(2,1)S(1)}, u32[]{:S(2)}, u32[]{:S(2)}) collective-permute-start(bf16[2,32,1376]{2,1,0:T(8,128)(2,1)S(1)} %pad_maximum_fusion.15), channel_id=1, source_target_pairs={{0,8},{1,9},{2,10},{3,11},{4,12},{5,13},{6,14},{7,15},{8,0},{9,1},... | collective-permute-start | bytes 528392 | tf_op jit(solution)/shard_map/ppermute | solution.py:49
  378.8 15.4 %collective-permute-start.37 = (bf16[8,32,1408]{2,1,0:T(8,128)(2,1)}, bf16[8,32,1408]{2,1,0:T(8,128)(2,1)S(1)}, u32[]{:S(2)}, u32[]{:S(2)}) collective-permute-start(bf16[8,32,1408]{2,1,0:T(8,128)(2,1)} %get-tuple-element.76), channel_id=1, source_target_pairs={{0,4},{1,5},{2,6},{3,7},{4,0},{5,1},{6,2},{7,3},{8,12},{9,13},{10,... | collective-permute-start | bytes 2162696 | tf_op jit(solution)/shard_map/ppermute | solution.py:49
  381.3 15.6 %collective-permute-start.39 = (bf16[8,32,1408]{2,1,0:T(8,128)(2,1)}, bf16[8,32,1408]{2,1,0:T(8,128)(2,1)S(1)}, u32[]{:S(2)}, u32[]{:S(2)}) collective-permute-start(bf16[8,32,1408]{2,1,0:T(8,128)(2,1)} %get-tuple-element.78), channel_id=1, source_target_pairs={{0,2},{1,3},{2,0},{3,1},{4,6},{5,7},{6,4},{7,5},{8,10},{9,11},{10,... | collective-permute-start | bytes 2162696 | tf_op jit(solution)/shard_map/ppermute | solution.py:49
  (61 other events, 525.7 us)

commit v2 on v1

v2 whole, which is shorter than its diff:
```python
import functools
import math

import jax
import jax.numpy as jnp
from jax import lax
from jax.experimental import pallas as pl
from jax.experimental.pallas import tpu as pltpu
from jax.sharding import PartitionSpec as P

H = 16
F = 16
EPS = 1e-05
AXES = ("dp", "fsdp")
LANES = 128
F32 = jnp.float32
BF16 = jnp.bfloat16

VMEM_SPEC = pl.BlockSpec(memory_space=pltpu.VMEM)
SMEM_SPEC = pl.BlockSpec(memory_space=pltpu.SMEM)
ANY_SPEC = pl.BlockSpec(memory_space=pl.ANY)


def dot_nn(a, b):
    return lax.dot_general(a, b, (((1,), (0,)), ((), ())), preferred_element_type=F32)


def dot_nt(a, b):
    return lax.dot_general(a, b, (((1,), (1,)), ((), ())), preferred_element_type=F32)


def dot_tn(a, b):
    return lax.dot_general(a, b, (((0,), (0,)), ((), ())), preferred_element_type=F32)


class Layout:
    def __init__(self, mesh):
        dp, fsdp = mesh.shape["dp"], mesh.shape["fsdp"]
        self.count = dp * fsdp
        x_bits = int(math.log2(fsdp)) - 1
        y_bits = int(math.log2(dp)) // 3
        all_bits = int(math.log2(self.count))
        self.x = [1 << (1 + i) for i in range(x_bits)]
        self.y = [1 << (1 + x_bits + i) for i in range(y_bits)]
        self.z = [1 << i for i in range(1 + x_bits + y_bits, all_bits)]

    def swap(self, value, bit):
        return lax.ppermute(value, AXES, [(i, i ^ bit) for i in range(self.count)])


def masks_of(bits):
    masks = [0]
    for bit in bits:
        masks = masks + [m | bit for m in masks]
    return masks


class Order:
    def __init__(self):
        self.last = None

    def __call__(self, *values):
        held = values if self.last is None else (*values, self.last)
        held = lax.optimization_barrier(held)
        self.last = held[0]
        return held[: len(values)] if len(values) > 1 else held[0]


def behind(value, order=None):
    return value if order is None else order(value)


def plane_masks(lay, base):
    found = []
    for half, bits in enumerate((lay.x + lay.y, lay.y + lay.x)):
        masks = [m | half for m in base]
        for bit in bits:
            masks = masks + [m | bit for m in masks]
        found.append(masks)
    return found


def split_masks(lay):
    return [
        part
        for masks in plane_masks(lay, masks_of(lay.z))
        for part in (masks[: len(masks) // 2], masks[len(masks) // 2 :])
    ]


class GatherZ:
    def __init__(self, lay, block):
        self.lay = lay
        self.bits = list(reversed(lay.z))
        self.found = {0: block}

    def first(self, *order):
        bit = self.bits[0]
        self.found[bit] = self.lay.swap(behind(self.found[0], *order), bit)

    def second(self, *order):
        for bit in self.bits[1:]:
            self.found[bit] = self.lay.swap(behind(self.found[0], *order), bit)

    def third(self, order, everything=False):
        if everything:
            for bit, value in zip(self.bits, order(*[self.found[bit] for bit in self.bits])):
                self.found[bit] = value
        else:
            self.found[self.bits[0]] = order(self.found[self.bits[0]])
        for i, bit in enumerate(self.bits[1:], 1):
            for m in masks_of(self.bits[:i])[1:]:
                self.found[m | bit] = self.lay.swap(self.found[m], bit)

    def done(self, order):
        masks = masks_of(self.lay.z)
        return order(*[self.found[m] for m in masks])


class GatherPlane:
    def __init__(self, lay, keep, other):
        self.lay, self.keep, self.other = lay, keep, other
        self.orders = (lay.x + lay.y, lay.y + lay.x)
        self.came = [lay.swap(h, bits[0]) for h, bits in zip((keep, other), self.orders)]

    def second(self, order):
        came = order(*self.came)
        self.held, self.came = [], []
        for held, got, bits in zip((self.keep, self.other), came, self.orders):
            held = jnp.concatenate([held, got], axis=0)
            for bit in bits[1:-1]:
                held = jnp.concatenate([held, self.lay.swap(held, bit)], axis=0)
            self.held.append(held)
            self.came.append(self.lay.swap(held, bits[-1]))

    def arrays(self):
        return [self.held[0], self.came[0], self.held[1], self.came[1]]

    def joined(self, order):
        came = order(*self.came)
        return jnp.concatenate([self.held[0], came[0], self.held[1], came[1]], axis=0)


def add_low(a, b):
    return (a.astype(F32) + b.astype(F32)).astype(BF16)


def fold(pairs, name="fold"):
    n = len(pairs)

    def body(*refs):
        ins, outs = refs[: 2 * n], refs[2 * n :]
        step = pl.program_id(0)
        for i in range(n):
            value = add_low(ins[2 * i][...], ins[2 * i + 1][...])

            def put(ref, value=value):
                ref[...] = value

            pl.when(step == 0)(functools.partial(put, outs[2 * i + 1]))
            pl.when(step == 1)(functools.partial(put, outs[2 * i]))

    def half(a):
        return (a.shape[0] // 2, *a.shape[1:])

    def spec(a, there):
        rest = (0,) * (a.ndim - 1)
        return pl.BlockSpec(half(a), (lambda i: (1 - i, *rest)) if there else (lambda i: (0, *rest)))

    flat = [a for pair in pairs for a in pair]
    outs = pl.pallas_call(
        body,
        name=name,
        grid=(2,),
        out_shape=tuple(jax.ShapeDtypeStruct(half(a), BF16) for a in flat),
        in_specs=[spec(a, True) for a in flat],
        out_specs=tuple(spec(a, False) for a in flat),
        compiler_params=params(FOLD_MEGABYTES),
        cost_estimate=cost(name),
    )(*flat)
    return [(outs[2 * i], outs[2 * i + 1]) for i in range(n)]


def fold_plane(pairs, wanted):
    shape = (len(wanted) // 2, 2, *pairs[0][0].shape[1:])
    n = shape[0]

    def body(*refs):
        ins, outs = refs[:4], refs[4:]
        for place, i in enumerate(wanted):
            for h in range(2):
                outs[place // n][place % n, h] = add_low(ins[2 * h][i], ins[2 * h + 1][i])

    return pl.pallas_call(
        body,
        name="fold_plane",
        out_shape=(jax.ShapeDtypeStruct(shape, BF16),) * 2,
        in_specs=[VMEM_SPEC] * 4,
        out_specs=(VMEM_SPEC,) * 2,
        compiler_params=params(FOLD_MEGABYTES),
        cost_estimate=cost("fold_plane"),
    )(*[a for pair in pairs for a in pair])


class ReducePlane:
    def __init__(self, lay, arrays):
        self.lay = lay
        self.kept = [arrays[0], arrays[2]]
        self.orders = (lay.x + lay.y, lay.y + lay.x)
        self.came = [lay.swap(a, bits[-1]) for a, bits in zip(arrays[1::2], self.orders)]

    def second(self, order):
        for level in reversed(range(len(self.orders[0]) - 1)):
            came = order(*self.came)
            found = fold(list(zip(self.kept, came)))
            self.kept = [kept for kept, _ in found]
            self.came = [
                self.lay.swap(sent, bits[level]) for (_, sent), bits in zip(found, self.orders)
            ]

    def pairs(self, order):
        return list(zip(self.kept, order(*self.came)))


class ReduceZ:
    def __init__(self, lay, kept, sent):
        self.lay = lay
        self.bits = list(lay.z)
        self.kept = kept
        self.came = lay.swap(sent, self.bits[0])

    def second(self, order):
        while len(self.bits) > 1:
            self.bits.pop(0)
            ((self.kept, sent),) = fold([(self.kept, order(self.came))], "fold_z")
            self.came = self.lay.swap(sent, self.bits[0])

    def last(self, order):
        return self.kept, order(self.came)


def add_up(ends):
    rows = ends[0][0].shape[2]
    cols = sum(kept.shape[3] for kept, _ in ends)

    def body(*refs):
        at = 0
        for i, (kept, _) in enumerate(ends):
            width = kept.shape[3]
            total = refs[2 * i][0].astype(F32) + refs[2 * i + 1][0].astype(F32)
            refs[-2][:, at : at + width] = total[0]
            refs[-1][:, at : at + width] = total[1]
            at += width

    return pl.pallas_call(
        body,
        name="add_up",
        out_shape=(jax.ShapeDtypeStruct((rows, cols), F32),) * 2,
        in_specs=[VMEM_SPEC] * (2 * len(ends)),
        out_specs=(VMEM_SPEC,) * 2,
        compiler_params=params(FOLD_MEGABYTES),
        cost_estimate=cost("add_up"),
    )(*[a for end in ends for a in end])


def wait_for(order, *streams):
    values = [v for s in streams for v in (s.came if isinstance(s.came, list) else [s.came])]
    values = list(order(*values))
    for s in streams:
        if isinstance(s.came, list):
            s.came = [values.pop(0) for _ in s.came]
        else:
            s.came = values.pop(0)


def low_first(lay):
    bits = lay.z
    masks = [0]
    for bit in reversed(bits):
        masks = masks + [m | bit for m in masks]
    return masks


class Blocks:
    def __init__(self, lay, rows):
        self.lay = lay
        self.rows = rows
        self.direct = rows % 16 == 0
        self.shape = (lay.count, rows) if self.direct else (1, lay.count * rows)

    def order(self, index):
        return jnp.bitwise_xor(index, jnp.arange(self.lay.count))

    def arrays(self, arrays, masks, index):
        if self.direct:
            return arrays
        masks = [m for ms in masks for m in ms]
        whole = jnp.concatenate(arrays, axis=0)
        place = [0] * len(masks)
        for i, m in enumerate(masks):
            place[m] = i
        whole = jnp.take(whole, jnp.asarray(place)[self.order(index)], axis=0)
        return [whole.reshape(1, -1, whole.shape[-1])]

    def copies_in(self, index, refs, masks, out_ref, sem, start, cols):
        at = pl.ds(start, cols)
        if not self.direct:
            return [pltpu.make_async_copy(refs[0].at[:, :, at], out_ref, sem)]
        return [
            pltpu.make_async_copy(
                ref.at[i, :, at], out_ref.at[jnp.bitwise_xor(index, m)], sem
            )
            for ref, ms in zip(refs, masks)
            for i, m in enumerate(ms)
        ]

    def out_shapes(self, masks, columns):
        if self.direct:
            return [jax.ShapeDtypeStruct((len(m), self.rows, columns), BF16) for m in masks]
        return [jax.ShapeDtypeStruct((1, self.lay.count * self.rows, columns), BF16)]

    def copies_out(self, index, in_ref, refs, masks, sem):
        if not self.direct:
            return [pltpu.make_async_copy(in_ref, refs[0], sem)]
        return [
            pltpu.make_async_copy(
                in_ref.at[jnp.bitwise_xor(index, m)], ref.at[i], sem
            )
            for ref, ms in zip(refs, masks)
            for i, m in enumerate(ms)
        ]

    def split(self, outs, masks, index):
        if self.direct:
            return outs
        whole = outs[0].reshape(self.lay.count, self.rows, -1)
        whole = jnp.take(whole, self.order(index), axis=0)
        return [jnp.take(whole, jnp.asarray(m), axis=0) for m in masks]


def start_all(copies):
    for copy in copies:
        copy.start()


WEIGHTS = {}
FOLD_MEGABYTES = 60


def cost(name):
    return pl.CostEstimate(
        flops=int(WEIGHTS.get(name, 0) * 1e9) + 1, bytes_accessed=1, transcendentals=0
    )


def params(megabytes):
    return pltpu.CompilerParams(vmem_limit_bytes=megabytes << 20)


def rows_spec(size, cols, last=None):
    return pl.BlockSpec((size, cols), lambda i: (i if last is None else jnp.minimum(i, last), 0))


def piece_of(i, pieces, steps, turn):
    block = lax.rem(i + steps // 2, steps) if turn else i
    return block // (steps // pieces), lax.rem(block, steps // pieces)


def piece_specs(pieces, steps, size, width, turn=False):
    def spec(q):
        def at(i):
            piece, block = piece_of(i, pieces, steps, turn)
            last = steps // pieces - 1
            return (jnp.where(piece == q, block, jnp.where(piece < q, 0, last)), 0)

        return pl.BlockSpec((size, width), at)

    return [spec(q) for q in range(pieces)]


def with_piece(refs, steps, body, turn=False):
    piece, _ = piece_of(pl.program_id(0), len(refs), steps, turn)
    for q, ref in enumerate(refs):
        pl.when(piece == q)(functools.partial(body, ref))


def row_chunks(total, size, body):
    def step(i, carry):
        body(pl.ds(pl.multiple_of(i * size, size), size))
        return carry

    lax.fori_loop(0, total // size, step, 0)


def make_mask(seq_ref, b, mask_ref):
    rows, cols = mask_ref.shape
    slots = seq_ref.shape[1]
    ends = []
    total = jnp.int32(0)
    for j in range(slots):
        total = total + seq_ref[b, j]
        ends.append(total)

    def body(at):
        t = lax.broadcasted_iota(jnp.int32, (at.size, cols), 0) + at.start
        s = lax.broadcasted_iota(jnp.int32, (at.size, cols), 1)
        seg_t = jnp.zeros_like(t)
        seg_s = jnp.zeros_like(s)
        for e in ends:
            seg_t = seg_t + (t >= e).astype(jnp.int32)
            seg_s = seg_s + (s >= e).astype(jnp.int32)
        seen = (s <= t) & (seg_t == seg_s) & (t < total)
        mask_ref[at, :] = jnp.where(seen, 0.5, 0.0).astype(F32)

    row_chunks(rows, 64, body)
    return total


class Weights:
    def __init__(self, blk, arrays, masks, index):
        self.blk, self.masks = blk, masks
        self.arrays = blk.arrays(arrays, masks, index)
        self.count = len(self.arrays)
        self.specs = [ANY_SPEC] * self.count

    def scratch(self, cols):
        return [pltpu.VMEM((*self.blk.shape, cols), BF16), pltpu.SemaphoreType.DMA]

    def load(self, index_ref, refs, w_ref, sem, start=0):
        cols = w_ref.shape[-1]
        start_all(self.blk.copies_in(index_ref[0], refs, self.masks, w_ref, sem, start, cols))

    def wait(self, w_ref, sem):
        pltpu.make_async_copy(w_ref, w_ref, sem).wait()


def prepare(core, groups, gains):
    rows = groups[0][0].shape[0]
    flat = [w for group in groups for w in group]
    padded = [w.shape[1] // 2 + -(w.shape[1] // 2) % LANES for w in flat]
    n_in = len(flat)
    widths, at = [], 0
    for group in groups:
        widths.append(sum(padded[at : at + len(group)]))
        at += len(group)
    widths[0] += LANES

    def body(core_ref, one_ref, two_ref, *refs):
        ins, keeps, give_ref = refs[:n_in], refs[n_in:-1], refs[-1]
        first = core_ref[0] == 0
        place, start = 0, 0
        for number, (group, keep_ref) in enumerate(zip(groups, keeps)):
            at = 0
            for _ in group:
                value = ins[place][...]
                half = value.shape[1] // 2
                low, high = value[:, :half].astype(F32), value[:, half:].astype(F32)
                spare = padded[place] - half
                for ref, base, one, two in (
                    (keep_ref, 0, low, high),
                    (give_ref, start, high, low),
                ):
                    ref[:, base + at : base + at + half] = jnp.where(first, one, two).astype(BF16)
                    if spare:
                        zeros = jnp.zeros((rows, spare), BF16)
                        ref[:, base + at + half : base + at + half + spare] = zeros
                at += padded[place]
                place += 1
            if number == 0:
                lines = []
                for ref in (one_ref, two_ref):
                    gain = ref[...]
                    high = gain.astype(BF16).astype(F32)
                    lines += [high, gain - high]
                lines = jnp.concatenate(lines + [jnp.zeros((LANES - 4, rows), F32)], axis=0)
                turned = lines.T.astype(BF16)
                keep_ref[:, at : at + LANES] = turned
                give_ref[:, at : at + LANES] = turned
                at += LANES
            start += at

    out = [jax.ShapeDtypeStruct((rows, n), BF16) for n in [*widths, sum(widths)]]
    return pl.pallas_call(
        body,
        name="prepare",
        out_shape=tuple(out),
        in_specs=[SMEM_SPEC] + [VMEM_SPEC] * (n_in + 2),
        out_specs=(VMEM_SPEC,) * len(out),
        compiler_params=params(60),
    )(core, *[g[None] for g in gains], *flat)


def conclude(core, mine, came, places):
    rows = mine.shape[0]
    n = len(places) - 1

    def body(core_ref, mine_ref, came_ref, *refs):
        first = core_ref[0] == 0
        for (at, half), ref in zip(places[:n], refs):
            own, other = mine_ref[:, at : at + half], came_ref[:, at : at + half]
            ref[:, :half] = jnp.where(first, own, other)
            ref[:, half:] = jnp.where(first, other, own)
        at = places[n][0]
        own = mine_ref[:, at : at + LANES].T
        other = came_ref[:, at : at + LANES].T
        refs[n][...] = own[0:1] + other[0:1]
        refs[n + 1][...] = own[1:2]

    out = [jax.ShapeDtypeStruct((rows, 2 * half), F32) for _, half in places[:n]]
    out += [jax.ShapeDtypeStruct((1, rows), F32)] * 2
    return pl.pallas_call(
        body,
        name="conclude",
        out_shape=tuple(out),
        in_specs=[SMEM_SPEC, VMEM_SPEC, VMEM_SPEC],
        out_specs=(VMEM_SPEC,) * len(out),
        compiler_params=params(60),
    )(core, mine, came)


def attn_fwd(weights, index, seq, tok, dims):
    n_tok, width, buffers = tok.shape[0], tok.shape[1], seq.shape[0]
    length = n_tok // buffers
    nq, nv, cols = dims
    n_qkv = 2 * nq + nv
    n_in = weights.count

    def body(index_ref, seq_ref, tok_ref, *refs):
        w_in = refs[:n_in]
        normed_ref, qkv_ref, y_ref, dinv_ref, gain_ref = refs[n_in : n_in + 5]
        part_refs = refs[n_in + 5 : n_in + 5 + 2 * buffers]
        mask_ref, w_ref, sem = refs[n_in + 5 + 2 * buffers :]
        weights.load(index_ref, w_in, w_ref, sem)
        weights.wait(w_ref, sem)
        w_gain = w_ref[:, :, n_qkv + nv :].reshape(width, LANES).astype(F32).T
        gain_ref[0:1, :] = w_gain[0:1] + w_gain[1:2]
        gain_ref[1:2, :] = w_gain[2:3] + w_gain[3:4]
        gain_ref[2:8, :] = jnp.zeros((6, width), F32)
        gain = gain_ref[0:1, :]

        def project(at):
            x = tok_ref[at, :].astype(F32)
            inverse = lax.rsqrt(jnp.mean(x * x, axis=-1, keepdims=True) + EPS)
            normed = (x * inverse * gain).astype(BF16)
            normed_ref[at, :] = normed
            w = w_ref[:, :, :n_qkv].reshape(width, n_qkv)
            qkv_ref[at, :] = dot_nn(normed, w).astype(BF16)

        row_chunks(n_tok, 256, project)

        for b in range(buffers):
            total = make_mask(seq_ref, b, mask_ref)
            base = b * length

            def pair(hp, carry):
                lane = lax.broadcasted_iota(jnp.int32, (1, LANES), 1)
                k = qkv_ref[base : base + length, nq : 2 * nq]
                v_at = pl.ds(pl.multiple_of(2 * nq + hp * LANES, LANES), LANES)
                v = qkv_ref[base : base + length, v_at]
                step = length // 2
                for tb in range(2):
                    rows = slice(base + tb * step, base + (tb + 1) * step)
                    seen = (tb + 1) * step
                    q = qkv_ref[rows, :nq] * jnp.asarray(0.25, BF16)
                    mask = mask_ref[tb * step : (tb + 1) * step, :seen]
                    row = lax.broadcasted_iota(jnp.int32, (step, 1), 0) + tb * step
                    pad = (row >= total).astype(F32)
                    found = []
                    for j in range(2):
                        k_h = jnp.where(lane // F == 2 * hp + j, k[:seen], jnp.zeros((), BF16))
                        v_h = jnp.where(lane // 64 == j, v[:seen], jnp.ones((), BF16))
                        one = dot_nt(q, k_h) + 1.0
                        share = ((one * one + 1.0) * mask).astype(BF16)
                        mixed = dot_nn(share, v_h)
                        inverse = 1.0 / (pltpu.roll(mixed, 64, 1) + pad)
                        found.append((mixed * inverse, inverse))
                    low = lane < 64
                    y_at = pl.ds(pl.multiple_of(hp * LANES, LANES), LANES)
                    y_ref[rows, y_at] = jnp.where(low, found[0][0], found[1][0]).astype(BF16)
                    dinv_ref[rows, y_at] = jnp.where(low, found[0][1], found[1][1])
                return carry

            lax.fori_loop(0, nv // LANES, pair, 0)
            w = w_ref[:, :, n_qkv : n_qkv + nv].reshape(width, nv)
            part = dot_nt(y_ref[base : base + length, :], w).astype(BF16)
            part_refs[2 * b][...] = part[: length // 2]
            part_refs[2 * b + 1][...] = part[length // 2 :]

    out = lambda *s, t=BF16: jax.ShapeDtypeStruct(s, t)
    return pl.pallas_call(
        body,
        name="attn_fwd",
        out_shape=(
            out(n_tok, width),
            out(n_tok, n_qkv),
            out(n_tok, nv),
            out(n_tok, nv, t=F32),
            out(8, width, t=F32),
            *(out(length // 2, width) for _ in range(2 * buffers)),
        ),
        in_specs=[SMEM_SPEC, SMEM_SPEC, VMEM_SPEC] + weights.specs,
        out_specs=(VMEM_SPEC,) * (5 + 2 * buffers),
        scratch_shapes=[pltpu.VMEM((length, length), F32)] + weights.scratch(cols),
        compiler_params=params(60),
        cost_estimate=cost("attn_fwd"),
    )(index, seq, tok, *weights.arrays)


def residual(tok, part, came, gains):
    n_tok, width = tok.shape
    steps = 4
    size = n_tok // steps

    n = len(part)

    def body(tok_ref, *refs):
        part_refs, came_refs = refs[:n], refs[n : 2 * n]
        gain_ref, hres_ref, normed_ref = refs[2 * n :]
        gain = gain_ref[1:2, :]

        def rows(at, part_ref, came_ref):
            x = tok_ref[at, :].astype(F32)
            x = x + (part_ref[at, :].astype(F32) + came_ref[at, :].astype(F32))
            hres_ref[at, :] = x
            inverse = lax.rsqrt(jnp.mean(x * x, axis=-1, keepdims=True) + EPS)
            normed_ref[at, :] = (x * inverse * gain).astype(BF16)

        pairs = list(zip(part_refs, came_refs[n // 2 :] + came_refs[: n // 2]))
        with_piece(pairs, steps, lambda pair: row_chunks(size, 64, lambda at: rows(at, *pair)))

    at = rows_spec(size, width)
    return pl.pallas_call(
        body,
        name="residual",
        grid=(steps,),
        out_shape=(
            jax.ShapeDtypeStruct((n_tok, width), F32),
            jax.ShapeDtypeStruct((n_tok, width), BF16),
        ),
        in_specs=[at]
        + piece_specs(n, steps, size, width)
        + piece_specs(n, steps, size, width, True)
        + [pl.BlockSpec((8, width), lambda i: (0, 0))],
        out_specs=(at, at),
        compiler_params=params(60),
        cost_estimate=cost("residual"),
    )(tok, *part, *came, gains)


def down_back(weights, index, grad_out, cols):
    n_tok, width = grad_out.shape
    n_in = weights.count
    steps = 4
    size = n_tok // steps

    def body(index_ref, grad_ref, *refs):
        out_ref, w_ref, sem = refs[n_in:]

        @pl.when(pl.program_id(0) == 0)
        def _():
            weights.load(index_ref, refs[:n_in], w_ref, sem)
            weights.wait(w_ref, sem)

        w = w_ref[...].reshape(width, cols)
        out_ref[...] = dot_nn(grad_ref[...], w).astype(BF16)

    return pl.pallas_call(
        body,
        name="down_back",
        grid=(steps,),
        out_shape=jax.ShapeDtypeStruct((n_tok, cols), BF16),
        in_specs=[SMEM_SPEC, rows_spec(size, width)] + weights.specs,
        out_specs=rows_spec(size, cols),
        scratch_shapes=weights.scratch(cols),
        compiler_params=params(60),
        cost_estimate=cost("down_back"),
    )(index, grad_out, *weights.arrays)


def gated(weights, index, normed, d_act, stride):
    n_tok, width = normed.shape
    cols = d_act.shape[1]
    n_in = weights.count
    steps = 4
    size = n_tok // steps

    def body(index_ref, normed_ref, d_act_ref, *refs):
        act_ref, d_gate_ref, d_up_ref, w_ref, sem = refs[n_in:]

        @pl.when(pl.program_id(0) == 0)
        def _():
            weights.load(index_ref, refs[:n_in], w_ref, sem)
            weights.wait(w_ref, sem)

        x = normed_ref[...]
        gate = dot_nn(x, w_ref[:, :, :cols].reshape(width, cols))
        up = dot_nn(x, w_ref[:, :, stride : stride + cols].reshape(width, cols))
        sig = 1.0 / (1.0 + jnp.exp(-gate))
        silu = gate * sig
        act_ref[...] = (silu * up).astype(BF16)
        d = d_act_ref[...].astype(F32)
        d_gate_ref[...] = (d * up * sig * (1.0 + gate * (1.0 - sig))).astype(BF16)
        d_up_ref[...] = (d * silu).astype(BF16)

    out = jax.ShapeDtypeStruct((n_tok, cols), BF16)
    at = rows_spec(size, cols)
    return pl.pallas_call(
        body,
        name="gated",
        grid=(steps,),
        out_shape=(out, out, out),
        in_specs=[SMEM_SPEC, rows_spec(size, width), at] + weights.specs,
        out_specs=(at, at, at),
        scratch_shapes=weights.scratch(2 * stride),
        compiler_params=params(60),
        cost_estimate=cost("gated"),
    )(index, normed, d_act, *weights.arrays)


def weight_grad(blk, masks, index, lefts, rights, gain=None, name="weight_grad"):
    n_tok, width = lefts[0].shape
    sizes = [r.shape[1] for r in rights]
    cols = sum(sizes) + (LANES if gain is not None else 0)
    out_shapes = blk.out_shapes(masks, cols)
    n_out = len(out_shapes)
    n = len(lefts)
    chunk = 256

    extras, specs, scratch = [], [], []
    if gain is not None:
        weights, gains, other = gain
        extras = [gains, other, *weights.arrays]
        specs = [pl.BlockSpec((8, chunk), lambda i: (0, i))] * 2 + weights.specs
        scratch = weights.scratch(sizes[0])

    def body(index_ref, *refs):
        left_refs, right_refs = refs[:n], refs[n : 2 * n]
        ins = refs[2 * n : 2 * n + len(extras)]
        outs, total_ref, sem = (*refs[2 * n + len(extras) :],)[:n_out], refs[-2 - len(scratch)], refs[-1 - len(scratch)]
        per = chunk // blk.rows if blk.direct else 1
        i = pl.program_id(0)

        def put(value, start):
            size = value.shape[1]
            if blk.direct:
                total_ref[pl.ds(i * per, per), :, start : start + size] = value.reshape(
                    per, blk.rows, size
                )
            else:
                at = pl.ds(pl.multiple_of(i * chunk, chunk), chunk)
                total_ref[0, at, start : start + size] = value

        if gain is not None:
            w_ref, w_sem = refs[-2], refs[-1]

            @pl.when(i == 0)
            def _():
                weights.load(index_ref, ins[2:], w_ref, w_sem)
                weights.wait(w_ref, w_sem)

        start = 0
        for left, right, size in zip(left_refs, right_refs, sizes):
            value = dot_tn(left[...], right[...])
            put(value.astype(BF16), start)
            if gain is not None and start == 0:
                if blk.direct:
                    w = w_ref[pl.ds(i * per, per), :, :].reshape(chunk, size)
                else:
                    w = w_ref[0, pl.ds(pl.multiple_of(i * chunk, chunk), chunk), :]
                one = jnp.sum(value * w.astype(F32), axis=-1, keepdims=True)
                two = jnp.sum(ins[1][...], axis=0, keepdims=True)
                rows = jnp.concatenate([ins[0][0:1, :], two, jnp.zeros((LANES - 2, chunk), F32)])
                turned = rows.T
                lane = lax.broadcasted_iota(jnp.int32, turned.shape, 1)
                put(jnp.where(lane == 0, one / turned, turned).astype(BF16), cols - LANES)
            start += size

        @pl.when(i == width // chunk - 1)
        def _():
            start_all(blk.copies_out(index_ref[0], total_ref, outs, masks, sem))
            pltpu.make_async_copy(total_ref, total_ref, sem).wait()

    return pl.pallas_call(
        body,
        name=name,
        grid=(width // chunk,),
        out_shape=tuple(out_shapes),
        in_specs=[SMEM_SPEC]
        + [pl.BlockSpec((n_tok, chunk), lambda i: (0, i))] * n
        + [pl.BlockSpec(r.shape, lambda i: (0, 0)) for r in rights]
        + specs,
        out_specs=(ANY_SPEC,) * n_out,
        scratch_shapes=[pltpu.VMEM((*blk.shape, cols), BF16), pltpu.SemaphoreType.DMA] + scratch,
        compiler_params=params(60),
        cost_estimate=cost(name),
    )(index, *lefts, *rights, *extras)


def sum_nt(weights, index, lefts, starts, total, pieces, name, base=0):
    n_tok, cols = lefts[0].shape
    width = weights.blk.shape[0] * weights.blk.shape[1]
    n, n_in = len(lefts), weights.count
    steps = 4
    size = n_tok // steps

    def body(index_ref, *refs):
        left_refs = refs[:n]
        out_refs, (w_ref, sem) = refs[n + n_in : -2], refs[-2:]

        @pl.when(pl.program_id(0) == 0)
        def _():
            weights.load(index_ref, refs[n : n + n_in], w_ref, sem, base)
            weights.wait(w_ref, sem)

        value = None
        for left, start in zip(left_refs, starts):
            term = dot_nt(left[...], w_ref[:, :, start : start + cols].reshape(width, cols))
            value = term if value is None else value + term
        value = value.astype(BF16)

        def put(ref):
            ref[...] = value

        with_piece(out_refs, steps, put)

    return pl.pallas_call(
        body,
        name=name,
        grid=(steps,),
        out_shape=(jax.ShapeDtypeStruct((n_tok // pieces, width), BF16),) * pieces,
        in_specs=[SMEM_SPEC] + [rows_spec(size, cols)] * n + weights.specs,
        out_specs=tuple(piece_specs(pieces, steps, size, width)),
        scratch_shapes=weights.scratch(total),
        compiler_params=params(60),
        cost_estimate=cost(name),
    )(index, *lefts, *weights.arrays)


def norm_back(weights, index, part, came, hres, grad_out, gains, dims):
    n_tok, width = hres.shape
    nq, nv, _ = dims
    n_qkv = 2 * nq + nv
    n_in = weights.count
    steps = 4
    size = n_tok // steps

    n = len(part)

    def body(index_ref, hres_ref, c_ref, gain_ref, *refs):
        part_refs, came_refs, refs = refs[:n], refs[n : 2 * n], refs[2 * n :]
        dh_ref, do_ref, dy_ref, gg_ref, w_ref, sem = refs[n_in:]
        gain = gain_ref[1:2, :]
        i = pl.program_id(0)

        @pl.when(i == 0)
        def _():
            weights.load(index_ref, refs[:n_in], w_ref, sem, n_qkv)
            gg_ref[...] = jnp.zeros_like(gg_ref)

        def rows(at, part_ref, came_ref):
            d = part_ref[at, :].astype(F32) + came_ref[at, :].astype(F32)
            h = hres_ref[at, :]
            inverse = lax.rsqrt(jnp.mean(h * h, axis=-1, keepdims=True) + EPS)
            hr = h * inverse
            gg_ref[...] += jnp.sum((d * hr).reshape(-1, 8, width), axis=0)
            dg = d * gain
            back = inverse * (dg - hr * jnp.mean(dg * hr, axis=-1, keepdims=True))
            dh = c_ref[at, :].astype(F32) + back

            @pl.when(i < steps // 2)
            def _():
                dh_ref[at, :] = dh

            do_ref[at, :] = dh.astype(BF16)

        pairs = list(zip(part_refs, came_refs[n // 2 :] + came_refs[: n // 2]))
        with_piece(pairs, steps, lambda pair: row_chunks(size, 64, lambda at: rows(at, *pair)))

        @pl.when(i == 0)
        def _():
            weights.wait(w_ref, sem)

        dy_ref[...] = dot_nn(do_ref[...], w_ref[...].reshape(width, nv)).astype(BF16)

    out = lambda *s, t=BF16: jax.ShapeDtypeStruct(s, t)
    at = rows_spec(size, width)
    keep = pl.BlockSpec((8, width), lambda i: (0, 0))
    return pl.pallas_call(
        body,
        name="norm_back",
        grid=(steps,),
        out_shape=(
            out(n_tok // 2, width, t=F32),
            out(n_tok, width),
            out(n_tok, nv),
            out(8, width, t=F32),
        ),
        in_specs=[SMEM_SPEC, at, at, keep]
        + piece_specs(n, steps, size, width)
        + piece_specs(n, steps, size, width, True)
        + weights.specs,
        out_specs=(
            rows_spec(size, width, last=steps // 2 - 1),
            at,
            rows_spec(size, nv),
            keep,
        ),
        scratch_shapes=weights.scratch(nv),
        compiler_params=params(60),
        cost_estimate=cost("norm_back"),
    )(index, hres, grad_out, gains, *part, *came, *weights.arrays)


def attn_bwd(seq, qkv, y, dy, dinv, dims):
    n_tok, buffers = qkv.shape[0], seq.shape[0]
    length = n_tok // buffers
    nq, nv, _ = dims

    def body(seq_ref, qkv_ref, y_ref, dy_ref, dinv_ref, out_ref, mask_ref, dq_acc, dk_acc, dv_acc):
        for b in range(buffers):
            make_mask(seq_ref, b, mask_ref)
            base = b * length
            dq_acc[...] = jnp.zeros_like(dq_acc)
            dk_acc[...] = jnp.zeros_like(dk_acc)

            def pair(hp, carry):
                lane = lax.broadcasted_iota(jnp.int32, (1, LANES), 1)
                zero = jnp.zeros((), BF16)
                k = qkv_ref[base : base + length, nq : 2 * nq]
                v_at = pl.ds(pl.multiple_of(2 * nq + hp * LANES, LANES), LANES)
                y_at = pl.ds(pl.multiple_of(hp * LANES, LANES), LANES)
                v = qkv_ref[base : base + length, v_at]
                dv_acc[...] = jnp.zeros_like(dv_acc)
                step = length // 2
                for tb in range(2):
                    rows = slice(base + tb * step, base + (tb + 1) * step)
                    here = slice(tb * step, (tb + 1) * step)
                    seen = (tb + 1) * step
                    q = qkv_ref[rows, :nq] * jnp.asarray(0.25, BF16)
                    mask = mask_ref[here, :seen]
                    dyn = dy_ref[rows, y_at].astype(F32) * dinv_ref[rows, y_at]
                    dot_y = dyn * y_ref[rows, y_at].astype(F32)
                    dyn = dyn.astype(BF16)
                    for j in range(2):
                        mine = lane // F == 2 * hp + j
                        side = lane // 64 == j
                        k_h = jnp.where(mine, k[:seen], zero)
                        v_h = jnp.where(side, v[:seen], zero)
                        one = dot_nt(q, k_h) + 1.0
                        half_one = one * mask
                        weights = (half_one * one + mask).astype(BF16)
                        d_p = dot_nt(dyn, v_h)
                        shift = jnp.sum(jnp.where(side, dot_y, 0.0), axis=-1, keepdims=True)
                        d_a = ((d_p - shift) * half_one).astype(BF16)
                        dv_acc[:seen, :] += dot_tn(weights, jnp.where(side, dyn, zero))
                        dq_acc[here, :] += dot_nn(d_a, k_h)
                        dk_acc[:seen, :] += dot_tn(d_a, jnp.where(mine, q, zero))
                out_ref[base : base + length, v_at] = dv_acc[...].astype(BF16)
                return carry

            lax.fori_loop(0, nv // LANES, pair, 0)
            out_ref[base : base + length, :nq] = (dq_acc[...] * 0.5).astype(BF16)
            out_ref[base : base + length, nq : 2 * nq] = (dk_acc[...] * 2.0).astype(BF16)

    return pl.pallas_call(
        body,
        name="attn_bwd",
        out_shape=jax.ShapeDtypeStruct(qkv.shape, BF16),
        in_specs=[SMEM_SPEC] + [VMEM_SPEC] * 4,
        out_specs=VMEM_SPEC,
        scratch_shapes=[
            pltpu.VMEM((length, length), F32),
            pltpu.VMEM((length, nq), F32),
            pltpu.VMEM((length, nq), F32),
            pltpu.VMEM((length, LANES), F32),
        ],
        compiler_params=params(60),
        cost_estimate=cost("attn_bwd"),
    )(seq, qkv, y, dy, dinv)


def norm_one_part(weights, index, d_qkv):
    n_tok, n_qkv = d_qkv.shape
    width = weights.blk.shape[0] * weights.blk.shape[1]
    n_in = weights.count
    steps = 4
    size = n_tok // steps

    def body(index_ref, d_ref, *refs):
        *out_refs, w_ref, sem = refs[n_in:]

        @pl.when(pl.program_id(0) == 0)
        def _():
            weights.load(index_ref, refs[:n_in], w_ref, sem)
            weights.wait(w_ref, sem)

        d = dot_nt(d_ref[...], w_ref[...].reshape(width, n_qkv))

        def put(ref):
            ref[...] = d.astype(BF16)

        with_piece(out_refs, steps, put)

    return pl.pallas_call(
        body,
        name="norm_one_part",
        grid=(steps,),
        out_shape=(
            jax.ShapeDtypeStruct((n_tok // 2, width), BF16),
            jax.ShapeDtypeStruct((n_tok // 2, width), BF16),
        ),
        in_specs=[SMEM_SPEC, rows_spec(size, n_qkv)] + weights.specs,
        out_specs=tuple(piece_specs(2, steps, size, width)),
        scratch_shapes=weights.scratch(n_qkv),
        compiler_params=params(60),
        cost_estimate=cost("norm_one_part"),
    )(index, d_qkv, *weights.arrays)


def finish(part, came, tok, dh, gains, hres, out_part, out_came):
    n_tok, width = tok.shape
    steps = 4
    size = n_tok // steps

    def body(part_ref, came_ref, tok_ref, dh_ref, gain_ref, h_ref, op_ref, oc_ref, grad_ref, out_ref):
        gain = gain_ref[0:1, :]

        def rows(at):
            d = (part_ref[at, :].astype(F32) + came_ref[at, :].astype(F32)) * gain
            x = tok_ref[at, :].astype(F32)
            inverse = lax.rsqrt(jnp.mean(x * x, axis=-1, keepdims=True) + EPS)
            xr = x * inverse
            back = inverse * (d - xr * jnp.mean(d * xr, axis=-1, keepdims=True))
            grad_ref[at, :] = (dh_ref[at, :] + back).astype(BF16)
            both = op_ref[at, :].astype(F32) + oc_ref[at, :].astype(F32)
            out_ref[at, :] = (h_ref[at, :] + both).astype(BF16)

        row_chunks(size, 64, rows)

    at = rows_spec(size, width)
    out = jax.ShapeDtypeStruct((n_tok, width), BF16)
    return pl.pallas_call(
        body,
        name="finish",
        grid=(steps,),
        out_shape=(out, out),
        in_specs=[at, at, at, at, pl.BlockSpec((8, width), lambda i: (0, 0)), at, at, at],
        out_specs=(at, at),
        compiler_params=params(60),
        cost_estimate=cost("finish"),
    )(part, came, tok, dh, gains, hres, out_part, out_came)


def local(
    lay,
    tokens,
    seq_lengths,
    w_query,
    w_key,
    w_value,
    w_output,
    w_gate,
    w_up,
    w_down,
    gain_attn,
    gain_mlp,
    cotangent,
):
    me = lax.axis_index(AXES).astype(jnp.int32)
    core = me % 2
    index = me.reshape(1)
    rows, length = w_query.shape[0], tokens.shape[0]
    nq, nv, nf = w_query.shape[1] // 2, w_value.shape[1] // 2, w_gate.shape[1] // 2
    stride = nf + -nf % LANES
    order = Order()
    blk = Blocks(lay, rows)
    masks = split_masks(lay)
    both = sum(plane_masks(lay, [0]), [])
    masks_z = [[m | z for m in both] for z in masks_of(lay.z)]
    dims = (nq, nv, 2 * nq + 2 * nv + LANES)

    keep_0, keep_gu, keep_d, give = prepare(
        core.reshape(1),
        [[w_query, w_key, w_value, w_output.T], [w_gate, w_up], [w_down.T]],
        [gain_attn, gain_mlp],
    )
    came = lay.swap(give, 1)
    tok_other, seq_other = lay.swap(tokens, 1), lay.swap(seq_lengths, 1)
    cot_other = lay.swap(cotangent, 1)
    came = order(came)
    at_d = dims[2] + 2 * stride

    z_0 = GatherZ(lay, jnp.stack([keep_0, came[:, : dims[2]]]))
    z_0.first()
    z_0.second()
    p_d = GatherPlane(lay, keep_d[None], came[None, :, at_d:])
    tok_other, seq_other, cot_other = order(tok_other, seq_other, cot_other)
    z_gu = GatherZ(lay, order(jnp.stack([keep_gu, came[:, dims[2] : at_d]])))
    z_gu.first()
    z_0.third(order)
    p_d.second(order)

    def halves(z):
        blocks = z.done(order)
        return [jnp.stack([b[h] for b in blocks]) for h in range(2)]

    p_0 = GatherPlane(lay, *halves(z_0))
    z_gu.second(order)
    held_d = p_d.joined(order)
    p_0.second(order)
    z_gu.third(order)
    z_d = GatherZ(lay, order(held_d))
    z_d.first()
    halves_gu = halves(z_gu)
    *arrays_0, keep_gu, other_gu = order(*p_0.arrays(), *halves_gu)
    p_gu = GatherPlane(lay, keep_gu, other_gu)
    z_d.second(order)
    w_0 = Weights(blk, arrays_0, masks, me)
    seq = jnp.concatenate([seq_lengths, seq_other], axis=0)
    tok = order(jnp.concatenate([tokens, tok_other], axis=0))
    grad_out = order(jnp.concatenate([cotangent, cot_other], axis=0))
    z_d.third(order, True)
    p_gu.second(order)
    tok = order(tok)

    def swap_all(values):
        return [lay.swap(v, 1) for v in values]

    normed_one, qkv, y, dinv, gains, *part_o = attn_fwd(w_0, index, seq, tok, dims)
    part_o = order(*part_o)
    came_o = swap_all(part_o)
    w_d = Weights(blk, z_d.done(order), masks_z, me)
    d_act = order(down_back(w_d, index, grad_out, stride))
    w_gu = Weights(blk, order(*p_gu.arrays()), masks, me)
    came_o = order(*came_o)
    hres, normed_two = residual(tok, part_o, came_o, gains)
    normed_two = order(normed_two)
    act, d_gate, d_up = order(*gated(w_gu, index, normed_two, d_act, stride))

    def grad(lefts, rights, gain=None, name="weight_grad"):
        outs = weight_grad(blk, masks, index, lefts, rights, gain, name)
        return blk.split(order(*outs), masks, me)

    wanted = [masks_of(lay.z).index(m) for m in low_first(lay)]

    def along_z(stream):
        return ReduceZ(lay, *fold_plane(stream.pairs(order), wanted))

    r_g = ReducePlane(lay, grad([normed_two], [d_gate], name="grad_gate"))
    d_up = order(d_up)
    part_n2 = order(*sum_nt(w_gu, index, [d_gate, d_up], [0, stride], 2 * stride, 2, "d_norm2"))
    came_n2 = swap_all(part_n2)
    r_g.second(order)
    act = order(act)
    r_d = ReducePlane(lay, grad([grad_out], [act], name="grad_down"))
    came_n2 = order(*came_n2)
    d_h, d_o, d_y, gg_mlp = norm_back(w_0, index, part_n2, came_n2, hres, grad_out, gains, dims)
    d_y = order(d_y)
    outs_u = grad([normed_two, d_o], [d_up, y], name="grad_up")
    zr_g = along_z(r_g)
    r_u = ReducePlane(lay, order(*outs_u))
    d_qkv = order(attn_bwd(seq, qkv, y, order(d_y), dinv, dims))
    wait_for(order, r_d, zr_g)
    r_d.second(order)
    wait_for(order, r_u)
    r_u.second(order)
    zr_g.second(order)
    d_qkv = order(d_qkv)
    outs_0 = grad([normed_one], [d_qkv], (w_0, gains, gg_mlp), name="grad_attn")
    zr_d = along_z(r_d)
    r_0 = ReducePlane(lay, order(*outs_0))
    part_n1 = order(*norm_one_part(w_0, index, order(d_qkv)))
    wait_for(order, zr_g, zr_d, r_u, r_0)
    r_0.second(order)
    zr_u = along_z(r_u)
    zr_d.second(order)
    part_out = order(*sum_nt(w_d, index, [order(act)], [0], stride, 2, "down"))
    came_rows = swap_all(order(part_n1[1], part_out[1]))
    wait_for(order, zr_u, r_0)
    zr_0 = along_z(r_0)
    zr_u.second(order)
    came_rows = order(*came_rows)
    grad_tokens, layer_out = finish(
        part_n1[0], came_rows[0], tokens, d_h, gains, hres, part_out[0], came_rows[1]
    )
    grad_tokens = order(grad_tokens)
    zr_0.second(order)
    end_d = zr_d.last(order)
    end_g = zr_g.last(order)
    end_u = zr_u.last(order)
    end_0 = zr_0.last(order)
    mine, give = add_up([end_0, end_d, end_g, end_u])
    came = lay.swap(give, 1)
    at = 2 * nq + nv
    at_d = at + LANES
    at_gu = at_d + stride
    places = [
        (0, nq),
        (nq, nq),
        (2 * nq, nv),
        (at_gu + 2 * stride, nv),
        (at_gu, nf),
        (at_gu + stride, nf),
        (at_d, nf),
        (at, LANES),
    ]
    *grads, g_one, g_two = conclude(core.reshape(1), mine, came, places)
    grads[3], grads[6] = grads[3].T, grads[6].T
    return (layer_out, grad_tokens, *grads, g_one[0], g_two[0])


def solution(mesh):
    rows, cols, flat = P(AXES, None), P(None, AXES), P(AXES)
    return jax.shard_map(
        functools.partial(local, Layout(mesh)),
        mesh=mesh,
        in_specs=(rows, rows, rows, rows, rows, cols, rows, rows, cols, flat, flat, rows),
        out_specs=(rows, rows, rows, rows, rows, cols, rows, rows, cols, flat, flat),
        check_vma=False,
    )
```

time: 431 us -> 342 us (0.79)
  waiting for transfers between devices: 151 us -> 86.6 us
  Pallas kernels: 149 us -> 181 us
  other arithmetic: 26.8 us -> 5.26 us
  local copies, waits for them, and re-layouts: 28.5 us -> 9.73 us
  starting transfers between devices: 73 us -> 56.5 us
    ppermute x66 -> x58, waiting for transfers between devices: 151 us -> 86.6 us  [swap(): return lax.ppermute(value, AXES, [(i, i ^ bit) for i in range(self.count)])]
    pallas_call x12 -> x27, Pallas kernels: 109 us -> 144 us  [the longest x4 32.3 us: weight_grad(): pl.pallas_call(body, name=name, grid=(width // chunk,), out_shape=tuple(o...]
    ppermute x66 -> x58, starting transfers between devices: 73 us -> 56.5 us  [swap(): return lax.ppermute(value, AXES, [(i, i ^ bit) for i in range(self.count)])]
    concatenate x13 -> x5, local copies, waits for them, and re-layouts: 12.5 us -> 0.19 us  [the longest x4 0.17 us: second(): held = jnp.concatenate([held, got], axis=0)]
    slice x19 -> x2, local copies, waits for them, and re-layouts: 8.01 us -> 0.1 us  [halves(): return [jnp.stack([b[h] for b in blocks]) for h in range(2)]]
    convert_element_type x12 -> x0, other arithmetic: 6.35 us -> none  [the longest x8 6.2 us: add_low(): return (a.astype(F32) + b.astype(F32)).astype(BF16)]
    another operation x33 -> x6, other arithmetic: 8.33 us -> 2.17 us  [the longest x1 0.96 us: local(): z_gu = GatherZ(lay, order(jnp.stack([keep_gu, came[:, dims[2]:at_d]])))]
    select_n x7 -> x0, other arithmetic: 5.49 us -> none  [the longest x4 3 us: halves(): return (jnp.where(core == 0, low, high), jnp.where(core == 0, high, low))]
  transfers between devices with their start and end apart: 66 -> 58, of which waited for: 34 -> 20; matrix products, arithmetic and copies ran while one was open for 10% -> 2% of each run, Pallas kernels for 29% -> 41%
where the time goes in v2:
time: 342 us; the launch traced here: 340 us
  Pallas kernels  181 us (53%)
  waiting for transfers between devices  86.6 us (25%)
  starting transfers between devices  56.5 us (17%)
  local copies, waits for them, and re-layouts  9.73 us (3%)
  other arithmetic  5.26 us (2%)
    ppermute x58, waiting for transfers between devices, swap(): return lax.ppermute(value, AXES, [(i, i ^ bit) for i in range(self.count)])  86.6 us
    ppermute x58, starting transfers between devices, swap(): return lax.ppermute(value, AXES, [(i, i ^ bit) for i in range(self.count)])  56.5 us
    pallas_call x4, Pallas kernels, weight_grad(): pl.pallas_call(body, name=name, grid=(width // chunk,), out_shape=tuple(o...  32.3 us
    pallas_call x2, Pallas kernels, sum_nt(): pl.pallas_call(body, name=name, grid=(steps,), out_shape=(jax.ShapeDtypeS...  21.6 us
    pallas_call x8, Pallas kernels, fold(): pl.pallas_call(body, name=name, grid=(2,), out_shape=tuple((jax.ShapeDtyp...  21.6 us
    pallas_call x1, Pallas kernels, attn_fwd(): pl.pallas_call(body, name='attn_fwd', out_shape=(out(n_tok, width), out(n...  18.6 us
    pallas_call x1, Pallas kernels, attn_bwd(): pl.pallas_call(body, name='attn_bwd', out_shape=jax.ShapeDtypeStruct(qkv....  18.5 us
    pallas_call x1, Pallas kernels, gated(): pl.pallas_call(body, name='gated', grid=(steps,), out_shape=(out, out, ou...  13.3 us
  transfers between devices with their start and end apart: 58, of which 20 were waited for; matrix products, arithmetic and copies ran while one was open for 2% of the time, Pallas kernels for 41%

profile of v2, /device:TPU:0, one launch (start us, length us, event | category | flops | bytes accessed | tf_op | source)
XLA Modules:
  0.0 340.2 jit_solution(14864313118091548370)
XLA Ops:
  10.6 2.7 collective-permute-start.6
  16.2 7.7 %collective-permute-done.6 = bf16[2,32,1408]{2,1,0:T(8,128)(2,1)S(1)} collective-permute-done((bf16[2,32,1408]{2,1,0:T(8,128)(2,1)S(1)}, bf16[2,32,1408]{2,1,0:T(8,128)(2,1)S(1)}, u32[]{:S(2)}, u32[]{:S(2)}) %collective-permute-start.6) | collective-permute-done | bytes 180256 | tf_op jit(solution)/shard_map/ppermute | solution.py:48
  24.6 8.0 %collective-permute-done.10 = bf16[2,32,1408]{2,1,0:T(8,128)(2,1)S(1)} collective-permute-done((bf16[2,32,1408]{2,1,0:T(8,128)(2,1)S(1)}, bf16[2,32,1408]{2,1,0:T(8,128)(2,1)S(1)}, u32[]{:S(2)}, u32[]{:S(2)}) %collective-permute-start.10) | collective-permute-done | bytes 180256 | tf_op jit(solution)/shard_map/ppermute | solution.py:48
  36.7 7.9 %collective-permute-done.12 = bf16[4,32,1408]{2,1,0:T(8,128)(2,1)S(1)} collective-permute-done((bf16[4,32,1408]{2,1,0:T(8,128)(2,1)S(1)}, bf16[4,32,1408]{2,1,0:T(8,128)(2,1)S(1)}, u32[]{:S(2)}, u32[]{:S(2)}) %collective-permute-start.12) | collective-permute-done | bytes 360480 | tf_op jit(solution)/shard_map/ppermute | solution.py:48
  49.2 10.3 %collective-permute-done.17 = bf16[2,32,2816]{2,1,0:T(8,128)(2,1)S(1)} collective-permute-done((bf16[2,32,2816]{2,1,0:T(8,128)(2,1)S(1)}, bf16[2,32,2816]{2,1,0:T(8,128)(2,1)S(1)}, u32[]{:S(2)}, u32[]{:S(2)}) %collective-permute-start.17) | collective-permute-done | bytes 360480 | tf_op jit(solution)/shard_map/ppermute | solution.py:48
  68.9 8.6 %collective-permute-done.20.refs_2_.refs_3_ = bf16[8,32,1408]{2,1,0:T(8,128)(2,1)} collective-permute-done((bf16[8,32,1408]{2,1,0:T(8,128)(2,1)S(1)}, bf16[8,32,1408]{2,1,0:T(8,128)(2,1)}, u32[]{:S(2)}, u32[]{:S(2)}) %collective-permute-start.20) | collective-permute-done | bytes 720928 | tf_op jit(solution)/shard_map/ppermute | solution.py:48
  77.5 8.2 %collective-permute-done.21.refs_1_.refs_2_ = bf16[8,32,1408]{2,1,0:T(8,128)(2,1)S(1)} collective-permute-done((bf16[8,32,1408]{2,1,0:T(8,128)(2,1)S(1)}, bf16[8,32,1408]{2,1,0:T(8,128)(2,1)S(1)}, u32[]{:S(2)}, u32[]{:S(2)}) %collective-permute-start.21) | collective-permute-done | bytes 720928 | tf_op jit(solution)/shard_map/ppermute | solution.py:48
  89.8 18.6 %attn_fwd.1 = (bf16[1024,1024]{1,0:T(8,128)(2,1)}, bf16[1024,768]{1,0:T(8,128)(2,1)}, bf16[1024,512]{1,0:T(8,128)(2,1)}, f32[1024,512]{1,0:T(8,128)}, f32[8,1024...) custom-call(s32[1]{0:T(128)} %bitcast.index_ref, ...), custom_call_target="tpu_custom_call" | custom-call | flops 1 | bytes 1 | tf_op jit(solution)/shard_map/attn_fwd/pallas_call | solution.py:590
  109.1 5.7 %collective-permute-done.26.refs_1_.refs_3_ = bf16[8,32,2816]{2,1,0:T(8,128)(2,1)} collective-permute-done((bf16[8,32,2816]{2,1,0:T(8,128)(2,1)S(1)}, bf16[8,32,2816]{2,1,0:T(8,128)(2,1)}, u32[]{:S(2)}, u32[]{:S(2)}) %collective-permute-start.26) | collective-permute-done | bytes 1441824 | tf_op jit(solution)/shard_map/ppermute | solution.py:48
  114.8 8.0 %down_back.1.d_act_ref = bf16[1024,1408]{1,0:T(8,128)(2,1)} custom-call(s32[1]{0:T(128)} %bitcast.index_ref, bf16[1024,1024]{1,0:T(8,128)(2,1)} %get-tuple-element.271.grad_ref.refs_0_.c_ref, bf16[8,32,1408]{2,1,0:T(8,128)(2,1)} %copy-done.7, bf16[8,32,1408]{2,1,0:T(8,128)(2,1)} %copy-done.8, bf16[8,32,1408]{2,1,0:T(8,128)(2,1)} %collective-permute-done.20.refs_2_.refs_3_, ...), custom_call_target="tpu_custom_call" | custom-call | flops 1 | bytes 1 | tf_op jit(solution)/shard_map/down_back/pallas_call | solution.py:667
  123.8 7.1 %residual.1 = (f32[1024,1024]{1,0:T(8,128)}, bf16[1024,1024]{1,0:T(8,128)(2,1)}) custom-call(bf16[1024,1024]{1,0:T(8,128)(2,1)} %get-tuple-element.274.tok_ref, bf16[256,1024]{1,0:T(8,128)(2,1)} %get-tuple-element.284.refs_0_, bf16[256,1024]{1,0:T(8,128)(2,1)} %get-tuple-element.285.refs_1_, bf16[256,1024]{1,0:T(8,128)(2,1)} %get-tuple-element.286.refs_2_, ...), custom_call_target="tpu_custom_call" | custom-call | flops 1 | bytes 1 | tf_op jit(solution)/shard_map/residual/pallas_call | solution.py:632
  130.9 13.3 %gated.1 = (bf16[1024,1408]{1,0:T(8,128)(2,1)}, bf16[1024,1408]{1,0:T(8,128)(2,1)}, bf16[1024,1408]{1,0:T(8,128)(2,1)}) custom-call(s32[1]{0:T(128)} %bitcast.index_ref, bf16[1024,1024]{1,0:T(8,128)(2,1)} %get-tuple-element.303.normed_ref.refs_0_, bf16[1024,1408]{1,0:T(8,128)(2,1)} %down_back.1.d_act_ref, bf16[8,32,2816]{2,1,0:T(8,128)(2,1)} %copy-done.4, ...), custom_call_target="tpu_custom_call" | custom-call | flops 1 | bytes 1 | tf_op jit(solution)/shard_map/gated/pallas_call | solution.py:707
  144.2 7.7 %grad_gate.1 = (bf16[8,32,1408]{2,1,0:T(8,128)(2,1)}, bf16[8,32,1408]{2,1,0:T(8,128)(2,1)}, bf16[8,32,1408]{2,1,0:T(8,128)(2,1)}, bf16[8,32,1408]{2,1,0:T(8,128)(2,1)}) custom-call(s32[1]{0:T(128)} %bitcast.index_ref, bf16[1024,1024]{1,0:T(8,128)(2,1)} %get-tuple-element.303.normed_ref.refs_0_, bf16[1024,1408]{1,0:T(8,128)(2,1)} %get-tuple-element.310.refs_1_.refs_0_), custom_call_target="tpu_custom_call" | custom-call | flops 1 | bytes 1 | tf_op jit(solution)/shard_map/grad_gate/pallas_call | solution.py:783
  154.9 12.7 %d_norm2.1 = (bf16[512,1024]{1,0:T(8,128)(2,1)}, bf16[512,1024]{1,0:T(8,128)(2,1)}) custom-call(s32[1]{0:T(128)} %bitcast.index_ref, bf16[1024,1408]{1,0:T(8,128)(2,1)} %get-tuple-element.310.refs_1_.refs_0_, bf16[1024,1408]{1,0:T(8,128)(2,1)} %get-tuple-element.318.refs_1_.refs_2_, bf16[8,32,2816]{2,1,0:T(8,128)(2,1)} %copy-done.4, ...), custom_call_target="tpu_custom_call" | custom-call | flops 1 | bytes 1 | tf_op jit(solution)/shard_map/d_norm2/pallas_call | solution.py:826
  172.8 3.2 fold.4
  178.6 7.6 %grad_down.1 = (bf16[8,32,1408]{2,1,0:T(8,128)(2,1)}, bf16[8,32,1408]{2,1,0:T(8,128)(2,1)}, bf16[8,32,1408]{2,1,0:T(8,128)(2,1)}, bf16[8,32,1408]{2,1,0:T(8,128)(2,1)}) custom-call(s32[1]{0:T(128)} %bitcast.index_ref, bf16[1024,1024]{1,0:T(8,128)(2,1)} %get-tuple-element.271.grad_ref.refs_0_.c_ref, bf16[1024,1408]{1,0:T(8,128)(2,1)} %get-tuple-element.413.refs_1_.refs_0_), custom_call_target="tpu_custom_call" | custom-call | flops 1 | bytes 1 | tf_op jit(solution)/shard_map/grad_down/pallas_call | solution.py:783
  188.7 9.5 %norm_back.1 = (f32[512,1024]{1,0:T(8,128)}, bf16[1024,1024]{1,0:T(8,128)(2,1)}, bf16[1024,512]{1,0:T(8,128)(2,1)}, f32[8,1024]{1,0:T(8,128)}) custom-call(s32[1]{0:T(128)} %bitcast.index_ref, f32[1024,1024]{1,0:T(8,128)} %get-tuple-element.301.hres_ref.h_ref, bf16[1024,1024]{1,0:T(8,128)(2,1)} %get-tuple-element.271.grad_ref.refs_0_.c_ref, ...), custom_call_target="tpu_custom_call" | custom-call | flops 1 | bytes 1 | tf_op jit(solution)/shard_map/norm_back/pallas_call | solution.py:888
  198.2 9.6 %grad_up.1 = (bf16[8,32,1920]{2,1,0:T(8,128)(2,1)}, bf16[8,32,1920]{2,1,0:T(8,128)(2,1)}, bf16[8,32,1920]{2,1,0:T(8,128)(2,1)}, bf16[8,32,1920]{2,1,0:T(8,128)(2,1)}) custom-call(s32[1]{0:T(128)} %bitcast.index_ref, bf16[1024,1024]{1,0:T(8,128)(2,1)} %get-tuple-element.303.normed_ref.refs_0_, bf16[1024,1024]{1,0:T(8,128)(2,1)} %get-tuple-element.336.refs_1_, ...), custom_call_target="tpu_custom_call" | custom-call | flops 1 | bytes 1 | tf_op jit(solution)/shard_map/grad_up/pallas_call | solution.py:783
  212.8 18.5 %attn_bwd.1.refs_1_.d_ref = bf16[1024,768]{1,0:T(8,128)(2,1)} custom-call(s32[2,4]{1,0:T(2,128)} %pad_add_fusion.seq_ref, bf16[1024,768]{1,0:T(8,128)(2,1)} %get-tuple-element.278.qkv_ref, bf16[1024,512]{1,0:T(8,128)(2,1)} %get-tuple-element.279.refs_3_.y_ref, bf16[1024,512]{1,0:T(8,128)(2,1)} %get-tuple-element.351.dy_ref, ...), custom_call_target="tpu_custom_call" | custom-call | flops 1 | bytes 1 | tf_op jit(solution)/shard_map/attn_bwd/pallas_call | solution.py:965
  232.4 3.3 fold.5
  237.2 2.7 fold_z.4
  239.9 8.3 %collective-permute-start.42 = (bf16[1,2,32,1408]{3,2,1,0:T(8,128)(2,1)}, bf16[1,2,32,1408]{3,2,1,0:T(8,128)(2,1)}, u32[]{:S(2)}, u32[]{:S(2)}) collective-permute-start(bf16[1,2,32,1408]{3,2,1,0:T(8,128)(2,1)} %get-tuple-element.393), channel_id=1, source_target_pairs={{0,16},{1,17},{2,18},{3,19},{4,20},{5,21},{6,22},{7,23},{8,24},{9,... | collective-permute-start | bytes 540680 | tf_op jit(solution)/shard_map/ppermute | solution.py:48
  248.3 3.8 %fold.6 = (bf16[4,32,1920]{2,1,0:T(8,128)(2,1)}, bf16[4,32,1920]{2,1,0:T(8,128)(2,1)}, bf16[4,32,1920]{2,1,0:T(8,128)(2,1)}, bf16[4,32,1920]{2,1,0:T(8,128)(2,1)}) custom-call(bf16[8,32,1920]{2,1,0:T(8,128)(2,1)} %get-tuple-element.350.refs_0_, bf16[8,32,1920]{2,1,0:T(8,128)(2,1)} %copy-done.15, bf16[8,32,1920]{2,1,0:T(8,128)(2,1)} %get-tuple-element.398.refs_2_, ...), custom_call_target="tpu_custom_call" | custom-call | flops 1 | bytes 1 | tf_op jit(solution)/shard_map/fold/pallas_call | solution.py:171
  253.5 7.3 %grad_attn.1 = (bf16[8,32,896]{2,1,0:T(8,128)(2,1)}, bf16[8,32,896]{2,1,0:T(8,128)(2,1)}, bf16[8,32,896]{2,1,0:T(8,128)(2,1)}, bf16[8,32,896]{2,1,0:T(8,128)(2,1)}) custom-call(s32[1]{0:T(128)} %bitcast.index_ref, bf16[1024,1024]{1,0:T(8,128)(2,1)} %get-tuple-element.371.refs_0_, bf16[1024,768]{1,0:T(8,128)(2,1)} %attn_bwd.1.refs_1_.d_ref, ...), custom_call_target="tpu_custom_call" | custom-call | flops 1 | bytes 1 | tf_op jit(solution)/shard_map/grad_attn/pallas_call | solution.py:783
  266.5 6.5 %norm_one_part.1 = (bf16[512,1024]{1,0:T(8,128)(2,1)}, bf16[512,1024]{1,0:T(8,128)(2,1)}) custom-call(s32[1]{0:T(128)} %bitcast.index_ref, bf16[1024,768]{1,0:T(8,128)(2,1)} %attn_bwd.1.refs_1_.d_ref, bf16[8,32,1408]{2,1,0:T(8,128)(2,1)} %copy-done.1, bf16[8,32,1408]{2,1,0:T(8,128)(2,1)} %copy-done.2, bf16[8,32,1408]{2,1,0:T(8,128)(2,1)} %copy-done, ...), custom_call_target="tpu_custom_call" | custom-call | flops 1 | bytes 1 | tf_op jit(solution)/shard_map/norm_one_part/pallas_call | solution.py:1004
  274.2 9.0 %down.1 = (bf16[512,1024]{1,0:T(8,128)(2,1)}, bf16[512,1024]{1,0:T(8,128)(2,1)}) custom-call(s32[1]{0:T(128)} %bitcast.index_ref, bf16[1024,1408]{1,0:T(8,128)(2,1)} %get-tuple-element.413.refs_1_.refs_0_, bf16[8,32,1408]{2,1,0:T(8,128)(2,1)} %copy-done.7, bf16[8,32,1408]{2,1,0:T(8,128)(2,1)} %copy-done.8, ...), custom_call_target="tpu_custom_call" | custom-call | flops 1 | bytes 1 | tf_op jit(solution)/shard_map/down/pallas_call | solution.py:826
  287.3 2.7 fold.7
  291.4 6.1 %collective-permute-done.51.refs_1_ = bf16[4,32,896]{2,1,0:T(8,128)(2,1)S(1)} collective-permute-done((bf16[4,32,896]{2,1,0:T(8,128)(2,1)}, bf16[4,32,896]{2,1,0:T(8,128)(2,1)S(1)}, u32[]{:S(2)}, u32[]{:S(2)}) %collective-permute-start.51) | collective-permute-done | bytes 229408 | tf_op jit(solution)/shard_map/ppermute | solution.py:48
  307.3 2.9 collective-permute-start.56
  311.5 6.6 %finish.1 = (bf16[512,1024]{1,0:T(8,128)(2,1)}, bf16[512,1024]{1,0:T(8,128)(2,1)}) custom-call(bf16[512,1024]{1,0:T(8,128)(2,1)} %get-tuple-element.390.part_ref, bf16[512,1024]{1,0:T(8,128)(2,1)} %copy-done.12, bf16[512,1024]{1,0:T(8,128)(2,1)} %tok_ref.1, f32[512,1024]{1,0:T(8,128)} %get-tuple-element.434.dh_ref, ...), custom_call_target="tpu_custom_call" | custom-call | flops 1 | bytes 1 | tf_op jit(solution)/shard_map/finish/pallas_call | solution.py:1042
  320.6 8.8 %collective-permute-done.56.refs_3_ = bf16[1,2,32,1408]{3,2,1,0:T(8,128)(2,1)S(1)} collective-permute-done((bf16[1,2,32,1408]{3,2,1,0:T(8,128)(2,1)}, bf16[1,2,32,1408]{3,2,1,0:T(8,128)(2,1)S(1)}, u32[]{:S(2)}, u32[]{:S(2)}) %collective-permute-start.56) | collective-permute-done | bytes 180256 | tf_op jit(solution)/shard_map/ppermute | solution.py:48
  331.7 2.6 add_up.1
  (225 shorter events, 93.4 us)
Async XLA Ops:
  3.6 20.3 %collective-permute-start.4 = (bf16[1,32,1408]{2,1,0:T(8,128)(2,1)}, bf16[1,32,1408]{2,1,0:T(8,128)(2,1)S(1)}, u32[]{:S(2)}, u32[]{:S(2)}) collective-permute-start(bf16[1,32,1408]{2,1,0:T(8,128)(2,1)} %bitcast.22), channel_id=1, source_target_pairs={{0,2},{1,3},{2,0},{3,1},{4,6},{5,7},{6,4},{7,5},{8,10},{9,11},{10,... | collective-permute-start | bytes 270344 | tf_op jit(solution)/shard_map/ppermute | solution.py:48
  8.0 15.9 %collective-permute-start.5 = (bf16[1,32,1408]{2,1,0:T(8,128)(2,1)S(1)}, bf16[1,32,1408]{2,1,0:T(8,128)(2,1)S(1)}, u32[]{:S(2)}, u32[]{:S(2)}) collective-permute-start(bf16[1,32,1408]{2,1,0:T(8,128)(2,1)S(1)} %get-tuple-element.478), channel_id=1, source_target_pairs={{0,4},{1,5},{2,6},{3,7},{4,0},{5,1},{6,2},{7,3},{8,12},{9,13},{10,... | collective-permute-start | bytes 270344 | tf_op jit(solution)/shard_map/ppermute | solution.py:48
  15.8 29.2 %collective-permute-start.11 = (bf16[2,32,2816]{2,1,0:T(8,128)(2,1)S(1)}, bf16[2,32,2816]{2,1,0:T(8,128)(2,1)S(1)}, u32[]{:S(2)}, u32[]{:S(2)}) collective-permute-start(bf16[2,32,2816]{2,1,0:T(8,128)(2,1)S(1)} %pad_maximum_fusion.4), channel_id=1, source_target_pairs={{0,16},{1,17},{2,18},{3,19},{4,20},{5,21},{6,22},{7,23},{8,24},{9,... | collective-permute-start | bytes 1081352 | tf_op jit(solution)/shard_map/ppermute | solution.py:48
  32.7 16.5 %collective-permute-start.16 = (bf16[2,32,2816]{2,1,0:T(8,128)(2,1)S(1)}, bf16[2,32,2816]{2,1,0:T(8,128)(2,1)S(1)}, u32[]{:S(2)}, u32[]{:S(2)}) collective-permute-start(bf16[2,32,2816]{2,1,0:T(8,128)(2,1)S(1)} %pad_maximum_fusion.4), channel_id=1, source_target_pairs={{0,8},{1,9},{2,10},{3,11},{4,12},{5,13},{6,14},{7,15},{8,0},{9,1},... | collective-permute-start | bytes 1081352 | tf_op jit(solution)/shard_map/ppermute | solution.py:48
  45.3 32.2 %collective-permute-start.20 = (bf16[8,32,1408]{2,1,0:T(8,128)(2,1)S(1)}, bf16[8,32,1408]{2,1,0:T(8,128)(2,1)}, u32[]{:S(2)}, u32[]{:S(2)}) collective-permute-start(bf16[8,32,1408]{2,1,0:T(8,128)(2,1)S(1)} %constant_dynamic-update-slice_fusion.refs_0_.refs_1_), channel_id=1, source_target_pairs={{0,16},{1,17},{2,18},{3,19},{4,20},{5,21},{6,22},{7,23},{8,24},{9,... | collective-permute-start | bytes 2162696 | tf_op jit(solution)/shard_map/ppermute | solution.py:48
  63.3 22.4 %collective-permute-start.21 = (bf16[8,32,1408]{2,1,0:T(8,128)(2,1)S(1)}, bf16[8,32,1408]{2,1,0:T(8,128)(2,1)S(1)}, u32[]{:S(2)}, u32[]{:S(2)}) collective-permute-start(bf16[8,32,1408]{2,1,0:T(8,128)(2,1)S(1)} %constant_dynamic-update-slice_fusion.refs_0_.refs_1_), channel_id=1, source_target_pairs={{0,8},{1,9},{2,10},{3,11},{4,12},{5,13},{6,14},{7,15},{8,0},{9,1},... | collective-permute-start | bytes 2162696 | tf_op jit(solution)/shard_map/ppermute | solution.py:48
  63.3 22.4 %collective-permute-start.18 = (bf16[4,32,2816]{2,1,0:T(8,128)(2,1)S(1)}, bf16[4,32,2816]{2,1,0:T(8,128)(2,1)S(1)}, u32[]{:S(2)}, u32[]{:S(2)}) collective-permute-start(bf16[4,32,2816]{2,1,0:T(8,128)(2,1)S(1)} %pad_maximum_fusion.2), channel_id=1, source_target_pairs={{0,2},{1,3},{2,0},{3,1},{4,6},{5,7},{6,4},{7,5},{8,10},{9,11},{10,... | collective-permute-start | bytes 2162696 | tf_op jit(solution)/shard_map/ppermute | solution.py:48
  64.8 20.9 %collective-permute-start.19 = (bf16[4,32,2816]{2,1,0:T(8,128)(2,1)S(1)}, bf16[4,32,2816]{2,1,0:T(8,128)(2,1)S(1)}, u32[]{:S(2)}, u32[]{:S(2)}) collective-permute-start(bf16[4,32,2816]{2,1,0:T(8,128)(2,1)S(1)} %pad_maximum_fusion.3), channel_id=1, source_target_pairs={{0,4},{1,5},{2,6},{3,7},{4,0},{5,1},{6,2},{7,3},{8,12},{9,13},{10,... | collective-permute-start | bytes 2162696 | tf_op jit(solution)/shard_map/ppermute | solution.py:48
  85.8 29.0 %collective-permute-start.26 = (bf16[8,32,2816]{2,1,0:T(8,128)(2,1)S(1)}, bf16[8,32,2816]{2,1,0:T(8,128)(2,1)}, u32[]{:S(2)}, u32[]{:S(2)}) collective-permute-start(bf16[8,32,2816]{2,1,0:T(8,128)(2,1)S(1)} %constant_dynamic-update-slice_fusion.16.refs_0_.refs_2_), channel_id=1, source_target_pairs={{0,4},{1,5},{2,6},{3,7},{4,0},{5,1},{6,2},{7,3},{8,12},{9,13},{10,... | collective-permute-start | bytes 4325384 | tf_op jit(solution)/shard_map/ppermute | solution.py:48
  87.2 35.6 %collective-permute-start.27 = (bf16[8,32,2816]{2,1,0:T(8,128)(2,1)S(1)}, bf16[8,32,2816]{2,1,0:T(8,128)(2,1)}, u32[]{:S(2)}, u32[]{:S(2)}) collective-permute-start(bf16[8,32,2816]{2,1,0:T(8,128)(2,1)S(1)} %constant_dynamic-update-slice_fusion.18.refs_2_.refs_4_), channel_id=1, source_target_pairs={{0,2},{1,3},{2,0},{3,1},{4,6},{5,7},{6,4},{7,5},{8,10},{9,11},{10,... | collective-permute-start | bytes 4325384 | tf_op jit(solution)/shard_map/ppermute | solution.py:48
  89.2 19.8 %collective-permute-start.28 = (bf16[8,32,1408]{2,1,0:T(8,128)(2,1)}, bf16[8,32,1408]{2,1,0:T(8,128)(2,1)S(1)}, u32[]{:S(2)}, u32[]{:S(2)}) collective-permute-start(bf16[8,32,1408]{2,1,0:T(8,128)(2,1)} %collective-permute-done.20.refs_2_.refs_3_), channel_id=1, source_target_pairs={{0,8},{1,9},{2,10},{3,11},{4,12},{5,13},{6,14},{7,15},{8,0},{9,1},... | collective-permute-start | bytes 2162696 | tf_op jit(solution)/shard_map/ppermute | solution.py:48
  152.0 18.8 %collective-permute-start.31 = (bf16[8,32,1408]{2,1,0:T(8,128)(2,1)}, bf16[8,32,1408]{2,1,0:T(8,128)(2,1)S(1)}, u32[]{:S(2)}, u32[]{:S(2)}) collective-permute-start(bf16[8,32,1408]{2,1,0:T(8,128)(2,1)} %get-tuple-element.323), channel_id=1, source_target_pairs={{0,4},{1,5},{2,6},{3,7},{4,0},{5,1},{6,2},{7,3},{8,12},{9,13},{10,... | collective-permute-start | bytes 2162696 | tf_op jit(solution)/shard_map/ppermute | solution.py:48
  153.4 18.5 %collective-permute-start.32 = (bf16[8,32,1408]{2,1,0:T(8,128)(2,1)}, bf16[8,32,1408]{2,1,0:T(8,128)(2,1)S(1)}, u32[]{:S(2)}, u32[]{:S(2)}) collective-permute-start(bf16[8,32,1408]{2,1,0:T(8,128)(2,1)} %get-tuple-element.324), channel_id=1, source_target_pairs={{0,2},{1,3},{2,0},{3,1},{4,6},{5,7},{6,4},{7,5},{8,10},{9,11},{10,... | collective-permute-start | bytes 2162696 | tf_op jit(solution)/shard_map/ppermute | solution.py:48
  167.6 19.6 %collective-permute-start.30 = (bf16[512,1024]{1,0:T(8,128)(2,1)}, bf16[512,1024]{1,0:T(8,128)(2,1)S(1)}, u32[]{:S(2)}, u32[]{:S(2)}) collective-permute-start(bf16[512,1024]{1,0:T(8,128)(2,1)} %get-tuple-element.322.refs_1_), channel_id=1, source_target_pairs={{0,1},{1,0},{2,3},{3,2},{4,5},{5,4},{6,7},{7,6},{8,9},{9,8},{10,11... | collective-permute-start | bytes 3145736 | tf_op jit(solution)/shard_map/ppermute | solution.py:48
  167.7 20.0 %collective-permute-start.29 = (bf16[512,1024]{1,0:T(8,128)(2,1)}, bf16[512,1024]{1,0:T(8,128)(2,1)S(1)}, u32[]{:S(2)}, u32[]{:S(2)}) collective-permute-start(bf16[512,1024]{1,0:T(8,128)(2,1)} %get-tuple-element.321.refs_0_), channel_id=1, source_target_pairs={{0,1},{1,0},{2,3},{3,2},{4,5},{5,4},{6,7},{7,6},{8,9},{9,8},{10,11... | collective-permute-start | bytes 3145736 | tf_op jit(solution)/shard_map/ppermute | solution.py:48
  175.9 31.9 %collective-permute-start.33 = (bf16[4,32,1408]{2,1,0:T(8,128)(2,1)}, bf16[4,32,1408]{2,1,0:T(8,128)(2,1)S(1)}, u32[]{:S(2)}, u32[]{:S(2)}) collective-permute-start(bf16[4,32,1408]{2,1,0:T(8,128)(2,1)} %get-tuple-element.347), channel_id=1, source_target_pairs={{0,2},{1,3},{2,0},{3,1},{4,6},{5,7},{6,4},{7,5},{8,10},{9,11},{10,... | collective-permute-start | bytes 1081352 | tf_op jit(solution)/shard_map/ppermute | solution.py:48
  177.4 30.4 %collective-permute-start.34 = (bf16[4,32,1408]{2,1,0:T(8,128)(2,1)}, bf16[4,32,1408]{2,1,0:T(8,128)(2,1)}, u32[]{:S(2)}, u32[]{:S(2)}) collective-permute-start(bf16[4,32,1408]{2,1,0:T(8,128)(2,1)} %get-tuple-element.348), channel_id=1, source_target_pairs={{0,4},{1,5},{2,6},{3,7},{4,0},{5,1},{6,2},{7,3},{8,12},{9,13},{10,... | collective-permute-start | bytes 1081352 | tf_op jit(solution)/shard_map/ppermute | solution.py:48
  186.2 45.1 %collective-permute-start.35 = (bf16[8,32,1408]{2,1,0:T(8,128)(2,1)}, bf16[8,32,1408]{2,1,0:T(8,128)(2,1)S(1)}, u32[]{:S(2)}, u32[]{:S(2)}) collective-permute-start(bf16[8,32,1408]{2,1,0:T(8,128)(2,1)} %get-tuple-element.354), channel_id=1, source_target_pairs={{0,4},{1,5},{2,6},{3,7},{4,0},{5,1},{6,2},{7,3},{8,12},{9,13},{10,... | collective-permute-start | bytes 2162696 | tf_op jit(solution)/shard_map/ppermute | solution.py:48
  187.2 44.2 %collective-permute-start.36 = (bf16[8,32,1408]{2,1,0:T(8,128)(2,1)}, bf16[8,32,1408]{2,1,0:T(8,128)(2,1)S(1)}, u32[]{:S(2)}, u32[]{:S(2)}) collective-permute-start(bf16[8,32,1408]{2,1,0:T(8,128)(2,1)} %get-tuple-element.355), channel_id=1, source_target_pairs={{0,2},{1,3},{2,0},{3,1},{4,6},{5,7},{6,4},{7,5},{8,10},{9,11},{10,... | collective-permute-start | bytes 2162696 | tf_op jit(solution)/shard_map/ppermute | solution.py:48
  207.9 29.4 %collective-permute-start.38 = (bf16[8,32,1920]{2,1,0:T(8,128)(2,1)}, bf16[8,32,1920]{2,1,0:T(8,128)(2,1)S(1)}, u32[]{:S(2)}, u32[]{:S(2)}) collective-permute-start(bf16[8,32,1920]{2,1,0:T(8,128)(2,1)} %get-tuple-element.361), channel_id=1, source_target_pairs={{0,4},{1,5},{2,6},{3,7},{4,0},{5,1},{6,2},{7,3},{8,12},{9,13},{10,... | collective-permute-start | bytes 2949128 | tf_op jit(solution)/shard_map/ppermute | solution.py:48
  209.0 28.2 %collective-permute-start.39 = (bf16[8,32,1920]{2,1,0:T(8,128)(2,1)}, bf16[8,32,1920]{2,1,0:T(8,128)(2,1)S(1)}, u32[]{:S(2)}, u32[]{:S(2)}) collective-permute-start(bf16[8,32,1920]{2,1,0:T(8,128)(2,1)} %get-tuple-element.362), channel_id=1, source_target_pairs={{0,2},{1,3},{2,0},{3,1},{4,6},{5,7},{6,4},{7,5},{8,10},{9,11},{10,... | collective-permute-start | bytes 2949128 | tf_op jit(solution)/shard_map/ppermute | solution.py:48
  212.8 18.5 %collective-permute-start.37 = (bf16[2,2,32,1408]{3,2,1,0:T(8,128)(2,1)}, bf16[2,2,32,1408]{3,2,1,0:T(8,128)(2,1)S(1)}, u32[]{:S(2)}, u32[]{:S(2)}) collective-permute-start(bf16[2,2,32,1408]{3,2,1,0:T(8,128)(2,1)} %get-tuple-element.359), channel_id=1, source_target_pairs={{0,8},{1,9},{2,10},{3,11},{4,12},{5,13},{6,14},{7,15},{8,0},{9,1},... | collective-permute-start | bytes 1081352 | tf_op jit(solution)/shard_map/ppermute | solution.py:48
  235.7 25.1 %collective-permute-start.40 = (bf16[4,32,1408]{2,1,0:T(8,128)(2,1)}, bf16[4,32,1408]{2,1,0:T(8,128)(2,1)S(1)}, u32[]{:S(2)}, u32[]{:S(2)}) collective-permute-start(bf16[4,32,1408]{2,1,0:T(8,128)(2,1)} %get-tuple-element.383), channel_id=1, source_target_pairs={{0,2},{1,3},{2,0},{3,1},{4,6},{5,7},{6,4},{7,5},{8,10},{9,11},{10,... | collective-permute-start | bytes 1081352 | tf_op jit(solution)/shard_map/ppermute | solution.py:48
  236.3 25.3 %collective-permute-start.41 = (bf16[4,32,1408]{2,1,0:T(8,128)(2,1)}, bf16[4,32,1408]{2,1,0:T(8,128)(2,1)}, u32[]{:S(2)}, u32[]{:S(2)}) collective-permute-start(bf16[4,32,1408]{2,1,0:T(8,128)(2,1)} %get-tuple-element.384), channel_id=1, source_target_pairs={{0,4},{1,5},{2,6},{3,7},{4,0},{5,1},{6,2},{7,3},{8,12},{9,13},{10,... | collective-permute-start | bytes 1081352 | tf_op jit(solution)/shard_map/ppermute | solution.py:48
  239.9 26.6 %collective-permute-start.42 = (bf16[1,2,32,1408]{3,2,1,0:T(8,128)(2,1)}, bf16[1,2,32,1408]{3,2,1,0:T(8,128)(2,1)}, u32[]{:S(2)}, u32[]{:S(2)}) collective-permute-start(bf16[1,2,32,1408]{3,2,1,0:T(8,128)(2,1)} %get-tuple-element.393), channel_id=1, source_target_pairs={{0,16},{1,17},{2,18},{3,19},{4,20},{5,21},{6,22},{7,23},{8,24},{9,... | collective-permute-start | bytes 540680 | tf_op jit(solution)/shard_map/ppermute | solution.py:48
  252.1 22.1 %collective-permute-start.44 = (bf16[4,32,1920]{2,1,0:T(8,128)(2,1)}, bf16[4,32,1920]{2,1,0:T(8,128)(2,1)S(1)}, u32[]{:S(2)}, u32[]{:S(2)}) collective-permute-start(bf16[4,32,1920]{2,1,0:T(8,128)(2,1)} %get-tuple-element.400), channel_id=1, source_target_pairs={{0,2},{1,3},{2,0},{3,1},{4,6},{5,7},{6,4},{7,5},{8,10},{9,11},{10,... | collective-permute-start | bytes 1474568 | tf_op jit(solution)/shard_map/ppermute | solution.py:48
  252.6 21.6 %collective-permute-start.45 = (bf16[4,32,1920]{2,1,0:T(8,128)(2,1)}, bf16[4,32,1920]{2,1,0:T(8,128)(2,1)S(1)}, u32[]{:S(2)}, u32[]{:S(2)}) collective-permute-start(bf16[4,32,1920]{2,1,0:T(8,128)(2,1)} %get-tuple-element.401), channel_id=1, source_target_pairs={{0,4},{1,5},{2,6},{3,7},{4,0},{5,1},{6,2},{7,3},{8,12},{9,13},{10,... | collective-permute-start | bytes 1474568 | tf_op jit(solution)/shard_map/ppermute | solution.py:48
  283.2 26.9 %collective-permute-start.49 = (bf16[512,1024]{1,0:T(8,128)(2,1)}, bf16[512,1024]{1,0:T(8,128)(2,1)S(1)}, u32[]{:S(2)}, u32[]{:S(2)}) collective-permute-start(bf16[512,1024]{1,0:T(8,128)(2,1)} %get-tuple-element.419), channel_id=1, source_target_pairs={{0,1},{1,0},{2,3},{3,2},{4,5},{5,4},{6,7},{7,6},{8,9},{9,8},{10,11... | collective-permute-start | bytes 3145736 | tf_op jit(solution)/shard_map/ppermute | solution.py:48
  283.3 26.9 %collective-permute-start.48 = (bf16[512,1024]{1,0:T(8,128)(2,1)}, bf16[512,1024]{1,0:T(8,128)(2,1)S(1)}, u32[]{:S(2)}, u32[]{:S(2)}) collective-permute-start(bf16[512,1024]{1,0:T(8,128)(2,1)} %get-tuple-element.418), channel_id=1, source_target_pairs={{0,1},{1,0},{2,3},{3,2},{4,5},{5,4},{6,7},{7,6},{8,9},{9,8},{10,11... | collective-permute-start | bytes 3145736 | tf_op jit(solution)/shard_map/ppermute | solution.py:48
  302.1 16.0 %collective-permute-start.53 = (bf16[2,2,32,896]{3,2,1,0:T(8,128)(2,1)}, bf16[2,2,32,896]{3,2,1,0:T(8,128)(2,1)S(1)}, u32[]{:S(2)}, u32[]{:S(2)}) collective-permute-start(bf16[2,2,32,896]{3,2,1,0:T(8,128)(2,1)} %get-tuple-element.443), channel_id=1, source_target_pairs={{0,8},{1,9},{2,10},{3,11},{4,12},{5,13},{6,14},{7,15},{8,0},{9,1},... | collective-permute-start | bytes 688136 | tf_op jit(solution)/shard_map/ppermute | solution.py:48
  305.2 24.2 %collective-permute-start.55 = (bf16[1,2,32,1920]{3,2,1,0:T(8,128)(2,1)}, bf16[1,2,32,1920]{3,2,1,0:T(8,128)(2,1)S(1)}, u32[]{:S(2)}, u32[]{:S(2)}) collective-permute-start(bf16[1,2,32,1920]{3,2,1,0:T(8,128)(2,1)} %get-tuple-element.448), channel_id=1, source_target_pairs={{0,16},{1,17},{2,18},{3,19},{4,20},{5,21},{6,22},{7,23},{8,24},{9,... | collective-permute-start | bytes 737288 | tf_op jit(solution)/shard_map/ppermute | solution.py:48
  307.3 22.1 %collective-permute-start.56 = (bf16[1,2,32,1408]{3,2,1,0:T(8,128)(2,1)}, bf16[1,2,32,1408]{3,2,1,0:T(8,128)(2,1)S(1)}, u32[]{:S(2)}, u32[]{:S(2)}) collective-permute-start(bf16[1,2,32,1408]{3,2,1,0:T(8,128)(2,1)} %get-tuple-element.450), channel_id=1, source_target_pairs={{0,16},{1,17},{2,18},{3,19},{4,20},{5,21},{6,22},{7,23},{8,24},{9,... | collective-permute-start | bytes 540680 | tf_op jit(solution)/shard_map/ppermute | solution.py:48
  (67 other events, 537.9 us)

commit v3 on v2

--- a/solution.py
+++ b/solution.py
@@ -118,15 +118,15 @@
 
 
 class GatherPlane:
-    def __init__(self, lay, keep, other):
-        self.lay, self.keep, self.other = lay, keep, other
+    def __init__(self, lay, *halves):
+        self.lay, self.halves = lay, halves
         self.orders = (lay.x + lay.y, lay.y + lay.x)
-        self.came = [lay.swap(h, bits[0]) for h, bits in zip((keep, other), self.orders)]
+        self.came = [lay.swap(h, bits[0]) for h, bits in zip(halves, self.orders)]
 
     def second(self, order):
         came = order(*self.came)
         self.held, self.came = [], []
-        for held, got, bits in zip((self.keep, self.other), came, self.orders):
+        for held, got, bits in zip(self.halves, came, self.orders):
             held = jnp.concatenate([held, got], axis=0)
             for bit in bits[1:-1]:
                 held = jnp.concatenate([held, self.lay.swap(held, bit)], axis=0)
@@ -239,28 +239,29 @@
         return self.kept, order(self.came)
 
 
-def add_up(ends):
+def add_up(core, ends):
     rows = ends[0][0].shape[2]
     cols = sum(kept.shape[3] for kept, _ in ends)
 
-    def body(*refs):
+    def body(core_ref, *refs):
+        first = core_ref[0] == 0
         at = 0
         for i, (kept, _) in enumerate(ends):
             width = kept.shape[3]
             total = refs[2 * i][0].astype(F32) + refs[2 * i + 1][0].astype(F32)
-            refs[-2][:, at : at + width] = total[0]
-            refs[-1][:, at : at + width] = total[1]
+            refs[-2][:, at : at + width] = jnp.where(first, total[0], total[1])
+            refs[-1][:, at : at + width] = jnp.where(first, total[1], total[0])
             at += width
 
     return pl.pallas_call(
         body,
         name="add_up",
         out_shape=(jax.ShapeDtypeStruct((rows, cols), F32),) * 2,
-        in_specs=[VMEM_SPEC] * (2 * len(ends)),
+        in_specs=[SMEM_SPEC] + [VMEM_SPEC] * (2 * len(ends)),
         out_specs=(VMEM_SPEC,) * 2,
         compiler_params=params(FOLD_MEGABYTES),
         cost_estimate=cost("add_up"),
-    )(*[a for end in ends for a in end])
+    )(core, *[a for end in ends for a in end])
 
 
 def wait_for(order, *streams):
@@ -281,76 +282,18 @@
     return masks
 
 
-class Blocks:
-    def __init__(self, lay, rows):
-        self.lay = lay
-        self.rows = rows
-        self.direct = rows % 16 == 0
-        self.shape = (lay.count, rows) if self.direct else (1, lay.count * rows)
-
-    def order(self, index):
-        return jnp.bitwise_xor(index, jnp.arange(self.lay.count))
-
-    def arrays(self, arrays, masks, index):
-        if self.direct:
-            return arrays
-        masks = [m for ms in masks for m in ms]
-        whole = jnp.concatenate(arrays, axis=0)
-        place = [0] * len(masks)
-        for i, m in enumerate(masks):
-            place[m] = i
-        whole = jnp.take(whole, jnp.asarray(place)[self.order(index)], axis=0)
-        return [whole.reshape(1, -1, whole.shape[-1])]
-
-    def copies_in(self, index, refs, masks, out_ref, sem, start, cols):
-        at = pl.ds(start, cols)
-        if not self.direct:
-            return [pltpu.make_async_copy(refs[0].at[:, :, at], out_ref, sem)]
-        return [
-            pltpu.make_async_copy(
-                ref.at[i, :, at], out_ref.at[jnp.bitwise_xor(index, m)], sem
-            )
-            for ref, ms in zip(refs, masks)
-            for i, m in enumerate(ms)
-        ]
-
-    def out_shapes(self, masks, columns):
-        if self.direct:
-            return [jax.ShapeDtypeStruct((len(m), self.rows, columns), BF16) for m in masks]
-        return [jax.ShapeDtypeStruct((1, self.lay.count * self.rows, columns), BF16)]
-
-    def copies_out(self, index, in_ref, refs, masks, sem):
-        if not self.direct:
-            return [pltpu.make_async_copy(in_ref, refs[0], sem)]
-        return [
-            pltpu.make_async_copy(
-                in_ref.at[jnp.bitwise_xor(index, m)], ref.at[i], sem
-            )
-            for ref, ms in zip(refs, masks)
-            for i, m in enumerate(ms)
-        ]
-
-    def split(self, outs, masks, index):
-        if self.direct:
-            return outs
-        whole = outs[0].reshape(self.lay.count, self.rows, -1)
-        whole = jnp.take(whole, self.order(index), axis=0)
-        return [jnp.take(whole, jnp.asarray(m), axis=0) for m in masks]
-
-
-def start_all(copies):
-    for copy in copies:
-        copy.start()
-
-
 WEIGHTS = {}
-FOLD_MEGABYTES = 60
+FOLD_MEGABYTES = 16
 
 
 def cost(name):
     return pl.CostEstimate(
         flops=int(WEIGHTS.get(name, 0) * 1e9) + 1, bytes_accessed=1, transcendentals=0
     )
+
+
+def near(*values):
+    return [pltpu.with_memory_space_constraint(v, pltpu.VMEM) for v in values]
 
 
 def params(megabytes):
@@ -416,22 +359,50 @@
     return total
 
 
-class Weights:
-    def __init__(self, blk, arrays, masks, index):
-        self.blk, self.masks = blk, masks
-        self.arrays = blk.arrays(arrays, masks, index)
-        self.count = len(self.arrays)
-        self.specs = [ANY_SPEC] * self.count
-
-    def scratch(self, cols):
-        return [pltpu.VMEM((*self.blk.shape, cols), BF16), pltpu.SemaphoreType.DMA]
-
-    def load(self, index_ref, refs, w_ref, sem, start=0):
-        cols = w_ref.shape[-1]
-        start_all(self.blk.copies_in(index_ref[0], refs, self.masks, w_ref, sem, start, cols))
-
-    def wait(self, w_ref, sem):
-        pltpu.make_async_copy(w_ref, w_ref, sem).wait()
+def stacked(refs, start, size):
+    return jnp.concatenate([r[:, start : start + size] for r in refs], axis=0)
+
+
+def whole_specs(arrays):
+    return [pl.BlockSpec(a.shape, lambda i: (0,) * a.ndim) for a in arrays]
+
+
+def shuffle(index, masks, values):
+    n, width = values[0].shape
+    rows = width // len(masks)
+    steps = n // 256
+    count = len(values)
+
+    def body(index_ref, masks_ref, *refs):
+        ins, outs, order_ref = refs[:count], refs[count:-1], refs[-1]
+
+        @pl.when(pl.program_id(0) == 0)
+        def _():
+            def fill(at):
+                r = lax.broadcasted_iota(jnp.int32, (at.size, width), 0) + at.start
+                c = lax.broadcasted_iota(jnp.int32, (at.size, width), 1)
+                block = jnp.bitwise_xor(masks_ref[...], index_ref[0])
+                here = (r // rows == block) & (r % rows == c % rows)
+                order_ref[at, :] = jnp.where(here, 1.0, 0.0).astype(BF16)
+
+            row_chunks(width, 128, fill)
+
+        for i, o in zip(ins, outs):
+            o[...] = dot_nn(i[...], order_ref[...]).astype(BF16)
+
+    table = jnp.repeat(jnp.asarray(masks, jnp.int32), rows)[None]
+    at = rows_spec(256, width)
+    keep = pl.BlockSpec((width, width), lambda i: (0, 0))
+    return pl.pallas_call(
+        body,
+        name="shuffle",
+        grid=(steps,),
+        out_shape=(*[pltpu.VMEM(v.shape, BF16) for v in values], pltpu.VMEM((width, width), BF16)),
+        in_specs=[SMEM_SPEC, pl.BlockSpec((1, width), lambda i: (0, 0))] + [at] * count,
+        out_specs=(*[at] * count, keep),
+        compiler_params=params(20),
+        cost_estimate=cost("shuffle"),
+    )(index, table, *values)
 
 
 def prepare(core, groups, gains):
@@ -486,7 +457,7 @@
         out_shape=tuple(out),
         in_specs=[SMEM_SPEC] + [VMEM_SPEC] * (n_in + 2),
         out_specs=(VMEM_SPEC,) * len(out),
-        compiler_params=params(60),
+        compiler_params=params(16),
     )(core, *[g[None] for g in gains], *flat)
 
 
@@ -514,25 +485,23 @@
         out_shape=tuple(out),
         in_specs=[SMEM_SPEC, VMEM_SPEC, VMEM_SPEC],
         out_specs=(VMEM_SPEC,) * len(out),
-        compiler_params=params(60),
+        compiler_params=params(16),
     )(core, mine, came)
 
 
-def attn_fwd(weights, index, seq, tok, dims):
+def attn_fwd(weights, seq, tok, dims):
     n_tok, width, buffers = tok.shape[0], tok.shape[1], seq.shape[0]
     length = n_tok // buffers
     nq, nv, cols = dims
     n_qkv = 2 * nq + nv
-    n_in = weights.count
-
-    def body(index_ref, seq_ref, tok_ref, *refs):
+    n_in = len(weights)
+
+    def body(seq_ref, tok_ref, *refs):
         w_in = refs[:n_in]
         normed_ref, qkv_ref, y_ref, dinv_ref, gain_ref = refs[n_in : n_in + 5]
         part_refs = refs[n_in + 5 : n_in + 5 + 2 * buffers]
-        mask_ref, w_ref, sem = refs[n_in + 5 + 2 * buffers :]
-        weights.load(index_ref, w_in, w_ref, sem)
-        weights.wait(w_ref, sem)
-        w_gain = w_ref[:, :, n_qkv + nv :].reshape(width, LANES).astype(F32).T
+        mask_ref = refs[n_in + 5 + 2 * buffers]
+        w_gain = stacked(w_in, n_qkv + nv, LANES).astype(F32).T
         gain_ref[0:1, :] = w_gain[0:1] + w_gain[1:2]
         gain_ref[1:2, :] = w_gain[2:3] + w_gain[3:4]
         gain_ref[2:8, :] = jnp.zeros((6, width), F32)
@@ -543,8 +512,7 @@
             inverse = lax.rsqrt(jnp.mean(x * x, axis=-1, keepdims=True) + EPS)
             normed = (x * inverse * gain).astype(BF16)
             normed_ref[at, :] = normed
-            w = w_ref[:, :, :n_qkv].reshape(width, n_qkv)
-            qkv_ref[at, :] = dot_nn(normed, w).astype(BF16)
+            qkv_ref[at, :] = dot_nn(normed, stacked(w_in, 0, n_qkv)).astype(BF16)
 
         row_chunks(n_tok, 256, project)
 
@@ -581,29 +549,28 @@
                 return carry
 
             lax.fori_loop(0, nv // LANES, pair, 0)
-            w = w_ref[:, :, n_qkv : n_qkv + nv].reshape(width, nv)
-            part = dot_nt(y_ref[base : base + length, :], w).astype(BF16)
-            part_refs[2 * b][...] = part[: length // 2]
-            part_refs[2 * b + 1][...] = part[length // 2 :]
-
-    out = lambda *s, t=BF16: jax.ShapeDtypeStruct(s, t)
+            for half in range(2):
+                at = slice(base + half * (length // 2), base + (half + 1) * (length // 2))
+                part = dot_nt(y_ref[at, :], stacked(w_in, n_qkv, nv))
+                part_refs[2 * b + half][...] = part.astype(BF16)
+
     return pl.pallas_call(
         body,
         name="attn_fwd",
         out_shape=(
-            out(n_tok, width),
-            out(n_tok, n_qkv),
-            out(n_tok, nv),
-            out(n_tok, nv, t=F32),
-            out(8, width, t=F32),
-            *(out(length // 2, width) for _ in range(2 * buffers)),
+            pltpu.VMEM((n_tok, width), BF16),
+            pltpu.VMEM((n_tok, n_qkv), BF16),
+            pltpu.VMEM((n_tok, nv), BF16),
+            pltpu.VMEM((n_tok, nv), F32),
+            jax.ShapeDtypeStruct((8, width), F32),
+            *(jax.ShapeDtypeStruct((length // 2, width), BF16) for _ in range(2 * buffers)),
         ),
-        in_specs=[SMEM_SPEC, SMEM_SPEC, VMEM_SPEC] + weights.specs,
+        in_specs=[SMEM_SPEC] + [VMEM_SPEC] * (1 + n_in),
         out_specs=(VMEM_SPEC,) * (5 + 2 * buffers),
-        scratch_shapes=[pltpu.VMEM((length, length), F32)] + weights.scratch(cols),
-        compiler_params=params(60),
+        scratch_shapes=[pltpu.VMEM((length, length), F32)],
+        compiler_params=params(28),
         cost_estimate=cost("attn_fwd"),
-    )(index, seq, tok, *weights.arrays)
+    )(seq, *near(tok), *weights)
 
 
 def residual(tok, part, came, gains):
@@ -633,68 +600,57 @@
         body,
         name="residual",
         grid=(steps,),
-        out_shape=(
-            jax.ShapeDtypeStruct((n_tok, width), F32),
-            jax.ShapeDtypeStruct((n_tok, width), BF16),
-        ),
+        out_shape=(pltpu.VMEM((n_tok, width), F32), pltpu.VMEM((n_tok, width), BF16)),
         in_specs=[at]
         + piece_specs(n, steps, size, width)
         + piece_specs(n, steps, size, width, True)
         + [pl.BlockSpec((8, width), lambda i: (0, 0))],
         out_specs=(at, at),
-        compiler_params=params(60),
+        compiler_params=params(16),
         cost_estimate=cost("residual"),
-    )(tok, *part, *came, gains)
-
-
-def down_back(weights, index, grad_out, cols):
+    )(*near(tok), *part, *came, gains)
+
+
+def in_order(refs, places, rows):
+    if places is None:
+        return jnp.concatenate([r[...] for r in refs], axis=0)
+    return jnp.concatenate([refs[j][i * rows : (i + 1) * rows, :] for j, i in places], axis=0)
+
+
+def down_back(weights, places, rows, grad_out):
     n_tok, width = grad_out.shape
-    n_in = weights.count
+    cols = weights[0].shape[1]
     steps = 4
     size = n_tok // steps
 
-    def body(index_ref, grad_ref, *refs):
-        out_ref, w_ref, sem = refs[n_in:]
-
-        @pl.when(pl.program_id(0) == 0)
-        def _():
-            weights.load(index_ref, refs[:n_in], w_ref, sem)
-            weights.wait(w_ref, sem)
-
-        w = w_ref[...].reshape(width, cols)
-        out_ref[...] = dot_nn(grad_ref[...], w).astype(BF16)
+    def body(grad_ref, *refs):
+        w = in_order(refs[:-1], places, rows)
+        refs[-1][...] = dot_nn(grad_ref[...], w).astype(BF16)
 
     return pl.pallas_call(
         body,
         name="down_back",
         grid=(steps,),
-        out_shape=jax.ShapeDtypeStruct((n_tok, cols), BF16),
-        in_specs=[SMEM_SPEC, rows_spec(size, width)] + weights.specs,
+        out_shape=pltpu.VMEM((n_tok, cols), BF16),
+        in_specs=[rows_spec(size, width)] + whole_specs(weights),
         out_specs=rows_spec(size, cols),
-        scratch_shapes=weights.scratch(cols),
-        compiler_params=params(60),
+        compiler_params=params(20),
         cost_estimate=cost("down_back"),
-    )(index, grad_out, *weights.arrays)
-
-
-def gated(weights, index, normed, d_act, stride):
+    )(*near(grad_out), *weights)
+
+
+def gated(weights, normed, d_act):
     n_tok, width = normed.shape
     cols = d_act.shape[1]
-    n_in = weights.count
+    n_in = len(weights)
     steps = 4
     size = n_tok // steps
 
-    def body(index_ref, normed_ref, d_act_ref, *refs):
-        act_ref, d_gate_ref, d_up_ref, w_ref, sem = refs[n_in:]
-
-        @pl.when(pl.program_id(0) == 0)
-        def _():
-            weights.load(index_ref, refs[:n_in], w_ref, sem)
-            weights.wait(w_ref, sem)
-
+    def body(normed_ref, d_act_ref, *refs):
+        act_ref, d_gate_ref, d_up_ref = refs[n_in:]
         x = normed_ref[...]
-        gate = dot_nn(x, w_ref[:, :, :cols].reshape(width, cols))
-        up = dot_nn(x, w_ref[:, :, stride : stride + cols].reshape(width, cols))
+        gate = dot_nn(x, stacked(refs[:n_in], 0, cols))
+        up = dot_nn(x, stacked(refs[:n_in], cols, cols))
         sig = 1.0 / (1.0 + jnp.exp(-gate))
         silu = gate * sig
         act_ref[...] = (silu * up).astype(BF16)
@@ -702,124 +658,97 @@
         d_gate_ref[...] = (d * up * sig * (1.0 + gate * (1.0 - sig))).astype(BF16)
         d_up_ref[...] = (d * silu).astype(BF16)
 
-    out = jax.ShapeDtypeStruct((n_tok, cols), BF16)
+    out = pltpu.VMEM((n_tok, cols), BF16)
     at = rows_spec(size, cols)
     return pl.pallas_call(
         body,
         name="gated",
         grid=(steps,),
         out_shape=(out, out, out),
-        in_specs=[SMEM_SPEC, rows_spec(size, width), at] + weights.specs,
+        in_specs=[rows_spec(size, width), at] + whole_specs(weights),
         out_specs=(at, at, at),
-        scratch_shapes=weights.scratch(2 * stride),
-        compiler_params=params(60),
+        compiler_params=params(30),
         cost_estimate=cost("gated"),
-    )(index, normed, d_act, *weights.arrays)
-
-
-def weight_grad(blk, masks, index, lefts, rights, gain=None, name="weight_grad"):
+    )(*near(normed, d_act), *weights)
+
+
+def weight_grad(lefts, rights, gain=None, name="weight_grad"):
     n_tok, width = lefts[0].shape
     sizes = [r.shape[1] for r in rights]
     cols = sum(sizes) + (LANES if gain is not None else 0)
-    out_shapes = blk.out_shapes(masks, cols)
-    n_out = len(out_shapes)
-    n = len(lefts)
-    chunk = 256
-
-    extras, specs, scratch = [], [], []
+    n, pieces = len(lefts), 4
+    chunk = width // pieces
+    extras, specs = [], []
     if gain is not None:
         weights, gains, other = gain
-        extras = [gains, other, *weights.arrays]
-        specs = [pl.BlockSpec((8, chunk), lambda i: (0, i))] * 2 + weights.specs
-        scratch = weights.scratch(sizes[0])
-
-    def body(index_ref, *refs):
+        extras = [gains, other, *weights]
+        specs = [pl.BlockSpec((8, chunk), lambda i: (0, i))] * 2 + whole_specs(weights)
+
+    def body(*refs):
         left_refs, right_refs = refs[:n], refs[n : 2 * n]
-        ins = refs[2 * n : 2 * n + len(extras)]
-        outs, total_ref, sem = (*refs[2 * n + len(extras) :],)[:n_out], refs[-2 - len(scratch)], refs[-1 - len(scratch)]
-        per = chunk // blk.rows if blk.direct else 1
-        i = pl.program_id(0)
-
-        def put(value, start):
-            size = value.shape[1]
-            if blk.direct:
-                total_ref[pl.ds(i * per, per), :, start : start + size] = value.reshape(
-                    per, blk.rows, size
-                )
-            else:
-                at = pl.ds(pl.multiple_of(i * chunk, chunk), chunk)
-                total_ref[0, at, start : start + size] = value
-
-        if gain is not None:
-            w_ref, w_sem = refs[-2], refs[-1]
-
-            @pl.when(i == 0)
-            def _():
-                weights.load(index_ref, ins[2:], w_ref, w_sem)
-                weights.wait(w_ref, w_sem)
-
-        start = 0
-        for left, right, size in zip(left_refs, right_refs, sizes):
-            value = dot_tn(left[...], right[...])
-            put(value.astype(BF16), start)
-            if gain is not None and start == 0:
-                if blk.direct:
-                    w = w_ref[pl.ds(i * per, per), :, :].reshape(chunk, size)
-                else:
-                    w = w_ref[0, pl.ds(pl.multiple_of(i * chunk, chunk), chunk), :]
-                one = jnp.sum(value * w.astype(F32), axis=-1, keepdims=True)
+        ins, outs = refs[2 * n : 2 * n + len(extras)], refs[2 * n + len(extras) :]
+
+        values = [dot_tn(left[...], right[...]) for left, right in zip(left_refs, right_refs)]
+
+        def put(out, w_ref):
+            start = 0
+            for value, size in zip(values, sizes):
+                out[:, start : start + size] = value.astype(BF16)
+                start += size
+            if gain is not None:
+                one = values[0] * w_ref[:, : sizes[0]].astype(F32)
+                one = jnp.sum(one, axis=-1, keepdims=True)
                 two = jnp.sum(ins[1][...], axis=0, keepdims=True)
-                rows = jnp.concatenate([ins[0][0:1, :], two, jnp.zeros((LANES - 2, chunk), F32)])
-                turned = rows.T
+                lines = [ins[0][0:1, :], two, jnp.zeros((LANES - 2, chunk), F32)]
+                turned = jnp.concatenate(lines).T
                 lane = lax.broadcasted_iota(jnp.int32, turned.shape, 1)
-                put(jnp.where(lane == 0, one / turned, turned).astype(BF16), cols - LANES)
-            start += size
-
-        @pl.when(i == width // chunk - 1)
-        def _():
-            start_all(blk.copies_out(index_ref[0], total_ref, outs, masks, sem))
-            pltpu.make_async_copy(total_ref, total_ref, sem).wait()
+                turned = jnp.where(lane == 0, one / turned, turned)
+                out[:, cols - LANES :] = turned.astype(BF16)
+
+        for q, out in enumerate(outs):
+            w_ref = ins[2 + q] if gain is not None else None
+            pl.when(pl.program_id(0) == q)(functools.partial(put, out, w_ref))
 
     return pl.pallas_call(
         body,
         name=name,
-        grid=(width // chunk,),
-        out_shape=tuple(out_shapes),
-        in_specs=[SMEM_SPEC]
-        + [pl.BlockSpec((n_tok, chunk), lambda i: (0, i))] * n
+        grid=(pieces,),
+        out_shape=(jax.ShapeDtypeStruct((chunk, cols), BF16),) * pieces,
+        in_specs=[pl.BlockSpec((n_tok, chunk), lambda i: (0, i))] * n
         + [pl.BlockSpec(r.shape, lambda i: (0, 0)) for r in rights]
         + specs,
-        out_specs=(ANY_SPEC,) * n_out,
-        scratch_shapes=[pltpu.VMEM((*blk.shape, cols), BF16), pltpu.SemaphoreType.DMA] + scratch,
-        compiler_params=params(60),
+        out_specs=(pl.BlockSpec((chunk, cols), lambda i: (0, 0)),) * pieces,
+        compiler_params=params(26),
         cost_estimate=cost(name),
-    )(index, *lefts, *rights, *extras)
-
-
-def sum_nt(weights, index, lefts, starts, total, pieces, name, base=0):
+    )(*near(*lefts, *rights), *extras)
+
+
+def sum_nt(weights, lefts, starts, pieces, name, places=None, rows=0):
     n_tok, cols = lefts[0].shape
-    width = weights.blk.shape[0] * weights.blk.shape[1]
-    n, n_in = len(lefts), weights.count
+    width = sum(w.shape[0] for w in weights)
+    n, n_in = len(lefts), len(weights)
     steps = 4
     size = n_tok // steps
 
-    def body(index_ref, *refs):
-        left_refs = refs[:n]
-        out_refs, (w_ref, sem) = refs[n + n_in : -2], refs[-2:]
-
-        @pl.when(pl.program_id(0) == 0)
-        def _():
-            weights.load(index_ref, refs[n : n + n_in], w_ref, sem, base)
-            weights.wait(w_ref, sem)
-
-        value = None
-        for left, start in zip(left_refs, starts):
-            term = dot_nt(left[...], w_ref[:, :, start : start + cols].reshape(width, cols))
-            value = term if value is None else value + term
-        value = value.astype(BF16)
+    def body(*refs):
+        left_refs, w_refs, out_refs = refs[:n], refs[n : n + n_in], refs[n + n_in :]
+
+        if places is not None:
+            values = [dot_nt(left_refs[0][...], in_order(w_refs, places, rows))]
+        else:
+            values = []
+            for w in w_refs:
+                value = None
+                for left, start in zip(left_refs, starts):
+                    term = dot_nt(left[...], w[:, start : start + cols])
+                    value = term if value is None else value + term
+                values.append(value)
 
         def put(ref):
-            ref[...] = value
+            at = 0
+            for value in values:
+                ref[:, at : at + value.shape[1]] = value.astype(BF16)
+                at += value.shape[1]
 
         with_piece(out_refs, steps, put)
 
@@ -828,33 +757,30 @@
         name=name,
         grid=(steps,),
         out_shape=(jax.ShapeDtypeStruct((n_tok // pieces, width), BF16),) * pieces,
-        in_specs=[SMEM_SPEC] + [rows_spec(size, cols)] * n + weights.specs,
+        in_specs=[rows_spec(size, cols)] * n + whole_specs(weights),
         out_specs=tuple(piece_specs(pieces, steps, size, width)),
-        scratch_shapes=weights.scratch(total),
-        compiler_params=params(60),
+        compiler_params=params(20),
         cost_estimate=cost(name),
-    )(index, *lefts, *weights.arrays)
-
-
-def norm_back(weights, index, part, came, hres, grad_out, gains, dims):
+    )(*near(*lefts), *weights)
+
+
+def norm_back(weights, part, came, hres, grad_out, gains, dims):
     n_tok, width = hres.shape
     nq, nv, _ = dims
     n_qkv = 2 * nq + nv
-    n_in = weights.count
+    n_in = len(weights)
     steps = 4
     size = n_tok // steps
-
     n = len(part)
 
-    def body(index_ref, hres_ref, c_ref, gain_ref, *refs):
+    def body(hres_ref, c_ref, gain_ref, *refs):
         part_refs, came_refs, refs = refs[:n], refs[n : 2 * n], refs[2 * n :]
-        dh_ref, do_ref, dy_ref, gg_ref, w_ref, sem = refs[n_in:]
+        dh_ref, do_ref, dy_ref, gg_ref = refs[n_in:]
         gain = gain_ref[1:2, :]
         i = pl.program_id(0)
 
         @pl.when(i == 0)
         def _():
-            weights.load(index_ref, refs[:n_in], w_ref, sem, n_qkv)
             gg_ref[...] = jnp.zeros_like(gg_ref)
 
         def rows(at, part_ref, came_ref):
@@ -876,13 +802,8 @@
         pairs = list(zip(part_refs, came_refs[n // 2 :] + came_refs[: n // 2]))
         with_piece(pairs, steps, lambda pair: row_chunks(size, 64, lambda at: rows(at, *pair)))
 
-        @pl.when(i == 0)
-        def _():
-            weights.wait(w_ref, sem)
-
-        dy_ref[...] = dot_nn(do_ref[...], w_ref[...].reshape(width, nv)).astype(BF16)
-
-    out = lambda *s, t=BF16: jax.ShapeDtypeStruct(s, t)
+        dy_ref[...] = dot_nn(do_ref[...], stacked(refs[:n_in], n_qkv, nv)).astype(BF16)
+
     at = rows_spec(size, width)
     keep = pl.BlockSpec((8, width), lambda i: (0, 0))
     return pl.pallas_call(
@@ -890,25 +811,24 @@
         name="norm_back",
         grid=(steps,),
         out_shape=(
-            out(n_tok // 2, width, t=F32),
-            out(n_tok, width),
-            out(n_tok, nv),
-            out(8, width, t=F32),
+            pltpu.VMEM((n_tok // 2, width), F32),
+            pltpu.VMEM((n_tok, width), BF16),
+            pltpu.VMEM((n_tok, nv), BF16),
+            jax.ShapeDtypeStruct((8, width), F32),
         ),
-        in_specs=[SMEM_SPEC, at, at, keep]
+        in_specs=[at, at, keep]
         + piece_specs(n, steps, size, width)
         + piece_specs(n, steps, size, width, True)
-        + weights.specs,
+        + whole_specs(weights),
         out_specs=(
             rows_spec(size, width, last=steps // 2 - 1),
             at,
             rows_spec(size, nv),
             keep,
         ),
-        scratch_shapes=weights.scratch(nv),
-        compiler_params=params(60),
+        compiler_params=params(20),
         cost_estimate=cost("norm_back"),
-    )(index, hres, grad_out, gains, *part, *came, *weights.arrays)
+    )(*near(hres, grad_out), gains, *part, *came, *weights)
 
 
 def attn_bwd(seq, qkv, y, dy, dinv, dims):
@@ -965,7 +885,7 @@
     return pl.pallas_call(
         body,
         name="attn_bwd",
-        out_shape=jax.ShapeDtypeStruct(qkv.shape, BF16),
+        out_shape=pltpu.VMEM(qkv.shape, BF16),
         in_specs=[SMEM_SPEC] + [VMEM_SPEC] * 4,
         out_specs=VMEM_SPEC,
         scratch_shapes=[
@@ -974,55 +894,20 @@
             pltpu.VMEM((length, nq), F32),
             pltpu.VMEM((length, LANES), F32),
         ],
-        compiler_params=params(60),
+        compiler_params=params(20),
         cost_estimate=cost("attn_bwd"),
-    )(seq, qkv, y, dy, dinv)
-
-
-def norm_one_part(weights, index, d_qkv):
-    n_tok, n_qkv = d_qkv.shape
-    width = weights.blk.shape[0] * weights.blk.shape[1]
-    n_in = weights.count
+    )(seq, *near(qkv, y, dy, dinv))
+
+
+def finish(part, came, tok, dh, gains, hres, out_part, out_came, placing):
+    n_tok, width = part.shape
     steps = 4
     size = n_tok // steps
 
-    def body(index_ref, d_ref, *refs):
-        *out_refs, w_ref, sem = refs[n_in:]
-
-        @pl.when(pl.program_id(0) == 0)
-        def _():
-            weights.load(index_ref, refs[:n_in], w_ref, sem)
-            weights.wait(w_ref, sem)
-
-        d = dot_nt(d_ref[...], w_ref[...].reshape(width, n_qkv))
-
-        def put(ref):
-            ref[...] = d.astype(BF16)
-
-        with_piece(out_refs, steps, put)
-
-    return pl.pallas_call(
-        body,
-        name="norm_one_part",
-        grid=(steps,),
-        out_shape=(
-            jax.ShapeDtypeStruct((n_tok // 2, width), BF16),
-            jax.ShapeDtypeStruct((n_tok // 2, width), BF16),
-        ),
-        in_specs=[SMEM_SPEC, rows_spec(size, n_qkv)] + weights.specs,
-        out_specs=tuple(piece_specs(2, steps, size, width)),
-        scratch_shapes=weights.scratch(n_qkv),
-        compiler_params=params(60),
-        cost_estimate=cost("norm_one_part"),
-    )(index, d_qkv, *weights.arrays)
-
-
-def finish(part, came, tok, dh, gains, hres, out_part, out_came):
-    n_tok, width = tok.shape
-    steps = 4
-    size = n_tok // steps
-
-    def body(part_ref, came_ref, tok_ref, dh_ref, gain_ref, h_ref, op_ref, oc_ref, grad_ref, out_ref):
+    def body(
+        part_ref, came_ref, tok_ref, dh_ref, gain_ref, h_ref, op_ref, oc_ref, p_ref,
+        grad_ref, out_ref, grad_low, out_low,
+    ):
         gain = gain_ref[0:1, :]
 
         def rows(at):
@@ -1031,11 +916,13 @@
             inverse = lax.rsqrt(jnp.mean(x * x, axis=-1, keepdims=True) + EPS)
             xr = x * inverse
             back = inverse * (d - xr * jnp.mean(d * xr, axis=-1, keepdims=True))
-            grad_ref[at, :] = (dh_ref[at, :] + back).astype(BF16)
+            grad_low[at, :] = (dh_ref[at, :] + back).astype(BF16)
             both = op_ref[at, :].astype(F32) + oc_ref[at, :].astype(F32)
-            out_ref[at, :] = (h_ref[at, :] + both).astype(BF16)
+            out_low[at, :] = (h_ref[at, :] + both).astype(BF16)
 
         row_chunks(size, 64, rows)
+        grad_ref[...] = dot_nt(grad_low[...], p_ref[...]).astype(BF16)
+        out_ref[...] = dot_nt(out_low[...], p_ref[...]).astype(BF16)
 
     at = rows_spec(size, width)
     out = jax.ShapeDtypeStruct((n_tok, width), BF16)
@@ -1044,11 +931,13 @@
         name="finish",
         grid=(steps,),
         out_shape=(out, out),
-        in_specs=[at, at, at, at, pl.BlockSpec((8, width), lambda i: (0, 0)), at, at, at],
+        in_specs=[at, at, at, at, pl.BlockSpec((8, width), lambda i: (0, 0)), at, at, at]
+        + [pl.BlockSpec((width, width), lambda i: (0, 0))],
         out_specs=(at, at),
-        compiler_params=params(60),
+        scratch_shapes=[pltpu.VMEM((size, width), BF16)] * 2,
+        compiler_params=params(16),
         cost_estimate=cost("finish"),
-    )(part, came, tok, dh, gains, hres, out_part, out_came)
+    )(part, came, *near(tok, dh), gains, *near(hres), out_part, out_came, *near(placing))
 
 
 def local(
@@ -1068,15 +957,22 @@
 ):
     me = lax.axis_index(AXES).astype(jnp.int32)
     core = me % 2
-    index = me.reshape(1)
+    index = (me - core).reshape(1)
     rows, length = w_query.shape[0], tokens.shape[0]
     nq, nv, nf = w_query.shape[1] // 2, w_value.shape[1] // 2, w_gate.shape[1] // 2
     stride = nf + -nf % LANES
     order = Order()
-    blk = Blocks(lay, rows)
     masks = split_masks(lay)
+    flat_masks = sum(masks, [])
     both = sum(plane_masks(lay, [0]), [])
-    masks_z = [[m | z for m in both] for z in masks_of(lay.z)]
+    places_z = {m | z: (j, i) for j, z in enumerate(masks_of(lay.z)) for i, m in enumerate(both)}
+    places_z = [places_z[m] for m in flat_masks]
+
+    def flat(arrays):
+        return [a.reshape(-1, a.shape[-1]) for a in arrays]
+
+    def blocks(arrays):
+        return [a.reshape(-1, rows, a.shape[-1]) for a in arrays]
     dims = (nq, nv, 2 * nq + 2 * nv + LANES)
 
     keep_0, keep_gu, keep_d, give = prepare(
@@ -1090,12 +986,16 @@
     came = order(came)
     at_d = dims[2] + 2 * stride
 
-    z_0 = GatherZ(lay, jnp.stack([keep_0, came[:, : dims[2]]]))
+    def by_core(own, other):
+        return jnp.where(core == 0, jnp.stack([own, other]), jnp.stack([other, own]))
+
+    z_0 = GatherZ(lay, by_core(keep_0, came[:, : dims[2]]))
     z_0.first()
     z_0.second()
-    p_d = GatherPlane(lay, keep_d[None], came[None, :, at_d:])
+    halves_d = by_core(keep_d, came[:, at_d:])
+    p_d = GatherPlane(lay, halves_d[:1], halves_d[1:])
     tok_other, seq_other, cot_other = order(tok_other, seq_other, cot_other)
-    z_gu = GatherZ(lay, order(jnp.stack([keep_gu, came[:, dims[2] : at_d]])))
+    z_gu = GatherZ(lay, order(by_core(keep_gu, came[:, dims[2] : at_d])))
     z_gu.first()
     z_0.third(order)
     p_d.second(order)
@@ -1112,34 +1012,37 @@
     z_d = GatherZ(lay, order(held_d))
     z_d.first()
     halves_gu = halves(z_gu)
-    *arrays_0, keep_gu, other_gu = order(*p_0.arrays(), *halves_gu)
-    p_gu = GatherPlane(lay, keep_gu, other_gu)
+    *arrays_0, low_gu, high_gu = order(*p_0.arrays(), *halves_gu)
+    p_gu = GatherPlane(lay, low_gu, high_gu)
     z_d.second(order)
-    w_0 = Weights(blk, arrays_0, masks, me)
+    w_0 = flat(arrays_0)
     seq = jnp.concatenate([seq_lengths, seq_other], axis=0)
-    tok = order(jnp.concatenate([tokens, tok_other], axis=0))
-    grad_out = order(jnp.concatenate([cotangent, cot_other], axis=0))
+    tok = jnp.concatenate([tokens, tok_other], axis=0)
+    grad_out = jnp.concatenate([cotangent, cot_other], axis=0)
+    tok, grad_out, placing = order(*shuffle(index, flat_masks, [tok, grad_out]))
     z_d.third(order, True)
     p_gu.second(order)
-    tok = order(tok)
-
     def swap_all(values):
         return [lay.swap(v, 1) for v in values]
 
-    normed_one, qkv, y, dinv, gains, *part_o = attn_fwd(w_0, index, seq, tok, dims)
+    normed_one, qkv, y, dinv, gains, *part_o = attn_fwd(w_0, seq, tok, dims)
     part_o = order(*part_o)
     came_o = swap_all(part_o)
-    w_d = Weights(blk, z_d.done(order), masks_z, me)
-    d_act = order(down_back(w_d, index, grad_out, stride))
-    w_gu = Weights(blk, order(*p_gu.arrays()), masks, me)
+    w_d = z_d.done(order)
+    if rows % 16:
+        order_d = [j * len(both) + i for j, i in places_z]
+        w_d = jnp.take(jnp.concatenate(w_d), jnp.asarray(order_d), axis=0)
+        w_d, places_z = jnp.split(w_d, 4), None
+    w_d = flat(w_d)
+    d_act = order(down_back(w_d, places_z, rows, grad_out))
+    w_gu = flat(order(*p_gu.arrays()))
     came_o = order(*came_o)
     hres, normed_two = residual(tok, part_o, came_o, gains)
     normed_two = order(normed_two)
-    act, d_gate, d_up = order(*gated(w_gu, index, normed_two, d_act, stride))
+    act, d_gate, d_up = order(*gated(w_gu, normed_two, d_act))
 
     def grad(lefts, rights, gain=None, name="weight_grad"):
-        outs = weight_grad(blk, masks, index, lefts, rights, gain, name)
-        return blk.split(order(*outs), masks, me)
+        return blocks(order(*weight_grad(lefts, rights, gain, name)))
 
     wanted = [masks_of(lay.z).index(m) for m in low_first(lay)]
 
@@ -1148,13 +1051,13 @@
 
     r_g = ReducePlane(lay, grad([normed_two], [d_gate], name="grad_gate"))
     d_up = order(d_up)
-    part_n2 = order(*sum_nt(w_gu, index, [d_gate, d_up], [0, stride], 2 * stride, 2, "d_norm2"))
+    part_n2 = order(*sum_nt(w_gu, [d_gate, d_up], [0, stride], 2, "d_norm2"))
     came_n2 = swap_all(part_n2)
     r_g.second(order)
     act = order(act)
     r_d = ReducePlane(lay, grad([grad_out], [act], name="grad_down"))
     came_n2 = order(*came_n2)
-    d_h, d_o, d_y, gg_mlp = norm_back(w_0, index, part_n2, came_n2, hres, grad_out, gains, dims)
+    d_h, d_o, d_y, gg_mlp = norm_back(w_0, part_n2, came_n2, hres, grad_out, gains, dims)
     d_y = order(d_y)
     outs_u = grad([normed_two, d_o], [d_up, y], name="grad_up")
     zr_g = along_z(r_g)
@@ -1169,19 +1072,19 @@
     outs_0 = grad([normed_one], [d_qkv], (w_0, gains, gg_mlp), name="grad_attn")
     zr_d = along_z(r_d)
     r_0 = ReducePlane(lay, order(*outs_0))
-    part_n1 = order(*norm_one_part(w_0, index, order(d_qkv)))
+    part_n1 = order(*sum_nt(w_0, [order(d_qkv)], [0], 2, "norm_one_part"))
     wait_for(order, zr_g, zr_d, r_u, r_0)
     r_0.second(order)
     zr_u = along_z(r_u)
     zr_d.second(order)
-    part_out = order(*sum_nt(w_d, index, [order(act)], [0], stride, 2, "down"))
+    part_out = order(*sum_nt(w_d, [order(act)], [0], 2, "down", places_z, rows))
     came_rows = swap_all(order(part_n1[1], part_out[1]))
     wait_for(order, zr_u, r_0)
     zr_0 = along_z(r_0)
     zr_u.second(order)
     came_rows = order(*came_rows)
     grad_tokens, layer_out = finish(
-        part_n1[0], came_rows[0], tokens, d_h, gains, hres, part_out[0], came_rows[1]
+        part_n1[0], came_rows[0], tok, d_h, gains, hres, part_out[0], came_rows[1], placing
     )
     grad_tokens = order(grad_tokens)
     zr_0.second(order)
@@ -1189,7 +1092,7 @@
     end_g = zr_g.last(order)
     end_u = zr_u.last(order)
     end_0 = zr_0.last(order)
-    mine, give = add_up([end_0, end_d, end_g, end_u])
+    mine, give = add_up(core.reshape(1), [end_0, end_d, end_g, end_u])
     came = lay.swap(give, 1)
     at = 2 * nq + nv
     at_d = at + LANES

time: 342 us -> 291 us (0.85)
  Pallas kernels: 181 us -> 110 us
  starting transfers between devices: 56.5 us -> 68.5 us
  local copies, waits for them, and re-layouts: 9.73 us -> 19.5 us
    pallas_call x10, Pallas kernels: 101 us -> 70.8 us  [the longest x4 21.1 us: weight_grad(): pl.pallas_call(body, name=name, grid=(pieces,), out_shape=(jax.ShapeDtype...]
    pallas_call x8, Pallas kernels: 21.6 us -> 3.38 us  [fold(): pl.pallas_call(body, name=name, grid=(2,), out_shape=tuple((jax.ShapeDtyp...]
    ppermute x58, starting transfers between devices: 56.5 us -> 68.5 us  [swap(): return lax.ppermute(value, AXES, [(i, i ^ bit) for i in range(self.count)])]
    pallas_call x4, Pallas kernels: 9.39 us -> 0.67 us  [fold_plane(): pl.pallas_call(body, name='fold_plane', out_shape=(jax.ShapeDtypeStruct(s...]
    unnamed x93 -> x68, local copies, waits for them, and re-layouts: 9.41 us -> 15.4 us
    pallas_call x1, Pallas kernels: 13.3 us -> 7.96 us  [gated(): pl.pallas_call(body, name='gated', grid=(steps,), out_shape=(out, out, ou...]
    pallas_call x2 -> x3, Pallas kernels: 21.6 us -> 16.3 us  [sum_nt(): pl.pallas_call(body, name=name, grid=(steps,), out_shape=(jax.ShapeDtypeS...]
  transfers between devices with their start and end apart: 58 -> 58, of which waited for: 20 -> 21; matrix products, arithmetic and copies ran while one was open for 2% -> 5% of each run, Pallas kernels for 41% -> 30%
where the time goes in v3:
time: 291 us; the launch traced here: 290 us
  Pallas kernels  110 us (38%)
  waiting for transfers between devices  85.7 us (29%)
  starting transfers between devices  68.5 us (24%)
  local copies, waits for them, and re-layouts  19.5 us (7%)
  other arithmetic  4.79 us (2%)
    ppermute x58, waiting for transfers between devices, swap(): return lax.ppermute(value, AXES, [(i, i ^ bit) for i in range(self.count)])  85.7 us
    ppermute x58, starting transfers between devices, swap(): return lax.ppermute(value, AXES, [(i, i ^ bit) for i in range(self.count)])  68.5 us
    pallas_call x4, Pallas kernels, weight_grad(): pl.pallas_call(body, name=name, grid=(pieces,), out_shape=(jax.ShapeDtype...  21.1 us
    pallas_call x3, Pallas kernels, sum_nt(): pl.pallas_call(body, name=name, grid=(steps,), out_shape=(jax.ShapeDtypeS...  16.3 us
    unnamed x68, local copies, waits for them, and re-layouts  15.4 us
    pallas_call x1, Pallas kernels, attn_bwd(): pl.pallas_call(body, name='attn_bwd', out_shape=pltpu.VMEM(qkv.shape, BF1...  15.2 us
    pallas_call x1, Pallas kernels, attn_fwd(): pl.pallas_call(body, name='attn_fwd', out_shape=(pltpu.VMEM((n_tok, width...  13.8 us
    pallas_call x1, Pallas kernels, finish(): pl.pallas_call(body, name='finish', grid=(steps,), out_shape=(out, out),...  9.03 us
  transfers between devices with their start and end apart: 58, of which 21 were waited for; matrix products, arithmetic and copies ran while one was open for 5% of the time, Pallas kernels for 30%

profile of v3, /device:TPU:0, one launch (start us, length us, event | category | flops | bytes accessed | tf_op | source)
XLA Modules:
  0.0 289.9 jit_solution(12047325112909933614)
XLA Ops:
  10.2 4.0 %collective-permute-start.6 = (bf16[2,32,1408]{2,1,0:T(8,128)(2,1)S(1)}, bf16[2,32,1408]{2,1,0:T(8,128)(2,1)S(1)}, u32[]{:S(2)}, u32[]{:S(2)}) collective-permute-start(bf16[2,32,1408]{2,1,0:T(8,128)(2,1)S(1)} %maximum_select_fusion.2), channel_id=1, source_target_pairs={{0,16},{1,17},{2,18},{3,19},{4,20},{5,21},{6,22},{7,23},{8,24},{9,... | collective-permute-start | bytes 540680 | tf_op jit(solution)/shard_map/ppermute | solution.py:48
  20.1 4.2 %collective-permute-done.6 = bf16[2,32,1408]{2,1,0:T(8,128)(2,1)S(1)} collective-permute-done((bf16[2,32,1408]{2,1,0:T(8,128)(2,1)S(1)}, bf16[2,32,1408]{2,1,0:T(8,128)(2,1)S(1)}, u32[]{:S(2)}, u32[]{:S(2)}) %collective-permute-start.6) | collective-permute-done | bytes 180256 | tf_op jit(solution)/shard_map/ppermute | solution.py:48
  28.2 6.4 %collective-permute-done.10 = bf16[2,32,1408]{2,1,0:T(8,128)(2,1)S(1)} collective-permute-done((bf16[2,32,1408]{2,1,0:T(8,128)(2,1)S(1)}, bf16[2,32,1408]{2,1,0:T(8,128)(2,1)S(1)}, u32[]{:S(2)}, u32[]{:S(2)}) %collective-permute-start.10) | collective-permute-done | bytes 180256 | tf_op jit(solution)/shard_map/ppermute | solution.py:48
  42.5 4.7 %collective-permute-done.12 = bf16[4,32,1408]{2,1,0:T(8,128)(2,1)S(1)} collective-permute-done((bf16[4,32,1408]{2,1,0:T(8,128)(2,1)S(1)}, bf16[4,32,1408]{2,1,0:T(8,128)(2,1)S(1)}, u32[]{:S(2)}, u32[]{:S(2)}) %collective-permute-start.12) | collective-permute-done | bytes 360480 | tf_op jit(solution)/shard_map/ppermute | solution.py:48
  48.8 5.9 %collective-permute-start.20 = (bf16[8,32,1408]{2,1,0:T(8,128)(2,1)}, bf16[8,32,1408]{2,1,0:T(8,128)(2,1)}, u32[]{:S(2)}, u32[]{:S(2)}) collective-permute-start(bf16[8,32,1408]{2,1,0:T(8,128)(2,1)} %constant_dynamic-update-slice_fusion), channel_id=1, source_target_pairs={{0,16},{1,17},{2,18},{3,19},{4,20},{5,21},{6,22},{7,23},{8,24},{9,... | collective-permute-start | bytes 2162696 | tf_op jit(solution)/shard_map/ppermute | solution.py:48
  55.0 2.7 collective-permute-done.17
  59.7 7.0 %collective-permute-done.14 = bf16[8,32,1408]{2,1,0:T(8,128)(2,1)S(1)} collective-permute-done((bf16[8,32,1408]{2,1,0:T(8,128)(2,1)S(1)}, bf16[8,32,1408]{2,1,0:T(8,128)(2,1)S(1)}, u32[]{:S(2)}, u32[]{:S(2)}) %collective-permute-start.14) | collective-permute-done | bytes 720928 | tf_op jit(solution)/shard_map/ppermute | solution.py:48
  66.7 3.0 %collective-permute-done.15 = bf16[8,32,1408]{2,1,0:T(8,128)(2,1)S(1)} collective-permute-done((bf16[8,32,1408]{2,1,0:T(8,128)(2,1)S(1)}, bf16[8,32,1408]{2,1,0:T(8,128)(2,1)S(1)}, u32[]{:S(2)}, u32[]{:S(2)}) %collective-permute-start.15) | collective-permute-done | bytes 720928 | tf_op jit(solution)/shard_map/ppermute | solution.py:48
  75.9 6.3 %shuffle.1 = (bf16[1024,1024]{1,0:T(8,128)(2,1)S(1)}, bf16[1024,1024]{1,0:T(8,128)(2,1)S(1)}, bf16[1024,1024]{1,0:T(8,128)(2,1)S(1)}) custom-call(s32[1]{0:T(128)} %bitcast.5.index_ref, s32[1,1024]{1,0:T(1,128)S(1)} %broadcast_in_dim_reshape.3.masks_ref, bf16[1024,1024]{1,0:T(8,128)(2,1)S(1)} %get-tuple-element.504.refs_0_, ...), custom_call_target="tpu_custom_call" | custom-call | flops 1 | bytes 1 | tf_op jit(solution)/shard_map/shuffle/pallas_call | solution.py:396
  83.9 4.9 %collective-permute-done.21 = bf16[8,32,1408]{2,1,0:T(8,128)(2,1)} collective-permute-done((bf16[8,32,1408]{2,1,0:T(8,128)(2,1)}, bf16[8,32,1408]{2,1,0:T(8,128)(2,1)}, u32[]{:S(2)}, u32[]{:S(2)}) %collective-permute-start.21) | collective-permute-done | bytes 720928 | tf_op jit(solution)/shard_map/ppermute | solution.py:48
  95.8 13.8 %attn_fwd.1 = (bf16[1024,1024]{1,0:T(8,128)(2,1)S(1)}, bf16[1024,768]{1,0:T(8,128)(2,1)S(1)}, bf16[1024,512]{1,0:T(8,128)(2,1)S(1)}, f32[1024,512]{1,0:T(8,128)S...) custom-call(s32[2,4]{1,0:T(2,128)S(1)} %pad_add_fusion.seq_ref, ...), custom_call_target="tpu_custom_call" | custom-call | flops 1 | bytes 1 | tf_op jit(solution)/shard_map/attn_fwd/pallas_call | solution.py:557
  111.5 6.3 %collective-permute-done.26 = bf16[8,32,2816]{2,1,0:T(8,128)(2,1)S(1)} collective-permute-done((bf16[8,32,2816]{2,1,0:T(8,128)(2,1)S(1)}, bf16[8,32,2816]{2,1,0:T(8,128)(2,1)S(1)}, u32[]{:S(2)}, u32[]{:S(2)}) %collective-permute-start.26) | collective-permute-done | bytes 1441824 | tf_op jit(solution)/shard_map/ppermute | solution.py:48
  117.7 6.1 %down_back.1.d_act_ref = bf16[1024,1408]{1,0:T(8,128)(2,1)S(1)} custom-call(bf16[1024,1024]{1,0:T(8,128)(2,1)S(1)} %get-tuple-element.293.grad_ref.refs_0_.c_ref, bf16[256,1408]{1,0:T(8,128)(2,1)} %bitcast.16.refs_0_.refs_1_, bf16[256,1408]{1,0:T(8,128)(2,1)} %bitcast.17.refs_1_.refs_2_, bf16[256,1408]{1,0:T(8,128)(2,1)} %bitcast.18.refs_2_.refs_3_, ...), custom_call_target="tpu_custom_call" | custom-call | flops 1 | bytes 1 | tf_op jit(solution)/shard_map/down_back/pallas_call | solution.py:630
  127.9 8.0 %gated.1 = (bf16[1024,1408]{1,0:T(8,128)(2,1)S(1)}, bf16[1024,1408]{1,0:T(8,128)(2,1)S(1)}, bf16[1024,1408]{1,0:T(8,128)(2,1)S(1)}) custom-call(bf16[1024,1024]{1,0:T(8,128)(2,1)S(1)} %get-tuple-element.308.normed_ref.refs_0_, bf16[1024,1408]{1,0:T(8,128)(2,1)S(1)} %down_back.1.d_act_ref, bf16[256,2816]{1,0:T(8,128)(2,1)S(1)} %bitcast.63, ...), custom_call_target="tpu_custom_call" | custom-call | flops 1 | bytes 1 | tf_op jit(solution)/shard_map/gated/pallas_call | solution.py:663
  135.9 4.7 %grad_gate.1 = (bf16[256,1408]{1,0:T(8,128)(2,1)S(1)}, bf16[256,1408]{1,0:T(8,128)(2,1)S(1)}, bf16[256,1408]{1,0:T(8,128)(2,1)S(1)}, bf16[256,1408]{1,0:T(8,128)(2,1)S(1)}) custom-call(bf16[1024,1024]{1,0:T(8,128)(2,1)S(1)} %get-tuple-element.308.normed_ref.refs_0_, bf16[1024,1408]{1,0:T(8,128)(2,1)S(1)} %get-tuple-element.315.refs_1_.refs_0_), custom_call_target="tpu_custom_call" | custom-call | flops 1 | bytes 1 | tf_op jit(solution)/shard_map/grad_gate/pallas_call | solution.py:712
  145.1 7.6 %d_norm2.1 = (bf16[512,1024]{1,0:T(8,128)(2,1)S(1)}, bf16[512,1024]{1,0:T(8,128)(2,1)S(1)}) custom-call(bf16[1024,1408]{1,0:T(8,128)(2,1)S(1)} %get-tuple-element.315.refs_1_.refs_0_, bf16[1024,1408]{1,0:T(8,128)(2,1)S(1)} %get-tuple-element.323.refs_1_.refs_2_, bf16[256,2816]{1,0:T(8,128)(2,1)S(1)} %bitcast.64, bf16[256,2816]{1,0:T(8,128)(2,1)S(1)} %bitcast.68, ...), custom_call_target="tpu_custom_call" | custom-call | flops 1 | bytes 1 | tf_op jit(solution)/shard_map/d_norm2/pallas_call | solution.py:755
  153.2 6.4 %collective-permute-done.32.refs_3_ = bf16[8,32,1408]{2,1,0:T(8,128)(2,1)S(1)} collective-permute-done((bf16[8,32,1408]{2,1,0:T(8,128)(2,1)S(1)}, bf16[8,32,1408]{2,1,0:T(8,128)(2,1)S(1)}, u32[]{:S(2)}, u32[]{:S(2)}) %collective-permute-start.32) | collective-permute-done | bytes 720928 | tf_op jit(solution)/shard_map/ppermute | solution.py:48
  163.9 5.8 %grad_down.1 = (bf16[256,1408]{1,0:T(8,128)(2,1)S(1)}, bf16[256,1408]{1,0:T(8,128)(2,1)}, bf16[256,1408]{1,0:T(8,128)(2,1)S(1)}, bf16[256,1408]{1,0:T(8,128)(2,1)}) custom-call(bf16[1024,1024]{1,0:T(8,128)(2,1)S(1)} %get-tuple-element.293.grad_ref.refs_0_.c_ref, bf16[1024,1408]{1,0:T(8,128)(2,1)S(1)} %get-tuple-element.418.refs_1_.refs_0_), custom_call_target="tpu_custom_call" | custom-call | flops 1 | bytes 1 | tf_op jit(solution)/shard_map/grad_down/pallas_call | solution.py:712
  171.7 5.7 %norm_back.1 = (f32[512,1024]{1,0:T(8,128)S(1)}, bf16[1024,1024]{1,0:T(8,128)(2,1)S(1)}, bf16[1024,512]{1,0:T(8,128)(2,1)S(1)}, f32[8,1024]{1,0:T(8,128)S(1)}) custom-call(f32[1024,1024]{1,0:T(8,128)S(1)} %get-tuple-element.306.hres_ref.h_ref, bf16[1024,1024]{1,0:T(8,128)(2,1)S(1)} %get-tuple-element.293.grad_ref.refs_0_.c_ref, ...), custom_call_target="tpu_custom_call" | custom-call | flops 1 | bytes 1 | tf_op jit(solution)/shard_map/norm_back/pallas_call | solution.py:809
  177.4 7.1 %grad_up.1 = (bf16[256,1920]{1,0:T(8,128)(2,1)S(1)}, bf16[256,1920]{1,0:T(8,128)(2,1)}, bf16[256,1920]{1,0:T(8,128)(2,1)S(1)}, bf16[256,1920]{1,0:T(8,128)(2,1)S(1)}) custom-call(bf16[1024,1024]{1,0:T(8,128)(2,1)S(1)} %get-tuple-element.308.normed_ref.refs_0_, bf16[1024,1024]{1,0:T(8,128)(2,1)S(1)} %get-tuple-element.341.refs_1_, ...), custom_call_target="tpu_custom_call" | custom-call | flops 1 | bytes 1 | tf_op jit(solution)/shard_map/grad_up/pallas_call | solution.py:712
  188.4 15.2 %attn_bwd.1.refs_1_.refs_0_ = bf16[1024,768]{1,0:T(8,128)(2,1)S(1)} custom-call(s32[2,4]{1,0:T(2,128)S(1)} %pad_add_fusion.seq_ref, bf16[1024,768]{1,0:T(8,128)(2,1)S(1)} %copy-done.17, bf16[1024,512]{1,0:T(8,128)(2,1)S(1)} %copy-done.7, bf16[1024,512]{1,0:T(8,128)(2,1)S(1)} %get-tuple-element.356.dy_ref, f32[1024,512]{1,0:T(8,128)S(1)} %copy-done.15), custom_call_target="tpu_custom_call" | custom-call | flops 1 | bytes 1 | tf_op jit(solution)/shard_map/attn_bwd/pallas_call | solution.py:885
  205.2 5.8 %collective-permute-done.38.refs_1_ = bf16[8,32,1920]{2,1,0:T(8,128)(2,1)S(1)} collective-permute-done((bf16[8,32,1920]{2,1,0:T(8,128)(2,1)}, bf16[8,32,1920]{2,1,0:T(8,128)(2,1)S(1)}, u32[]{:S(2)}, u32[]{:S(2)}) %collective-permute-start.38) | collective-permute-done | bytes 983072 | tf_op jit(solution)/shard_map/ppermute | solution.py:48
  211.3 3.4 %collective-permute-start.42 = (bf16[1,2,32,1408]{3,2,1,0:T(8,128)(2,1)S(1)}, bf16[1,2,32,1408]{3,2,1,0:T(8,128)(2,1)S(1)}, u32[]{:S(2)}, u32[]{:S(2)}) collective-permute-start(bf16[1,2,32,1408]{3,2,1,0:T(8,128)(2,1)S(1)} %get-tuple-element.398), channel_id=1, source_target_pairs={{0,16},{1,17},{2,18},{3,19},{4,20},{5,21},{6,22},{7,23},{8,24},{9,... | collective-permute-start | bytes 540680 | tf_op jit(solution)/shard_map/ppermute | solution.py:48
  216.9 3.5 %grad_attn.1 = (bf16[256,896]{1,0:T(8,128)(2,1)S(1)}, bf16[256,896]{1,0:T(8,128)(2,1)S(1)}, bf16[256,896]{1,0:T(8,128)(2,1)S(1)}, bf16[256,896]{1,0:T(8,128)(2,1)S(1)}) custom-call(bf16[1024,1024]{1,0:T(8,128)(2,1)S(1)} %copy-done.13, bf16[1024,768]{1,0:T(8,128)(2,1)S(1)} %attn_bwd.1.refs_1_.refs_0_, ...), custom_call_target="tpu_custom_call" | custom-call | flops 1 | bytes 1 | tf_op jit(solution)/shard_map/grad_attn/pallas_call | solution.py:712
  231.5 5.2 %collective-permute-done.46.refs_1_ = bf16[8,32,896]{2,1,0:T(8,128)(2,1)S(1)} collective-permute-done((bf16[8,32,896]{2,1,0:T(8,128)(2,1)S(1)}, bf16[8,32,896]{2,1,0:T(8,128)(2,1)S(1)}, u32[]{:S(2)}, u32[]{:S(2)}) %collective-permute-start.46) | collective-permute-done | bytes 458784 | tf_op jit(solution)/shard_map/ppermute | solution.py:48
  236.7 6.1 %down.1 = (bf16[512,1024]{1,0:T(8,128)(2,1)S(1)}, bf16[512,1024]{1,0:T(8,128)(2,1)S(1)}) custom-call(bf16[1024,1408]{1,0:T(8,128)(2,1)S(1)} %get-tuple-element.418.refs_1_.refs_0_, bf16[256,1408]{1,0:T(8,128)(2,1)} %bitcast.16.refs_0_.refs_1_, bf16[256,1408]{1,0:T(8,128)(2,1)} %bitcast.17.refs_1_.refs_2_, bf16[256,1408]{1,0:T(8,128)(2,1)} %bitcast.18.refs_2_.refs_3_, ...), custom_call_target="tpu_custom_call" | custom-call | flops 1 | bytes 1 | tf_op jit(solution)/shard_map/down/pallas_call | solution.py:755
  247.0 5.1 %collective-permute-done.51.refs_1_ = bf16[4,32,896]{2,1,0:T(8,128)(2,1)S(1)} collective-permute-done((bf16[4,32,896]{2,1,0:T(8,128)(2,1)S(1)}, bf16[4,32,896]{2,1,0:T(8,128)(2,1)S(1)}, u32[]{:S(2)}, u32[]{:S(2)}) %collective-permute-start.51) | collective-permute-done | bytes 229408 | tf_op jit(solution)/shard_map/ppermute | solution.py:48
  253.2 3.8 %collective-permute-done.50.refs_1_ = bf16[2,2,32,1920]{3,2,1,0:T(8,128)(2,1)S(1)} collective-permute-done((bf16[2,2,32,1920]{3,2,1,0:T(8,128)(2,1)S(1)}, bf16[2,2,32,1920]{3,2,1,0:T(8,128)(2,1)S(1)}, u32[]{:S(2)}, u32[]{:S(2)}) %collective-permute-start.50) | collective-permute-done | bytes 491552 | tf_op jit(solution)/shard_map/ppermute | solution.py:48
  257.9 5.3 %collective-permute-start.55 = (bf16[1,2,32,1920]{3,2,1,0:T(8,128)(2,1)S(1)}, bf16[1,2,32,1920]{3,2,1,0:T(8,128)(2,1)S(1)}, u32[]{:S(2)}, u32[]{:S(2)}) collective-permute-start(bf16[1,2,32,1920]{3,2,1,0:T(8,128)(2,1)S(1)} %get-tuple-element.454), channel_id=1, source_target_pairs={{0,16},{1,17},{2,18},{3,19},{4,20},{5,21},{6,22},{7,23},{8,24},{9,... | collective-permute-start | bytes 737288 | tf_op jit(solution)/shard_map/ppermute | solution.py:48
  263.5 9.0 %finish.1 = (bf16[512,1024]{1,0:T(8,128)(2,1)}, bf16[512,1024]{1,0:T(8,128)(2,1)}) custom-call(bf16[512,1024]{1,0:T(8,128)(2,1)S(1)} %get-tuple-element.395.part_ref, bf16[512,1024]{1,0:T(8,128)(2,1)S(1)} %collective-permute-done.48.came_ref, bf16[1024,1024]{1,0:T(8,128)(2,1)S(1)} %get-tuple-element.274.tok_ref, f32[512,1024]{1,0:T(8,128)S(1)} %get-tuple-element.439.dh_ref, ...), custom_call_target="tpu_custom_call" | custom-call | flops 1 | bytes 1 | tf_op jit(solution)/shard_map/finish/pallas_call | solution.py:929
  272.6 2.9 %collective-permute-start.54 = (bf16[1,2,32,896]{3,2,1,0:T(8,128)(2,1)S(1)}, bf16[1,2,32,896]{3,2,1,0:T(8,128)(2,1)S(1)}, u32[]{:S(2)}, u32[]{:S(2)}) collective-permute-start(bf16[1,2,32,896]{3,2,1,0:T(8,128)(2,1)S(1)} %get-tuple-element.452), channel_id=1, source_target_pairs={{0,16},{1,17},{2,18},{3,19},{4,20},{5,21},{6,22},{7,23},{8,24},{9,... | collective-permute-start | bytes 344072 | tf_op jit(solution)/shard_map/ppermute | solution.py:48
  275.6 9.4 %collective-permute-done.56.refs_3_ = bf16[1,2,32,1408]{3,2,1,0:T(8,128)(2,1)S(1)} collective-permute-done((bf16[1,2,32,1408]{3,2,1,0:T(8,128)(2,1)S(1)}, bf16[1,2,32,1408]{3,2,1,0:T(8,128)(2,1)S(1)}, u32[]{:S(2)}, u32[]{:S(2)}) %collective-permute-start.56) | collective-permute-done | bytes 180256 | tf_op jit(solution)/shard_map/ppermute | solution.py:48
  (205 shorter events, 93.3 us)
Async XLA Ops:
  19.7 28.8 %collective-permute-start.11 = (bf16[2,32,2816]{2,1,0:T(8,128)(2,1)S(1)}, bf16[2,32,2816]{2,1,0:T(8,128)(2,1)S(1)}, u32[]{:S(2)}, u32[]{:S(2)}) collective-permute-start(bf16[2,32,2816]{2,1,0:T(8,128)(2,1)S(1)} %maximum_select_fusion), channel_id=1, source_target_pairs={{0,16},{1,17},{2,18},{3,19},{4,20},{5,21},{6,22},{7,23},{8,24},{9,... | collective-permute-start | bytes 1081352 | tf_op jit(solution)/shard_map/ppermute | solution.py:48
  34.7 20.3 %collective-permute-start.16 = (bf16[2,32,2816]{2,1,0:T(8,128)(2,1)S(1)}, bf16[2,32,2816]{2,1,0:T(8,128)(2,1)S(1)}, u32[]{:S(2)}, u32[]{:S(2)}) collective-permute-start(bf16[2,32,2816]{2,1,0:T(8,128)(2,1)S(1)} %maximum_select_fusion), channel_id=1, source_target_pairs={{0,8},{1,9},{2,10},{3,11},{4,12},{5,13},{6,14},{7,15},{8,0},{9,1},... | collective-permute-start | bytes 1081352 | tf_op jit(solution)/shard_map/ppermute | solution.py:48
  48.8 35.1 %collective-permute-start.20 = (bf16[8,32,1408]{2,1,0:T(8,128)(2,1)}, bf16[8,32,1408]{2,1,0:T(8,128)(2,1)}, u32[]{:S(2)}, u32[]{:S(2)}) collective-permute-start(bf16[8,32,1408]{2,1,0:T(8,128)(2,1)} %constant_dynamic-update-slice_fusion), channel_id=1, source_target_pairs={{0,16},{1,17},{2,18},{3,19},{4,20},{5,21},{6,22},{7,23},{8,24},{9,... | collective-permute-start | bytes 2162696 | tf_op jit(solution)/shard_map/ppermute | solution.py:48
  54.9 14.8 %collective-permute-start.15 = (bf16[8,32,1408]{2,1,0:T(8,128)(2,1)S(1)}, bf16[8,32,1408]{2,1,0:T(8,128)(2,1)S(1)}, u32[]{:S(2)}, u32[]{:S(2)}) collective-permute-start(bf16[8,32,1408]{2,1,0:T(8,128)(2,1)S(1)} %constant_dynamic-update-slice_fusion.11), channel_id=1, source_target_pairs={{0,2},{1,3},{2,0},{3,1},{4,6},{5,7},{6,4},{7,5},{8,10},{9,11},{10,... | collective-permute-start | bytes 2162696 | tf_op jit(solution)/shard_map/ppermute | solution.py:48
  69.7 19.1 %collective-permute-start.21 = (bf16[8,32,1408]{2,1,0:T(8,128)(2,1)}, bf16[8,32,1408]{2,1,0:T(8,128)(2,1)}, u32[]{:S(2)}, u32[]{:S(2)}) collective-permute-start(bf16[8,32,1408]{2,1,0:T(8,128)(2,1)} %constant_dynamic-update-slice_fusion), channel_id=1, source_target_pairs={{0,8},{1,9},{2,10},{3,11},{4,12},{5,13},{6,14},{7,15},{8,0},{9,1},... | collective-permute-start | bytes 2162696 | tf_op jit(solution)/shard_map/ppermute | solution.py:48
  71.8 17.1 %collective-permute-start.18 = (bf16[4,32,2816]{2,1,0:T(8,128)(2,1)}, bf16[4,32,2816]{2,1,0:T(8,128)(2,1)}, u32[]{:S(2)}, u32[]{:S(2)}) collective-permute-start(bf16[4,32,2816]{2,1,0:T(8,128)(2,1)} %pad_maximum_fusion.2), channel_id=1, source_target_pairs={{0,2},{1,3},{2,0},{3,1},{4,6},{5,7},{6,4},{7,5},{8,10},{9,11},{10,... | collective-permute-start | bytes 2162696 | tf_op jit(solution)/shard_map/ppermute | solution.py:48
  71.8 17.1 %collective-permute-start.19 = (bf16[4,32,2816]{2,1,0:T(8,128)(2,1)}, bf16[4,32,2816]{2,1,0:T(8,128)(2,1)}, u32[]{:S(2)}, u32[]{:S(2)}) collective-permute-start(bf16[4,32,2816]{2,1,0:T(8,128)(2,1)} %pad_maximum_fusion.3), channel_id=1, source_target_pairs={{0,4},{1,5},{2,6},{3,7},{4,0},{5,1},{6,2},{7,3},{8,12},{9,13},{10,... | collective-permute-start | bytes 2162696 | tf_op jit(solution)/shard_map/ppermute | solution.py:48
  90.0 27.7 %collective-permute-start.26 = (bf16[8,32,2816]{2,1,0:T(8,128)(2,1)S(1)}, bf16[8,32,2816]{2,1,0:T(8,128)(2,1)S(1)}, u32[]{:S(2)}, u32[]{:S(2)}) collective-permute-start(bf16[8,32,2816]{2,1,0:T(8,128)(2,1)S(1)} %constant_dynamic-update-slice_fusion.16), channel_id=1, source_target_pairs={{0,4},{1,5},{2,6},{3,7},{4,0},{5,1},{6,2},{7,3},{8,12},{9,13},{10,... | collective-permute-start | bytes 4325384 | tf_op jit(solution)/shard_map/ppermute | solution.py:48
  93.5 30.3 %collective-permute-start.27 = (bf16[8,32,2816]{2,1,0:T(8,128)(2,1)S(1)}, bf16[8,32,2816]{2,1,0:T(8,128)(2,1)S(1)}, u32[]{:S(2)}, u32[]{:S(2)}) collective-permute-start(bf16[8,32,2816]{2,1,0:T(8,128)(2,1)S(1)} %constant_dynamic-update-slice_fusion.18), channel_id=1, source_target_pairs={{0,2},{1,3},{2,0},{3,1},{4,6},{5,7},{6,4},{7,5},{8,10},{9,11},{10,... | collective-permute-start | bytes 4325384 | tf_op jit(solution)/shard_map/ppermute | solution.py:48
  95.8 15.6 %collective-permute-start.28 = (bf16[8,32,1408]{2,1,0:T(8,128)(2,1)}, bf16[8,32,1408]{2,1,0:T(8,128)(2,1)S(1)}, u32[]{:S(2)}, u32[]{:S(2)}) collective-permute-start(bf16[8,32,1408]{2,1,0:T(8,128)(2,1)} %collective-permute-done.20), channel_id=1, source_target_pairs={{0,8},{1,9},{2,10},{3,11},{4,12},{5,13},{6,14},{7,15},{8,0},{9,1},... | collective-permute-start | bytes 2162696 | tf_op jit(solution)/shard_map/ppermute | solution.py:48
  140.6 19.0 %collective-permute-start.32 = (bf16[8,32,1408]{2,1,0:T(8,128)(2,1)S(1)}, bf16[8,32,1408]{2,1,0:T(8,128)(2,1)S(1)}, u32[]{:S(2)}, u32[]{:S(2)}) collective-permute-start(bf16[8,32,1408]{2,1,0:T(8,128)(2,1)S(1)} %bitcast.90), channel_id=1, source_target_pairs={{0,2},{1,3},{2,0},{3,1},{4,6},{5,7},{6,4},{7,5},{8,10},{9,11},{10,... | collective-permute-start | bytes 2162696 | tf_op jit(solution)/shard_map/ppermute | solution.py:48
  143.3 17.8 %collective-permute-start.31 = (bf16[8,32,1408]{2,1,0:T(8,128)(2,1)S(1)}, bf16[8,32,1408]{2,1,0:T(8,128)(2,1)S(1)}, u32[]{:S(2)}, u32[]{:S(2)}) collective-permute-start(bf16[8,32,1408]{2,1,0:T(8,128)(2,1)S(1)} %bitcast.89), channel_id=1, source_target_pairs={{0,4},{1,5},{2,6},{3,7},{4,0},{5,1},{6,2},{7,3},{8,12},{9,13},{10,... | collective-permute-start | bytes 2162696 | tf_op jit(solution)/shard_map/ppermute | solution.py:48
  152.6 18.7 %collective-permute-start.30 = (bf16[512,1024]{1,0:T(8,128)(2,1)S(1)}, bf16[512,1024]{1,0:T(8,128)(2,1)S(1)}, u32[]{:S(2)}, u32[]{:S(2)}) collective-permute-start(bf16[512,1024]{1,0:T(8,128)(2,1)S(1)} %get-tuple-element.327.refs_1_), channel_id=1, source_target_pairs={{0,1},{1,0},{2,3},{3,2},{4,5},{5,4},{6,7},{7,6},{8,9},{9,8},{10,11... | collective-permute-start | bytes 3145736 | tf_op jit(solution)/shard_map/ppermute | solution.py:48
  152.7 18.9 %collective-permute-start.29 = (bf16[512,1024]{1,0:T(8,128)(2,1)S(1)}, bf16[512,1024]{1,0:T(8,128)(2,1)S(1)}, u32[]{:S(2)}, u32[]{:S(2)}) collective-permute-start(bf16[512,1024]{1,0:T(8,128)(2,1)S(1)} %get-tuple-element.326.refs_0_), channel_id=1, source_target_pairs={{0,1},{1,0},{2,3},{3,2},{4,5},{5,4},{6,7},{7,6},{8,9},{9,8},{10,11... | collective-permute-start | bytes 3145736 | tf_op jit(solution)/shard_map/ppermute | solution.py:48
  161.7 22.8 %collective-permute-start.33 = (bf16[4,32,1408]{2,1,0:T(8,128)(2,1)S(1)}, bf16[4,32,1408]{2,1,0:T(8,128)(2,1)S(1)}, u32[]{:S(2)}, u32[]{:S(2)}) collective-permute-start(bf16[4,32,1408]{2,1,0:T(8,128)(2,1)S(1)} %get-tuple-element.352), channel_id=1, source_target_pairs={{0,2},{1,3},{2,0},{3,1},{4,6},{5,7},{6,4},{7,5},{8,10},{9,11},{10,... | collective-permute-start | bytes 1081352 | tf_op jit(solution)/shard_map/ppermute | solution.py:48
  162.2 22.4 %collective-permute-start.34 = (bf16[4,32,1408]{2,1,0:T(8,128)(2,1)S(1)}, bf16[4,32,1408]{2,1,0:T(8,128)(2,1)S(1)}, u32[]{:S(2)}, u32[]{:S(2)}) collective-permute-start(bf16[4,32,1408]{2,1,0:T(8,128)(2,1)S(1)} %get-tuple-element.353), channel_id=1, source_target_pairs={{0,4},{1,5},{2,6},{3,7},{4,0},{5,1},{6,2},{7,3},{8,12},{9,13},{10,... | collective-permute-start | bytes 1081352 | tf_op jit(solution)/shard_map/ppermute | solution.py:48
  169.7 33.8 %collective-permute-start.36 = (bf16[8,32,1408]{2,1,0:T(8,128)(2,1)}, bf16[8,32,1408]{2,1,0:T(8,128)(2,1)S(1)}, u32[]{:S(2)}, u32[]{:S(2)}) collective-permute-start(bf16[8,32,1408]{2,1,0:T(8,128)(2,1)} %bitcast.33), channel_id=1, source_target_pairs={{0,2},{1,3},{2,0},{3,1},{4,6},{5,7},{6,4},{7,5},{8,10},{9,11},{10,... | collective-permute-start | bytes 2162696 | tf_op jit(solution)/shard_map/ppermute | solution.py:48
  171.4 32.2 %collective-permute-start.35 = (bf16[8,32,1408]{2,1,0:T(8,128)(2,1)}, bf16[8,32,1408]{2,1,0:T(8,128)(2,1)S(1)}, u32[]{:S(2)}, u32[]{:S(2)}) collective-permute-start(bf16[8,32,1408]{2,1,0:T(8,128)(2,1)} %bitcast.32), channel_id=1, source_target_pairs={{0,4},{1,5},{2,6},{3,7},{4,0},{5,1},{6,2},{7,3},{8,12},{9,13},{10,... | collective-permute-start | bytes 2162696 | tf_op jit(solution)/shard_map/ppermute | solution.py:48
  184.5 26.5 %collective-permute-start.38 = (bf16[8,32,1920]{2,1,0:T(8,128)(2,1)}, bf16[8,32,1920]{2,1,0:T(8,128)(2,1)S(1)}, u32[]{:S(2)}, u32[]{:S(2)}) collective-permute-start(bf16[8,32,1920]{2,1,0:T(8,128)(2,1)} %bitcast.27), channel_id=1, source_target_pairs={{0,4},{1,5},{2,6},{3,7},{4,0},{5,1},{6,2},{7,3},{8,12},{9,13},{10,... | collective-permute-start | bytes 2949128 | tf_op jit(solution)/shard_map/ppermute | solution.py:48
  186.3 24.8 %collective-permute-start.39 = (bf16[8,32,1920]{2,1,0:T(8,128)(2,1)S(1)}, bf16[8,32,1920]{2,1,0:T(8,128)(2,1)S(1)}, u32[]{:S(2)}, u32[]{:S(2)}) collective-permute-start(bf16[8,32,1920]{2,1,0:T(8,128)(2,1)S(1)} %bitcast.88), channel_id=1, source_target_pairs={{0,2},{1,3},{2,0},{3,1},{4,6},{5,7},{6,4},{7,5},{8,10},{9,11},{10,... | collective-permute-start | bytes 2949128 | tf_op jit(solution)/shard_map/ppermute | solution.py:48
  186.8 16.8 %collective-permute-start.37 = (bf16[2,2,32,1408]{3,2,1,0:T(8,128)(2,1)S(1)}, bf16[2,2,32,1408]{3,2,1,0:T(8,128)(2,1)S(1)}, u32[]{:S(2)}, u32[]{:S(2)}) collective-permute-start(bf16[2,2,32,1408]{3,2,1,0:T(8,128)(2,1)S(1)} %get-tuple-element.364), channel_id=1, source_target_pairs={{0,8},{1,9},{2,10},{3,11},{4,12},{5,13},{6,14},{7,15},{8,0},{9,1},... | collective-permute-start | bytes 1081352 | tf_op jit(solution)/shard_map/ppermute | solution.py:48
  204.3 16.2 %collective-permute-start.40 = (bf16[4,32,1408]{2,1,0:T(8,128)(2,1)S(1)}, bf16[4,32,1408]{2,1,0:T(8,128)(2,1)S(1)}, u32[]{:S(2)}, u32[]{:S(2)}) collective-permute-start(bf16[4,32,1408]{2,1,0:T(8,128)(2,1)S(1)} %get-tuple-element.388), channel_id=1, source_target_pairs={{0,2},{1,3},{2,0},{3,1},{4,6},{5,7},{6,4},{7,5},{8,10},{9,11},{10,... | collective-permute-start | bytes 1081352 | tf_op jit(solution)/shard_map/ppermute | solution.py:48
  204.9 15.5 %collective-permute-start.41 = (bf16[4,32,1408]{2,1,0:T(8,128)(2,1)S(1)}, bf16[4,32,1408]{2,1,0:T(8,128)(2,1)S(1)}, u32[]{:S(2)}, u32[]{:S(2)}) collective-permute-start(bf16[4,32,1408]{2,1,0:T(8,128)(2,1)S(1)} %get-tuple-element.389), channel_id=1, source_target_pairs={{0,4},{1,5},{2,6},{3,7},{4,0},{5,1},{6,2},{7,3},{8,12},{9,13},{10,... | collective-permute-start | bytes 1081352 | tf_op jit(solution)/shard_map/ppermute | solution.py:48
  215.6 21.2 %collective-permute-start.44 = (bf16[4,32,1920]{2,1,0:T(8,128)(2,1)S(1)}, bf16[4,32,1920]{2,1,0:T(8,128)(2,1)S(1)}, u32[]{:S(2)}, u32[]{:S(2)}) collective-permute-start(bf16[4,32,1920]{2,1,0:T(8,128)(2,1)S(1)} %get-tuple-element.405), channel_id=1, source_target_pairs={{0,2},{1,3},{2,0},{3,1},{4,6},{5,7},{6,4},{7,5},{8,10},{9,11},{10,... | collective-permute-start | bytes 1474568 | tf_op jit(solution)/shard_map/ppermute | solution.py:48
  216.3 20.4 %collective-permute-start.45 = (bf16[4,32,1920]{2,1,0:T(8,128)(2,1)S(1)}, bf16[4,32,1920]{2,1,0:T(8,128)(2,1)S(1)}, u32[]{:S(2)}, u32[]{:S(2)}) collective-permute-start(bf16[4,32,1920]{2,1,0:T(8,128)(2,1)S(1)} %get-tuple-element.406), channel_id=1, source_target_pairs={{0,4},{1,5},{2,6},{3,7},{4,0},{5,1},{6,2},{7,3},{8,12},{9,13},{10,... | collective-permute-start | bytes 1474568 | tf_op jit(solution)/shard_map/ppermute | solution.py:48
  220.5 16.2 %collective-permute-start.46 = (bf16[8,32,896]{2,1,0:T(8,128)(2,1)S(1)}, bf16[8,32,896]{2,1,0:T(8,128)(2,1)S(1)}, u32[]{:S(2)}, u32[]{:S(2)}) collective-permute-start(bf16[8,32,896]{2,1,0:T(8,128)(2,1)S(1)} %bitcast.92), channel_id=1, source_target_pairs={{0,4},{1,5},{2,6},{3,7},{4,0},{5,1},{6,2},{7,3},{8,12},{9,13},{10,... | collective-permute-start | bytes 1376264 | tf_op jit(solution)/shard_map/ppermute | solution.py:48
  222.0 14.7 %collective-permute-start.47 = (bf16[8,32,896]{2,1,0:T(8,128)(2,1)S(1)}, bf16[8,32,896]{2,1,0:T(8,128)(2,1)S(1)}, u32[]{:S(2)}, u32[]{:S(2)}) collective-permute-start(bf16[8,32,896]{2,1,0:T(8,128)(2,1)S(1)} %bitcast.91), channel_id=1, source_target_pairs={{0,2},{1,3},{2,0},{3,1},{4,6},{5,7},{6,4},{7,5},{8,10},{9,11},{10,... | collective-permute-start | bytes 1376264 | tf_op jit(solution)/shard_map/ppermute | solution.py:48
  242.8 20.6 %collective-permute-start.49 = (bf16[512,1024]{1,0:T(8,128)(2,1)S(1)}, bf16[512,1024]{1,0:T(8,128)(2,1)S(1)}, u32[]{:S(2)}, u32[]{:S(2)}) collective-permute-start(bf16[512,1024]{1,0:T(8,128)(2,1)S(1)} %get-tuple-element.424), channel_id=1, source_target_pairs={{0,1},{1,0},{2,3},{3,2},{4,5},{5,4},{6,7},{7,6},{8,9},{9,8},{10,11... | collective-permute-start | bytes 3145736 | tf_op jit(solution)/shard_map/ppermute | solution.py:48
  242.9 20.6 %collective-permute-start.48 = (bf16[512,1024]{1,0:T(8,128)(2,1)S(1)}, bf16[512,1024]{1,0:T(8,128)(2,1)S(1)}, u32[]{:S(2)}, u32[]{:S(2)}) collective-permute-start(bf16[512,1024]{1,0:T(8,128)(2,1)S(1)} %get-tuple-element.423), channel_id=1, source_target_pairs={{0,1},{1,0},{2,3},{3,2},{4,5},{5,4},{6,7},{7,6},{8,9},{9,8},{10,11... | collective-permute-start | bytes 3145736 | tf_op jit(solution)/shard_map/ppermute | solution.py:48
  257.0 15.5 %collective-permute-start.53 = (bf16[2,2,32,896]{3,2,1,0:T(8,128)(2,1)S(1)}, bf16[2,2,32,896]{3,2,1,0:T(8,128)(2,1)S(1)}, u32[]{:S(2)}, u32[]{:S(2)}) collective-permute-start(bf16[2,2,32,896]{3,2,1,0:T(8,128)(2,1)S(1)} %get-tuple-element.449), channel_id=1, source_target_pairs={{0,8},{1,9},{2,10},{3,11},{4,12},{5,13},{6,14},{7,15},{8,0},{9,1},... | collective-permute-start | bytes 688136 | tf_op jit(solution)/shard_map/ppermute | solution.py:48
  257.9 27.1 %collective-permute-start.55 = (bf16[1,2,32,1920]{3,2,1,0:T(8,128)(2,1)S(1)}, bf16[1,2,32,1920]{3,2,1,0:T(8,128)(2,1)S(1)}, u32[]{:S(2)}, u32[]{:S(2)}) collective-permute-start(bf16[1,2,32,1920]{3,2,1,0:T(8,128)(2,1)S(1)} %get-tuple-element.454), channel_id=1, source_target_pairs={{0,16},{1,17},{2,18},{3,19},{4,20},{5,21},{6,22},{7,23},{8,24},{9,... | collective-permute-start | bytes 737288 | tf_op jit(solution)/shard_map/ppermute | solution.py:48
  263.4 21.6 %collective-permute-start.56 = (bf16[1,2,32,1408]{3,2,1,0:T(8,128)(2,1)S(1)}, bf16[1,2,32,1408]{3,2,1,0:T(8,128)(2,1)S(1)}, u32[]{:S(2)}, u32[]{:S(2)}) collective-permute-start(bf16[1,2,32,1408]{3,2,1,0:T(8,128)(2,1)S(1)} %get-tuple-element.456), channel_id=1, source_target_pairs={{0,16},{1,17},{2,18},{3,19},{4,20},{5,21},{6,22},{7,23},{8,24},{9,... | collective-permute-start | bytes 540680 | tf_op jit(solution)/shard_map/ppermute | solution.py:48
  (55 other events, 446.3 us)

commit v4 on v3

--- a/solution.py
+++ b/solution.py
@@ -181,7 +181,7 @@
     return [(outs[2 * i], outs[2 * i + 1]) for i in range(n)]
 
 
-def fold_plane(pairs, wanted):
+def fold_plane(pairs, wanted, name="fold_plane"):
     shape = (len(wanted) // 2, 2, *pairs[0][0].shape[1:])
     n = shape[0]
 
@@ -193,12 +193,12 @@
 
     return pl.pallas_call(
         body,
-        name="fold_plane",
+        name=name,
         out_shape=(jax.ShapeDtypeStruct(shape, BF16),) * 2,
         in_specs=[VMEM_SPEC] * 4,
         out_specs=(VMEM_SPEC,) * 2,
         compiler_params=params(FOLD_MEGABYTES),
-        cost_estimate=cost("fold_plane"),
+        cost_estimate=cost(name),
     )(*[a for pair in pairs for a in pair])
 
 
@@ -209,10 +209,12 @@
         self.orders = (lay.x + lay.y, lay.y + lay.x)
         self.came = [lay.swap(a, bits[-1]) for a, bits in zip(arrays[1::2], self.orders)]
 
-    def second(self, order):
+    def second(self, order, name="fold"):
         for level in reversed(range(len(self.orders[0]) - 1)):
             came = order(*self.came)
-            found = fold(list(zip(self.kept, came)))
+            found = fold(list(zip(self.kept, came)), name)
+            flat = order(*[a for pair in found for a in pair])
+            found = list(zip(flat[::2], flat[1::2]))
             self.kept = [kept for kept, _ in found]
             self.came = [
                 self.lay.swap(sent, bits[level]) for (_, sent), bits in zip(found, self.orders)
@@ -232,41 +234,65 @@
     def second(self, order):
         while len(self.bits) > 1:
             self.bits.pop(0)
-            ((self.kept, sent),) = fold([(self.kept, order(self.came))], "fold_z")
+            self.kept, sent = order(*fold([(self.kept, order(self.came))], "fold_z")[0])
             self.came = self.lay.swap(sent, self.bits[0])
 
     def last(self, order):
         return self.kept, order(self.came)
 
 
+def fold_four(kept, came):
+    n = kept.shape[0] // 4
+
+    def body(kept_ref, came_ref, *outs):
+        for i, out in enumerate(outs):
+            out[...] = add_low(kept_ref[i * n : (i + 1) * n], came_ref[i * n : (i + 1) * n])
+
+    return pl.pallas_call(
+        body,
+        name="fold_four",
+        out_shape=(jax.ShapeDtypeStruct((n, *kept.shape[1:]), BF16),) * 4,
+        in_specs=[VMEM_SPEC] * 2,
+        out_specs=(VMEM_SPEC,) * 4,
+        compiler_params=params(FOLD_MEGABYTES),
+        cost_estimate=cost("fold_four"),
+    )(kept, came)
+
+
 def add_up(core, ends):
     rows = ends[0][0].shape[2]
-    cols = sum(kept.shape[3] for kept, _ in ends)
+    widths = [end[0].shape[-1] for end in ends]
+    flat = [a for end in ends for a in end]
 
     def body(core_ref, *refs):
         first = core_ref[0] == 0
+        ins = list(refs[:-2])
         at = 0
-        for i, (kept, _) in enumerate(ends):
-            width = kept.shape[3]
-            total = refs[2 * i][0].astype(F32) + refs[2 * i + 1][0].astype(F32)
-            refs[-2][:, at : at + width] = jnp.where(first, total[0], total[1])
-            refs[-1][:, at : at + width] = jnp.where(first, total[1], total[0])
+        for end, width in zip(ends, widths):
+            used = [ins.pop(0)[0].astype(F32) for _ in end]
+            if len(end) == 2:
+                total = used[0] + used[1]
+                low, high = total[0], total[1]
+            else:
+                low, high = used[0] + used[1], used[2] + used[3]
+            refs[-2][:, at : at + width] = jnp.where(first, low, high)
+            refs[-1][:, at : at + width] = jnp.where(first, high, low)
             at += width
 
     return pl.pallas_call(
         body,
         name="add_up",
-        out_shape=(jax.ShapeDtypeStruct((rows, cols), F32),) * 2,
-        in_specs=[SMEM_SPEC] + [VMEM_SPEC] * (2 * len(ends)),
+        out_shape=(jax.ShapeDtypeStruct((rows, sum(widths)), F32),) * 2,
+        in_specs=[SMEM_SPEC] + [VMEM_SPEC] * len(flat),
         out_specs=(VMEM_SPEC,) * 2,
         compiler_params=params(FOLD_MEGABYTES),
         cost_estimate=cost("add_up"),
-    )(core, *[a for end in ends for a in end])
+    )(core, *flat)
 
 
 def wait_for(order, *streams):
     values = [v for s in streams for v in (s.came if isinstance(s.came, list) else [s.came])]
-    values = list(order(*values))
+    values = list(order(*values)) if len(values) > 1 else [order(values[0])]
     for s in streams:
         if isinstance(s.came, list):
             s.came = [values.pop(0) for _ in s.came]
@@ -282,14 +308,14 @@
     return masks
 
 
-WEIGHTS = {}
+SAID_FLOPS = {"shuffle": 10**10, "attn_fwd": 10**10, "down_back": 10**10, "residual": 10**10, "gated": 10**10, "fold_first": 5 * 10**9, "fold_next": 10**10}
+FOLD_FLOPS = 10**9
 FOLD_MEGABYTES = 16
 
 
 def cost(name):
-    return pl.CostEstimate(
-        flops=int(WEIGHTS.get(name, 0) * 1e9) + 1, bytes_accessed=1, transcendentals=0
-    )
+    flops = SAID_FLOPS.get(name, FOLD_FLOPS if name.startswith("fold") else 1)
+    return pl.CostEstimate(flops=flops, bytes_accessed=1, transcendentals=0)
 
 
 def near(*values):
@@ -397,7 +423,7 @@
         body,
         name="shuffle",
         grid=(steps,),
-        out_shape=(*[pltpu.VMEM(v.shape, BF16) for v in values], pltpu.VMEM((width, width), BF16)),
+        out_shape=(*[pltpu.HBM(v.shape, BF16) for v in values], pltpu.HBM((width, width), BF16)),
         in_specs=[SMEM_SPEC, pl.BlockSpec((1, width), lambda i: (0, 0))] + [at] * count,
         out_specs=(*[at] * count, keep),
         compiler_params=params(20),
@@ -457,7 +483,7 @@
         out_shape=tuple(out),
         in_specs=[SMEM_SPEC] + [VMEM_SPEC] * (n_in + 2),
         out_specs=(VMEM_SPEC,) * len(out),
-        compiler_params=params(16),
+        compiler_params=params(60),
     )(core, *[g[None] for g in gains], *flat)
 
 
@@ -558,7 +584,7 @@
         body,
         name="attn_fwd",
         out_shape=(
-            pltpu.VMEM((n_tok, width), BF16),
+            pltpu.HBM((n_tok, width), BF16),
             pltpu.VMEM((n_tok, n_qkv), BF16),
             pltpu.VMEM((n_tok, nv), BF16),
             pltpu.VMEM((n_tok, nv), F32),
@@ -570,7 +596,7 @@
         scratch_shapes=[pltpu.VMEM((length, length), F32)],
         compiler_params=params(28),
         cost_estimate=cost("attn_fwd"),
-    )(seq, *near(tok), *weights)
+    )(seq, tok, *weights)
 
 
 def residual(tok, part, came, gains):
@@ -608,7 +634,7 @@
         out_specs=(at, at),
         compiler_params=params(16),
         cost_estimate=cost("residual"),
-    )(*near(tok), *part, *came, gains)
+    )(tok, *part, *came, gains)
 
 
 def in_order(refs, places, rows):
@@ -636,7 +662,7 @@
         out_specs=rows_spec(size, cols),
         compiler_params=params(20),
         cost_estimate=cost("down_back"),
-    )(*near(grad_out), *weights)
+    )(grad_out, *weights)
 
 
 def gated(weights, normed, d_act):
@@ -672,12 +698,13 @@
     )(*near(normed, d_act), *weights)
 
 
-def weight_grad(lefts, rights, gain=None, name="weight_grad"):
+def weight_grad(lefts, rights, gain=None, name="weight_grad", places=None, rows=0):
     n_tok, width = lefts[0].shape
     sizes = [r.shape[1] for r in rights]
     cols = sum(sizes) + (LANES if gain is not None else 0)
     n, pieces = len(lefts), 4
     chunk = width // pieces
+    out_rows = chunk if places is None else width // 2
     extras, specs = [], []
     if gain is not None:
         weights, gains, other = gain
@@ -705,6 +732,17 @@
                 turned = jnp.where(lane == 0, one / turned, turned)
                 out[:, cols - LANES :] = turned.astype(BF16)
 
+        if places is not None:
+            value = values[0].astype(BF16)
+            for p, (j, i) in enumerate(places):
+                at = p * rows % chunk
+
+                @pl.when(pl.program_id(0) == p * rows // chunk)
+                def _(j=j, i=i, at=at):
+                    outs[j][i * rows : (i + 1) * rows, :] = value[at : at + rows]
+
+            return
+
         for q, out in enumerate(outs):
             w_ref = ins[2 + q] if gain is not None else None
             pl.when(pl.program_id(0) == q)(functools.partial(put, out, w_ref))
@@ -713,14 +751,14 @@
         body,
         name=name,
         grid=(pieces,),
-        out_shape=(jax.ShapeDtypeStruct((chunk, cols), BF16),) * pieces,
+        out_shape=(jax.ShapeDtypeStruct((out_rows, cols), BF16),) * (width // out_rows),
         in_specs=[pl.BlockSpec((n_tok, chunk), lambda i: (0, i))] * n
         + [pl.BlockSpec(r.shape, lambda i: (0, 0)) for r in rights]
         + specs,
-        out_specs=(pl.BlockSpec((chunk, cols), lambda i: (0, 0)),) * pieces,
+        out_specs=(pl.BlockSpec((out_rows, cols), lambda i: (0, 0)),) * (width // out_rows),
         compiler_params=params(26),
         cost_estimate=cost(name),
-    )(*near(*lefts, *rights), *extras)
+    )(*lefts, *near(*rights), *extras)
 
 
 def sum_nt(weights, lefts, starts, pieces, name, places=None, rows=0):
@@ -828,7 +866,7 @@
         ),
         compiler_params=params(20),
         cost_estimate=cost("norm_back"),
-    )(*near(hres, grad_out), gains, *part, *came, *weights)
+    )(*near(hres), grad_out, gains, *part, *came, *weights)
 
 
 def attn_bwd(seq, qkv, y, dy, dinv, dims):
@@ -901,12 +939,12 @@
 
 def finish(part, came, tok, dh, gains, hres, out_part, out_came, placing):
     n_tok, width = part.shape
-    steps = 4
+    steps = 2
     size = n_tok // steps
 
     def body(
         part_ref, came_ref, tok_ref, dh_ref, gain_ref, h_ref, op_ref, oc_ref, p_ref,
-        grad_ref, out_ref, grad_low, out_low,
+        grad_ref, out_ref, low_ref,
     ):
         gain = gain_ref[0:1, :]
 
@@ -916,13 +954,15 @@
             inverse = lax.rsqrt(jnp.mean(x * x, axis=-1, keepdims=True) + EPS)
             xr = x * inverse
             back = inverse * (d - xr * jnp.mean(d * xr, axis=-1, keepdims=True))
-            grad_low[at, :] = (dh_ref[at, :] + back).astype(BF16)
+            low_ref[at, :] = (dh_ref[at, :] + back).astype(BF16)
             both = op_ref[at, :].astype(F32) + oc_ref[at, :].astype(F32)
-            out_low[at, :] = (h_ref[at, :] + both).astype(BF16)
+            below = pl.ds(pl.multiple_of(size + at.start, 64), at.size)
+            low_ref[below, :] = (h_ref[at, :] + both).astype(BF16)
 
         row_chunks(size, 64, rows)
-        grad_ref[...] = dot_nt(grad_low[...], p_ref[...]).astype(BF16)
-        out_ref[...] = dot_nt(out_low[...], p_ref[...]).astype(BF16)
+        placed = dot_nt(low_ref[...], p_ref[...]).astype(BF16)
+        grad_ref[...] = placed[:size]
+        out_ref[...] = placed[size:]
 
     at = rows_spec(size, width)
     out = jax.ShapeDtypeStruct((n_tok, width), BF16)
@@ -934,10 +974,10 @@
         in_specs=[at, at, at, at, pl.BlockSpec((8, width), lambda i: (0, 0)), at, at, at]
         + [pl.BlockSpec((width, width), lambda i: (0, 0))],
         out_specs=(at, at),
-        scratch_shapes=[pltpu.VMEM((size, width), BF16)] * 2,
-        compiler_params=params(16),
+        scratch_shapes=[pltpu.VMEM((2 * size, width), BF16)],
+        compiler_params=params(28),
         cost_estimate=cost("finish"),
-    )(part, came, *near(tok, dh), gains, *near(hres), out_part, out_came, *near(placing))
+    )(part, came, tok, *near(dh), gains, *near(hres), out_part, out_came, placing)
 
 
 def local(
@@ -1007,20 +1047,19 @@
     p_0 = GatherPlane(lay, *halves(z_0))
     z_gu.second(order)
     held_d = p_d.joined(order)
+    z_gu.third(order)
     p_0.second(order)
-    z_gu.third(order)
     z_d = GatherZ(lay, order(held_d))
     z_d.first()
-    halves_gu = halves(z_gu)
-    *arrays_0, low_gu, high_gu = order(*p_0.arrays(), *halves_gu)
-    p_gu = GatherPlane(lay, low_gu, high_gu)
+    p_gu = GatherPlane(lay, *order(*halves(z_gu)))
+    arrays_0 = order(*p_0.arrays())
     z_d.second(order)
     w_0 = flat(arrays_0)
     seq = jnp.concatenate([seq_lengths, seq_other], axis=0)
     tok = jnp.concatenate([tokens, tok_other], axis=0)
     grad_out = jnp.concatenate([cotangent, cot_other], axis=0)
     tok, grad_out, placing = order(*shuffle(index, flat_masks, [tok, grad_out]))
-    z_d.third(order, True)
+    z_d.third(order)
     p_gu.second(order)
     def swap_all(values):
         return [lay.swap(v, 1) for v in values]
@@ -1041,57 +1080,71 @@
     normed_two = order(normed_two)
     act, d_gate, d_up = order(*gated(w_gu, normed_two, d_act))
 
-    def grad(lefts, rights, gain=None, name="weight_grad"):
-        return blocks(order(*weight_grad(lefts, rights, gain, name)))
+    def grad(lefts, rights, gain=None, name="weight_grad", places=None):
+        return blocks(order(*weight_grad(lefts, rights, gain, name, places, rows)))
+
+    z_order = low_first(lay)
+    half_z = len(z_order) // 2
+    places_r = {}
+    for k, z in enumerate(z_order):
+        for i, m in enumerate(both):
+            places_r[m | z] = (k // half_z, (k % half_z) * len(both) + i)
+    places_r = [places_r[m] for m in flat_masks]
+
+    def down_grad():
+        if rows % 16 == 0:
+            return grad([grad_out], [act], name="grad_down", places=places_r)
+        found = jnp.concatenate(grad([grad_out], [act], name="grad_down"))
+        back = [0] * len(places_r)
+        for p, (j, i) in enumerate(places_r):
+            back[j * len(back) // 2 + i] = p
+        return jnp.split(jnp.take(found, jnp.asarray(back), axis=0), 2)
 
     wanted = [masks_of(lay.z).index(m) for m in low_first(lay)]
 
-    def along_z(stream):
-        return ReduceZ(lay, *fold_plane(stream.pairs(order), wanted))
-
-    r_g = ReducePlane(lay, grad([normed_two], [d_gate], name="grad_gate"))
+    def along_z(stream, name="fold_plane"):
+        return ReduceZ(lay, *order(*fold_plane(stream.pairs(order), wanted, name)))
+
+    r_g = ReducePlane(lay, grad(near(normed_two), [d_gate], name="grad_gate"))
     d_up = order(d_up)
     part_n2 = order(*sum_nt(w_gu, [d_gate, d_up], [0, stride], 2, "d_norm2"))
     came_n2 = swap_all(part_n2)
-    r_g.second(order)
     act = order(act)
-    r_d = ReducePlane(lay, grad([grad_out], [act], name="grad_down"))
+    zr_d = ReduceZ(lay, *down_grad())
+    r_g.second(order, "fold_first")
     came_n2 = order(*came_n2)
     d_h, d_o, d_y, gg_mlp = norm_back(w_0, part_n2, came_n2, hres, grad_out, gains, dims)
     d_y = order(d_y)
-    outs_u = grad([normed_two, d_o], [d_up, y], name="grad_up")
-    zr_g = along_z(r_g)
+    outs_u = grad(near(normed_two, d_o), [d_up, y], name="grad_up")
     r_u = ReducePlane(lay, order(*outs_u))
+    zr_g = along_z(r_g, "fold_next")
     d_qkv = order(attn_bwd(seq, qkv, y, order(d_y), dinv, dims))
-    wait_for(order, r_d, zr_g)
+    zr_d.second(order)
+    outs_0 = grad([normed_one], [order(d_qkv)], (w_0, gains, gg_mlp), name="grad_attn")
+    wait_for(order, zr_g)
+    r_u.second(order)
+    part_n1 = order(*sum_nt(w_0, [order(d_qkv)], [0], 2, "norm_one_part"))
+    part_out = order(*sum_nt(w_d, [order(act)], [0], 2, "down", places_z, rows))
+    zr_u = along_z(r_u)
+    r_0 = ReducePlane(lay, order(*outs_0))
+    last_d = order(*fold_four(*zr_d.last(order)))
+    zr_u.second(order)
+    r_0.second(order)
+    r_d = ReducePlane(lay, order(*last_d))
+    zr_0 = along_z(r_0)
     r_d.second(order)
-    wait_for(order, r_u)
-    r_u.second(order)
+    zr_0.second(order)
     zr_g.second(order)
-    d_qkv = order(d_qkv)
-    outs_0 = grad([normed_one], [d_qkv], (w_0, gains, gg_mlp), name="grad_attn")
-    zr_d = along_z(r_d)
-    r_0 = ReducePlane(lay, order(*outs_0))
-    part_n1 = order(*sum_nt(w_0, [order(d_qkv)], [0], 2, "norm_one_part"))
-    wait_for(order, zr_g, zr_d, r_u, r_0)
-    r_0.second(order)
-    zr_u = along_z(r_u)
-    zr_d.second(order)
-    part_out = order(*sum_nt(w_d, [order(act)], [0], 2, "down", places_z, rows))
+    end_u = zr_u.last(order)
     came_rows = swap_all(order(part_n1[1], part_out[1]))
-    wait_for(order, zr_u, r_0)
-    zr_0 = along_z(r_0)
-    zr_u.second(order)
+    end_d = [a for pair in r_d.pairs(order) for a in pair]
     came_rows = order(*came_rows)
     grad_tokens, layer_out = finish(
         part_n1[0], came_rows[0], tok, d_h, gains, hres, part_out[0], came_rows[1], placing
     )
     grad_tokens = order(grad_tokens)
-    zr_0.second(order)
-    end_d = zr_d.last(order)
+    end_0 = zr_0.last(order)
     end_g = zr_g.last(order)
-    end_u = zr_u.last(order)
-    end_0 = zr_0.last(order)
     mine, give = add_up(core.reshape(1), [end_0, end_d, end_g, end_u])
     came = lay.swap(give, 1)
     at = 2 * nq + nv

time: 291 us -> 272 us (0.935)
  local copies, waits for them, and re-layouts: 19.5 us -> 5.62 us
  starting transfers between devices: 68.5 us -> 56.3 us
  waiting for transfers between devices: 85.7 us -> 97.2 us
  Pallas kernels: 110 us -> 106 us
    ppermute x58, starting transfers between devices: 68.5 us -> 56.3 us  [swap(): return lax.ppermute(value, AXES, [(i, i ^ bit) for i in range(self.count)])]
    unnamed x68 -> x58, local copies, waits for them, and re-layouts: 15.4 us -> 3.56 us
    ppermute x58, waiting for transfers between devices: 85.7 us -> 97.2 us  [swap(): return lax.ppermute(value, AXES, [(i, i ^ bit) for i in range(self.count)])]
    pallas_call x1, Pallas kernels: 9.03 us -> 5.61 us  [finish(): pl.pallas_call(body, name='finish', grid=(steps,), out_shape=(out, out),...]
    select_n x3, other arithmetic: 0.1 us -> 3.15 us  [by_core(): jnp.where(core == 0, jnp.stack([own, other]), jnp.stack([other, own]))]
  transfers between devices with their start and end apart: 58 -> 58, of which waited for: 21 -> 28; matrix products, arithmetic and copies ran while one was open for 5% -> 3% of each run, Pallas kernels for 30% -> 31%
where the time goes in v4:
time: 272 us
  Pallas kernels  106 us (39%)
  waiting for transfers between devices  97.2 us (36%)
  starting transfers between devices  56.3 us (21%)
  local copies, waits for them, and re-layouts  5.62 us (2%)
  other arithmetic  5.49 us (2%)
    ppermute x58, waiting for transfers between devices, swap(): return lax.ppermute(value, AXES, [(i, i ^ bit) for i in range(self.count)])  97.2 us
    ppermute x58, starting transfers between devices, swap(): return lax.ppermute(value, AXES, [(i, i ^ bit) for i in range(self.count)])  56.3 us
    pallas_call x4, Pallas kernels, weight_grad(): pl.pallas_call(body, name=name, grid=(pieces,), out_shape=(jax.ShapeDtype...  19.2 us
    pallas_call x1, Pallas kernels, attn_bwd(): pl.pallas_call(body, name='attn_bwd', out_shape=pltpu.VMEM(qkv.shape, BF1...  15.1 us
    pallas_call x3, Pallas kernels, sum_nt(): pl.pallas_call(body, name=name, grid=(steps,), out_shape=(jax.ShapeDtypeS...  14.8 us
    pallas_call x1, Pallas kernels, attn_fwd(): pl.pallas_call(body, name='attn_fwd', out_shape=(pltpu.HBM((n_tok, width)...  14.4 us
    pallas_call x1, Pallas kernels, gated(): pl.pallas_call(body, name='gated', grid=(steps,), out_shape=(out, out, ou...  8.69 us
    pallas_call x1, Pallas kernels, shuffle(): pl.pallas_call(body, name='shuffle', grid=(steps,), out_shape=(*[pltpu.HB...  7.53 us
  transfers between devices with their start and end apart: 58, of which 28 were waited for; matrix products, arithmetic and copies ran while one was open for 3% of the time, Pallas kernels for 31%

profile of v4, /device:TPU:0, one launch (start us, length us, event | category | flops | bytes accessed | tf_op | source)
XLA Modules:
  0.0 271.9 jit_solution(18142337159564906260)
XLA Ops:
  0.7 2.6 prepare.1
  6.3 4.0 %collective-permute-start.6 = (bf16[2,32,1408]{2,1,0:T(8,128)(2,1)S(1)}, bf16[2,32,1408]{2,1,0:T(8,128)(2,1)S(1)}, u32[]{:S(2)}, u32[]{:S(2)}) collective-permute-start(bf16[2,32,1408]{2,1,0:T(8,128)(2,1)S(1)} %maximum_select_fusion.2), channel_id=1, source_target_pairs={{0,16},{1,17},{2,18},{3,19},{4,20},{5,21},{6,22},{7,23},{8,24},{9,... | collective-permute-start | bytes 540680 | tf_op jit(solution)/shard_map/ppermute | solution.py:48
  25.7 7.4 %collective-permute-done.10 = bf16[2,32,1408]{2,1,0:T(8,128)(2,1)S(1)} collective-permute-done((bf16[2,32,1408]{2,1,0:T(8,128)(2,1)S(1)}, bf16[2,32,1408]{2,1,0:T(8,128)(2,1)S(1)}, u32[]{:S(2)}, u32[]{:S(2)}) %collective-permute-start.10) | collective-permute-done | bytes 180256 | tf_op jit(solution)/shard_map/ppermute | solution.py:48
  33.1 2.5 collective-permute-start.16
  37.3 7.1 %collective-permute-done.11 = bf16[4,32,1408]{2,1,0:T(8,128)(2,1)S(1)} collective-permute-done((bf16[4,32,1408]{2,1,0:T(8,128)(2,1)S(1)}, bf16[4,32,1408]{2,1,0:T(8,128)(2,1)S(1)}, u32[]{:S(2)}, u32[]{:S(2)}) %collective-permute-start.11) | collective-permute-done | bytes 360480 | tf_op jit(solution)/shard_map/ppermute | solution.py:48
  48.7 8.6 %collective-permute-done.17 = bf16[2,32,2816]{2,1,0:T(8,128)(2,1)S(1)} collective-permute-done((bf16[2,32,2816]{2,1,0:T(8,128)(2,1)S(1)}, bf16[2,32,2816]{2,1,0:T(8,128)(2,1)S(1)}, u32[]{:S(2)}, u32[]{:S(2)}) %collective-permute-start.17) | collective-permute-done | bytes 360480 | tf_op jit(solution)/shard_map/ppermute | solution.py:48
  58.1 7.5 %shuffle.1 = (bf16[1024,1024]{1,0:T(8,128)(2,1)}, bf16[1024,1024]{1,0:T(8,128)(2,1)}, bf16[1024,1024]{1,0:T(8,128)(2,1)}) custom-call(s32[1]{0:T(128)} %bitcast.5.index_ref, s32[1,1024]{1,0:T(1,128)S(1)} %broadcast_in_dim_reshape.3.masks_ref, bf16[1024,1024]{1,0:T(8,128)(2,1)S(1)} %get-tuple-element.548.refs_0_, ...), custom_call_target="tpu_custom_call" | custom-call | flops 10000000000 | bytes 1 | tf_op jit(solution)/shard_map/shuffle/pallas_call | solution.py:422
  66.0 10.7 %collective-permute-done.20 = bf16[8,32,1408]{2,1,0:T(8,128)(2,1)S(1)} collective-permute-done((bf16[8,32,1408]{2,1,0:T(8,128)(2,1)S(1)}, bf16[8,32,1408]{2,1,0:T(8,128)(2,1)S(1)}, u32[]{:S(2)}, u32[]{:S(2)}) %collective-permute-start.20) | collective-permute-done | bytes 720928 | tf_op jit(solution)/shard_map/ppermute | solution.py:48
  83.9 14.4 %attn_fwd.1 = (bf16[1024,1024]{1,0:T(8,128)(2,1)}, bf16[1024,768]{1,0:T(8,128)(2,1)S(1)}, bf16[1024,512]{1,0:T(8,128)(2,1)S(1)}, f32[1024,512]{1,0:T(8,128)S(1)}...) custom-call(s32[2,4]{1,0:T(2,128)S(1)} %pad_add_fusion.seq_ref, ...), custom_call_target="tpu_custom_call" | custom-call | flops 10000000000 | bytes 1 | tf_op jit(solution)/shard_map/attn_fwd/pallas_call | solution.py:583
  99.4 11.1 %collective-permute-done.28 = bf16[8,32,1408]{2,1,0:T(8,128)(2,1)S(1)} collective-permute-done((bf16[8,32,1408]{2,1,0:T(8,128)(2,1)S(1)}, bf16[8,32,1408]{2,1,0:T(8,128)(2,1)S(1)}, u32[]{:S(2)}, u32[]{:S(2)}) %collective-permute-start.28) | collective-permute-done | bytes 720928 | tf_op jit(solution)/shard_map/ppermute | solution.py:48
  111.0 4.0 %down_back.1.d_act_ref = bf16[1024,1408]{1,0:T(8,128)(2,1)S(1)} custom-call(bf16[1024,1024]{1,0:T(8,128)(2,1)S(1)} %copy-done, bf16[256,1408]{1,0:T(8,128)(2,1)S(1)} %bitcast.71, bf16[256,1408]{1,0:T(8,128)(2,1)S(1)} %bitcast.75, bf16[256,1408]{1,0:T(8,128)(2,1)S(1)} %bitcast.73, bf16[256,1408]{1,0:T(8,128)(2,1)S(1)} %bitcast.77), custom_call_target="tpu_custom_call" | custom-call | flops 10000000000 | bytes 1 | tf_op jit(solution)/shard_map/down_back/pallas_call | solution.py:656
  115.1 2.6 residual.1
  120.9 8.7 %gated.1 = (bf16[1024,1408]{1,0:T(8,128)(2,1)S(1)}, bf16[1024,1408]{1,0:T(8,128)(2,1)S(1)}, bf16[1024,1408]{1,0:T(8,128)(2,1)S(1)}) custom-call(bf16[1024,1024]{1,0:T(8,128)(2,1)S(1)} %get-tuple-element.329.normed_ref.refs_0_, bf16[1024,1408]{1,0:T(8,128)(2,1)S(1)} %copy-done.19, bf16[256,2816]{1,0:T(8,128)(2,1)S(1)} %bitcast.61, ...), custom_call_target="tpu_custom_call" | custom-call | flops 10000000000 | bytes 1 | tf_op jit(solution)/shard_map/gated/pallas_call | solution.py:689
  129.6 4.8 %grad_gate.1 = (bf16[256,1408]{1,0:T(8,128)(2,1)S(1)}, bf16[256,1408]{1,0:T(8,128)(2,1)S(1)}, bf16[256,1408]{1,0:T(8,128)(2,1)S(1)}, bf16[256,1408]{1,0:T(8,128)(2,1)S(1)}) custom-call(bf16[1024,1024]{1,0:T(8,128)(2,1)S(1)} %get-tuple-element.329.normed_ref.refs_0_, bf16[1024,1408]{1,0:T(8,128)(2,1)S(1)} %get-tuple-element.336.refs_1_.refs_0_), custom_call_target="tpu_custom_call" | custom-call | flops 1 | bytes 1 | tf_op jit(solution)/shard_map/grad_gate/pallas_call | solution.py:750
  136.5 7.5 %d_norm2.1 = (bf16[512,1024]{1,0:T(8,128)(2,1)S(1)}, bf16[512,1024]{1,0:T(8,128)(2,1)S(1)}) custom-call(bf16[1024,1408]{1,0:T(8,128)(2,1)S(1)} %get-tuple-element.336.refs_1_.refs_0_, bf16[1024,1408]{1,0:T(8,128)(2,1)S(1)} %get-tuple-element.344.refs_1_.refs_2_, bf16[256,2816]{1,0:T(8,128)(2,1)S(1)} %bitcast.62, bf16[256,2816]{1,0:T(8,128)(2,1)S(1)} %bitcast.66, ...), custom_call_target="tpu_custom_call" | custom-call | flops 1 | bytes 1 | tf_op jit(solution)/shard_map/d_norm2/pallas_call | solution.py:793
  144.6 4.7 %grad_down.1 = (bf16[512,1408]{1,0:T(8,128)(2,1)S(1)}, bf16[512,1408]{1,0:T(8,128)(2,1)S(1)}) custom-call(bf16[1024,1024]{1,0:T(8,128)(2,1)S(1)} %copy-done, bf16[1024,1408]{1,0:T(8,128)(2,1)S(1)} %get-tuple-element.418.refs_1_.refs_0_), custom_call_target="tpu_custom_call" | custom-call | flops 1 | bytes 1 | tf_op jit(solution)/shard_map/grad_down/pallas_call | solution.py:750
  149.3 3.2 %collective-permute-done.32.refs_3_ = bf16[8,32,1408]{2,1,0:T(8,128)(2,1)S(1)} collective-permute-done((bf16[8,32,1408]{2,1,0:T(8,128)(2,1)S(1)}, bf16[8,32,1408]{2,1,0:T(8,128)(2,1)S(1)}, u32[]{:S(2)}, u32[]{:S(2)}) %collective-permute-start.32) | collective-permute-done | bytes 720928 | tf_op jit(solution)/shard_map/ppermute | solution.py:48
  156.2 5.8 %norm_back.1 = (f32[512,1024]{1,0:T(8,128)S(1)}, bf16[1024,1024]{1,0:T(8,128)(2,1)S(1)}, bf16[1024,512]{1,0:T(8,128)(2,1)S(1)}, f32[8,1024]{1,0:T(8,128)S(1)}) custom-call(f32[1024,1024]{1,0:T(8,128)S(1)} %get-tuple-element.327.hres_ref.h_ref, bf16[1024,1024]{1,0:T(8,128)(2,1)S(1)} %copy-done, f32[8,1024]{1,0:T(8,128)S(1)} %get-tuple-element.326.refs_8_.gain_ref.refs_2_, ...), custom_call_target="tpu_custom_call" | custom-call | flops 1 | bytes 1 | tf_op jit(solution)/shard_map/norm_back/pallas_call | solution.py:847
  162.0 6.2 %grad_up.1 = (bf16[256,1920]{1,0:T(8,128)(2,1)S(1)}, bf16[256,1920]{1,0:T(8,128)(2,1)S(1)}, bf16[256,1920]{1,0:T(8,128)(2,1)S(1)}, bf16[256,1920]{1,0:T(8,128)(2,1)S(1)}) custom-call(bf16[1024,1024]{1,0:T(8,128)(2,1)S(1)} %get-tuple-element.329.normed_ref.refs_0_, bf16[1024,1024]{1,0:T(8,128)(2,1)S(1)} %get-tuple-element.369.refs_1_, ...), custom_call_target="tpu_custom_call" | custom-call | flops 1 | bytes 1 | tf_op jit(solution)/shard_map/grad_up/pallas_call | solution.py:750
  173.0 15.1 %attn_bwd.1.refs_1_.refs_0_ = bf16[1024,768]{1,0:T(8,128)(2,1)S(1)} custom-call(s32[2,4]{1,0:T(2,128)S(1)} %pad_add_fusion.seq_ref, bf16[1024,768]{1,0:T(8,128)(2,1)S(1)} %copy-done.8, bf16[1024,512]{1,0:T(8,128)(2,1)S(1)} %get-tuple-element.302.refs_3_.y_ref, bf16[1024,512]{1,0:T(8,128)(2,1)S(1)} %get-tuple-element.385.dy_ref, f32[1024,512]{1,0:T(8,128)S(1)} %copy-done.6), custom_call_target="tpu_custom_call" | custom-call | flops 1 | bytes 1 | tf_op jit(solution)/shard_map/attn_bwd/pallas_call | solution.py:923
  188.1 2.3 collective-permute-done.38.refs_1_
  191.2 3.6 %grad_attn.1 = (bf16[256,896]{1,0:T(8,128)(2,1)S(1)}, bf16[256,896]{1,0:T(8,128)(2,1)S(1)}, bf16[256,896]{1,0:T(8,128)(2,1)S(1)}, bf16[256,896]{1,0:T(8,128)(2,1)S(1)}) custom-call(bf16[1024,1024]{1,0:T(8,128)(2,1)S(1)} %copy-done.4, bf16[1024,768]{1,0:T(8,128)(2,1)S(1)} %attn_bwd.1.refs_1_.refs_0_, ...), custom_call_target="tpu_custom_call" | custom-call | flops 1 | bytes 1 | tf_op jit(solution)/shard_map/grad_attn/pallas_call | solution.py:750
  200.1 2.7 norm_one_part.1
  202.8 4.5 %down.1 = (bf16[512,1024]{1,0:T(8,128)(2,1)S(1)}, bf16[512,1024]{1,0:T(8,128)(2,1)S(1)}) custom-call(bf16[1024,1408]{1,0:T(8,128)(2,1)S(1)} %get-tuple-element.418.refs_1_.refs_0_, bf16[256,1408]{1,0:T(8,128)(2,1)S(1)} %bitcast.72, bf16[256,1408]{1,0:T(8,128)(2,1)S(1)} %bitcast.76, bf16[256,1408]{1,0:T(8,128)(2,1)S(1)} %bitcast.74, ...), custom_call_target="tpu_custom_call" | custom-call | flops 1 | bytes 1 | tf_op jit(solution)/shard_map/down/pallas_call | solution.py:793
  211.2 19.1 %collective-permute-done.42.came_ref = bf16[8,32,1408]{2,1,0:T(8,128)(2,1)S(1)} collective-permute-done((bf16[8,32,1408]{2,1,0:T(8,128)(2,1)S(1)}, bf16[8,32,1408]{2,1,0:T(8,128)(2,1)S(1)}, u32[]{:S(2)}, u32[]{:S(2)}) %collective-permute-start.42) | collective-permute-done | bytes 720928 | tf_op jit(solution)/shard_map/ppermute | solution.py:48
  230.5 2.5 collective-permute-done.41.refs_1_
  237.8 2.9 %collective-permute-done.46.refs_1_ = bf16[4,32,896]{2,1,0:T(8,128)(2,1)S(1)} collective-permute-done((bf16[4,32,896]{2,1,0:T(8,128)(2,1)S(1)}, bf16[4,32,896]{2,1,0:T(8,128)(2,1)S(1)}, u32[]{:S(2)}, u32[]{:S(2)}) %collective-permute-start.46) | collective-permute-done | bytes 229408 | tf_op jit(solution)/shard_map/ppermute | solution.py:48
  241.2 2.6 collective-permute-start.43
  244.0 5.6 %collective-permute-done.48.refs_1_ = bf16[2,2,32,896]{3,2,1,0:T(8,128)(2,1)S(1)} collective-permute-done((bf16[2,2,32,896]{3,2,1,0:T(8,128)(2,1)S(1)}, bf16[2,2,32,896]{3,2,1,0:T(8,128)(2,1)S(1)}, u32[]{:S(2)}, u32[]{:S(2)}) %collective-permute-start.48) | collective-permute-done | bytes 229408 | tf_op jit(solution)/shard_map/ppermute | solution.py:48
  252.9 2.9 %collective-permute-start.55 = (bf16[1,2,32,896]{3,2,1,0:T(8,128)(2,1)S(1)}, bf16[1,2,32,896]{3,2,1,0:T(8,128)(2,1)S(1)}, u32[]{:S(2)}, u32[]{:S(2)}) collective-permute-start(bf16[1,2,32,896]{3,2,1,0:T(8,128)(2,1)S(1)} %get-tuple-element.502), channel_id=1, source_target_pairs={{0,16},{1,17},{2,18},{3,19},{4,20},{5,21},{6,22},{7,23},{8,24},{9,... | collective-permute-start | bytes 344072 | tf_op jit(solution)/shard_map/ppermute | solution.py:48
  257.0 3.6 %collective-permute-done.54.refs_5_ = bf16[1,32,1408]{2,1,0:T(8,128)(2,1)S(1)} collective-permute-done((bf16[1,32,1408]{2,1,0:T(8,128)(2,1)S(1)}, bf16[1,32,1408]{2,1,0:T(8,128)(2,1)S(1)}, u32[]{:S(2)}, u32[]{:S(2)}) %collective-permute-start.54) | collective-permute-done | bytes 90144 | tf_op jit(solution)/shard_map/ppermute | solution.py:48
  260.6 5.6 %finish.1 = (bf16[512,1024]{1,0:T(8,128)(2,1)}, bf16[512,1024]{1,0:T(8,128)(2,1)}) custom-call(bf16[512,1024]{1,0:T(8,128)(2,1)S(1)} %get-tuple-element.416.part_ref, bf16[512,1024]{1,0:T(8,128)(2,1)S(1)} %collective-permute-done.51.came_ref, bf16[1024,1024]{1,0:T(8,128)(2,1)S(1)} %copy-done.2, f32[512,1024]{1,0:T(8,128)S(1)} %get-tuple-element.496.dh_ref, ...), custom_call_target="tpu_custom_call" | custom-call | flops 1 | bytes 1 | tf_op jit(solution)/shard_map/finish/pallas_call | solution.py:969
  (195 shorter events, 74.0 us)
Async XLA Ops:
  4.2 14.0 %collective-permute-start.2 = (bf16[512,1024]{1,0:T(8,128)(2,1)}, bf16[512,1024]{1,0:T(8,128)(2,1)}, u32[]{:S(2)}, u32[]{:S(2)}) collective-permute-start(bf16[512,1024]{1,0:T(8,128)(2,1)} %param.24), channel_id=1, source_target_pairs={{0,1},{1,0},{2,3},{3,2},{4,5},{5,4},{6,7},{7,6},{8,9},{9,8},{10,11... | collective-permute-start | bytes 3145736 | tf_op jit(solution)/shard_map/ppermute | solution.py:48
  18.2 19.0 %collective-permute-start.13 = (bf16[2,32,2816]{2,1,0:T(8,128)(2,1)S(1)}, bf16[2,32,2816]{2,1,0:T(8,128)(2,1)S(1)}, u32[]{:S(2)}, u32[]{:S(2)}) collective-permute-start(bf16[2,32,2816]{2,1,0:T(8,128)(2,1)S(1)} %maximum_select_fusion), channel_id=1, source_target_pairs={{0,16},{1,17},{2,18},{3,19},{4,20},{5,21},{6,22},{7,23},{8,24},{9,... | collective-permute-start | bytes 1081352 | tf_op jit(solution)/shard_map/ppermute | solution.py:48
  19.1 14.0 %collective-permute-start.10 = (bf16[2,32,1408]{2,1,0:T(8,128)(2,1)S(1)}, bf16[2,32,1408]{2,1,0:T(8,128)(2,1)S(1)}, u32[]{:S(2)}, u32[]{:S(2)}) collective-permute-start(bf16[2,32,1408]{2,1,0:T(8,128)(2,1)S(1)} %collective-permute-done.6), channel_id=1, source_target_pairs={{0,8},{1,9},{2,10},{3,11},{4,12},{5,13},{6,14},{7,15},{8,0},{9,1},... | collective-permute-start | bytes 540680 | tf_op jit(solution)/shard_map/ppermute | solution.py:48
  20.0 15.7 %collective-permute-start.7 = (bf16[2,32,1408]{2,1,0:T(8,128)(2,1)S(1)}, bf16[2,32,1408]{2,1,0:T(8,128)(2,1)S(1)}, u32[]{:S(2)}, u32[]{:S(2)}) collective-permute-start(bf16[2,32,1408]{2,1,0:T(8,128)(2,1)S(1)} %pad_maximum_fusion.6), channel_id=1, source_target_pairs={{0,4},{1,5},{2,6},{3,7},{4,0},{5,1},{6,2},{7,3},{8,12},{9,13},{10,... | collective-permute-start | bytes 540680 | tf_op jit(solution)/shard_map/ppermute | solution.py:48
  21.6 14.1 %collective-permute-start.8 = (bf16[2,32,1408]{2,1,0:T(8,128)(2,1)S(1)}, bf16[2,32,1408]{2,1,0:T(8,128)(2,1)S(1)}, u32[]{:S(2)}, u32[]{:S(2)}) collective-permute-start(bf16[2,32,1408]{2,1,0:T(8,128)(2,1)S(1)} %pad_maximum_fusion.7), channel_id=1, source_target_pairs={{0,2},{1,3},{2,0},{3,1},{4,6},{5,7},{6,4},{7,5},{8,10},{9,11},{10,... | collective-permute-start | bytes 540680 | tf_op jit(solution)/shard_map/ppermute | solution.py:48
  33.1 15.5 %collective-permute-start.16 = (bf16[2,32,2816]{2,1,0:T(8,128)(2,1)S(1)}, bf16[2,32,2816]{2,1,0:T(8,128)(2,1)S(1)}, u32[]{:S(2)}, u32[]{:S(2)}) collective-permute-start(bf16[2,32,2816]{2,1,0:T(8,128)(2,1)S(1)} %maximum_select_fusion), channel_id=1, source_target_pairs={{0,8},{1,9},{2,10},{3,11},{4,12},{5,13},{6,14},{7,15},{8,0},{9,1},... | collective-permute-start | bytes 1081352 | tf_op jit(solution)/shard_map/ppermute | solution.py:48
  37.2 20.1 %collective-permute-start.17 = (bf16[2,32,2816]{2,1,0:T(8,128)(2,1)S(1)}, bf16[2,32,2816]{2,1,0:T(8,128)(2,1)S(1)}, u32[]{:S(2)}, u32[]{:S(2)}) collective-permute-start(bf16[2,32,2816]{2,1,0:T(8,128)(2,1)S(1)} %collective-permute-done.13), channel_id=1, source_target_pairs={{0,8},{1,9},{2,10},{3,11},{4,12},{5,13},{6,14},{7,15},{8,0},{9,1},... | collective-permute-start | bytes 1081352 | tf_op jit(solution)/shard_map/ppermute | solution.py:48
  44.8 31.9 %collective-permute-start.20 = (bf16[8,32,1408]{2,1,0:T(8,128)(2,1)S(1)}, bf16[8,32,1408]{2,1,0:T(8,128)(2,1)S(1)}, u32[]{:S(2)}, u32[]{:S(2)}) collective-permute-start(bf16[8,32,1408]{2,1,0:T(8,128)(2,1)S(1)} %constant_dynamic-update-slice_fusion), channel_id=1, source_target_pairs={{0,16},{1,17},{2,18},{3,19},{4,20},{5,21},{6,22},{7,23},{8,24},{9,... | collective-permute-start | bytes 2162696 | tf_op jit(solution)/shard_map/ppermute | solution.py:48
  46.5 19.2 %collective-permute-start.14 = (bf16[8,32,1408]{2,1,0:T(8,128)(2,1)S(1)}, bf16[8,32,1408]{2,1,0:T(8,128)(2,1)S(1)}, u32[]{:S(2)}, u32[]{:S(2)}) collective-permute-start(bf16[8,32,1408]{2,1,0:T(8,128)(2,1)S(1)} %constant_dynamic-update-slice_fusion.6), channel_id=1, source_target_pairs={{0,4},{1,5},{2,6},{3,7},{4,0},{5,1},{6,2},{7,3},{8,12},{9,13},{10,... | collective-permute-start | bytes 2162696 | tf_op jit(solution)/shard_map/ppermute | solution.py:48
  46.9 19.1 %collective-permute-start.15 = (bf16[8,32,1408]{2,1,0:T(8,128)(2,1)S(1)}, bf16[8,32,1408]{2,1,0:T(8,128)(2,1)S(1)}, u32[]{:S(2)}, u32[]{:S(2)}) collective-permute-start(bf16[8,32,1408]{2,1,0:T(8,128)(2,1)S(1)} %constant_dynamic-update-slice_fusion.11), channel_id=1, source_target_pairs={{0,2},{1,3},{2,0},{3,1},{4,6},{5,7},{6,4},{7,5},{8,10},{9,11},{10,... | collective-permute-start | bytes 2162696 | tf_op jit(solution)/shard_map/ppermute | solution.py:48
  57.6 20.6 %collective-permute-start.19 = (bf16[4,32,2816]{2,1,0:T(8,128)(2,1)S(1)}, bf16[4,32,2816]{2,1,0:T(8,128)(2,1)S(1)}, u32[]{:S(2)}, u32[]{:S(2)}) collective-permute-start(bf16[4,32,2816]{2,1,0:T(8,128)(2,1)S(1)} %pad_maximum_fusion.3), channel_id=1, source_target_pairs={{0,4},{1,5},{2,6},{3,7},{4,0},{5,1},{6,2},{7,3},{8,12},{9,13},{10,... | collective-permute-start | bytes 2162696 | tf_op jit(solution)/shard_map/ppermute | solution.py:48
  58.1 20.5 %collective-permute-start.18 = (bf16[4,32,2816]{2,1,0:T(8,128)(2,1)S(1)}, bf16[4,32,2816]{2,1,0:T(8,128)(2,1)S(1)}, u32[]{:S(2)}, u32[]{:S(2)}) collective-permute-start(bf16[4,32,2816]{2,1,0:T(8,128)(2,1)S(1)} %pad_maximum_fusion.2), channel_id=1, source_target_pairs={{0,2},{1,3},{2,0},{3,1},{4,6},{5,7},{6,4},{7,5},{8,10},{9,11},{10,... | collective-permute-start | bytes 2162696 | tf_op jit(solution)/shard_map/ppermute | solution.py:48
  78.7 31.8 %collective-permute-start.25 = (bf16[8,32,2816]{2,1,0:T(8,128)(2,1)S(1)}, bf16[8,32,2816]{2,1,0:T(8,128)(2,1)S(1)}, u32[]{:S(2)}, u32[]{:S(2)}) collective-permute-start(bf16[8,32,2816]{2,1,0:T(8,128)(2,1)S(1)} %constant_dynamic-update-slice_fusion.16), channel_id=1, source_target_pairs={{0,4},{1,5},{2,6},{3,7},{4,0},{5,1},{6,2},{7,3},{8,12},{9,13},{10,... | collective-permute-start | bytes 4325384 | tf_op jit(solution)/shard_map/ppermute | solution.py:48
  80.2 19.1 %collective-permute-start.27 = (bf16[8,32,1408]{2,1,0:T(8,128)(2,1)S(1)}, bf16[8,32,1408]{2,1,0:T(8,128)(2,1)S(1)}, u32[]{:S(2)}, u32[]{:S(2)}) collective-permute-start(bf16[8,32,1408]{2,1,0:T(8,128)(2,1)S(1)} %constant_dynamic-update-slice_fusion), channel_id=1, source_target_pairs={{0,8},{1,9},{2,10},{3,11},{4,12},{5,13},{6,14},{7,15},{8,0},{9,1},... | collective-permute-start | bytes 2162696 | tf_op jit(solution)/shard_map/ppermute | solution.py:48
  80.3 30.2 %collective-permute-start.28 = (bf16[8,32,1408]{2,1,0:T(8,128)(2,1)S(1)}, bf16[8,32,1408]{2,1,0:T(8,128)(2,1)S(1)}, u32[]{:S(2)}, u32[]{:S(2)}) collective-permute-start(bf16[8,32,1408]{2,1,0:T(8,128)(2,1)S(1)} %collective-permute-done.20), channel_id=1, source_target_pairs={{0,8},{1,9},{2,10},{3,11},{4,12},{5,13},{6,14},{7,15},{8,0},{9,1},... | collective-permute-start | bytes 2162696 | tf_op jit(solution)/shard_map/ppermute | solution.py:48
  82.4 32.7 %collective-permute-start.26 = (bf16[8,32,2816]{2,1,0:T(8,128)(2,1)S(1)}, bf16[8,32,2816]{2,1,0:T(8,128)(2,1)S(1)}, u32[]{:S(2)}, u32[]{:S(2)}) collective-permute-start(bf16[8,32,2816]{2,1,0:T(8,128)(2,1)S(1)} %constant_dynamic-update-slice_fusion.18), channel_id=1, source_target_pairs={{0,2},{1,3},{2,0},{3,1},{4,6},{5,7},{6,4},{7,5},{8,10},{9,11},{10,... | collective-permute-start | bytes 4325384 | tf_op jit(solution)/shard_map/ppermute | solution.py:48
  98.3 16.7 %collective-permute-start.22 = (bf16[256,1024]{1,0:T(8,128)(2,1)S(1)}, bf16[256,1024]{1,0:T(8,128)(2,1)S(1)}, u32[]{:S(2)}, u32[]{:S(2)}) collective-permute-start(bf16[256,1024]{1,0:T(8,128)(2,1)S(1)} %get-tuple-element.311.refs_1_), channel_id=1, source_target_pairs={{0,1},{1,0},{2,3},{3,2},{4,5},{5,4},{6,7},{7,6},{8,9},{9,8},{10,11... | collective-permute-start | bytes 1572872 | tf_op jit(solution)/shard_map/ppermute | solution.py:48
  99.4 15.7 %collective-permute-start.23 = (bf16[256,1024]{1,0:T(8,128)(2,1)S(1)}, bf16[256,1024]{1,0:T(8,128)(2,1)S(1)}, u32[]{:S(2)}, u32[]{:S(2)}) collective-permute-start(bf16[256,1024]{1,0:T(8,128)(2,1)S(1)} %get-tuple-element.312.refs_2_), channel_id=1, source_target_pairs={{0,1},{1,0},{2,3},{3,2},{4,5},{5,4},{6,7},{7,6},{8,9},{9,8},{10,11... | collective-permute-start | bytes 1572872 | tf_op jit(solution)/shard_map/ppermute | solution.py:48
  134.4 18.2 %collective-permute-start.32 = (bf16[8,32,1408]{2,1,0:T(8,128)(2,1)S(1)}, bf16[8,32,1408]{2,1,0:T(8,128)(2,1)S(1)}, u32[]{:S(2)}, u32[]{:S(2)}) collective-permute-start(bf16[8,32,1408]{2,1,0:T(8,128)(2,1)S(1)} %bitcast.86), channel_id=1, source_target_pairs={{0,2},{1,3},{2,0},{3,1},{4,6},{5,7},{6,4},{7,5},{8,10},{9,11},{10,... | collective-permute-start | bytes 2162696 | tf_op jit(solution)/shard_map/ppermute | solution.py:48
  135.9 17.8 %collective-permute-start.31 = (bf16[8,32,1408]{2,1,0:T(8,128)(2,1)S(1)}, bf16[8,32,1408]{2,1,0:T(8,128)(2,1)S(1)}, u32[]{:S(2)}, u32[]{:S(2)}) collective-permute-start(bf16[8,32,1408]{2,1,0:T(8,128)(2,1)S(1)} %bitcast.85), channel_id=1, source_target_pairs={{0,4},{1,5},{2,6},{3,7},{4,0},{5,1},{6,2},{7,3},{8,12},{9,13},{10,... | collective-permute-start | bytes 2162696 | tf_op jit(solution)/shard_map/ppermute | solution.py:48
  154.4 16.5 %collective-permute-start.33 = (bf16[4,32,1408]{2,1,0:T(8,128)(2,1)S(1)}, bf16[4,32,1408]{2,1,0:T(8,128)(2,1)S(1)}, u32[]{:S(2)}, u32[]{:S(2)}) collective-permute-start(bf16[4,32,1408]{2,1,0:T(8,128)(2,1)S(1)} %get-tuple-element.367), channel_id=1, source_target_pairs={{0,2},{1,3},{2,0},{3,1},{4,6},{5,7},{6,4},{7,5},{8,10},{9,11},{10,... | collective-permute-start | bytes 1081352 | tf_op jit(solution)/shard_map/ppermute | solution.py:48
  155.0 15.9 %collective-permute-start.34 = (bf16[4,32,1408]{2,1,0:T(8,128)(2,1)S(1)}, bf16[4,32,1408]{2,1,0:T(8,128)(2,1)S(1)}, u32[]{:S(2)}, u32[]{:S(2)}) collective-permute-start(bf16[4,32,1408]{2,1,0:T(8,128)(2,1)S(1)} %get-tuple-element.368), channel_id=1, source_target_pairs={{0,4},{1,5},{2,6},{3,7},{4,0},{5,1},{6,2},{7,3},{8,12},{9,13},{10,... | collective-permute-start | bytes 1081352 | tf_op jit(solution)/shard_map/ppermute | solution.py:48
  155.9 34.5 %collective-permute-start.38 = (bf16[16,32,1408]{2,1,0:T(8,128)(2,1)S(1)}, bf16[16,32,1408]{2,1,0:T(8,128)(2,1)S(1)}, u32[]{:S(2)}, u32[]{:S(2)}) collective-permute-start(bf16[16,32,1408]{2,1,0:T(8,128)(2,1)S(1)} %bitcast.80), channel_id=1, source_target_pairs={{0,8},{1,9},{2,10},{3,11},{4,12},{5,13},{6,14},{7,15},{8,0},{9,1},... | collective-permute-start | bytes 4325384 | tf_op jit(solution)/shard_map/ppermute | solution.py:48
  168.2 27.3 %collective-permute-start.35 = (bf16[8,32,1920]{2,1,0:T(8,128)(2,1)S(1)}, bf16[8,32,1920]{2,1,0:T(8,128)(2,1)S(1)}, u32[]{:S(2)}, u32[]{:S(2)}) collective-permute-start(bf16[8,32,1920]{2,1,0:T(8,128)(2,1)S(1)} %bitcast.82), channel_id=1, source_target_pairs={{0,4},{1,5},{2,6},{3,7},{4,0},{5,1},{6,2},{7,3},{8,12},{9,13},{10,... | collective-permute-start | bytes 2949128 | tf_op jit(solution)/shard_map/ppermute | solution.py:48
  169.4 26.1 %collective-permute-start.36 = (bf16[8,32,1920]{2,1,0:T(8,128)(2,1)S(1)}, bf16[8,32,1920]{2,1,0:T(8,128)(2,1)S(1)}, u32[]{:S(2)}, u32[]{:S(2)}) collective-permute-start(bf16[8,32,1920]{2,1,0:T(8,128)(2,1)S(1)} %bitcast.81), channel_id=1, source_target_pairs={{0,2},{1,3},{2,0},{3,1},{4,6},{5,7},{6,4},{7,5},{8,10},{9,11},{10,... | collective-permute-start | bytes 2949128 | tf_op jit(solution)/shard_map/ppermute | solution.py:48
  171.2 24.3 %collective-permute-start.37 = (bf16[2,2,32,1408]{3,2,1,0:T(8,128)(2,1)S(1)}, bf16[2,2,32,1408]{3,2,1,0:T(8,128)(2,1)S(1)}, u32[]{:S(2)}, u32[]{:S(2)}) collective-permute-start(bf16[2,2,32,1408]{3,2,1,0:T(8,128)(2,1)S(1)} %get-tuple-element.390), channel_id=1, source_target_pairs={{0,8},{1,9},{2,10},{3,11},{4,12},{5,13},{6,14},{7,15},{8,0},{9,1},... | collective-permute-start | bytes 1081352 | tf_op jit(solution)/shard_map/ppermute | solution.py:48
  199.2 31.1 %collective-permute-start.42 = (bf16[8,32,1408]{2,1,0:T(8,128)(2,1)S(1)}, bf16[8,32,1408]{2,1,0:T(8,128)(2,1)S(1)}, u32[]{:S(2)}, u32[]{:S(2)}) collective-permute-start(bf16[8,32,1408]{2,1,0:T(8,128)(2,1)S(1)} %get-tuple-element.432), channel_id=1, source_target_pairs={{0,16},{1,17},{2,18},{3,19},{4,20},{5,21},{6,22},{7,23},{8,24},{9,... | collective-permute-start | bytes 2162696 | tf_op jit(solution)/shard_map/ppermute | solution.py:48
  208.2 24.8 %collective-permute-start.41 = (bf16[2,2,32,1920]{3,2,1,0:T(8,128)(2,1)S(1)}, bf16[2,2,32,1920]{3,2,1,0:T(8,128)(2,1)S(1)}, u32[]{:S(2)}, u32[]{:S(2)}) collective-permute-start(bf16[2,2,32,1920]{3,2,1,0:T(8,128)(2,1)S(1)} %get-tuple-element.431), channel_id=1, source_target_pairs={{0,8},{1,9},{2,10},{3,11},{4,12},{5,13},{6,14},{7,15},{8,0},{9,1},... | collective-permute-start | bytes 1474568 | tf_op jit(solution)/shard_map/ppermute | solution.py:48
  209.4 23.8 %collective-permute-start.44 = (bf16[8,32,896]{2,1,0:T(8,128)(2,1)S(1)}, bf16[8,32,896]{2,1,0:T(8,128)(2,1)S(1)}, u32[]{:S(2)}, u32[]{:S(2)}) collective-permute-start(bf16[8,32,896]{2,1,0:T(8,128)(2,1)S(1)} %bitcast.90), channel_id=1, source_target_pairs={{0,4},{1,5},{2,6},{3,7},{4,0},{5,1},{6,2},{7,3},{8,12},{9,13},{10,... | collective-permute-start | bytes 1376264 | tf_op jit(solution)/shard_map/ppermute | solution.py:48
  210.5 22.7 %collective-permute-start.45 = (bf16[8,32,896]{2,1,0:T(8,128)(2,1)S(1)}, bf16[8,32,896]{2,1,0:T(8,128)(2,1)S(1)}, u32[]{:S(2)}, u32[]{:S(2)}) collective-permute-start(bf16[8,32,896]{2,1,0:T(8,128)(2,1)S(1)} %bitcast.89), channel_id=1, source_target_pairs={{0,2},{1,3},{2,0},{3,1},{4,6},{5,7},{6,4},{7,5},{8,10},{9,11},{10,... | collective-permute-start | bytes 1376264 | tf_op jit(solution)/shard_map/ppermute | solution.py:48
  252.9 15.3 %collective-permute-start.56 = (bf16[1,2,32,1408]{3,2,1,0:T(8,128)(2,1)S(1)}, bf16[1,2,32,1408]{3,2,1,0:T(8,128)(2,1)S(1)}, u32[]{:S(2)}, u32[]{:S(2)}) collective-permute-start(bf16[1,2,32,1408]{3,2,1,0:T(8,128)(2,1)S(1)} %get-tuple-element.506), channel_id=1, source_target_pairs={{0,16},{1,17},{2,18},{3,19},{4,20},{5,21},{6,22},{7,23},{8,24},{9,... | collective-permute-start | bytes 540680 | tf_op jit(solution)/shard_map/ppermute | solution.py:48
  252.9 15.3 %collective-permute-start.55 = (bf16[1,2,32,896]{3,2,1,0:T(8,128)(2,1)S(1)}, bf16[1,2,32,896]{3,2,1,0:T(8,128)(2,1)S(1)}, u32[]{:S(2)}, u32[]{:S(2)}) collective-permute-start(bf16[1,2,32,896]{3,2,1,0:T(8,128)(2,1)S(1)} %get-tuple-element.502), channel_id=1, source_target_pairs={{0,16},{1,17},{2,18},{3,19},{4,20},{5,21},{6,22},{7,23},{8,24},{9,... | collective-permute-start | bytes 344072 | tf_op jit(solution)/shard_map/ppermute | solution.py:48
  (50 other events, 470.9 us)

commit v5 on v4

--- a/solution.py
+++ b/solution.py
@@ -308,7 +308,7 @@
     return masks
 
 
-SAID_FLOPS = {"shuffle": 10**10, "attn_fwd": 10**10, "down_back": 10**10, "residual": 10**10, "gated": 10**10, "fold_first": 5 * 10**9, "fold_next": 10**10}
+SAID_FLOPS = {"shuffle": 10**10, "attn_fwd": 10**10, "down_back": 10**10, "residual": 10**10, "gated": 10**10, "fold_first": 5 * 10**9, "fold_next": 10**9, "fold_far": 5 * 10**9}
 FOLD_FLOPS = 10**9
 FOLD_MEGABYTES = 16
 
@@ -493,17 +493,21 @@
 
     def body(core_ref, mine_ref, came_ref, *refs):
         first = core_ref[0] == 0
-        for (at, half), ref in zip(places[:n], refs):
-            own, other = mine_ref[:, at : at + half], came_ref[:, at : at + half]
-            ref[:, :half] = jnp.where(first, own, other)
-            ref[:, half:] = jnp.where(first, other, own)
-        at = places[n][0]
+        for segments, ref in zip(places[:n], refs):
+            half, done = sum(size for _, size in segments), 0
+            for at, size in segments:
+                own, other = mine_ref[:, at : at + size], came_ref[:, at : at + size]
+                ref[:, done : done + size] = jnp.where(first, own, other)
+                ref[:, half + done : half + done + size] = jnp.where(first, other, own)
+                done += size
+        at = places[n][0][0]
         own = mine_ref[:, at : at + LANES].T
         other = came_ref[:, at : at + LANES].T
         refs[n][...] = own[0:1] + other[0:1]
         refs[n + 1][...] = own[1:2]
 
-    out = [jax.ShapeDtypeStruct((rows, 2 * half), F32) for _, half in places[:n]]
+    halves = [sum(size for _, size in segments) for segments in places[:n]]
+    out = [jax.ShapeDtypeStruct((rows, 2 * half), F32) for half in halves]
     out += [jax.ShapeDtypeStruct((1, rows), F32)] * 2
     return pl.pallas_call(
         body,
@@ -665,7 +669,7 @@
     )(grad_out, *weights)
 
 
-def gated(weights, normed, d_act):
+def gated(weights, normed, d_act, first):
     n_tok, width = normed.shape
     cols = d_act.shape[1]
     n_in = len(weights)
@@ -673,26 +677,27 @@
     size = n_tok // steps
 
     def body(normed_ref, d_act_ref, *refs):
-        act_ref, d_gate_ref, d_up_ref = refs[n_in:]
+        act_ref, rest_ref, d_gate_ref, d_up_ref = refs[n_in:]
         x = normed_ref[...]
         gate = dot_nn(x, stacked(refs[:n_in], 0, cols))
         up = dot_nn(x, stacked(refs[:n_in], cols, cols))
         sig = 1.0 / (1.0 + jnp.exp(-gate))
         silu = gate * sig
-        act_ref[...] = (silu * up).astype(BF16)
+        act = (silu * up).astype(BF16)
+        act_ref[...] = act[:, :first]
+        rest_ref[...] = act[:, first:]
         d = d_act_ref[...].astype(F32)
         d_gate_ref[...] = (d * up * sig * (1.0 + gate * (1.0 - sig))).astype(BF16)
         d_up_ref[...] = (d * silu).astype(BF16)
 
-    out = pltpu.VMEM((n_tok, cols), BF16)
-    at = rows_spec(size, cols)
+    parts = (first, cols - first, cols, cols)
     return pl.pallas_call(
         body,
         name="gated",
         grid=(steps,),
-        out_shape=(out, out, out),
-        in_specs=[rows_spec(size, width), at] + whole_specs(weights),
-        out_specs=(at, at, at),
+        out_shape=tuple(pltpu.VMEM((n_tok, c), BF16) for c in parts),
+        in_specs=[rows_spec(size, width), rows_spec(size, cols)] + whole_specs(weights),
+        out_specs=tuple(rows_spec(size, c) for c in parts),
         compiler_params=params(30),
         cost_estimate=cost("gated"),
     )(*near(normed, d_act), *weights)
@@ -762,7 +767,7 @@
 
 
 def sum_nt(weights, lefts, starts, pieces, name, places=None, rows=0):
-    n_tok, cols = lefts[0].shape
+    n_tok = lefts[0].shape[0]
     width = sum(w.shape[0] for w in weights)
     n, n_in = len(lefts), len(weights)
     steps = 4
@@ -772,13 +777,14 @@
         left_refs, w_refs, out_refs = refs[:n], refs[n : n + n_in], refs[n + n_in :]
 
         if places is not None:
-            values = [dot_nt(left_refs[0][...], in_order(w_refs, places, rows))]
+            left = jnp.concatenate([ref[...] for ref in left_refs], axis=1)
+            values = [dot_nt(left, in_order(w_refs, places, rows))]
         else:
             values = []
             for w in w_refs:
                 value = None
                 for left, start in zip(left_refs, starts):
-                    term = dot_nt(left[...], w[:, start : start + cols])
+                    term = dot_nt(left[...], w[:, start : start + left.shape[1]])
                     value = term if value is None else value + term
                 values.append(value)
 
@@ -795,7 +801,7 @@
         name=name,
         grid=(steps,),
         out_shape=(jax.ShapeDtypeStruct((n_tok // pieces, width), BF16),) * pieces,
-        in_specs=[rows_spec(size, cols)] * n + whole_specs(weights),
+        in_specs=[rows_spec(size, x.shape[1]) for x in lefts] + whole_specs(weights),
         out_specs=tuple(piece_specs(pieces, steps, size, width)),
         compiler_params=params(20),
         cost_estimate=cost(name),
@@ -1078,7 +1084,8 @@
     came_o = order(*came_o)
     hres, normed_two = residual(tok, part_o, came_o, gains)
     normed_two = order(normed_two)
-    act, d_gate, d_up = order(*gated(w_gu, normed_two, d_act))
+    first = stride // 2 + -(stride // 2) % LANES
+    act, act_rest, d_gate, d_up = order(*gated(w_gu, normed_two, d_act, first))
 
     def grad(lefts, rights, gain=None, name="weight_grad", places=None):
         return blocks(order(*weight_grad(lefts, rights, gain, name, places, rows)))
@@ -1105,60 +1112,62 @@
     def along_z(stream, name="fold_plane"):
         return ReduceZ(lay, *order(*fold_plane(stream.pairs(order), wanted, name)))
 
-    r_g = ReducePlane(lay, grad(near(normed_two), [d_gate], name="grad_gate"))
+    r_g = ReducePlane(
+        lay, grad([*near(normed_two), grad_out], [d_gate, act_rest], name="grad_gate")
+    )
     d_up = order(d_up)
     part_n2 = order(*sum_nt(w_gu, [d_gate, d_up], [0, stride], 2, "d_norm2"))
     came_n2 = swap_all(part_n2)
     act = order(act)
     zr_d = ReduceZ(lay, *down_grad())
+    outs_u = grad(near(normed_two), [order(d_up)], name="grad_up")
     r_g.second(order, "fold_first")
     came_n2 = order(*came_n2)
-    d_h, d_o, d_y, gg_mlp = norm_back(w_0, part_n2, came_n2, hres, grad_out, gains, dims)
+    r_u = ReducePlane(lay, order(*outs_u))
+    d_h, d_o, d_y, gg_mlp = norm_back(w_0, part_n2, came_n2, hres, order(grad_out), gains, dims)
     d_y = order(d_y)
-    outs_u = grad(near(normed_two, d_o), [d_up, y], name="grad_up")
-    r_u = ReducePlane(lay, order(*outs_u))
+    zr_d.second(order)
+    d_qkv = order(attn_bwd(seq, qkv, y, order(d_y), dinv, dims))
+    last_d = zr_d.last(order)
+    r_u.second(order)
+    wait_for(order, r_g)
+    outs_0 = grad([normed_one, *near(d_o)], [order(d_qkv), y], (w_0, gains, gg_mlp), name="grad_attn")
+    r_0 = ReducePlane(lay, order(*outs_0))
+    zr_u = along_z(r_u, "fold_far")
     zr_g = along_z(r_g, "fold_next")
-    d_qkv = order(attn_bwd(seq, qkv, y, order(d_y), dinv, dims))
-    zr_d.second(order)
-    outs_0 = grad([normed_one], [order(d_qkv)], (w_0, gains, gg_mlp), name="grad_attn")
-    wait_for(order, zr_g)
-    r_u.second(order)
     part_n1 = order(*sum_nt(w_0, [order(d_qkv)], [0], 2, "norm_one_part"))
-    part_out = order(*sum_nt(w_d, [order(act)], [0], 2, "down", places_z, rows))
-    zr_u = along_z(r_u)
-    r_0 = ReducePlane(lay, order(*outs_0))
-    last_d = order(*fold_four(*zr_d.last(order)))
+    part_out = order(*sum_nt(w_d, [act, order(act_rest)], [0, first], 2, "down", places_z, rows))
+    r_0.second(order)
     zr_u.second(order)
-    r_0.second(order)
-    r_d = ReducePlane(lay, order(*last_d))
+    zr_g.second(order)
     zr_0 = along_z(r_0)
-    r_d.second(order)
-    zr_0.second(order)
-    zr_g.second(order)
-    end_u = zr_u.last(order)
-    came_rows = swap_all(order(part_n1[1], part_out[1]))
-    end_d = [a for pair in r_d.pairs(order) for a in pair]
-    came_rows = order(*came_rows)
+    came_rows = order(*swap_all(order(part_n1[1], part_out[1])))
     grad_tokens, layer_out = finish(
         part_n1[0], came_rows[0], tok, d_h, gains, hres, part_out[0], came_rows[1], placing
     )
     grad_tokens = order(grad_tokens)
+    r_d = ReducePlane(lay, order(*fold_four(*order(*last_d))))
+    zr_0.second(order)
+    r_d.second(order)
+    end_u = zr_u.last(order)
+    end_g = zr_g.last(order)
+    end_d = [a for pair in r_d.pairs(order) for a in pair]
     end_0 = zr_0.last(order)
-    end_g = zr_g.last(order)
     mine, give = add_up(core.reshape(1), [end_0, end_d, end_g, end_u])
     came = lay.swap(give, 1)
-    at = 2 * nq + nv
+    at = 2 * nq + 2 * nv
     at_d = at + LANES
-    at_gu = at_d + stride
+    at_g = at_d + first
+    at_u = at_g + 2 * stride - first
     places = [
-        (0, nq),
-        (nq, nq),
-        (2 * nq, nv),
-        (at_gu + 2 * stride, nv),
-        (at_gu, nf),
-        (at_gu + stride, nf),
-        (at_d, nf),
-        (at, LANES),
+        [(0, nq)],
+        [(nq, nq)],
+        [(2 * nq, nv)],
+        [(2 * nq + nv, nv)],
+        [(at_g, nf)],
+        [(at_u, nf)],
+        [(at_d, first), (at_g + stride, nf - first)],
+        [(at, LANES)],
     ]
     *grads, g_one, g_two = conclude(core.reshape(1), mine, came, places)
     grads[3], grads[6] = grads[3].T, grads[6].T

time: 272 us -> 266 us (0.978)
  waiting for transfers between devices: 97.2 us -> 91.1 us
  starting transfers between devices: 56.3 us -> 52.9 us
  Pallas kernels: 106 us -> 109 us
    ppermute x58, waiting for transfers between devices: 97.2 us -> 91.1 us  [swap(): return lax.ppermute(value, AXES, [(i, i ^ bit) for i in range(self.count)])]
    ppermute x58, starting transfers between devices: 56.3 us -> 52.9 us  [swap(): return lax.ppermute(value, AXES, [(i, i ^ bit) for i in range(self.count)])]
  transfers between devices with their start and end apart: 58 -> 58, of which waited for: 28 -> 30; matrix products, arithmetic and copies ran while one was open for 3% -> 3% of each run, Pallas kernels for 31% -> 32%
where the time goes in v5:
time: 266 us
  Pallas kernels  109 us (41%)
  waiting for transfers between devices  91.1 us (34%)
  starting transfers between devices  52.9 us (20%)
  local copies, waits for them, and re-layouts  6.38 us (2%)
  other arithmetic  5.49 us (2%)
    ppermute x58, waiting for transfers between devices, swap(): return lax.ppermute(value, AXES, [(i, i ^ bit) for i in range(self.count)])  91.1 us
    ppermute x58, starting transfers between devices, swap(): return lax.ppermute(value, AXES, [(i, i ^ bit) for i in range(self.count)])  52.9 us
    pallas_call x4, Pallas kernels, weight_grad(): pl.pallas_call(body, name=name, grid=(pieces,), out_shape=(jax.ShapeDtype...  20.9 us
    pallas_call x1, Pallas kernels, attn_bwd(): pl.pallas_call(body, name='attn_bwd', out_shape=pltpu.VMEM(qkv.shape, BF1...  15.2 us
    pallas_call x3, Pallas kernels, sum_nt(): pl.pallas_call(body, name=name, grid=(steps,), out_shape=(jax.ShapeDtypeS...  14.6 us
    pallas_call x1, Pallas kernels, attn_fwd(): pl.pallas_call(body, name='attn_fwd', out_shape=(pltpu.HBM((n_tok, width)...  14.4 us
    pallas_call x1, Pallas kernels, gated(): pl.pallas_call(body, name='gated', grid=(steps,), out_shape=tuple((pltpu....  8.7 us
    pallas_call x1, Pallas kernels, shuffle(): pl.pallas_call(body, name='shuffle', grid=(steps,), out_shape=(*[pltpu.HB...  7.55 us
  transfers between devices with their start and end apart: 58, of which 30 were waited for; matrix products, arithmetic and copies ran while one was open for 3% of the time, Pallas kernels for 32%

profile of v5, /device:TPU:0, one launch (start us, length us, event | category | flops | bytes accessed | tf_op | source)
XLA Modules:
  0.0 266.0 jit_solution(14679288400880212869)
XLA Ops:
  0.7 2.6 prepare.1
  6.3 4.0 %collective-permute-start.6 = (bf16[2,32,1408]{2,1,0:T(8,128)(2,1)S(1)}, bf16[2,32,1408]{2,1,0:T(8,128)(2,1)S(1)}, u32[]{:S(2)}, u32[]{:S(2)}) collective-permute-start(bf16[2,32,1408]{2,1,0:T(8,128)(2,1)S(1)} %maximum_select_fusion.2), channel_id=1, source_target_pairs={{0,16},{1,17},{2,18},{3,19},{4,20},{5,21},{6,22},{7,23},{8,24},{9,... | collective-permute-start | bytes 540680 | tf_op jit(solution)/shard_map/ppermute | solution.py:48
  25.7 7.4 %collective-permute-done.10 = bf16[2,32,1408]{2,1,0:T(8,128)(2,1)S(1)} collective-permute-done((bf16[2,32,1408]{2,1,0:T(8,128)(2,1)S(1)}, bf16[2,32,1408]{2,1,0:T(8,128)(2,1)S(1)}, u32[]{:S(2)}, u32[]{:S(2)}) %collective-permute-start.10) | collective-permute-done | bytes 180256 | tf_op jit(solution)/shard_map/ppermute | solution.py:48
  33.1 2.5 collective-permute-start.16
  37.3 7.1 %collective-permute-done.11 = bf16[4,32,1408]{2,1,0:T(8,128)(2,1)S(1)} collective-permute-done((bf16[4,32,1408]{2,1,0:T(8,128)(2,1)S(1)}, bf16[4,32,1408]{2,1,0:T(8,128)(2,1)S(1)}, u32[]{:S(2)}, u32[]{:S(2)}) %collective-permute-start.11) | collective-permute-done | bytes 360480 | tf_op jit(solution)/shard_map/ppermute | solution.py:48
  48.7 8.6 %collective-permute-done.17 = bf16[2,32,2816]{2,1,0:T(8,128)(2,1)S(1)} collective-permute-done((bf16[2,32,2816]{2,1,0:T(8,128)(2,1)S(1)}, bf16[2,32,2816]{2,1,0:T(8,128)(2,1)S(1)}, u32[]{:S(2)}, u32[]{:S(2)}) %collective-permute-start.17) | collective-permute-done | bytes 360480 | tf_op jit(solution)/shard_map/ppermute | solution.py:48
  58.1 7.6 %shuffle.1 = (bf16[1024,1024]{1,0:T(8,128)(2,1)}, bf16[1024,1024]{1,0:T(8,128)(2,1)}, bf16[1024,1024]{1,0:T(8,128)(2,1)}) custom-call(s32[1]{0:T(128)} %bitcast.5.index_ref, s32[1,1024]{1,0:T(1,128)S(1)} %broadcast_in_dim_reshape.3.masks_ref, bf16[1024,1024]{1,0:T(8,128)(2,1)S(1)} %get-tuple-element.554.refs_0_, ...), custom_call_target="tpu_custom_call" | custom-call | flops 10000000000 | bytes 1 | tf_op jit(solution)/shard_map/shuffle/pallas_call | solution.py:422
  66.0 10.7 %collective-permute-done.20 = bf16[8,32,1408]{2,1,0:T(8,128)(2,1)S(1)} collective-permute-done((bf16[8,32,1408]{2,1,0:T(8,128)(2,1)S(1)}, bf16[8,32,1408]{2,1,0:T(8,128)(2,1)S(1)}, u32[]{:S(2)}, u32[]{:S(2)}) %collective-permute-start.20) | collective-permute-done | bytes 720928 | tf_op jit(solution)/shard_map/ppermute | solution.py:48
  83.9 14.4 %attn_fwd.1 = (bf16[1024,1024]{1,0:T(8,128)(2,1)}, bf16[1024,768]{1,0:T(8,128)(2,1)S(1)}, bf16[1024,512]{1,0:T(8,128)(2,1)S(1)}, f32[1024,512]{1,0:T(8,128)S(1)}...) custom-call(s32[2,4]{1,0:T(2,128)S(1)} %pad_add_fusion.seq_ref, ...), custom_call_target="tpu_custom_call" | custom-call | flops 10000000000 | bytes 1 | tf_op jit(solution)/shard_map/attn_fwd/pallas_call | solution.py:587
  99.4 11.1 %collective-permute-done.28 = bf16[8,32,1408]{2,1,0:T(8,128)(2,1)S(1)} collective-permute-done((bf16[8,32,1408]{2,1,0:T(8,128)(2,1)S(1)}, bf16[8,32,1408]{2,1,0:T(8,128)(2,1)S(1)}, u32[]{:S(2)}, u32[]{:S(2)}) %collective-permute-start.28) | collective-permute-done | bytes 720928 | tf_op jit(solution)/shard_map/ppermute | solution.py:48
  111.0 4.0 %down_back.1.d_act_ref = bf16[1024,1408]{1,0:T(8,128)(2,1)S(1)} custom-call(bf16[1024,1024]{1,0:T(8,128)(2,1)S(1)} %copy-done, bf16[256,1408]{1,0:T(8,128)(2,1)S(1)} %bitcast.69, bf16[256,1408]{1,0:T(8,128)(2,1)S(1)} %bitcast.73, bf16[256,1408]{1,0:T(8,128)(2,1)S(1)} %bitcast.71, bf16[256,1408]{1,0:T(8,128)(2,1)S(1)} %bitcast.75), custom_call_target="tpu_custom_call" | custom-call | flops 10000000000 | bytes 1 | tf_op jit(solution)/shard_map/down_back/pallas_call | solution.py:660
  116.6 2.6 residual.1
  120.7 8.7 %gated.1 = (bf16[1024,768]{1,0:T(8,128)(2,1)S(1)}, bf16[1024,640]{1,0:T(8,128)(2,1)S(1)}, bf16[1024,1408]{1,0:T(8,128)(2,1)S(1)}, bf16[1024,1408]{1,0:T(8,128)(2,1)S(1)}) custom-call(bf16[1024,1024]{1,0:T(8,128)(2,1)S(1)} %get-tuple-element.332.normed_ref.refs_0_, bf16[1024,1408]{1,0:T(8,128)(2,1)S(1)} %copy-done.25, bf16[256,2816]{1,0:T(8,128)(2,1)S(1)} %bitcast.61, ...), custom_call_target="tpu_custom_call" | custom-call | flops 10000000000 | bytes 1 | tf_op jit(solution)/shard_map/gated/pallas_call | solution.py:694
  129.4 8.1 %grad_gate.1 = (bf16[256,2048]{1,0:T(8,128)(2,1)S(1)}, bf16[256,2048]{1,0:T(8,128)(2,1)}, bf16[256,2048]{1,0:T(8,128)(2,1)S(1)}, bf16[256,2048]{1,0:T(8,128)(2,1)}) custom-call(bf16[1024,1024]{1,0:T(8,128)(2,1)S(1)} %get-tuple-element.332.normed_ref.refs_0_, bf16[1024,1024]{1,0:T(8,128)(2,1)S(1)} %copy-done, ...), custom_call_target="tpu_custom_call" | custom-call | flops 1 | bytes 1 | tf_op jit(solution)/shard_map/grad_gate/pallas_call | solution.py:755
  140.5 7.6 %d_norm2.1 = (bf16[512,1024]{1,0:T(8,128)(2,1)S(1)}, bf16[512,1024]{1,0:T(8,128)(2,1)S(1)}) custom-call(bf16[1024,1408]{1,0:T(8,128)(2,1)S(1)} %get-tuple-element.341.refs_2_.refs_0_, bf16[1024,1408]{1,0:T(8,128)(2,1)S(1)} %get-tuple-element.357.refs_1_, bf16[256,2816]{1,0:T(8,128)(2,1)S(1)} %bitcast.62, bf16[256,2816]{1,0:T(8,128)(2,1)S(1)} %bitcast.66, ...), custom_call_target="tpu_custom_call" | custom-call | flops 1 | bytes 1 | tf_op jit(solution)/shard_map/d_norm2/pallas_call | solution.py:799
  148.7 3.0 %grad_down.1 = (bf16[512,768]{1,0:T(8,128)(2,1)S(1)}, bf16[512,768]{1,0:T(8,128)(2,1)S(1)}) custom-call(bf16[1024,1024]{1,0:T(8,128)(2,1)S(1)} %copy-done, bf16[1024,768]{1,0:T(8,128)(2,1)S(1)} %get-tuple-element.353.refs_1_.refs_0_), custom_call_target="tpu_custom_call" | custom-call | flops 1 | bytes 1 | tf_op jit(solution)/shard_map/grad_down/pallas_call | solution.py:755
  152.1 4.7 %grad_up.1 = (bf16[256,1408]{1,0:T(8,128)(2,1)S(1)}, bf16[256,1408]{1,0:T(8,128)(2,1)S(1)}, bf16[256,1408]{1,0:T(8,128)(2,1)S(1)}, bf16[256,1408]{1,0:T(8,128)(2,1)S(1)}) custom-call(bf16[1024,1024]{1,0:T(8,128)(2,1)S(1)} %get-tuple-element.332.normed_ref.refs_0_, bf16[1024,1408]{1,0:T(8,128)(2,1)S(1)} %get-tuple-element.357.refs_1_), custom_call_target="tpu_custom_call" | custom-call | flops 1 | bytes 1 | tf_op jit(solution)/shard_map/grad_up/pallas_call | solution.py:755
  156.8 7.1 %collective-permute-done.32.refs_3_ = bf16[8,32,2048]{2,1,0:T(8,128)(2,1)S(1)} collective-permute-done((bf16[8,32,2048]{2,1,0:T(8,128)(2,1)}, bf16[8,32,2048]{2,1,0:T(8,128)(2,1)S(1)}, u32[]{:S(2)}, u32[]{:S(2)}) %collective-permute-start.32) | collective-permute-done | bytes 1048608 | tf_op jit(solution)/shard_map/ppermute | solution.py:48
  165.2 2.1 fold_first.1
  168.9 5.8 %norm_back.1 = (f32[512,1024]{1,0:T(8,128)S(1)}, bf16[1024,1024]{1,0:T(8,128)(2,1)S(1)}, bf16[1024,512]{1,0:T(8,128)(2,1)S(1)}, f32[8,1024]{1,0:T(8,128)S(1)}) custom-call(f32[1024,1024]{1,0:T(8,128)S(1)} %get-tuple-element.330.hres_ref.h_ref, bf16[1024,1024]{1,0:T(8,128)(2,1)S(1)} %copy-done, f32[8,1024]{1,0:T(8,128)S(1)} %get-tuple-element.329.refs_8_.gain_ref.refs_4_, ...), custom_call_target="tpu_custom_call" | custom-call | flops 1 | bytes 1 | tf_op jit(solution)/shard_map/norm_back/pallas_call | solution.py:853
  178.7 15.2 %attn_bwd.1.refs_2_.refs_0_ = bf16[1024,768]{1,0:T(8,128)(2,1)S(1)} custom-call(s32[2,4]{1,0:T(2,128)S(1)} %pad_add_fusion.seq_ref, bf16[1024,768]{1,0:T(8,128)(2,1)S(1)} %copy-done.8, bf16[1024,512]{1,0:T(8,128)(2,1)S(1)} %get-tuple-element.305.y_ref.refs_3_, bf16[1024,512]{1,0:T(8,128)(2,1)S(1)} %get-tuple-element.388.dy_ref, f32[1024,512]{1,0:T(8,128)S(1)} %copy-done.6), custom_call_target="tpu_custom_call" | custom-call | flops 1 | bytes 1 | tf_op jit(solution)/shard_map/attn_bwd/pallas_call | solution.py:929
  197.1 5.0 %grad_attn.1 = (bf16[256,1408]{1,0:T(8,128)(2,1)S(1)}, bf16[256,1408]{1,0:T(8,128)(2,1)S(1)}, bf16[256,1408]{1,0:T(8,128)(2,1)S(1)}, bf16[256,1408]{1,0:T(8,128)(2,1)S(1)}) custom-call(bf16[1024,1024]{1,0:T(8,128)(2,1)S(1)} %copy-done.4, bf16[1024,1024]{1,0:T(8,128)(2,1)S(1)} %get-tuple-element.410.refs_1_, bf16[1024,768]{1,0:T(8,128)(2,1)S(1)} %attn_bwd.1.refs_2_.refs_0_, ...), custom_call_target="tpu_custom_call" | custom-call | flops 1 | bytes 1 | tf_op jit(solution)/shard_map/grad_attn/pallas_call | solution.py:755
  207.3 2.0 collective-permute-start.46
  209.4 2.7 %norm_one_part.1 = (bf16[512,1024]{1,0:T(8,128)(2,1)S(1)}, bf16[512,1024]{1,0:T(8,128)(2,1)S(1)}) custom-call(bf16[1024,768]{1,0:T(8,128)(2,1)S(1)} %attn_bwd.1.refs_2_.refs_0_, bf16[256,1408]{1,0:T(8,128)(2,1)S(1)} %bitcast.52, bf16[256,1408]{1,0:T(8,128)(2,1)S(1)} %bitcast.56, bf16[256,1408]{1,0:T(8,128)(2,1)S(1)} %bitcast.48, bf16[256,1408]{1,0:T(8,128)(2,1)S(1)} %bitcast.60), custom_call_target="tpu_custom_call" | custom-call | flops 1 | bytes 1 | tf_op jit(solution)/shard_map/norm_one_part/pallas_call | solution.py:799
  212.1 4.3 %down.1 = (bf16[512,1024]{1,0:T(8,128)(2,1)S(1)}, bf16[512,1024]{1,0:T(8,128)(2,1)S(1)}) custom-call(bf16[1024,768]{1,0:T(8,128)(2,1)S(1)} %get-tuple-element.353.refs_1_.refs_0_, bf16[1024,640]{1,0:T(8,128)(2,1)S(1)} %get-tuple-element.439.refs_3_.refs_1_, bf16[256,1408]{1,0:T(8,128)(2,1)S(1)} %bitcast.70, bf16[256,1408]{1,0:T(8,128)(2,1)S(1)} %bitcast.74, ...), custom_call_target="tpu_custom_call" | custom-call | flops 1 | bytes 1 | tf_op jit(solution)/shard_map/down/pallas_call | solution.py:799
  216.4 4.6 %collective-permute-done.41.refs_1_ = bf16[8,32,1408]{2,1,0:T(8,128)(2,1)S(1)} collective-permute-done((bf16[8,32,1408]{2,1,0:T(8,128)(2,1)S(1)}, bf16[8,32,1408]{2,1,0:T(8,128)(2,1)S(1)}, u32[]{:S(2)}, u32[]{:S(2)}) %collective-permute-start.41) | collective-permute-done | bytes 720928 | tf_op jit(solution)/shard_map/ppermute | solution.py:48
  223.9 2.6 collective-permute-done.46.refs_1_
  227.0 3.9 %collective-permute-done.43.refs_1_ = bf16[4,32,1408]{2,1,0:T(8,128)(2,1)S(1)} collective-permute-done((bf16[4,32,1408]{2,1,0:T(8,128)(2,1)S(1)}, bf16[4,32,1408]{2,1,0:T(8,128)(2,1)S(1)}, u32[]{:S(2)}, u32[]{:S(2)}) %collective-permute-start.43) | collective-permute-done | bytes 360480 | tf_op jit(solution)/shard_map/ppermute | solution.py:48
  232.0 2.7 %collective-permute-start.56 = (bf16[1,2,32,1408]{3,2,1,0:T(8,128)(2,1)S(1)}, bf16[1,2,32,1408]{3,2,1,0:T(8,128)(2,1)S(1)}, u32[]{:S(2)}, u32[]{:S(2)}) collective-permute-start(bf16[1,2,32,1408]{3,2,1,0:T(8,128)(2,1)S(1)} %get-tuple-element.506), channel_id=1, source_target_pairs={{0,16},{1,17},{2,18},{3,19},{4,20},{5,21},{6,22},{7,23},{8,24},{9,... | collective-permute-start | bytes 540680 | tf_op jit(solution)/shard_map/ppermute | solution.py:48
  235.6 5.6 %finish.1 = (bf16[512,1024]{1,0:T(8,128)(2,1)}, bf16[512,1024]{1,0:T(8,128)(2,1)}) custom-call(bf16[512,1024]{1,0:T(8,128)(2,1)S(1)} %get-tuple-element.437.part_ref, bf16[512,1024]{1,0:T(8,128)(2,1)S(1)} %collective-permute-done.47.came_ref, bf16[1024,1024]{1,0:T(8,128)(2,1)S(1)} %copy-done.2, f32[512,1024]{1,0:T(8,128)S(1)} %get-tuple-element.475.dh_ref, ...), custom_call_target="tpu_custom_call" | custom-call | flops 1 | bytes 1 | tf_op jit(solution)/shard_map/finish/pallas_call | solution.py:975
  241.3 8.3 %collective-permute-done.49.refs_1_ = bf16[2,2,32,1408]{3,2,1,0:T(8,128)(2,1)S(1)} collective-permute-done((bf16[2,2,32,1408]{3,2,1,0:T(8,128)(2,1)S(1)}, bf16[2,2,32,1408]{3,2,1,0:T(8,128)(2,1)S(1)}, u32[]{:S(2)}, u32[]{:S(2)}) %collective-permute-start.49) | collective-permute-done | bytes 360480 | tf_op jit(solution)/shard_map/ppermute | solution.py:48
  262.5 2.2 collective-permute-done.57.came_ref
  (207 shorter events, 75.8 us)
Async XLA Ops:
  18.2 19.0 %collective-permute-start.13 = (bf16[2,32,2816]{2,1,0:T(8,128)(2,1)S(1)}, bf16[2,32,2816]{2,1,0:T(8,128)(2,1)S(1)}, u32[]{:S(2)}, u32[]{:S(2)}) collective-permute-start(bf16[2,32,2816]{2,1,0:T(8,128)(2,1)S(1)} %maximum_select_fusion), channel_id=1, source_target_pairs={{0,16},{1,17},{2,18},{3,19},{4,20},{5,21},{6,22},{7,23},{8,24},{9,... | collective-permute-start | bytes 1081352 | tf_op jit(solution)/shard_map/ppermute | solution.py:48
  20.0 15.7 %collective-permute-start.7 = (bf16[2,32,1408]{2,1,0:T(8,128)(2,1)S(1)}, bf16[2,32,1408]{2,1,0:T(8,128)(2,1)S(1)}, u32[]{:S(2)}, u32[]{:S(2)}) collective-permute-start(bf16[2,32,1408]{2,1,0:T(8,128)(2,1)S(1)} %pad_maximum_fusion.6), channel_id=1, source_target_pairs={{0,4},{1,5},{2,6},{3,7},{4,0},{5,1},{6,2},{7,3},{8,12},{9,13},{10,... | collective-permute-start | bytes 540680 | tf_op jit(solution)/shard_map/ppermute | solution.py:48
  33.1 15.5 %collective-permute-start.16 = (bf16[2,32,2816]{2,1,0:T(8,128)(2,1)S(1)}, bf16[2,32,2816]{2,1,0:T(8,128)(2,1)S(1)}, u32[]{:S(2)}, u32[]{:S(2)}) collective-permute-start(bf16[2,32,2816]{2,1,0:T(8,128)(2,1)S(1)} %maximum_select_fusion), channel_id=1, source_target_pairs={{0,8},{1,9},{2,10},{3,11},{4,12},{5,13},{6,14},{7,15},{8,0},{9,1},... | collective-permute-start | bytes 1081352 | tf_op jit(solution)/shard_map/ppermute | solution.py:48
  37.2 20.1 %collective-permute-start.17 = (bf16[2,32,2816]{2,1,0:T(8,128)(2,1)S(1)}, bf16[2,32,2816]{2,1,0:T(8,128)(2,1)S(1)}, u32[]{:S(2)}, u32[]{:S(2)}) collective-permute-start(bf16[2,32,2816]{2,1,0:T(8,128)(2,1)S(1)} %collective-permute-done.13), channel_id=1, source_target_pairs={{0,8},{1,9},{2,10},{3,11},{4,12},{5,13},{6,14},{7,15},{8,0},{9,1},... | collective-permute-start | bytes 1081352 | tf_op jit(solution)/shard_map/ppermute | solution.py:48
  44.8 31.9 %collective-permute-start.20 = (bf16[8,32,1408]{2,1,0:T(8,128)(2,1)S(1)}, bf16[8,32,1408]{2,1,0:T(8,128)(2,1)S(1)}, u32[]{:S(2)}, u32[]{:S(2)}) collective-permute-start(bf16[8,32,1408]{2,1,0:T(8,128)(2,1)S(1)} %constant_dynamic-update-slice_fusion), channel_id=1, source_target_pairs={{0,16},{1,17},{2,18},{3,19},{4,20},{5,21},{6,22},{7,23},{8,24},{9,... | collective-permute-start | bytes 2162696 | tf_op jit(solution)/shard_map/ppermute | solution.py:48
  46.5 19.2 %collective-permute-start.14 = (bf16[8,32,1408]{2,1,0:T(8,128)(2,1)S(1)}, bf16[8,32,1408]{2,1,0:T(8,128)(2,1)S(1)}, u32[]{:S(2)}, u32[]{:S(2)}) collective-permute-start(bf16[8,32,1408]{2,1,0:T(8,128)(2,1)S(1)} %constant_dynamic-update-slice_fusion.6), channel_id=1, source_target_pairs={{0,4},{1,5},{2,6},{3,7},{4,0},{5,1},{6,2},{7,3},{8,12},{9,13},{10,... | collective-permute-start | bytes 2162696 | tf_op jit(solution)/shard_map/ppermute | solution.py:48
  46.9 19.1 %collective-permute-start.15 = (bf16[8,32,1408]{2,1,0:T(8,128)(2,1)S(1)}, bf16[8,32,1408]{2,1,0:T(8,128)(2,1)S(1)}, u32[]{:S(2)}, u32[]{:S(2)}) collective-permute-start(bf16[8,32,1408]{2,1,0:T(8,128)(2,1)S(1)} %constant_dynamic-update-slice_fusion.11), channel_id=1, source_target_pairs={{0,2},{1,3},{2,0},{3,1},{4,6},{5,7},{6,4},{7,5},{8,10},{9,11},{10,... | collective-permute-start | bytes 2162696 | tf_op jit(solution)/shard_map/ppermute | solution.py:48
  57.6 20.6 %collective-permute-start.19 = (bf16[4,32,2816]{2,1,0:T(8,128)(2,1)S(1)}, bf16[4,32,2816]{2,1,0:T(8,128)(2,1)S(1)}, u32[]{:S(2)}, u32[]{:S(2)}) collective-permute-start(bf16[4,32,2816]{2,1,0:T(8,128)(2,1)S(1)} %pad_maximum_fusion.3), channel_id=1, source_target_pairs={{0,4},{1,5},{2,6},{3,7},{4,0},{5,1},{6,2},{7,3},{8,12},{9,13},{10,... | collective-permute-start | bytes 2162696 | tf_op jit(solution)/shard_map/ppermute | solution.py:48
  58.1 20.5 %collective-permute-start.18 = (bf16[4,32,2816]{2,1,0:T(8,128)(2,1)S(1)}, bf16[4,32,2816]{2,1,0:T(8,128)(2,1)S(1)}, u32[]{:S(2)}, u32[]{:S(2)}) collective-permute-start(bf16[4,32,2816]{2,1,0:T(8,128)(2,1)S(1)} %pad_maximum_fusion.2), channel_id=1, source_target_pairs={{0,2},{1,3},{2,0},{3,1},{4,6},{5,7},{6,4},{7,5},{8,10},{9,11},{10,... | collective-permute-start | bytes 2162696 | tf_op jit(solution)/shard_map/ppermute | solution.py:48
  78.7 31.8 %collective-permute-start.25 = (bf16[8,32,2816]{2,1,0:T(8,128)(2,1)S(1)}, bf16[8,32,2816]{2,1,0:T(8,128)(2,1)S(1)}, u32[]{:S(2)}, u32[]{:S(2)}) collective-permute-start(bf16[8,32,2816]{2,1,0:T(8,128)(2,1)S(1)} %constant_dynamic-update-slice_fusion.16), channel_id=1, source_target_pairs={{0,4},{1,5},{2,6},{3,7},{4,0},{5,1},{6,2},{7,3},{8,12},{9,13},{10,... | collective-permute-start | bytes 4325384 | tf_op jit(solution)/shard_map/ppermute | solution.py:48
  80.2 19.1 %collective-permute-start.27 = (bf16[8,32,1408]{2,1,0:T(8,128)(2,1)S(1)}, bf16[8,32,1408]{2,1,0:T(8,128)(2,1)S(1)}, u32[]{:S(2)}, u32[]{:S(2)}) collective-permute-start(bf16[8,32,1408]{2,1,0:T(8,128)(2,1)S(1)} %constant_dynamic-update-slice_fusion), channel_id=1, source_target_pairs={{0,8},{1,9},{2,10},{3,11},{4,12},{5,13},{6,14},{7,15},{8,0},{9,1},... | collective-permute-start | bytes 2162696 | tf_op jit(solution)/shard_map/ppermute | solution.py:48
  80.3 30.2 %collective-permute-start.28 = (bf16[8,32,1408]{2,1,0:T(8,128)(2,1)S(1)}, bf16[8,32,1408]{2,1,0:T(8,128)(2,1)S(1)}, u32[]{:S(2)}, u32[]{:S(2)}) collective-permute-start(bf16[8,32,1408]{2,1,0:T(8,128)(2,1)S(1)} %collective-permute-done.20), channel_id=1, source_target_pairs={{0,8},{1,9},{2,10},{3,11},{4,12},{5,13},{6,14},{7,15},{8,0},{9,1},... | collective-permute-start | bytes 2162696 | tf_op jit(solution)/shard_map/ppermute | solution.py:48
  82.4 34.2 %collective-permute-start.26 = (bf16[8,32,2816]{2,1,0:T(8,128)(2,1)S(1)}, bf16[8,32,2816]{2,1,0:T(8,128)(2,1)S(1)}, u32[]{:S(2)}, u32[]{:S(2)}) collective-permute-start(bf16[8,32,2816]{2,1,0:T(8,128)(2,1)S(1)} %constant_dynamic-update-slice_fusion.18), channel_id=1, source_target_pairs={{0,2},{1,3},{2,0},{3,1},{4,6},{5,7},{6,4},{7,5},{8,10},{9,11},{10,... | collective-permute-start | bytes 4325384 | tf_op jit(solution)/shard_map/ppermute | solution.py:48
  98.4 18.2 %collective-permute-start.22 = (bf16[256,1024]{1,0:T(8,128)(2,1)S(1)}, bf16[256,1024]{1,0:T(8,128)(2,1)S(1)}, u32[]{:S(2)}, u32[]{:S(2)}) collective-permute-start(bf16[256,1024]{1,0:T(8,128)(2,1)S(1)} %get-tuple-element.314.refs_1_), channel_id=1, source_target_pairs={{0,1},{1,0},{2,3},{3,2},{4,5},{5,4},{6,7},{7,6},{8,9},{9,8},{10,11... | collective-permute-start | bytes 1572872 | tf_op jit(solution)/shard_map/ppermute | solution.py:48
  99.4 17.2 %collective-permute-start.23 = (bf16[256,1024]{1,0:T(8,128)(2,1)S(1)}, bf16[256,1024]{1,0:T(8,128)(2,1)S(1)}, u32[]{:S(2)}, u32[]{:S(2)}) collective-permute-start(bf16[256,1024]{1,0:T(8,128)(2,1)S(1)} %get-tuple-element.315.refs_2_), channel_id=1, source_target_pairs={{0,1},{1,0},{2,3},{3,2},{4,5},{5,4},{6,7},{7,6},{8,9},{9,8},{10,11... | collective-permute-start | bytes 1572872 | tf_op jit(solution)/shard_map/ppermute | solution.py:48
  138.6 25.3 %collective-permute-start.32 = (bf16[8,32,2048]{2,1,0:T(8,128)(2,1)}, bf16[8,32,2048]{2,1,0:T(8,128)(2,1)S(1)}, u32[]{:S(2)}, u32[]{:S(2)}) collective-permute-start(bf16[8,32,2048]{2,1,0:T(8,128)(2,1)} %bitcast.30), channel_id=1, source_target_pairs={{0,2},{1,3},{2,0},{3,1},{4,6},{5,7},{6,4},{7,5},{8,10},{9,11},{10,... | collective-permute-start | bytes 3145736 | tf_op jit(solution)/shard_map/ppermute | solution.py:48
  140.0 25.2 %collective-permute-start.31 = (bf16[8,32,2048]{2,1,0:T(8,128)(2,1)}, bf16[8,32,2048]{2,1,0:T(8,128)(2,1)}, u32[]{:S(2)}, u32[]{:S(2)}) collective-permute-start(bf16[8,32,2048]{2,1,0:T(8,128)(2,1)} %bitcast.29), channel_id=1, source_target_pairs={{0,4},{1,5},{2,6},{3,7},{4,0},{5,1},{6,2},{7,3},{8,12},{9,13},{10,... | collective-permute-start | bytes 3145736 | tf_op jit(solution)/shard_map/ppermute | solution.py:48
  148.1 19.2 %collective-permute-start.30 = (bf16[512,1024]{1,0:T(8,128)(2,1)S(1)}, bf16[512,1024]{1,0:T(8,128)(2,1)S(1)}, u32[]{:S(2)}, u32[]{:S(2)}) collective-permute-start(bf16[512,1024]{1,0:T(8,128)(2,1)S(1)} %get-tuple-element.366.refs_1_), channel_id=1, source_target_pairs={{0,1},{1,0},{2,3},{3,2},{4,5},{5,4},{6,7},{7,6},{8,9},{9,8},{10,11... | collective-permute-start | bytes 3145736 | tf_op jit(solution)/shard_map/ppermute | solution.py:48
  148.2 19.2 %collective-permute-start.29 = (bf16[512,1024]{1,0:T(8,128)(2,1)S(1)}, bf16[512,1024]{1,0:T(8,128)(2,1)S(1)}, u32[]{:S(2)}, u32[]{:S(2)}) collective-permute-start(bf16[512,1024]{1,0:T(8,128)(2,1)S(1)} %get-tuple-element.352.refs_0_), channel_id=1, source_target_pairs={{0,1},{1,0},{2,3},{3,2},{4,5},{5,4},{6,7},{7,6},{8,9},{9,8},{10,11... | collective-permute-start | bytes 3145736 | tf_op jit(solution)/shard_map/ppermute | solution.py:48
  151.7 22.9 %collective-permute-start.33 = (bf16[16,32,768]{2,1,0:T(8,128)(2,1)S(1)}, bf16[16,32,768]{2,1,0:T(8,128)(2,1)S(1)}, u32[]{:S(2)}, u32[]{:S(2)}) collective-permute-start(bf16[16,32,768]{2,1,0:T(8,128)(2,1)S(1)} %bitcast.80), channel_id=1, source_target_pairs={{0,8},{1,9},{2,10},{3,11},{4,12},{5,13},{6,14},{7,15},{8,0},{9,1},... | collective-permute-start | bytes 2359304 | tf_op jit(solution)/shard_map/ppermute | solution.py:48
  167.4 26.5 %collective-permute-start.36 = (bf16[8,32,1408]{2,1,0:T(8,128)(2,1)S(1)}, bf16[8,32,1408]{2,1,0:T(8,128)(2,1)S(1)}, u32[]{:S(2)}, u32[]{:S(2)}) collective-permute-start(bf16[8,32,1408]{2,1,0:T(8,128)(2,1)S(1)} %bitcast.84), channel_id=1, source_target_pairs={{0,4},{1,5},{2,6},{3,7},{4,0},{5,1},{6,2},{7,3},{8,12},{9,13},{10,... | collective-permute-start | bytes 2162696 | tf_op jit(solution)/shard_map/ppermute | solution.py:48
  168.0 26.0 %collective-permute-start.37 = (bf16[8,32,1408]{2,1,0:T(8,128)(2,1)S(1)}, bf16[8,32,1408]{2,1,0:T(8,128)(2,1)S(1)}, u32[]{:S(2)}, u32[]{:S(2)}) collective-permute-start(bf16[8,32,1408]{2,1,0:T(8,128)(2,1)S(1)} %bitcast.83), channel_id=1, source_target_pairs={{0,2},{1,3},{2,0},{3,1},{4,6},{5,7},{6,4},{7,5},{8,10},{9,11},{10,... | collective-permute-start | bytes 2162696 | tf_op jit(solution)/shard_map/ppermute | solution.py:48
  175.1 18.8 %collective-permute-start.38 = (bf16[8,32,768]{2,1,0:T(8,128)(2,1)S(1)}, bf16[8,32,768]{2,1,0:T(8,128)(2,1)S(1)}, u32[]{:S(2)}, u32[]{:S(2)}) collective-permute-start(bf16[8,32,768]{2,1,0:T(8,128)(2,1)S(1)} %get-tuple-element.395), channel_id=1, source_target_pairs={{0,16},{1,17},{2,18},{3,19},{4,20},{5,21},{6,22},{7,23},{8,24},{9,... | collective-permute-start | bytes 1179656 | tf_op jit(solution)/shard_map/ppermute | solution.py:48
  177.0 20.1 %collective-permute-start.34 = (bf16[4,32,2048]{2,1,0:T(8,128)(2,1)S(1)}, bf16[4,32,2048]{2,1,0:T(8,128)(2,1)S(1)}, u32[]{:S(2)}, u32[]{:S(2)}) collective-permute-start(bf16[4,32,2048]{2,1,0:T(8,128)(2,1)S(1)} %get-tuple-element.391), channel_id=1, source_target_pairs={{0,2},{1,3},{2,0},{3,1},{4,6},{5,7},{6,4},{7,5},{8,10},{9,11},{10,... | collective-permute-start | bytes 1572872 | tf_op jit(solution)/shard_map/ppermute | solution.py:48
  177.4 19.6 %collective-permute-start.35 = (bf16[4,32,2048]{2,1,0:T(8,128)(2,1)S(1)}, bf16[4,32,2048]{2,1,0:T(8,128)(2,1)S(1)}, u32[]{:S(2)}, u32[]{:S(2)}) collective-permute-start(bf16[4,32,2048]{2,1,0:T(8,128)(2,1)S(1)} %get-tuple-element.392), channel_id=1, source_target_pairs={{0,4},{1,5},{2,6},{3,7},{4,0},{5,1},{6,2},{7,3},{8,12},{9,13},{10,... | collective-permute-start | bytes 1572872 | tf_op jit(solution)/shard_map/ppermute | solution.py:48
  202.1 18.9 %collective-permute-start.41 = (bf16[8,32,1408]{2,1,0:T(8,128)(2,1)S(1)}, bf16[8,32,1408]{2,1,0:T(8,128)(2,1)S(1)}, u32[]{:S(2)}, u32[]{:S(2)}) collective-permute-start(bf16[8,32,1408]{2,1,0:T(8,128)(2,1)S(1)} %bitcast.88), channel_id=1, source_target_pairs={{0,4},{1,5},{2,6},{3,7},{4,0},{5,1},{6,2},{7,3},{8,12},{9,13},{10,... | collective-permute-start | bytes 2162696 | tf_op jit(solution)/shard_map/ppermute | solution.py:48
  202.6 18.4 %collective-permute-start.42 = (bf16[8,32,1408]{2,1,0:T(8,128)(2,1)S(1)}, bf16[8,32,1408]{2,1,0:T(8,128)(2,1)S(1)}, u32[]{:S(2)}, u32[]{:S(2)}) collective-permute-start(bf16[8,32,1408]{2,1,0:T(8,128)(2,1)S(1)} %bitcast.87), channel_id=1, source_target_pairs={{0,2},{1,3},{2,0},{3,1},{4,6},{5,7},{6,4},{7,5},{8,10},{9,11},{10,... | collective-permute-start | bytes 2162696 | tf_op jit(solution)/shard_map/ppermute | solution.py:48
  207.3 19.4 %collective-permute-start.45 = (bf16[2,2,32,2048]{3,2,1,0:T(8,128)(2,1)S(1)}, bf16[2,2,32,2048]{3,2,1,0:T(8,128)(2,1)S(1)}, u32[]{:S(2)}, u32[]{:S(2)}) collective-permute-start(bf16[2,2,32,2048]{3,2,1,0:T(8,128)(2,1)S(1)} %get-tuple-element.456), channel_id=1, source_target_pairs={{0,8},{1,9},{2,10},{3,11},{4,12},{5,13},{6,14},{7,15},{8,0},{9,1},... | collective-permute-start | bytes 1572872 | tf_op jit(solution)/shard_map/ppermute | solution.py:48
  207.3 19.1 %collective-permute-start.46 = (bf16[2,2,32,1408]{3,2,1,0:T(8,128)(2,1)S(1)}, bf16[2,2,32,1408]{3,2,1,0:T(8,128)(2,1)S(1)}, u32[]{:S(2)}, u32[]{:S(2)}) collective-permute-start(bf16[2,2,32,1408]{3,2,1,0:T(8,128)(2,1)S(1)} %get-tuple-element.457), channel_id=1, source_target_pairs={{0,8},{1,9},{2,10},{3,11},{4,12},{5,13},{6,14},{7,15},{8,0},{9,1},... | collective-permute-start | bytes 1081352 | tf_op jit(solution)/shard_map/ppermute | solution.py:48
  231.9 17.7 %collective-permute-start.49 = (bf16[2,2,32,1408]{3,2,1,0:T(8,128)(2,1)S(1)}, bf16[2,2,32,1408]{3,2,1,0:T(8,128)(2,1)S(1)}, u32[]{:S(2)}, u32[]{:S(2)}) collective-permute-start(bf16[2,2,32,1408]{3,2,1,0:T(8,128)(2,1)S(1)} %get-tuple-element.481), channel_id=1, source_target_pairs={{0,8},{1,9},{2,10},{3,11},{4,12},{5,13},{6,14},{7,15},{8,0},{9,1},... | collective-permute-start | bytes 1081352 | tf_op jit(solution)/shard_map/ppermute | solution.py:48
  232.0 25.7 %collective-permute-start.56 = (bf16[1,2,32,1408]{3,2,1,0:T(8,128)(2,1)S(1)}, bf16[1,2,32,1408]{3,2,1,0:T(8,128)(2,1)S(1)}, u32[]{:S(2)}, u32[]{:S(2)}) collective-permute-start(bf16[1,2,32,1408]{3,2,1,0:T(8,128)(2,1)S(1)} %get-tuple-element.506), channel_id=1, source_target_pairs={{0,16},{1,17},{2,18},{3,19},{4,20},{5,21},{6,22},{7,23},{8,24},{9,... | collective-permute-start | bytes 540680 | tf_op jit(solution)/shard_map/ppermute | solution.py:48
  234.7 24.1 %collective-permute-start.55 = (bf16[1,2,32,2048]{3,2,1,0:T(8,128)(2,1)S(1)}, bf16[1,2,32,2048]{3,2,1,0:T(8,128)(2,1)S(1)}, u32[]{:S(2)}, u32[]{:S(2)}) collective-permute-start(bf16[1,2,32,2048]{3,2,1,0:T(8,128)(2,1)S(1)} %get-tuple-element.505), channel_id=1, source_target_pairs={{0,16},{1,17},{2,18},{3,19},{4,20},{5,21},{6,22},{7,23},{8,24},{9,... | collective-permute-start | bytes 786440 | tf_op jit(solution)/shard_map/ppermute | solution.py:48
  (56 other events, 521.4 us)

commit v6 on v5

--- a/solution.py
+++ b/solution.py
@@ -770,7 +770,7 @@
     n_tok = lefts[0].shape[0]
     width = sum(w.shape[0] for w in weights)
     n, n_in = len(lefts), len(weights)
-    steps = 4
+    steps = 2
     size = n_tok // steps
 
     def body(*refs):
@@ -803,7 +803,7 @@
         out_shape=(jax.ShapeDtypeStruct((n_tok // pieces, width), BF16),) * pieces,
         in_specs=[rows_spec(size, x.shape[1]) for x in lefts] + whole_specs(weights),
         out_specs=tuple(piece_specs(pieces, steps, size, width)),
-        compiler_params=params(20),
+        compiler_params=params(30),
         cost_estimate=cost(name),
     )(*near(*lefts), *weights)
 

time: 266 us -> 266 us (level)
  no operation moved by 1% of the time
where the time goes in v6:
time: 266 us; the launch traced here: 265 us
  Pallas kernels  108 us (41%)
  waiting for transfers between devices  91.9 us (35%)
  starting transfers between devices  53 us (20%)
  other arithmetic  5.49 us (2%)
  local copies, waits for them, and re-layouts  5.28 us (2%)
    ppermute x58, waiting for transfers between devices, swap(): return lax.ppermute(value, AXES, [(i, i ^ bit) for i in range(self.count)])  91.9 us
    ppermute x58, starting transfers between devices, swap(): return lax.ppermute(value, AXES, [(i, i ^ bit) for i in range(self.count)])  53 us
    pallas_call x4, Pallas kernels, weight_grad(): pl.pallas_call(body, name=name, grid=(pieces,), out_shape=(jax.ShapeDtype...  21.1 us
    pallas_call x1, Pallas kernels, attn_bwd(): pl.pallas_call(body, name='attn_bwd', out_shape=pltpu.VMEM(qkv.shape, BF1...  15.2 us
    pallas_call x1, Pallas kernels, attn_fwd(): pl.pallas_call(body, name='attn_fwd', out_shape=(pltpu.HBM((n_tok, width)...  14.4 us
    pallas_call x3, Pallas kernels, sum_nt(): pl.pallas_call(body, name=name, grid=(steps,), out_shape=(jax.ShapeDtypeS...  13.6 us
    pallas_call x1, Pallas kernels, gated(): pl.pallas_call(body, name='gated', grid=(steps,), out_shape=tuple((pltpu....  8.7 us
    pallas_call x1, Pallas kernels, shuffle(): pl.pallas_call(body, name='shuffle', grid=(steps,), out_shape=(*[pltpu.HB...  7.48 us
  transfers between devices with their start and end apart: 58, of which 30 were waited for; matrix products, arithmetic and copies ran while one was open for 3% of the time, Pallas kernels for 32%

profile of v6, /device:TPU:0, one launch (start us, length us, event | category | flops | bytes accessed | tf_op | source)
XLA Modules:
  0.0 265.3 jit_solution(4717439561700153362)
XLA Ops:
  0.7 2.6 prepare.1
  6.3 4.0 %collective-permute-start.6 = (bf16[2,32,1408]{2,1,0:T(8,128)(2,1)S(1)}, bf16[2,32,1408]{2,1,0:T(8,128)(2,1)S(1)}, u32[]{:S(2)}, u32[]{:S(2)}) collective-permute-start(bf16[2,32,1408]{2,1,0:T(8,128)(2,1)S(1)} %maximum_select_fusion.2), channel_id=1, source_target_pairs={{0,16},{1,17},{2,18},{3,19},{4,20},{5,21},{6,22},{7,23},{8,24},{9,... | collective-permute-start | bytes 540680 | tf_op jit(solution)/shard_map/ppermute | solution.py:48
  25.7 7.4 %collective-permute-done.10 = bf16[2,32,1408]{2,1,0:T(8,128)(2,1)S(1)} collective-permute-done((bf16[2,32,1408]{2,1,0:T(8,128)(2,1)S(1)}, bf16[2,32,1408]{2,1,0:T(8,128)(2,1)S(1)}, u32[]{:S(2)}, u32[]{:S(2)}) %collective-permute-start.10) | collective-permute-done | bytes 180256 | tf_op jit(solution)/shard_map/ppermute | solution.py:48
  33.1 2.5 collective-permute-start.16
  37.3 7.1 %collective-permute-done.11 = bf16[4,32,1408]{2,1,0:T(8,128)(2,1)S(1)} collective-permute-done((bf16[4,32,1408]{2,1,0:T(8,128)(2,1)S(1)}, bf16[4,32,1408]{2,1,0:T(8,128)(2,1)S(1)}, u32[]{:S(2)}, u32[]{:S(2)}) %collective-permute-start.11) | collective-permute-done | bytes 360480 | tf_op jit(solution)/shard_map/ppermute | solution.py:48
  48.7 8.6 %collective-permute-done.17 = bf16[2,32,2816]{2,1,0:T(8,128)(2,1)S(1)} collective-permute-done((bf16[2,32,2816]{2,1,0:T(8,128)(2,1)S(1)}, bf16[2,32,2816]{2,1,0:T(8,128)(2,1)S(1)}, u32[]{:S(2)}, u32[]{:S(2)}) %collective-permute-start.17) | collective-permute-done | bytes 360480 | tf_op jit(solution)/shard_map/ppermute | solution.py:48
  58.1 7.5 %shuffle.1 = (bf16[1024,1024]{1,0:T(8,128)(2,1)}, bf16[1024,1024]{1,0:T(8,128)(2,1)}, bf16[1024,1024]{1,0:T(8,128)(2,1)}) custom-call(s32[1]{0:T(128)} %bitcast.5.index_ref, s32[1,1024]{1,0:T(1,128)S(1)} %broadcast_in_dim_reshape.3.masks_ref, bf16[1024,1024]{1,0:T(8,128)(2,1)S(1)} %get-tuple-element.554.refs_0_, ...), custom_call_target="tpu_custom_call" | custom-call | flops 10000000000 | bytes 1 | tf_op jit(solution)/shard_map/shuffle/pallas_call | solution.py:422
  66.0 10.7 %collective-permute-done.20 = bf16[8,32,1408]{2,1,0:T(8,128)(2,1)S(1)} collective-permute-done((bf16[8,32,1408]{2,1,0:T(8,128)(2,1)S(1)}, bf16[8,32,1408]{2,1,0:T(8,128)(2,1)S(1)}, u32[]{:S(2)}, u32[]{:S(2)}) %collective-permute-start.20) | collective-permute-done | bytes 720928 | tf_op jit(solution)/shard_map/ppermute | solution.py:48
  80.3 2.0 collective-permute-start.28
  84.0 14.4 %attn_fwd.1 = (bf16[1024,1024]{1,0:T(8,128)(2,1)}, bf16[1024,768]{1,0:T(8,128)(2,1)S(1)}, bf16[1024,512]{1,0:T(8,128)(2,1)S(1)}, f32[1024,512]{1,0:T(8,128)S(1)}...) custom-call(s32[2,4]{1,0:T(2,128)S(1)} %pad_add_fusion.seq_ref, ...), custom_call_target="tpu_custom_call" | custom-call | flops 10000000000 | bytes 1 | tf_op jit(solution)/shard_map/attn_fwd/pallas_call | solution.py:587
  99.4 11.1 %collective-permute-done.28 = bf16[8,32,1408]{2,1,0:T(8,128)(2,1)S(1)} collective-permute-done((bf16[8,32,1408]{2,1,0:T(8,128)(2,1)S(1)}, bf16[8,32,1408]{2,1,0:T(8,128)(2,1)S(1)}, u32[]{:S(2)}, u32[]{:S(2)}) %collective-permute-start.28) | collective-permute-done | bytes 720928 | tf_op jit(solution)/shard_map/ppermute | solution.py:48
  111.0 4.0 %down_back.1.d_act_ref = bf16[1024,1408]{1,0:T(8,128)(2,1)S(1)} custom-call(bf16[1024,1024]{1,0:T(8,128)(2,1)S(1)} %copy-done, bf16[256,1408]{1,0:T(8,128)(2,1)S(1)} %bitcast.69, bf16[256,1408]{1,0:T(8,128)(2,1)S(1)} %bitcast.73, bf16[256,1408]{1,0:T(8,128)(2,1)S(1)} %bitcast.71, bf16[256,1408]{1,0:T(8,128)(2,1)S(1)} %bitcast.75), custom_call_target="tpu_custom_call" | custom-call | flops 10000000000 | bytes 1 | tf_op jit(solution)/shard_map/down_back/pallas_call | solution.py:660
  115.1 2.6 residual.1
  119.6 8.7 %gated.1 = (bf16[1024,768]{1,0:T(8,128)(2,1)S(1)}, bf16[1024,640]{1,0:T(8,128)(2,1)S(1)}, bf16[1024,1408]{1,0:T(8,128)(2,1)S(1)}, bf16[1024,1408]{1,0:T(8,128)(2,1)S(1)}) custom-call(bf16[1024,1024]{1,0:T(8,128)(2,1)S(1)} %get-tuple-element.332.normed_ref.refs_0_, bf16[1024,1408]{1,0:T(8,128)(2,1)S(1)} %copy-done.28, bf16[256,2816]{1,0:T(8,128)(2,1)S(1)} %bitcast.61, ...), custom_call_target="tpu_custom_call" | custom-call | flops 10000000000 | bytes 1 | tf_op jit(solution)/shard_map/gated/pallas_call | solution.py:694
  128.4 8.1 %grad_gate.1 = (bf16[256,2048]{1,0:T(8,128)(2,1)S(1)}, bf16[256,2048]{1,0:T(8,128)(2,1)}, bf16[256,2048]{1,0:T(8,128)(2,1)S(1)}, bf16[256,2048]{1,0:T(8,128)(2,1)}) custom-call(bf16[1024,1024]{1,0:T(8,128)(2,1)S(1)} %get-tuple-element.332.normed_ref.refs_0_, bf16[1024,1024]{1,0:T(8,128)(2,1)S(1)} %copy-done, ...), custom_call_target="tpu_custom_call" | custom-call | flops 1 | bytes 1 | tf_op jit(solution)/shard_map/grad_gate/pallas_call | solution.py:755
  139.5 7.4 %d_norm2.1 = (bf16[512,1024]{1,0:T(8,128)(2,1)S(1)}, bf16[512,1024]{1,0:T(8,128)(2,1)S(1)}) custom-call(bf16[1024,1408]{1,0:T(8,128)(2,1)S(1)} %get-tuple-element.341.refs_2_.refs_0_, bf16[1024,1408]{1,0:T(8,128)(2,1)S(1)} %get-tuple-element.357.refs_1_, bf16[256,2816]{1,0:T(8,128)(2,1)S(1)} %bitcast.62, bf16[256,2816]{1,0:T(8,128)(2,1)S(1)} %bitcast.66, ...), custom_call_target="tpu_custom_call" | custom-call | flops 1 | bytes 1 | tf_op jit(solution)/shard_map/d_norm2/pallas_call | solution.py:799
  147.5 3.0 %grad_down.1 = (bf16[512,768]{1,0:T(8,128)(2,1)S(1)}, bf16[512,768]{1,0:T(8,128)(2,1)S(1)}) custom-call(bf16[1024,1024]{1,0:T(8,128)(2,1)S(1)} %copy-done, bf16[1024,768]{1,0:T(8,128)(2,1)S(1)} %get-tuple-element.353.refs_1_.refs_0_), custom_call_target="tpu_custom_call" | custom-call | flops 1 | bytes 1 | tf_op jit(solution)/shard_map/grad_down/pallas_call | solution.py:755
  150.9 4.7 %grad_up.1 = (bf16[256,1408]{1,0:T(8,128)(2,1)S(1)}, bf16[256,1408]{1,0:T(8,128)(2,1)S(1)}, bf16[256,1408]{1,0:T(8,128)(2,1)S(1)}, bf16[256,1408]{1,0:T(8,128)(2,1)S(1)}) custom-call(bf16[1024,1024]{1,0:T(8,128)(2,1)S(1)} %get-tuple-element.332.normed_ref.refs_0_, bf16[1024,1408]{1,0:T(8,128)(2,1)S(1)} %get-tuple-element.357.refs_1_), custom_call_target="tpu_custom_call" | custom-call | flops 1 | bytes 1 | tf_op jit(solution)/shard_map/grad_up/pallas_call | solution.py:755
  155.6 7.3 %collective-permute-done.32.refs_3_ = bf16[8,32,2048]{2,1,0:T(8,128)(2,1)} collective-permute-done((bf16[8,32,2048]{2,1,0:T(8,128)(2,1)}, bf16[8,32,2048]{2,1,0:T(8,128)(2,1)}, u32[]{:S(2)}, u32[]{:S(2)}) %collective-permute-start.32) | collective-permute-done | bytes 1048608 | tf_op jit(solution)/shard_map/ppermute | solution.py:48
  164.2 2.3 fold_first.1
  168.0 5.8 %norm_back.1 = (f32[512,1024]{1,0:T(8,128)S(1)}, bf16[1024,1024]{1,0:T(8,128)(2,1)S(1)}, bf16[1024,512]{1,0:T(8,128)(2,1)S(1)}, f32[8,1024]{1,0:T(8,128)S(1)}) custom-call(f32[1024,1024]{1,0:T(8,128)S(1)} %get-tuple-element.330.hres_ref.h_ref, bf16[1024,1024]{1,0:T(8,128)(2,1)S(1)} %copy-done, f32[8,1024]{1,0:T(8,128)S(1)} %get-tuple-element.329.refs_8_.gain_ref.refs_4_, ...), custom_call_target="tpu_custom_call" | custom-call | flops 1 | bytes 1 | tf_op jit(solution)/shard_map/norm_back/pallas_call | solution.py:853
  177.8 15.2 %attn_bwd.1.refs_2_.refs_0_ = bf16[1024,768]{1,0:T(8,128)(2,1)S(1)} custom-call(s32[2,4]{1,0:T(2,128)S(1)} %pad_add_fusion.seq_ref, bf16[1024,768]{1,0:T(8,128)(2,1)S(1)} %copy-done.12, bf16[1024,512]{1,0:T(8,128)(2,1)S(1)} %get-tuple-element.305.y_ref.refs_3_, bf16[1024,512]{1,0:T(8,128)(2,1)S(1)} %get-tuple-element.388.dy_ref, f32[1024,512]{1,0:T(8,128)S(1)} %copy-done.10), custom_call_target="tpu_custom_call" | custom-call | flops 1 | bytes 1 | tf_op jit(solution)/shard_map/attn_bwd/pallas_call | solution.py:929
  196.2 5.3 %grad_attn.1 = (bf16[256,1408]{1,0:T(8,128)(2,1)S(1)}, bf16[256,1408]{1,0:T(8,128)(2,1)S(1)}, bf16[256,1408]{1,0:T(8,128)(2,1)S(1)}, bf16[256,1408]{1,0:T(8,128)(2,1)S(1)}) custom-call(bf16[1024,1024]{1,0:T(8,128)(2,1)S(1)} %copy-done.8, bf16[1024,1024]{1,0:T(8,128)(2,1)S(1)} %get-tuple-element.410.refs_1_, bf16[1024,768]{1,0:T(8,128)(2,1)S(1)} %attn_bwd.1.refs_2_.refs_0_, ...), custom_call_target="tpu_custom_call" | custom-call | flops 1 | bytes 1 | tf_op jit(solution)/shard_map/grad_attn/pallas_call | solution.py:755
  208.3 2.3 norm_one_part.1
  210.6 3.9 %down.1 = (bf16[512,1024]{1,0:T(8,128)(2,1)S(1)}, bf16[512,1024]{1,0:T(8,128)(2,1)S(1)}) custom-call(bf16[1024,768]{1,0:T(8,128)(2,1)S(1)} %get-tuple-element.353.refs_1_.refs_0_, bf16[1024,640]{1,0:T(8,128)(2,1)S(1)} %get-tuple-element.439.refs_3_.refs_1_, bf16[256,1408]{1,0:T(8,128)(2,1)S(1)} %bitcast.70, bf16[256,1408]{1,0:T(8,128)(2,1)S(1)} %bitcast.74, ...), custom_call_target="tpu_custom_call" | custom-call | flops 1 | bytes 1 | tf_op jit(solution)/shard_map/down/pallas_call | solution.py:799
  214.5 5.6 %collective-permute-done.41.refs_1_ = bf16[8,32,1408]{2,1,0:T(8,128)(2,1)S(1)} collective-permute-done((bf16[8,32,1408]{2,1,0:T(8,128)(2,1)S(1)}, bf16[8,32,1408]{2,1,0:T(8,128)(2,1)S(1)}, u32[]{:S(2)}, u32[]{:S(2)}) %collective-permute-start.41) | collective-permute-done | bytes 720928 | tf_op jit(solution)/shard_map/ppermute | solution.py:48
  223.0 2.6 collective-permute-done.46.refs_1_
  226.1 4.1 %collective-permute-done.43.refs_1_ = bf16[4,32,1408]{2,1,0:T(8,128)(2,1)S(1)} collective-permute-done((bf16[4,32,1408]{2,1,0:T(8,128)(2,1)S(1)}, bf16[4,32,1408]{2,1,0:T(8,128)(2,1)S(1)}, u32[]{:S(2)}, u32[]{:S(2)}) %collective-permute-start.43) | collective-permute-done | bytes 360480 | tf_op jit(solution)/shard_map/ppermute | solution.py:48
  231.3 2.7 %collective-permute-start.56 = (bf16[1,2,32,1408]{3,2,1,0:T(8,128)(2,1)S(1)}, bf16[1,2,32,1408]{3,2,1,0:T(8,128)(2,1)S(1)}, u32[]{:S(2)}, u32[]{:S(2)}) collective-permute-start(bf16[1,2,32,1408]{3,2,1,0:T(8,128)(2,1)S(1)} %get-tuple-element.506), channel_id=1, source_target_pairs={{0,16},{1,17},{2,18},{3,19},{4,20},{5,21},{6,22},{7,23},{8,24},{9,... | collective-permute-start | bytes 540680 | tf_op jit(solution)/shard_map/ppermute | solution.py:48
  234.9 5.7 %finish.1 = (bf16[512,1024]{1,0:T(8,128)(2,1)}, bf16[512,1024]{1,0:T(8,128)(2,1)}) custom-call(bf16[512,1024]{1,0:T(8,128)(2,1)S(1)} %get-tuple-element.437.part_ref, bf16[512,1024]{1,0:T(8,128)(2,1)S(1)} %collective-permute-done.47.came_ref, bf16[1024,1024]{1,0:T(8,128)(2,1)S(1)} %copy-done.6, f32[512,1024]{1,0:T(8,128)S(1)} %get-tuple-element.475.dh_ref, ...), custom_call_target="tpu_custom_call" | custom-call | flops 1 | bytes 1 | tf_op jit(solution)/shard_map/finish/pallas_call | solution.py:975
  240.7 8.2 %collective-permute-done.49.refs_1_ = bf16[2,2,32,1408]{3,2,1,0:T(8,128)(2,1)S(1)} collective-permute-done((bf16[2,2,32,1408]{3,2,1,0:T(8,128)(2,1)S(1)}, bf16[2,2,32,1408]{3,2,1,0:T(8,128)(2,1)S(1)}, u32[]{:S(2)}, u32[]{:S(2)}) %collective-permute-start.49) | collective-permute-done | bytes 360480 | tf_op jit(solution)/shard_map/ppermute | solution.py:48
  261.9 2.2 collective-permute-done.57.came_ref
  (213 shorter events, 74.2 us)
Async XLA Ops:
  18.2 19.0 %collective-permute-start.13 = (bf16[2,32,2816]{2,1,0:T(8,128)(2,1)S(1)}, bf16[2,32,2816]{2,1,0:T(8,128)(2,1)S(1)}, u32[]{:S(2)}, u32[]{:S(2)}) collective-permute-start(bf16[2,32,2816]{2,1,0:T(8,128)(2,1)S(1)} %maximum_select_fusion), channel_id=1, source_target_pairs={{0,16},{1,17},{2,18},{3,19},{4,20},{5,21},{6,22},{7,23},{8,24},{9,... | collective-permute-start | bytes 1081352 | tf_op jit(solution)/shard_map/ppermute | solution.py:48
  20.0 15.7 %collective-permute-start.7 = (bf16[2,32,1408]{2,1,0:T(8,128)(2,1)S(1)}, bf16[2,32,1408]{2,1,0:T(8,128)(2,1)S(1)}, u32[]{:S(2)}, u32[]{:S(2)}) collective-permute-start(bf16[2,32,1408]{2,1,0:T(8,128)(2,1)S(1)} %pad_maximum_fusion.6), channel_id=1, source_target_pairs={{0,4},{1,5},{2,6},{3,7},{4,0},{5,1},{6,2},{7,3},{8,12},{9,13},{10,... | collective-permute-start | bytes 540680 | tf_op jit(solution)/shard_map/ppermute | solution.py:48
  33.1 15.5 %collective-permute-start.16 = (bf16[2,32,2816]{2,1,0:T(8,128)(2,1)S(1)}, bf16[2,32,2816]{2,1,0:T(8,128)(2,1)S(1)}, u32[]{:S(2)}, u32[]{:S(2)}) collective-permute-start(bf16[2,32,2816]{2,1,0:T(8,128)(2,1)S(1)} %maximum_select_fusion), channel_id=1, source_target_pairs={{0,8},{1,9},{2,10},{3,11},{4,12},{5,13},{6,14},{7,15},{8,0},{9,1},... | collective-permute-start | bytes 1081352 | tf_op jit(solution)/shard_map/ppermute | solution.py:48
  37.2 20.1 %collective-permute-start.17 = (bf16[2,32,2816]{2,1,0:T(8,128)(2,1)S(1)}, bf16[2,32,2816]{2,1,0:T(8,128)(2,1)S(1)}, u32[]{:S(2)}, u32[]{:S(2)}) collective-permute-start(bf16[2,32,2816]{2,1,0:T(8,128)(2,1)S(1)} %collective-permute-done.13), channel_id=1, source_target_pairs={{0,8},{1,9},{2,10},{3,11},{4,12},{5,13},{6,14},{7,15},{8,0},{9,1},... | collective-permute-start | bytes 1081352 | tf_op jit(solution)/shard_map/ppermute | solution.py:48
  44.8 31.9 %collective-permute-start.20 = (bf16[8,32,1408]{2,1,0:T(8,128)(2,1)S(1)}, bf16[8,32,1408]{2,1,0:T(8,128)(2,1)S(1)}, u32[]{:S(2)}, u32[]{:S(2)}) collective-permute-start(bf16[8,32,1408]{2,1,0:T(8,128)(2,1)S(1)} %constant_dynamic-update-slice_fusion), channel_id=1, source_target_pairs={{0,16},{1,17},{2,18},{3,19},{4,20},{5,21},{6,22},{7,23},{8,24},{9,... | collective-permute-start | bytes 2162696 | tf_op jit(solution)/shard_map/ppermute | solution.py:48
  46.5 19.2 %collective-permute-start.14 = (bf16[8,32,1408]{2,1,0:T(8,128)(2,1)S(1)}, bf16[8,32,1408]{2,1,0:T(8,128)(2,1)S(1)}, u32[]{:S(2)}, u32[]{:S(2)}) collective-permute-start(bf16[8,32,1408]{2,1,0:T(8,128)(2,1)S(1)} %constant_dynamic-update-slice_fusion.6), channel_id=1, source_target_pairs={{0,4},{1,5},{2,6},{3,7},{4,0},{5,1},{6,2},{7,3},{8,12},{9,13},{10,... | collective-permute-start | bytes 2162696 | tf_op jit(solution)/shard_map/ppermute | solution.py:48
  46.9 19.1 %collective-permute-start.15 = (bf16[8,32,1408]{2,1,0:T(8,128)(2,1)S(1)}, bf16[8,32,1408]{2,1,0:T(8,128)(2,1)S(1)}, u32[]{:S(2)}, u32[]{:S(2)}) collective-permute-start(bf16[8,32,1408]{2,1,0:T(8,128)(2,1)S(1)} %constant_dynamic-update-slice_fusion.11), channel_id=1, source_target_pairs={{0,2},{1,3},{2,0},{3,1},{4,6},{5,7},{6,4},{7,5},{8,10},{9,11},{10,... | collective-permute-start | bytes 2162696 | tf_op jit(solution)/shard_map/ppermute | solution.py:48
  57.6 20.6 %collective-permute-start.19 = (bf16[4,32,2816]{2,1,0:T(8,128)(2,1)S(1)}, bf16[4,32,2816]{2,1,0:T(8,128)(2,1)S(1)}, u32[]{:S(2)}, u32[]{:S(2)}) collective-permute-start(bf16[4,32,2816]{2,1,0:T(8,128)(2,1)S(1)} %pad_maximum_fusion.3), channel_id=1, source_target_pairs={{0,4},{1,5},{2,6},{3,7},{4,0},{5,1},{6,2},{7,3},{8,12},{9,13},{10,... | collective-permute-start | bytes 2162696 | tf_op jit(solution)/shard_map/ppermute | solution.py:48
  58.1 20.5 %collective-permute-start.18 = (bf16[4,32,2816]{2,1,0:T(8,128)(2,1)S(1)}, bf16[4,32,2816]{2,1,0:T(8,128)(2,1)S(1)}, u32[]{:S(2)}, u32[]{:S(2)}) collective-permute-start(bf16[4,32,2816]{2,1,0:T(8,128)(2,1)S(1)} %pad_maximum_fusion.2), channel_id=1, source_target_pairs={{0,2},{1,3},{2,0},{3,1},{4,6},{5,7},{6,4},{7,5},{8,10},{9,11},{10,... | collective-permute-start | bytes 2162696 | tf_op jit(solution)/shard_map/ppermute | solution.py:48
  78.7 31.8 %collective-permute-start.25 = (bf16[8,32,2816]{2,1,0:T(8,128)(2,1)S(1)}, bf16[8,32,2816]{2,1,0:T(8,128)(2,1)S(1)}, u32[]{:S(2)}, u32[]{:S(2)}) collective-permute-start(bf16[8,32,2816]{2,1,0:T(8,128)(2,1)S(1)} %constant_dynamic-update-slice_fusion.16), channel_id=1, source_target_pairs={{0,4},{1,5},{2,6},{3,7},{4,0},{5,1},{6,2},{7,3},{8,12},{9,13},{10,... | collective-permute-start | bytes 4325384 | tf_op jit(solution)/shard_map/ppermute | solution.py:48
  80.2 19.1 %collective-permute-start.27 = (bf16[8,32,1408]{2,1,0:T(8,128)(2,1)S(1)}, bf16[8,32,1408]{2,1,0:T(8,128)(2,1)S(1)}, u32[]{:S(2)}, u32[]{:S(2)}) collective-permute-start(bf16[8,32,1408]{2,1,0:T(8,128)(2,1)S(1)} %constant_dynamic-update-slice_fusion), channel_id=1, source_target_pairs={{0,8},{1,9},{2,10},{3,11},{4,12},{5,13},{6,14},{7,15},{8,0},{9,1},... | collective-permute-start | bytes 2162696 | tf_op jit(solution)/shard_map/ppermute | solution.py:48
  80.3 30.2 %collective-permute-start.28 = (bf16[8,32,1408]{2,1,0:T(8,128)(2,1)S(1)}, bf16[8,32,1408]{2,1,0:T(8,128)(2,1)S(1)}, u32[]{:S(2)}, u32[]{:S(2)}) collective-permute-start(bf16[8,32,1408]{2,1,0:T(8,128)(2,1)S(1)} %collective-permute-done.20), channel_id=1, source_target_pairs={{0,8},{1,9},{2,10},{3,11},{4,12},{5,13},{6,14},{7,15},{8,0},{9,1},... | collective-permute-start | bytes 2162696 | tf_op jit(solution)/shard_map/ppermute | solution.py:48
  82.4 32.6 %collective-permute-start.26 = (bf16[8,32,2816]{2,1,0:T(8,128)(2,1)S(1)}, bf16[8,32,2816]{2,1,0:T(8,128)(2,1)S(1)}, u32[]{:S(2)}, u32[]{:S(2)}) collective-permute-start(bf16[8,32,2816]{2,1,0:T(8,128)(2,1)S(1)} %constant_dynamic-update-slice_fusion.18), channel_id=1, source_target_pairs={{0,2},{1,3},{2,0},{3,1},{4,6},{5,7},{6,4},{7,5},{8,10},{9,11},{10,... | collective-permute-start | bytes 4325384 | tf_op jit(solution)/shard_map/ppermute | solution.py:48
  98.4 16.7 %collective-permute-start.22 = (bf16[256,1024]{1,0:T(8,128)(2,1)S(1)}, bf16[256,1024]{1,0:T(8,128)(2,1)S(1)}, u32[]{:S(2)}, u32[]{:S(2)}) collective-permute-start(bf16[256,1024]{1,0:T(8,128)(2,1)S(1)} %get-tuple-element.314.refs_1_), channel_id=1, source_target_pairs={{0,1},{1,0},{2,3},{3,2},{4,5},{5,4},{6,7},{7,6},{8,9},{9,8},{10,11... | collective-permute-start | bytes 1572872 | tf_op jit(solution)/shard_map/ppermute | solution.py:48
  99.4 15.7 %collective-permute-start.23 = (bf16[256,1024]{1,0:T(8,128)(2,1)S(1)}, bf16[256,1024]{1,0:T(8,128)(2,1)S(1)}, u32[]{:S(2)}, u32[]{:S(2)}) collective-permute-start(bf16[256,1024]{1,0:T(8,128)(2,1)S(1)} %get-tuple-element.315.refs_2_), channel_id=1, source_target_pairs={{0,1},{1,0},{2,3},{3,2},{4,5},{5,4},{6,7},{7,6},{8,9},{9,8},{10,11... | collective-permute-start | bytes 1572872 | tf_op jit(solution)/shard_map/ppermute | solution.py:48
  137.5 25.5 %collective-permute-start.32 = (bf16[8,32,2048]{2,1,0:T(8,128)(2,1)}, bf16[8,32,2048]{2,1,0:T(8,128)(2,1)}, u32[]{:S(2)}, u32[]{:S(2)}) collective-permute-start(bf16[8,32,2048]{2,1,0:T(8,128)(2,1)} %bitcast.30), channel_id=1, source_target_pairs={{0,2},{1,3},{2,0},{3,1},{4,6},{5,7},{6,4},{7,5},{8,10},{9,11},{10,... | collective-permute-start | bytes 3145736 | tf_op jit(solution)/shard_map/ppermute | solution.py:48
  139.0 25.2 %collective-permute-start.31 = (bf16[8,32,2048]{2,1,0:T(8,128)(2,1)}, bf16[8,32,2048]{2,1,0:T(8,128)(2,1)}, u32[]{:S(2)}, u32[]{:S(2)}) collective-permute-start(bf16[8,32,2048]{2,1,0:T(8,128)(2,1)} %bitcast.29), channel_id=1, source_target_pairs={{0,4},{1,5},{2,6},{3,7},{4,0},{5,1},{6,2},{7,3},{8,12},{9,13},{10,... | collective-permute-start | bytes 3145736 | tf_op jit(solution)/shard_map/ppermute | solution.py:48
  146.9 19.6 %collective-permute-start.30 = (bf16[512,1024]{1,0:T(8,128)(2,1)S(1)}, bf16[512,1024]{1,0:T(8,128)(2,1)S(1)}, u32[]{:S(2)}, u32[]{:S(2)}) collective-permute-start(bf16[512,1024]{1,0:T(8,128)(2,1)S(1)} %get-tuple-element.366.refs_1_), channel_id=1, source_target_pairs={{0,1},{1,0},{2,3},{3,2},{4,5},{5,4},{6,7},{7,6},{8,9},{9,8},{10,11... | collective-permute-start | bytes 3145736 | tf_op jit(solution)/shard_map/ppermute | solution.py:48
  147.0 19.5 %collective-permute-start.29 = (bf16[512,1024]{1,0:T(8,128)(2,1)S(1)}, bf16[512,1024]{1,0:T(8,128)(2,1)S(1)}, u32[]{:S(2)}, u32[]{:S(2)}) collective-permute-start(bf16[512,1024]{1,0:T(8,128)(2,1)S(1)} %get-tuple-element.352.refs_0_), channel_id=1, source_target_pairs={{0,1},{1,0},{2,3},{3,2},{4,5},{5,4},{6,7},{7,6},{8,9},{9,8},{10,11... | collective-permute-start | bytes 3145736 | tf_op jit(solution)/shard_map/ppermute | solution.py:48
  150.5 23.3 %collective-permute-start.33 = (bf16[16,32,768]{2,1,0:T(8,128)(2,1)S(1)}, bf16[16,32,768]{2,1,0:T(8,128)(2,1)S(1)}, u32[]{:S(2)}, u32[]{:S(2)}) collective-permute-start(bf16[16,32,768]{2,1,0:T(8,128)(2,1)S(1)} %bitcast.80), channel_id=1, source_target_pairs={{0,8},{1,9},{2,10},{3,11},{4,12},{5,13},{6,14},{7,15},{8,0},{9,1},... | collective-permute-start | bytes 2359304 | tf_op jit(solution)/shard_map/ppermute | solution.py:48
  166.5 26.5 %collective-permute-start.36 = (bf16[8,32,1408]{2,1,0:T(8,128)(2,1)S(1)}, bf16[8,32,1408]{2,1,0:T(8,128)(2,1)S(1)}, u32[]{:S(2)}, u32[]{:S(2)}) collective-permute-start(bf16[8,32,1408]{2,1,0:T(8,128)(2,1)S(1)} %bitcast.84), channel_id=1, source_target_pairs={{0,4},{1,5},{2,6},{3,7},{4,0},{5,1},{6,2},{7,3},{8,12},{9,13},{10,... | collective-permute-start | bytes 2162696 | tf_op jit(solution)/shard_map/ppermute | solution.py:48
  167.1 25.9 %collective-permute-start.37 = (bf16[8,32,1408]{2,1,0:T(8,128)(2,1)S(1)}, bf16[8,32,1408]{2,1,0:T(8,128)(2,1)S(1)}, u32[]{:S(2)}, u32[]{:S(2)}) collective-permute-start(bf16[8,32,1408]{2,1,0:T(8,128)(2,1)S(1)} %bitcast.83), channel_id=1, source_target_pairs={{0,2},{1,3},{2,0},{3,1},{4,6},{5,7},{6,4},{7,5},{8,10},{9,11},{10,... | collective-permute-start | bytes 2162696 | tf_op jit(solution)/shard_map/ppermute | solution.py:48
  174.2 18.8 %collective-permute-start.38 = (bf16[8,32,768]{2,1,0:T(8,128)(2,1)S(1)}, bf16[8,32,768]{2,1,0:T(8,128)(2,1)S(1)}, u32[]{:S(2)}, u32[]{:S(2)}) collective-permute-start(bf16[8,32,768]{2,1,0:T(8,128)(2,1)S(1)} %get-tuple-element.395), channel_id=1, source_target_pairs={{0,16},{1,17},{2,18},{3,19},{4,20},{5,21},{6,22},{7,23},{8,24},{9,... | collective-permute-start | bytes 1179656 | tf_op jit(solution)/shard_map/ppermute | solution.py:48
  176.1 20.0 %collective-permute-start.34 = (bf16[4,32,2048]{2,1,0:T(8,128)(2,1)S(1)}, bf16[4,32,2048]{2,1,0:T(8,128)(2,1)S(1)}, u32[]{:S(2)}, u32[]{:S(2)}) collective-permute-start(bf16[4,32,2048]{2,1,0:T(8,128)(2,1)S(1)} %get-tuple-element.391), channel_id=1, source_target_pairs={{0,2},{1,3},{2,0},{3,1},{4,6},{5,7},{6,4},{7,5},{8,10},{9,11},{10,... | collective-permute-start | bytes 1572872 | tf_op jit(solution)/shard_map/ppermute | solution.py:48
  176.6 19.6 %collective-permute-start.35 = (bf16[4,32,2048]{2,1,0:T(8,128)(2,1)S(1)}, bf16[4,32,2048]{2,1,0:T(8,128)(2,1)S(1)}, u32[]{:S(2)}, u32[]{:S(2)}) collective-permute-start(bf16[4,32,2048]{2,1,0:T(8,128)(2,1)S(1)} %get-tuple-element.392), channel_id=1, source_target_pairs={{0,4},{1,5},{2,6},{3,7},{4,0},{5,1},{6,2},{7,3},{8,12},{9,13},{10,... | collective-permute-start | bytes 1572872 | tf_op jit(solution)/shard_map/ppermute | solution.py:48
  201.4 18.6 %collective-permute-start.41 = (bf16[8,32,1408]{2,1,0:T(8,128)(2,1)S(1)}, bf16[8,32,1408]{2,1,0:T(8,128)(2,1)S(1)}, u32[]{:S(2)}, u32[]{:S(2)}) collective-permute-start(bf16[8,32,1408]{2,1,0:T(8,128)(2,1)S(1)} %bitcast.88), channel_id=1, source_target_pairs={{0,4},{1,5},{2,6},{3,7},{4,0},{5,1},{6,2},{7,3},{8,12},{9,13},{10,... | collective-permute-start | bytes 2162696 | tf_op jit(solution)/shard_map/ppermute | solution.py:48
  202.0 18.1 %collective-permute-start.42 = (bf16[8,32,1408]{2,1,0:T(8,128)(2,1)S(1)}, bf16[8,32,1408]{2,1,0:T(8,128)(2,1)S(1)}, u32[]{:S(2)}, u32[]{:S(2)}) collective-permute-start(bf16[8,32,1408]{2,1,0:T(8,128)(2,1)S(1)} %bitcast.87), channel_id=1, source_target_pairs={{0,2},{1,3},{2,0},{3,1},{4,6},{5,7},{6,4},{7,5},{8,10},{9,11},{10,... | collective-permute-start | bytes 2162696 | tf_op jit(solution)/shard_map/ppermute | solution.py:48
  206.2 19.6 %collective-permute-start.45 = (bf16[2,2,32,2048]{3,2,1,0:T(8,128)(2,1)S(1)}, bf16[2,2,32,2048]{3,2,1,0:T(8,128)(2,1)S(1)}, u32[]{:S(2)}, u32[]{:S(2)}) collective-permute-start(bf16[2,2,32,2048]{3,2,1,0:T(8,128)(2,1)S(1)} %get-tuple-element.456), channel_id=1, source_target_pairs={{0,8},{1,9},{2,10},{3,11},{4,12},{5,13},{6,14},{7,15},{8,0},{9,1},... | collective-permute-start | bytes 1572872 | tf_op jit(solution)/shard_map/ppermute | solution.py:48
  206.3 19.3 %collective-permute-start.46 = (bf16[2,2,32,1408]{3,2,1,0:T(8,128)(2,1)S(1)}, bf16[2,2,32,1408]{3,2,1,0:T(8,128)(2,1)S(1)}, u32[]{:S(2)}, u32[]{:S(2)}) collective-permute-start(bf16[2,2,32,1408]{3,2,1,0:T(8,128)(2,1)S(1)} %get-tuple-element.457), channel_id=1, source_target_pairs={{0,8},{1,9},{2,10},{3,11},{4,12},{5,13},{6,14},{7,15},{8,0},{9,1},... | collective-permute-start | bytes 1081352 | tf_op jit(solution)/shard_map/ppermute | solution.py:48
  231.3 17.7 %collective-permute-start.49 = (bf16[2,2,32,1408]{3,2,1,0:T(8,128)(2,1)S(1)}, bf16[2,2,32,1408]{3,2,1,0:T(8,128)(2,1)S(1)}, u32[]{:S(2)}, u32[]{:S(2)}) collective-permute-start(bf16[2,2,32,1408]{3,2,1,0:T(8,128)(2,1)S(1)} %get-tuple-element.481), channel_id=1, source_target_pairs={{0,8},{1,9},{2,10},{3,11},{4,12},{5,13},{6,14},{7,15},{8,0},{9,1},... | collective-permute-start | bytes 1081352 | tf_op jit(solution)/shard_map/ppermute | solution.py:48
  231.3 25.8 %collective-permute-start.56 = (bf16[1,2,32,1408]{3,2,1,0:T(8,128)(2,1)S(1)}, bf16[1,2,32,1408]{3,2,1,0:T(8,128)(2,1)S(1)}, u32[]{:S(2)}, u32[]{:S(2)}) collective-permute-start(bf16[1,2,32,1408]{3,2,1,0:T(8,128)(2,1)S(1)} %get-tuple-element.506), channel_id=1, source_target_pairs={{0,16},{1,17},{2,18},{3,19},{4,20},{5,21},{6,22},{7,23},{8,24},{9,... | collective-permute-start | bytes 540680 | tf_op jit(solution)/shard_map/ppermute | solution.py:48
  234.0 24.3 %collective-permute-start.55 = (bf16[1,2,32,2048]{3,2,1,0:T(8,128)(2,1)S(1)}, bf16[1,2,32,2048]{3,2,1,0:T(8,128)(2,1)S(1)}, u32[]{:S(2)}, u32[]{:S(2)}) collective-permute-start(bf16[1,2,32,2048]{3,2,1,0:T(8,128)(2,1)S(1)} %get-tuple-element.505), channel_id=1, source_target_pairs={{0,16},{1,17},{2,18},{3,19},{4,20},{5,21},{6,22},{7,23},{8,24},{9,... | collective-permute-start | bytes 786440 | tf_op jit(solution)/shard_map/ppermute | solution.py:48
  (59 other events, 612.0 us)
